TPU v7x, 32 devices: a whole 2x2x4 slice. The times are simulated.
32 devices in a mesh: az: 4 (over y, x), ax: 4 (over z), pl: 2 (over core).
Axes of the slice: x: 2, y: 2, z: 4, core: 2. Of those that a mesh axis runs over, the one named last changes fastest.
Arguments:
- cells: float32 [2, 10, 32, 32768], P('pl', None, 'ax', 'az'), may hold values from 0.05 to 3, as said below
- speeds: float32 [2, 2, 32, 32768], P('pl', None, 'ax', 'az'), may hold values from -1 to 1
- supply: float32 [10, 4, 32768], P(None, 'ax', 'az'), may hold values from 0.25 to 2
- mix: float32 [9, 9], replicated, may hold values from -2 to 2
- prefactor: float32 [9], replicated, may hold values from 1 to 4
- activation: float32 [9], replicated, may hold values from 1 to 4
- heat: float32 [9], replicated, may hold values from 0.5 to 2
- inj_column: int32 [128, 1], P(('az', 'ax')), may hold values from 0 to 3; in each aligned block of 8 rows (0 to 7, 8 to 15, ...) at most 4 rows name the same one
- inj_slot: int32 [128], P(('az', 'ax')), may hold values from 0 to 7
- inj_open: int32 [128], P(('az', 'ax')), may hold values 0 or 1
Outputs:
- cells_next: float32 [2, 10, 32, 32768], P('pl', None, 'ax', 'az')
Inputs may be any that keep to these rules, and one draw needn't show every extreme that they name: `cells`: the last component (temperature) is at least 0.25; species densities are positive. `inj_column`: within the 8 blocks of one device at most 4 name one column, a bound that some block reaches.
All inputs are finite; a program needn't handle non-finite values. No bound on the sum of `inj_open` on one device may be relied on, other than what follows from the above.
Results may differ from a plain program's by a relative error of at most 0.00005.
Values sent between devices are 32-bit elements; how exact they have to be, the bound alone decides.
No kernel may reach another device: no remote copies, remote signals or barrier semaphores. Data moves between devices by JAX's collectives and lax.ppermute only.
A program may use at most 128 MiB of HBM per device.

v0:
```python
import jax
import jax.numpy as jnp
from jax import lax
from jax.sharding import PartitionSpec as P

NV = 10
NR = 64
CAZ = 128
CAX = 8
TB = 16


step_dt = 0.2
high = lax.Precision.HIGHEST


def with_halo(cells, sides, width):
    for axis, dim in sides:
        count = lax.axis_size(axis)
        head = lax.slice_in_dim(cells, 0, width, axis=dim)
        tail = lax.slice_in_dim(cells, cells.shape[dim] - width, cells.shape[dim], axis=dim)
        cells = jnp.concatenate(
            [
                lax.ppermute(tail, axis, [(i, (i + 1) % count) for i in range(count)]),
                cells,
                lax.ppermute(head, axis, [((i + 1) % count, i) for i in range(count)]),
            ],
            axis=dim,
        )
    return cells


def swapped(array, axis, distance):
    return lax.ppermute(array, axis, [(i, i ^ 1 << distance) for i in range(lax.axis_size(axis))])


def divergence(field, vel, dim):
    count = field.shape[dim]
    lower = lax.slice_in_dim(field, 0, count - 1, axis=field.ndim + dim)
    upper = lax.slice_in_dim(field, 1, count, axis=field.ndim + dim)
    vel_low = lax.slice_in_dim(vel, 0, count - 1, axis=vel.ndim + dim)
    vel_up = lax.slice_in_dim(vel, 1, count, axis=vel.ndim + dim)
    flux = 0.5 * (vel_low * lower + vel_up * upper) - 0.5 * (upper - lower)
    faces = count - 1
    axis = flux.ndim + dim
    return lax.slice_in_dim(flux, 1, faces, axis=axis) - lax.slice_in_dim(
        flux, 0, faces - 1, axis=axis
    )


def reaction(state, mix, prefactor, activation, heat):
    species = state[:-1]
    theta = jnp.maximum(state[-1], 0.5)
    shape_k = (-1,) + (1,) * (species.ndim - 1)
    rate = (
        prefactor.reshape(shape_k)
        * jnp.exp(-activation.reshape(shape_k) / theta[None])
        * jnp.maximum(species, 0.0)
    )
    dspec = jnp.einsum("vk,k...->v...", mix, rate, precision=high)
    dtheta = jnp.einsum("k,k...->...", heat, rate, precision=high)
    return jnp.concatenate([dspec, dtheta[None]], axis=0)


def local(cells, speeds, supply, mix, prefactor, activation, heat, inj_column, inj_slot, inj_open):
    n_az = lax.axis_size("az")
    n_ax = lax.axis_size("ax")
    is_plenum = lax.axis_index("pl") == 1
    ax_index = lax.axis_index("ax")
    blocks_dev = CAZ // TB
    tiles_col = CAZ // TB
    width = TB * NR
    state = cells[0].reshape(NV, CAX, CAZ, NR)
    vel = speeds[0].reshape(2, CAX, CAZ, NR)
    vel_pad = with_halo(vel, (("az", 2), ("ax", 1)), 1)
    u_az = vel_pad[0, 1:-1]
    w_full = vel_pad[1]
    keep_low = jnp.logical_and(jnp.logical_not(is_plenum), ax_index > 0)
    keep_high = jnp.logical_and(jnp.logical_not(is_plenum), ax_index < n_ax - 1)
    w_low = jnp.where(keep_low, w_full[:1, 1:-1], 0.0)
    w_high = jnp.where(keep_high, w_full[-1:, 1:-1], 0.0)
    w_ax = jnp.concatenate([w_low, w_full[1:-1, 1:-1], w_high], axis=0)
    supply_row = supply.reshape(NV, 1, CAZ, NR)
    column = inj_column[:, 0]
    open_plenum = inj_open.astype(jnp.float32) * is_plenum.astype(jnp.float32)

    def inlet_face(field):
        face_blocks = field[:, -1].reshape(NV, blocks_dev, width)
        tile = column * tiles_col + inj_slot
        tiles = jnp.arange(n_az * tiles_col, dtype=jnp.int32)
        weights = (tiles[:, None] == tile[None, :]).astype(jnp.float32) * open_plenum[None, :]
        dense = jnp.einsum("tb,vbx->vtx", weights, face_blocks, precision=high)
        part_sum = lax.psum_scatter(dense, "az", scatter_dimension=1, tiled=True)
        cycles_total = lax.psum(part_sum, "ax")
        first_row = field[:, 0].reshape(NV, tiles_col, width)
        outgoing = jnp.where(is_plenum, cycles_total, first_row)
        received = swapped(outgoing, "pl", 0)
        return received.reshape(NV, 1, CAZ, NR)

    def tendency(field):
        padded = with_halo(field, (("az", 2), ("ax", 1)), 1)
        received = inlet_face(field)
        neighbour_low = padded[:, :1, 1:-1]
        neighbour_high = padded[:, -1:, 1:-1]
        chamber_low = jnp.where(ax_index == 0, received, neighbour_low)
        row_low = jnp.where(is_plenum, supply_row, chamber_low)
        chamber_high = jnp.where(ax_index == n_ax - 1, field[:, -1:], neighbour_high)
        row_high = jnp.where(is_plenum, received, chamber_high)
        q_ax = jnp.concatenate([row_low, field, row_high], axis=1)
        moved = divergence(padded[:, 1:-1], u_az, -2) + divergence(q_ax, w_ax, -3)
        return -moved + reaction(field, mix, prefactor, activation, heat)

    section_one = state + step_dt * tendency(state)
    final = 0.5 * state + 0.5 * (section_one + step_dt * tendency(section_one))
    return final.reshape(1, NV, CAX, CAZ * NR)


def solution(mesh):
    return jax.shard_map(
        local,
        mesh=mesh,
        in_specs=(
            P("pl", None, "ax", "az"),
            P("pl", None, "ax", "az"),
            P(None, "ax", "az"),
            P(),
            P(),
            P(),
            P(),
            P(("az", "ax"), None),
            P(("az", "ax")),
            P(("az", "ax")),
        ),
        out_specs=P("pl", None, "ax", "az"),
        check_vma=False,
    )
```

profile of v0, /device:TPU:0, one launch (start us, length us, event | category | flops | bytes accessed | tf_op | source)
XLA Modules:
  0.0 290.2 jit_solution(3670830189013622497)
XLA Ops:
  6.5 5.5 %reshape_squeeze.18 = f32[10,8,128,64]{3,2,1,0:T(8,128)} reshape(f32[1,10,8,8192]{3,2,1,0:T(8,128)} %param.10) | data formatting | bytes 5242880 | tf_op jit(solution)/shard_map/reshape;squeeze | solution.py:73
  12.0 6.2 %copy.89 = f32[10,8,128,64]{2,0,3,1:T(8,128)} copy(f32[10,8,128,64]{3,2,1,0:T(8,128)} %reshape_squeeze.18) | data formatting | bytes 5242880 | tf_op jit(solution)/shard_map/reshape;squeeze | solution.py:73
  23.5 3.9 %collective-permute-start.3 = (f32[10,8,1,64]{3,1,2,0:T(8,128)S(1)}, f32[10,8,1,64]{3,1,2,0:T(8,128)S(1)}, u32[]{:S(2)}, u32[]{:S(2)}) collective-permute-start(f32[10,8,1,64]{3,1,2,0:T(8,128)S(1)} %bitcast.75), channel_id=1, source_target_pairs={{8,0},{16,8},{24,16},{0,24},{9,1},{17,9},{25,17},{1,25},{10,2},{18... | collective-permute-start | bytes 61448 | tf_op jit(solution)/shard_map/ppermute | solution.py:26
  28.0 3.0 %collective-permute-start.1 = (f32[2,8,1,64]{3,2,1,0:T(1,128)S(1)}, f32[2,8,1,64]{3,2,1,0:T(1,128)S(1)}, u32[]{:S(2)}, u32[]{:S(2)}) collective-permute-start(f32[2,8,1,64]{3,2,1,0:T(1,128)S(1)} %get-tuple-element.18), channel_id=1, source_target_pairs={{8,0},{16,8},{24,16},{0,24},{9,1},{17,9},{25,17},{1,25},{10,2},{18... | collective-permute-start | bytes 12296 | tf_op jit(solution)/shard_map/ppermute | solution.py:26
  30.9 3.4 %slice_maximum_fusion.1 = f32[1,9,8,8192]{3,2,1,0:T(8,128)} fusion(f32[1,10,8,8192]{3,2,1,0:T(8,128)} %param.10), kind=kLoop, calls=%fused_computation.35 | loop fusion | flops 589824 | bytes 4718592 | tf_op jit(solution)/shard_map/max | solution.py:58
  35.3 5.4 %max.26 = f32[9,8,128,64]{3,2,1,0:T(8,128)} reshape(f32[1,9,8,8192]{3,2,1,0:T(8,128)} %slice_maximum_fusion.1) | data formatting | bytes 4718592 | tf_op jit(solution)/shard_map/max | solution.py:58
  40.7 6.5 %copy.72 = f32[9,8,128,64]{2,0,3,1:T(8,128)} copy(f32[9,8,128,64]{3,2,1,0:T(8,128)} %max.26) | data formatting | bytes 4718592 | tf_op jit(solution)/shard_map/max | solution.py:58
  47.7 9.4 %convolution_bitcast_fusion.1 = f32[9,8,128,64]{2,0,3,1:T(8,128)} fusion(f32[9,9]{1,0:T(8,128)S(1)} %copy-done, f32[9,8,128,64]{2,0,3,1:T(8,128)} %copy.72, f32[8,128,64]{1,2,0:T(8,128)S(1)} %copy.71, f32[9]{0:T(128)S(1)} %neg.12, f32[9]{0:T(128)S(1)} %copy-done.22), kind=kOutput, calls=%fused_computation.37 | convolution fusion | flops 65470464 | bytes 4981132 | tf_op jit(solution)/shard_map/vk,k...->v.../dot_general | solution.py:60
  57.2 5.1 %fusion.35 = f32[1,8,128,64]{2,0,3,1:T(1,128)} fusion(f32[9]{0:T(128)S(1)} %copy-done.20, f32[9,8,128,64]{2,0,3,1:T(8,128)S(1)} %copy-done.6, f32[8,128,64]{1,2,0:T(8,128)S(1)} %copy.71, f32[9]{0:T(128)S(1)} %neg.12, f32[9]{0:T(128)S(1)} %copy-done.22), kind=kOutput, calls=%fused_computation.86 | convolution fusion | flops 8847360 | bytes 2883692 | tf_op jit(solution)/shard_map/k,k...->.../dot_general | solution.py:61
  65.4 3.6 %collective-permute-start.5 = (f32[2,1,130,64]{3,2,1,0:T(8,128)}, f32[2,1,130,64]{3,2,1,0:T(8,128)}, u32[]{:S(2)}, u32[]{:S(2)}) collective-permute-start(f32[2,1,130,64]{3,2,1,0:T(8,128)} %get-tuple-element.16), channel_id=1, source_target_pairs={{2,0},{4,2},{6,4},{0,6},{3,1},{5,3},{7,5},{1,7},{10,8},{12,10},{14... | collective-permute-start | bytes 199688 | tf_op jit(solution)/shard_map/ppermute | solution.py:26
  77.9 3.8 %collective-permute-start.8 = (f32[10,1,130,64]{2,3,1,0:T(8,128)}, f32[10,1,130,64]{2,3,1,0:T(8,128)}, u32[]{:S(2)}, u32[]{:S(2)}) collective-permute-start(f32[10,1,130,64]{2,3,1,0:T(8,128)} %copy.67), channel_id=1, source_target_pairs={{2,0},{4,2},{6,4},{0,6},{3,1},{5,3},{7,5},{1,7},{10,8},{12,10},{14... | collective-permute-start | bytes 998408 | tf_op jit(solution)/shard_map/ppermute | solution.py:26
  81.7 2.8 copy.55
  84.5 2.8 copy.50
  87.3 9.7 %multiply_subtract_fusion.1 = f32[10,8,129,64]{2,0,3,1:T(8,128)} fusion(f32[10,8,1,64]{2,0,3,1:T(8,128)} %copy.55, f32[10,8,128,64]{2,0,3,1:T(8,128)} %copy.89, f32[10,8,1,64]{2,0,3,1:T(8,128)} %copy.50, f32[8,129,64]{1,2,0:T(8,128)S(1)} %copy.52, f32[8,129,64]{1,2,0:T(8,128)S(1)} %copy.48), kind=kLoop, calls=%fused_computation.5 | loop fusion | flops 5944320 | bytes 5832704 | tf_op jit(solution)/shard_map/sub | solution.py:43
  98.8 34.2 %all-reduce.3.cloned.1.call-done = f32[10,8,1024]{2,1,0:T(8,128)} async-done(((f32[10,8,1024]{2,1,0:T(8,128)}), f32[10,8,1024]{2,1,0:T(8,128)}) %all-reduce.3.cloned.1.call-update) | async-done | bytes 327696 | tf_op jit(solution)/shard_map/psum | solution.py:94
  144.7 4.4 %multiply_subtract_fusion.3 = f32[10,9,128,64]{2,0,3,1:T(8,128)S(1)} fusion(f32[10,1,128,64]{2,0,3,1:T(8,128)S(1)} %get-tuple-element.28, f32[10,8,128,64]{2,0,3,1:T(8,128)} %copy.89, f32[10,1,128,64]{2,0,3,1:T(8,128)S(1)} %get-tuple-element.27, f32[9,128,64]{1,2,0:T(8,128)S(1)} %copy.66, f32[9,128,64]{1,2,0:T(8,128)S(1)} %copy.56), kind=kLoop, calls=%fused_computation.11 | loop fusion | flops 6635520 | bytes 6815744 | tf_op jit(solution)/shard_map/sub | solution.py:43
  150.6 5.9 %fusion.15 = f32[10,8,128,64]{2,0,3,1:T(8,128)S(1)} fusion(f32[10,8,128,64]{2,0,3,1:T(8,128)S(1)} %copy-done.3, f32[10,9,128,64]{2,0,3,1:T(8,128)S(1)} %multiply_subtract_fusion.3, f32[10,8,129,64]{2,0,3,1:T(8,128)} %multiply_subtract_fusion.1, f32[1,8,128,64]{2,0,3,1:T(1,128)S(1)} %copy-done.10, f32[9,8,128,64]{2,0,3,1:T(8,128)S(1)} %copy-done.5), kind=kLoop, calls=%fused_computation.33 | loop fusion | flops 5242880 | bytes 18350080 | tf_op jit(solution)/shard_map/add | solution.py:113
  161.6 3.4 %convolution_bitcast_fusion.2 = f32[10,32,1024]{2,1,0:T(8,128)} fusion(f32[10,8,1024]{2,1,0:T(8,128)} %reshape_squeeze.22, f32[8]{0:T(128)S(1)} %copy-done.13, s32[8]{0:T(128)S(1)} %copy-done.15), kind=kOutput, calls=%fused_computation.38 | convolution fusion | flops 31457792 | bytes 1638464 | tf_op jit(solution)/shard_map/tb,vbx->vtx/dot_general | solution.py:92
  165.0 8.0 %fusion.44 = (f32[10,8,1,64]{2,0,3,1:T(8,128)}, f32[10,8,1,64]{2,0,3,1:T(8,128)}) fusion(f32[10,8,128,64]{2,0,3,1:T(8,128)} %copy-done.1), kind=kLoop, calls=%fused_computation.93 | loop fusion | bytes 81920 | tf_op jit(solution)/shard_map/slice | solution.py:21
  173.1 3.0 %copy.76 = f32[10,8,1,64]{3,1,2,0:T(8,128)S(1)} copy(f32[10,8,1,64]{2,0,3,1:T(8,128)} %get-tuple-element.12) | data formatting | bytes 40960 | tf_op jit(solution)/shard_map/slice | solution.py:20
  178.7 3.0 %copy.74 = f32[10,8,1,64]{3,1,2,0:T(8,128)S(1)} copy(f32[10,8,1,64]{2,0,3,1:T(8,128)} %get-tuple-element.11) | data formatting | bytes 40960 | tf_op jit(solution)/shard_map/slice | solution.py:21
  183.7 9.4 %convolution_bitcast_fusion = f32[9,8,128,64]{2,0,3,1:T(8,128)} fusion(f32[9,9]{1,0:T(8,128)S(1)} %copy-done, f32[10,8,128,64]{2,0,3,1:T(8,128)} %copy-done.1, f32[8,128,64]{1,2,0:T(8,128)S(1)} %bitcast.70, f32[9]{0:T(128)S(1)} %copy-done.25, f32[9]{0:T(128)S(1)} %copy-done.23), kind=kOutput, calls=%fused_computation.36 | convolution fusion | flops 66060288 | bytes 5243276 | tf_op jit(solution)/shard_map/vk,k...->v.../dot_general | solution.py:60
  195.2 7.4 %fusion.33 = f32[1,8,128,64]{2,0,3,1:T(1,128)} fusion(f32[9]{0:T(128)S(1)} %copy-done.21, f32[10,8,128,64]{2,0,3,1:T(8,128)} %copy-done.1, f32[8,128,64]{1,2,0:T(8,128)S(1)} %bitcast.71, f32[9]{0:T(128)S(1)} %copy-done.25, f32[9]{0:T(128)S(1)} %copy-done.23), kind=kOutput, calls=%fused_computation.84 | convolution fusion | flops 9437184 | bytes 3145836 | tf_op jit(solution)/shard_map/k,k...->.../dot_general | solution.py:61
  203.7 3.1 %copy.77 = f32[10,8,1,64]{2,0,3,1:T(8,128)} copy(f32[10,8,1,64]{3,1,2,0:T(8,128)S(1)} %collective-permute-done.10) | data formatting | bytes 40960 | tf_op jit(solution)/shard_map/ppermute | solution.py:26
  206.8 2.8 copy.75
  209.6 2.7 pad_maximum_fusion.11
  218.6 21.9 %all-reduce.5.cloned.1.call-done = f32[10,8,1024]{2,1,0:T(8,128)} async-done(((f32[10,8,1024]{2,1,0:T(8,128)}), f32[10,8,1024]{2,1,0:T(8,128)}) %all-reduce.5.cloned.1.call-update) | async-done | bytes 327696 | tf_op jit(solution)/shard_map/psum | solution.py:94
  241.6 10.0 %multiply_subtract_fusion = f32[10,8,129,64]{2,0,3,1:T(8,128)} fusion(f32[10,8,1,64]{2,0,3,1:T(8,128)} %copy.77, f32[10,8,128,64]{2,0,3,1:T(8,128)} %copy-done.1, f32[10,8,1,64]{2,0,3,1:T(8,128)} %copy.75, f32[8,129,64]{1,2,0:T(8,128)S(1)} %copy.52, f32[8,129,64]{1,2,0:T(8,128)S(1)} %copy.48), kind=kLoop, calls=%fused_computation.4 | loop fusion | flops 5944320 | bytes 5832704 | tf_op jit(solution)/shard_map/sub | solution.py:43
  258.9 4.4 %multiply_subtract_fusion.2 = f32[10,9,128,64]{2,0,3,1:T(8,128)S(1)} fusion(f32[10,1,128,64]{2,0,3,1:T(8,128)S(1)} %get-tuple-element.24, f32[10,8,128,64]{2,0,3,1:T(8,128)} %copy-done.1, f32[10,1,128,64]{2,0,3,1:T(8,128)S(1)} %get-tuple-element.23, f32[9,128,64]{1,2,0:T(8,128)S(1)} %copy.66, f32[9,128,64]{1,2,0:T(8,128)S(1)} %copy.56), kind=kLoop, calls=%fused_computation.10 | loop fusion | flops 6635520 | bytes 6815744 | tf_op jit(solution)/shard_map/sub | solution.py:43
  264.9 7.2 %fusion.10 = f32[10,8,128,64]{2,0,3,1:T(8,128)} fusion(f32[10,8,128,64]{2,0,3,1:T(8,128)S(1)} %copy-done.4, f32[10,8,128,64]{2,0,3,1:T(8,128)S(1)} %copy-done.2, f32[10,9,128,64]{2,0,3,1:T(8,128)S(1)} %multiply_subtract_fusion.2, f32[10,8,129,64]{2,0,3,1:T(8,128)} %multiply_subtract_fusion, f32[1,8,128,64]{2,0,3,1:T(1,128)S(1)} %copy-done.11, ...), kind=kLoop, calls=%fused_computation.26 | loop fusion | flops 6553600 | bytes 20971520 | tf_op jit(solution)/shard_map/add | solution.py:114
  272.1 5.7 %copy.90 = f32[10,8,128,64]{3,2,1,0:T(8,128)} copy(f32[10,8,128,64]{2,0,3,1:T(8,128)} %fusion.10) | data formatting | bytes 5242880 | tf_op jit(solution)/shard_map/add | solution.py:114
  277.8 5.4 %reshape.42 = f32[1,10,8,8192]{3,2,1,0:T(8,128)} reshape(f32[10,8,128,64]{3,2,1,0:T(8,128)} %copy.90) | data formatting | bytes 5242880 | tf_op jit(solution)/shard_map/reshape | solution.py:115
  (140 shorter events, 63.1 us)
Async XLA Ops:
  6.5 41.1 %copy-start = (f32[9,9]{1,0:T(8,128)S(1)}, f32[9,9]{1,0:T(8,128)}, u32[]{:S(2)}) copy-start(f32[9,9]{1,0:T(8,128)} %param.13) | copy-start | bytes 976
  6.5 80.7 %reduce-scatter.3.cloned.1.call-start = ((), (), s32[]{:S(2)}) async-start(), calls=%async_computation.2 | async-start | bytes 1638400 | tf_op jit(solution)/shard_map/reduce_scatter | solution.py:93
  12.0 7.9 %copy-start.16 = (s32[8]{0:T(128)S(1)}, s32[8]{0:T(128)}, u32[]{:S(2)}) copy-start(s32[8]{0:T(128)} %param.19) | copy-start | bytes 100
  12.0 7.9 %copy-start.17 = (s32[8]{0:T(128)S(1)}, s32[8]{0:T(128)}, u32[]{:S(2)}) copy-start(s32[8]{0:T(128)} %param.18) | copy-start | bytes 100
  12.0 7.9 %copy-start.18 = (s32[8,1]{0,1:T(1,128)S(1)}, s32[8,1]{0,1:T(1,128)}, u32[]{:S(2)}) copy-start(s32[8,1]{0,1:T(1,128)} %param.17) | copy-start | bytes 100
  18.3 9.2 %copy-start.8 = (f32[1,2,8,8192]{3,2,1,0:T(8,128)S(1)}, f32[1,2,8,8192]{3,2,1,0:T(8,128)}, u32[]{:S(2)}) copy-start(f32[1,2,8,8192]{3,2,1,0:T(8,128)} %param.11) | copy-start | bytes 1572868
  19.9 7.6 %copy-start.12 = (f32[8]{0:T(128)}, f32[8]{0:T(128)S(1)}, u32[]{:S(2)}) copy-start(f32[8]{0:T(128)S(1)} %convert_multiply_fusion) | copy-start | bytes 100
  20.0 7.5 %copy-start.14 = (s32[8]{0:T(128)}, s32[8]{0:T(128)S(1)}, u32[]{:S(2)}) copy-start(s32[8]{0:T(128)S(1)} %bitcast_add_fusion) | copy-start | bytes 100
  22.4 110.7 %all-reduce.3.cloned.1.call-start = ((), (), s32[]{:S(2)}) async-start(), calls=%async_computation.3 | async-start | bytes 655360 | tf_op jit(solution)/shard_map/psum | solution.py:94
  23.5 48.4 %collective-permute-start.3 = (f32[10,8,1,64]{3,1,2,0:T(8,128)S(1)}, f32[10,8,1,64]{3,1,2,0:T(8,128)S(1)}, u32[]{:S(2)}, u32[]{:S(2)}) collective-permute-start(f32[10,8,1,64]{3,1,2,0:T(8,128)S(1)} %bitcast.75), channel_id=1, source_target_pairs={{8,0},{16,8},{24,16},{0,24},{9,1},{17,9},{25,17},{1,25},{10,2},{18... | collective-permute-start | bytes 61448 | tf_op jit(solution)/shard_map/ppermute | solution.py:26
  27.5 44.5 %collective-permute-start.2 = (f32[10,8,1,64]{3,1,2,0:T(8,128)S(1)}, f32[10,8,1,64]{3,1,2,0:T(8,128)S(1)}, u32[]{:S(2)}, u32[]{:S(2)}) collective-permute-start(f32[10,8,1,64]{3,1,2,0:T(8,128)S(1)} %bitcast.74), channel_id=1, source_target_pairs={{0,8},{8,16},{16,24},{24,0},{1,9},{9,17},{17,25},{25,1},{2,10},{10... | collective-permute-start | bytes 61448 | tf_op jit(solution)/shard_map/ppermute | solution.py:24
  28.0 36.7 %collective-permute-start.1 = (f32[2,8,1,64]{3,2,1,0:T(1,128)S(1)}, f32[2,8,1,64]{3,2,1,0:T(1,128)S(1)}, u32[]{:S(2)}, u32[]{:S(2)}) collective-permute-start(f32[2,8,1,64]{3,2,1,0:T(1,128)S(1)} %get-tuple-element.18), channel_id=1, source_target_pairs={{8,0},{16,8},{24,16},{0,24},{9,1},{17,9},{25,17},{1,25},{10,2},{18... | collective-permute-start | bytes 12296 | tf_op jit(solution)/shard_map/ppermute | solution.py:26
  30.9 33.7 %collective-permute-start = (f32[2,8,1,64]{3,2,1,0:T(1,128)S(1)}, f32[2,8,1,64]{3,2,1,0:T(1,128)S(1)}, u32[]{:S(2)}, u32[]{:S(2)}) collective-permute-start(f32[2,8,1,64]{3,2,1,0:T(1,128)S(1)} %get-tuple-element.17), channel_id=1, source_target_pairs={{0,8},{8,16},{16,24},{24,0},{1,9},{9,17},{17,25},{25,1},{2,10},{10... | collective-permute-start | bytes 12296 | tf_op jit(solution)/shard_map/ppermute | solution.py:24
  40.7 6.9 %copy-start.22 = (f32[9]{0:T(128)S(1)}, f32[9]{0:T(128)}, u32[]{:S(2)}) copy-start(f32[9]{0:T(128)} %param.14) | copy-start | bytes 112
  47.7 9.5 %copy-start.24 = (f32[9]{0:T(128)}, f32[9]{0:T(128)S(1)}, u32[]{:S(2)}) copy-start(f32[9]{0:T(128)S(1)} %neg.12) | copy-start | bytes 112
  47.7 9.4 %copy-start.6 = (f32[9,8,128,64]{2,0,3,1:T(8,128)S(1)}, f32[9,8,128,64]{2,0,3,1:T(8,128)}, u32[]{:S(2)}) copy-start(f32[9,8,128,64]{2,0,3,1:T(8,128)} %copy.72) | copy-start | bytes 7077892
  47.7 9.4 %copy-start.20 = (f32[9]{0:T(128)S(1)}, f32[9]{0:T(128)}, u32[]{:S(2)}) copy-start(f32[9]{0:T(128)} %param.16) | copy-start | bytes 112
  65.4 31.6 %collective-permute-start.5 = (f32[2,1,130,64]{3,2,1,0:T(8,128)}, f32[2,1,130,64]{3,2,1,0:T(8,128)}, u32[]{:S(2)}, u32[]{:S(2)}) collective-permute-start(f32[2,1,130,64]{3,2,1,0:T(8,128)} %get-tuple-element.16), channel_id=1, source_target_pairs={{2,0},{4,2},{6,4},{0,6},{3,1},{5,3},{7,5},{1,7},{10,8},{12,10},{14... | collective-permute-start | bytes 199688 | tf_op jit(solution)/shard_map/ppermute | solution.py:26
  69.0 27.9 %collective-permute-start.4 = (f32[2,1,130,64]{3,2,1,0:T(8,128)}, f32[2,1,130,64]{3,2,1,0:T(8,128)}, u32[]{:S(2)}, u32[]{:S(2)}) collective-permute-start(f32[2,1,130,64]{3,2,1,0:T(8,128)} %get-tuple-element.15), channel_id=1, source_target_pairs={{0,2},{2,4},{4,6},{6,0},{1,3},{3,5},{5,7},{7,1},{8,10},{10,12},{12... | collective-permute-start | bytes 199688 | tf_op jit(solution)/shard_map/ppermute | solution.py:24
  76.6 59.9 %collective-permute-start.7 = (f32[10,1,130,64]{2,3,1,0:T(8,128)}, f32[10,1,130,64]{2,3,1,0:T(8,128)}, u32[]{:S(2)}, u32[]{:S(2)}) collective-permute-start(f32[10,1,130,64]{2,3,1,0:T(8,128)} %copy.61), channel_id=1, source_target_pairs={{0,2},{2,4},{4,6},{6,0},{1,3},{3,5},{5,7},{7,1},{8,10},{10,12},{12... | collective-permute-start | bytes 998408 | tf_op jit(solution)/shard_map/ppermute | solution.py:24
  77.9 60.7 %collective-permute-start.8 = (f32[10,1,130,64]{2,3,1,0:T(8,128)}, f32[10,1,130,64]{2,3,1,0:T(8,128)}, u32[]{:S(2)}, u32[]{:S(2)}) collective-permute-start(f32[10,1,130,64]{2,3,1,0:T(8,128)} %copy.67), channel_id=1, source_target_pairs={{2,0},{4,2},{6,4},{0,6},{3,1},{5,3},{7,5},{1,7},{10,8},{12,10},{14... | collective-permute-start | bytes 998408 | tf_op jit(solution)/shard_map/ppermute | solution.py:26
  87.3 107.9 %reduce-scatter.5.cloned.1.call-start = ((), (), s32[]{:S(2)}) async-start(), calls=%async_computation.4 | async-start | bytes 1638400 | tf_op jit(solution)/shard_map/reduce_scatter | solution.py:93
  134.8 5.7 %collective-permute-start.6 = (f32[10,8,1024]{2,1,0:T(8,128)}, f32[10,8,1024]{2,1,0:T(8,128)}, u32[]{:S(2)}, u32[]{:S(2)}) collective-permute-start(f32[10,8,1024]{2,1,0:T(8,128)} %broadcast_select_fusion.1), channel_id=1, source_target_pairs={{0,1},{1,0},{2,3},{3,2},{4,5},{5,4},{6,7},{7,6},{8,9},{9,8},{10,11... | collective-permute-start | bytes 983048 | tf_op jit(solution)/shard_map/ppermute | solution.py:34
  165.0 75.5 %all-reduce.5.cloned.1.call-start = ((), (), s32[]{:S(2)}) async-start(), calls=%async_computation.5 | async-start | bytes 655360 | tf_op jit(solution)/shard_map/psum | solution.py:94
  173.1 10.6 %copy-start.23 = (f32[9]{0:T(128)S(1)}, f32[9]{0:T(128)}, u32[]{:S(2)}) copy-start(f32[9]{0:T(128)} %param.14) | copy-start | bytes 112
  173.1 10.6 %copy-start.25 = (f32[9]{0:T(128)S(1)}, f32[9]{0:T(128)}, u32[]{:S(2)}) copy-start(f32[9]{0:T(128)} %copy-done.24) | copy-start | bytes 112
  176.1 27.7 %collective-permute-start.10 = (f32[10,8,1,64]{3,1,2,0:T(8,128)S(1)}, f32[10,8,1,64]{3,1,2,0:T(8,128)S(1)}, u32[]{:S(2)}, u32[]{:S(2)}) collective-permute-start(f32[10,8,1,64]{3,1,2,0:T(8,128)S(1)} %copy.76), channel_id=1, source_target_pairs={{8,0},{16,8},{24,16},{0,24},{9,1},{17,9},{25,17},{1,25},{10,2},{18... | collective-permute-start | bytes 61448 | tf_op jit(solution)/shard_map/ppermute | solution.py:26
  181.7 25.1 %collective-permute-start.9 = (f32[10,8,1,64]{3,1,2,0:T(8,128)S(1)}, f32[10,8,1,64]{3,1,2,0:T(8,128)S(1)}, u32[]{:S(2)}, u32[]{:S(2)}) collective-permute-start(f32[10,8,1,64]{3,1,2,0:T(8,128)S(1)} %copy.74), channel_id=1, source_target_pairs={{0,8},{8,16},{16,24},{24,0},{1,9},{9,17},{17,25},{25,1},{2,10},{10... | collective-permute-start | bytes 61448 | tf_op jit(solution)/shard_map/ppermute | solution.py:24
  183.7 11.5 %copy-start.21 = (f32[9]{0:T(128)S(1)}, f32[9]{0:T(128)}, u32[]{:S(2)}) copy-start(f32[9]{0:T(128)} %param.16) | copy-start | bytes 112
  213.5 38.1 %collective-permute-start.12 = (f32[10,1,130,64]{2,3,1,0:T(8,128)}, f32[10,1,130,64]{2,3,1,0:T(8,128)}, u32[]{:S(2)}, u32[]{:S(2)}) collective-permute-start(f32[10,1,130,64]{2,3,1,0:T(8,128)} %copy.82), channel_id=1, source_target_pairs={{0,2},{2,4},{4,6},{6,0},{1,3},{3,5},{5,7},{7,1},{8,10},{10,12},{12... | collective-permute-start | bytes 998408 | tf_op jit(solution)/shard_map/ppermute | solution.py:24
  216.3 37.3 %collective-permute-start.13 = (f32[10,1,130,64]{2,3,1,0:T(8,128)}, f32[10,1,130,64]{2,3,1,0:T(8,128)}, u32[]{:S(2)}, u32[]{:S(2)}) collective-permute-start(f32[10,1,130,64]{2,3,1,0:T(8,128)} %copy.86), channel_id=1, source_target_pairs={{2,0},{4,2},{6,4},{0,6},{3,1},{5,3},{7,5},{1,7},{10,8},{12,10},{14... | collective-permute-start | bytes 998408 | tf_op jit(solution)/shard_map/ppermute | solution.py:26
  241.5 14.1 %collective-permute-start.11 = (f32[10,8,1024]{2,1,0:T(8,128)S(1)}, f32[10,8,1024]{2,1,0:T(8,128)S(1)}, u32[]{:S(2)}, u32[]{:S(2)}) collective-permute-start(f32[10,8,1024]{2,1,0:T(8,128)S(1)} %broadcast_select_fusion), channel_id=1, source_target_pairs={{0,1},{1,0},{2,3},{3,2},{4,5},{5,4},{6,7},{7,6},{8,9},{9,8},{10,11... | collective-permute-start | bytes 983048 | tf_op jit(solution)/shard_map/ppermute | solution.py:34
  (13 other events, 61.5 us)
Sparse Core Ops, SparseCore 0:
  22.5 32.0 reduce-scatter.2
  87.4 45.5 all-reduce.2
  165.1 30.0 reduce-scatter.4
  197.4 43.0 all-reduce.4
where the time goes:
time: 295 us; the launch traced here: 290 us
  local copies, waits for them, and re-layouts  96 us (33%)
  other arithmetic  63.5 us (22%)
  waiting for transfers between devices  58.2 us (20%)
  matrix products  37 us (13%)
  starting transfers between devices  21.3 us (7%)
  between operations  14.1 us (5%)
    psum x2, waiting for transfers between devices, inlet_face(): cycles_total = lax.psum(part_sum, 'ax')  56.1 us
    sub x4, other arithmetic, divergence(): flux = 0.5 * (vel_low * lower + vel_up * upper) - 0.5 * (upper - lower)  28.5 us
    ppermute x6, starting transfers between devices, with_halo(): lax.ppermute(head, axis, [((i + 1) % count, i) for i in range(count)])  19.3 us
    dot_general x2, matrix products, reaction(): dspec = jnp.einsum('vk,k...->v...', mix, rate, precision=high)  18.9 us
    slice x6, local copies, waits for them, and re-layouts, with_halo(): lax.slice_in_dim(cells, cells.shape[dim] - width, cells.shape[dim], axis=...  15.7 us
    dot_general x2, matrix products, reaction(): dtheta = jnp.einsum('k,k...->...', heat, rate, precision=high)  12.4 us
    max x2, local copies, waits for them, and re-layouts, reaction(): jnp.maximum(species, 0.0)  11.9 us
    another operation x2, local copies, waits for them, and re-layouts, local(): state = cells[0].reshape(NV, CAX, CAZ, NR)  11.7 us
  transfers between devices with their start and end apart: 18, of which 3 were waited for; matrix products, arithmetic and copies ran while one was open for 44% of the time, Pallas kernels for 0%

commit v1 on v0

v1 whole, which is shorter than its diff:
```python
import functools

import jax
import jax.numpy as jnp
from jax import lax
from jax.experimental import pallas as pl
from jax.experimental.pallas import tpu as pltpu
from jax.sharding import PartitionSpec as P

NV = 10
NS = 9
LANES = 128
CAX = 8
HALF = 64
AXES = ("az", "ax", "pl")
NJ = 4

f32 = jnp.float32


def roles():
    return lax.axis_index("az"), lax.axis_index("ax"), lax.axis_index("pl")


def low_half():
    return lax.broadcasted_iota(jnp.int32, (CAX, LANES), 1) < HALF


def extract(q_ref, vel_ref, col_ref, slot_ref, open_ref, out_refs, s_ref, own_ref, n_az):
    az, ax, plen = roles()
    n = q_ref.shape[1] // CAX
    for v in range(NV):
        s_ref[pl.ds(v * n, n), :] = q_ref[v, pl.ds(0, n, stride=CAX), :]

    @pl.when(plen == 0)
    def _():
        w_low = vel_ref[1, pl.ds(0, n, stride=CAX), :]
        w_top = vel_ref[1, pl.ds(CAX - 1, n, stride=CAX), :]
        even = ax % 2 == 0

        def put(up_ref, down_ref):
            for v in range(NV):
                up_ref[pl.ds(v * n, n), :] = (1.0 + w_top) * q_ref[v, pl.ds(CAX - 1, n, stride=CAX), :]
                down_ref[pl.ds(v * n, n), :] = (1.0 - w_low) * q_ref[v, pl.ds(0, n, stride=CAX), :]

        @pl.when(even)
        def _():
            put(out_refs[0], out_refs[1])

        @pl.when(jnp.logical_not(even))
        def _():
            put(out_refs[1], out_refs[0])

    @pl.when(plen == 1)
    def _():
        refs = (own_ref,) + tuple(out_refs)
        for ref in refs:
            ref[...] = jnp.zeros_like(ref)
        blocks = n // CAX
        for b in range(blocks):
            tile = slot_ref[b]
            for shift, ref in enumerate(refs):
                here = jnp.logical_and(col_ref[b] == (az + shift) % n_az, open_ref[b] != 0)

                @pl.when(here)
                def _(ref=ref, b=b, tile=tile):
                    for v in range(NV):
                        row = pl.multiple_of(v * n + tile * CAX, CAX)
                        ref[pl.ds(row, CAX), :] += q_ref[v, pl.ds(CAX * CAX * b + CAX - 1, CAX, stride=CAX), :]


def first_kernel(n_az, n_out, q_ref, vel_ref, col_ref, slot_ref, open_ref, *outs):
    out_refs, (s_ref, own_ref, er_ref, el_ref) = outs[:n_out], outs[n_out:]
    n = q_ref.shape[1] // CAX
    for v in range(NV):
        el_ref[pl.ds(v * CAX, CAX), :] = q_ref[v, pl.ds(0, CAX), :]
        er_ref[pl.ds(v * CAX, CAX), :] = q_ref[v, pl.ds((n - 1) * CAX, CAX), :]
    el_ref[pl.ds(NV * CAX, CAX), :] = vel_ref[0, pl.ds(0, CAX), :]
    er_ref[pl.ds(NV * CAX, CAX), :] = vel_ref[0, pl.ds((n - 1) * CAX, CAX), :]
    extract(q_ref, vel_ref, col_ref, slot_ref, open_ref, out_refs, s_ref, own_ref, n_az)


def source(state, mix_ref, pre_ref, act_ref, heat_ref):
    inv = 1.0 / jnp.maximum(state[NS], 0.5)
    rates = [pre_ref[k] * jnp.exp(-act_ref[k] * inv) * jnp.maximum(state[k], 0.0) for k in range(NS)]
    out = []
    for v in range(NV):
        acc = None
        for k in range(NS):
            term = (mix_ref[v, k] if v < NS else heat_ref[k]) * rates[k]
            acc = term if acc is None else acc + term
        out.append(0.2 * acc)
    return out


def choose_ghosts(q_ref, ra_ref, rb_ref, s_ref, supply_ref, lo_ref, hi_ref, n_ax):
    _, ax, plen = roles()
    n = q_ref.shape[1] // CAX
    even = ax % 2 == 0
    odd = jnp.logical_not(even)
    cham = plen == 0

    @pl.when(plen == 1)
    def _():
        lo_ref[...] = supply_ref[...]
        hi_ref[...] = s_ref[...]

    @pl.when(jnp.logical_and(cham, even))
    def _():
        hi_ref[...] = ra_ref[...]

    @pl.when(jnp.logical_and(cham, odd))
    def _():
        lo_ref[...] = ra_ref[...]

    @pl.when(jnp.logical_and(cham, ax == 0))
    def _():
        lo_ref[...] = jnp.zeros_like(lo_ref)

    @pl.when(jnp.logical_and(cham, jnp.logical_and(even, ax > 0)))
    def _():
        lo_ref[...] = rb_ref[...]

    @pl.when(jnp.logical_and(cham, jnp.logical_and(odd, ax < n_ax - 1)))
    def _():
        hi_ref[...] = rb_ref[...]

    @pl.when(jnp.logical_and(cham, ax == n_ax - 1))
    def _():
        for v in range(NV):
            hi_ref[pl.ds(v * n, n), :] = q_ref[v, pl.ds(CAX - 1, n, stride=CAX), :]


def advance(q_ref, vel_ref, hl_ref, hr_ref, ul, ur, lo_ref, hi_ref, mix_ref, pre_ref, act_ref, heat_ref, finish):
    n = q_ref.shape[1] // CAX
    left = low_half()
    sub = lax.broadcasted_iota(jnp.int32, (CAX, LANES), 0)
    bottom, top = sub == 0, sub == CAX - 1

    def column(ref, v, j0, head, tail):
        regs = [ref[v, pl.ds(pl.multiple_of((j0 + d) * CAX, CAX), CAX), :] for d in range(NJ)]
        before = ref[v, pl.ds(pl.multiple_of(jnp.maximum(j0 - 1, 0) * CAX, CAX), CAX), :]
        after = ref[v, pl.ds(pl.multiple_of(jnp.minimum(j0 + NJ, n - 1) * CAX, CAX), CAX), :]
        before = jnp.where(j0 == 0, head, before)
        after = jnp.where(j0 + NJ == n, tail, after)
        turned = [pltpu.roll(x, HALF, 1) for x in [before] + regs + [after]]
        lefts = [jnp.where(left, turned[d], turned[d + 1]) for d in range(NJ)]
        rights = [jnp.where(left, turned[d + 1], turned[d + 2]) for d in range(NJ)]
        return regs, lefts, rights

    def body(c, carry):
        j0 = c * NJ
        _, u_left, u_right = column(vel_ref, 0, j0, ul, ur)
        w = [vel_ref[1, pl.ds(pl.multiple_of((j0 + d) * CAX, CAX), CAX), :] for d in range(NJ)]
        al = [0.1 + 0.1 * x for x in u_left]
        ar = [0.1 - 0.1 * x for x in u_right]
        wu = [0.1 + 0.1 * x for x in w]
        wd = [0.1 - 0.1 * x for x in w]
        src = []
        for d in range(NJ):
            state = [q_ref[v, pl.ds(pl.multiple_of((j0 + d) * CAX, CAX), CAX), :] for v in range(NV)]
            src.append(source(state, mix_ref, pre_ref, act_ref, heat_ref))
        for v in range(NV):
            regs, lefts, rights = column(q_ref, v, j0, hl_ref[pl.ds(v * CAX, CAX), :], hr_ref[pl.ds(v * CAX, CAX), :])
            for d in range(NJ):
                lo = jnp.broadcast_to(lo_ref[pl.ds(v * n + j0 + d, 1), :], (CAX, LANES))
                hi = jnp.broadcast_to(hi_ref[pl.ds(v * n + j0 + d, 1), :], (CAX, LANES))
                below = jnp.where(bottom, 0.1 * lo, pltpu.roll(wu[d] * regs[d], 1, 0))
                above = jnp.where(top, 0.1 * hi, pltpu.roll(wd[d] * regs[d], CAX - 1, 0))
                new = (0.6 * regs[d] + src[d][v]) + (al[d] * lefts[d] + ar[d] * rights[d]) + (below + above)
                finish(j0 + d, v, new)
        return carry

    lax.fori_loop(0, n // NJ, body, 0)


def section_one_kernel(n_az, n_ax, n_out, q_ref, vel_ref, hl_ref, hr_ref, s_in_ref, supply_ref, own_in_ref,
                       col_ref, slot_ref, open_ref, mix_ref, pre_ref, act_ref, heat_ref, *rest):
    got, rest = rest[:n_out], rest[n_out:]
    out_refs, rest = rest[:n_out], rest[n_out:]
    q1_ref, tile_ref, s_ref, own_ref, er_ref, el_ref, lo_ref, hi_ref = rest
    n = q_ref.shape[1] // CAX
    _, _, plen = roles()
    choose_ghosts(q_ref, got[0], got[1], s_in_ref, supply_ref, lo_ref, hi_ref, n_ax)

    @pl.when(plen == 1)
    def _():
        total = own_in_ref[...]
        for ref in got:
            total = total + ref[...]
        tile_ref[...] = total

    def finish(j, v, new):
        q1_ref[v, pl.ds(pl.multiple_of(j * CAX, CAX), CAX), :] = new

    ul, ur = hl_ref[pl.ds(NV * CAX, CAX), :], hr_ref[pl.ds(NV * CAX, CAX), :]
    advance(q_ref, vel_ref, hl_ref, hr_ref, ul, ur, lo_ref, hi_ref, mix_ref, pre_ref, act_ref, heat_ref, finish)
    for v in range(NV):
        el_ref[pl.ds(v * CAX, CAX), :] = q1_ref[v, pl.ds(0, CAX), :]
        er_ref[pl.ds(v * CAX, CAX), :] = q1_ref[v, pl.ds((n - 1) * CAX, CAX), :]
    extract(q1_ref, vel_ref, col_ref, slot_ref, open_ref, out_refs, s_ref, own_ref, n_az)


def section_two_kernel(n_ax, q_ref, q1_ref, vel_ref, hl_ref, hr_ref, u_l_ref, u_r_ref, ra_ref, rb_ref, s_in_ref, supply_ref,
                       mix_ref, pre_ref, act_ref, heat_ref, out_ref, base_ref, row_ref, lo_ref, hi_ref):
    n = q_ref.shape[1] // CAX
    choose_ghosts(q1_ref, ra_ref, rb_ref, s_in_ref, supply_ref, lo_ref, hi_ref, n_ax)

    def finish(j, v, new):
        at = pl.ds(pl.multiple_of(j * CAX, CAX), CAX)
        out_ref[v, at, :] = 0.5 * q_ref[v, at, :] + 0.5 * new

    advance(q1_ref, vel_ref, hl_ref, hr_ref, u_l_ref[...], u_r_ref[...], lo_ref, hi_ref,
            mix_ref, pre_ref, act_ref, heat_ref, finish)
    row_ref[pl.ds(0, n), :] = vel_ref[0, pl.ds(0, n, stride=CAX), :]
    row_ref[pl.ds(n, n), :] = vel_ref[1, pl.ds(0, n, stride=CAX), :]
    w_next = vel_ref[1, pl.ds(1, n, stride=CAX), :]
    for v in range(NV):
        base_ref[pl.ds(v * n, n), :] = (
            0.5 * q_ref[v, pl.ds(0, n, stride=CAX), :]
            + 0.05 * ((1.0 - w_next) * q1_ref[v, pl.ds(1, n, stride=CAX), :]))


def last_kernel(part_ref, base_ref, row_ref, s1_ref, dq_ref, s_in_ref, f_in_ref, dl_ref, dr_ref, hl_ref, hr_ref,
                u_l_ref, u_r_ref, mix_ref, pre_ref, act_ref, heat_ref, out_ref):
    n = out_ref.shape[1] // CAX
    _, ax, plen = roles()
    out_ref[...] = part_ref[...]
    first = lax.broadcasted_iota(jnp.int32, (n, LANES), 0) == 0
    last = lax.broadcasted_iota(jnp.int32, (n, LANES), 0) == n - 1
    left = lax.broadcasted_iota(jnp.int32, (n, LANES), 1) < HALF

    def neighbours(x, head, tail):
        before = jnp.where(first, head, pltpu.roll(x, 1, 0))
        after = jnp.where(last, tail, pltpu.roll(x, n - 1, 0))
        mid = pltpu.roll(x, HALF, 1)
        return (jnp.where(left, pltpu.roll(before, HALF, 1), mid),
                jnp.where(left, mid, pltpu.roll(after, HALF, 1)))

    @pl.when(jnp.logical_and(ax == 0, plen == 0))
    def _():
        u = row_ref[pl.ds(0, n), :]
        w = row_ref[pl.ds(n, n), :]
        u_left, u_right = neighbours(u, u_l_ref[pl.ds(0, 1), :], u_r_ref[pl.ds(0, 1), :])
        state = [s1_ref[pl.ds(v * n, n), :] + dq_ref[pl.ds(v * n, n), :] for v in range(NV)]
        src = source(state, mix_ref, pre_ref, act_ref, heat_ref)
        for v in range(NV):
            head = hl_ref[pl.ds(v * CAX, 1), :] + dl_ref[pl.ds(v, 1), :]
            tail = hr_ref[pl.ds(v * CAX, 1), :] + dr_ref[pl.ds(v, 1), :]
            q_left, q_right = neighbours(state[v], head, tail)
            inlet = s_in_ref[pl.ds(v * n, n), :] + f_in_ref[pl.ds(v * n, n), :]
            new = 0.6 * state[v] + 0.1 * ((1.0 + u_left) * q_left + (1.0 - u_right) * q_right + inlet) + src[v]
            out_ref[v, pl.ds(0, n, stride=CAX), :] = base_ref[pl.ds(v * n, n), :] + 0.5 * new
            out_ref[v, pl.ds(1, n, stride=CAX), :] = (
                part_ref[v, pl.ds(1, n, stride=CAX), :] + 0.05 * ((1.0 + w) * dq_ref[pl.ds(v * n, n), :]))

    @pl.when(jnp.logical_and(ax == 0, plen == 1))
    def _():
        for v in range(NV):
            out_ref[v, pl.ds(CAX - 1, n, stride=CAX), :] = (
                part_ref[v, pl.ds(CAX - 1, n, stride=CAX), :] + 0.05 * s_in_ref[pl.ds(v * n, n), :])


def shape(*dims):
    return jax.ShapeDtypeStruct(dims, f32)


def call(kernel, inputs, kinds, outs, scratch=()):
    vmem = pl.BlockSpec(memory_space=pltpu.VMEM)
    smem = pl.BlockSpec(memory_space=pltpu.SMEM)
    return pl.pallas_call(
        kernel,
        in_specs=[smem if k == "s" else vmem for k in kinds],
        out_specs=[vmem] * len(outs),
        out_shape=outs,
        scratch_shapes=list(scratch),
        compiler_params=pltpu.CompilerParams(vmem_limit_bytes=56 * 1024 * 1024),
    )(*inputs)


def local(n_az, n_ax, cells, speeds, supply, mix, prefactor, activation, heat, inj_column, inj_slot, inj_open):
    size = cells.shape[-1]
    n = size // LANES
    rows = NV * n

    def view(array):
        k = array.shape[0]
        return array.reshape(k, CAX, n, LANES).transpose(0, 2, 1, 3).reshape(k, CAX * n, LANES)

    def number(i, j, p):
        return (i * n_ax + j) * 2 + p

    every = [(i, j) for i in range(n_az) for j in range(n_ax)]

    def send(x, route):
        return lax.ppermute(x, AXES, [(number(*a), number(*b)) for a, b in route])

    def ring(step):
        return [((i, j, p), ((i + step) % n_az, j, p)) for i, j in every for p in (0, 1)]

    swap = [((i, j, p), (i, j, 1 - p)) for i, j in every for p in (0, 1)]
    n_out = n_az - 1

    def mate(k, j):
        return j ^ 1 if k == 0 else ((j + 1) ^ 1) - 1 if 0 < j < n_ax - 1 else n_ax - 1 - j

    def spread(k):
        out = [((i, j, 1), ((i + k + 1) % n_az, j, 1)) for i, j in every]
        if k < 2:
            out += [((i, j, 0), (i, mate(k, j), 0)) for i, j in every]
        return out

    q, vel = view(cells[0]), view(speeds[0])
    sup = supply.reshape(rows, LANES)
    col, slot, opened = inj_column.reshape(-1), inj_slot, inj_open
    react = (mix, prefactor, activation, heat)
    row, edge = shape(rows, LANES), shape(NV * CAX, LANES)
    plen = lax.axis_index("pl")
    ax = lax.axis_index("ax")

    got = call(functools.partial(first_kernel, n_az, n_out), (q, vel, col, slot, opened), "vvsss",
               [row] * (n_out + 2) + [shape((NV + 1) * CAX, LANES)] * 2)
    outs, (s0, own0, er, el) = got[:n_out], got[n_out:]
    ra = [send(x, spread(k)) for k, x in enumerate(outs)]
    s0r = send(s0, swap)
    hl0, hr0 = send(er, ring(1)), send(el, ring(-1))

    got = call(functools.partial(section_one_kernel, n_az, n_ax, n_out),
               (q, vel, hl0, hr0, s0r, sup, own0, col, slot, opened) + react + tuple(ra),
               "v" * 7 + "s" * 7 + "v" * n_out,
               [row] * n_out + [shape(*q.shape)] + [row] * 3 + [edge] * 2,
               [pltpu.VMEM((rows, LANES), f32)] * 2)
    outs, (q1, tile0, s1, own1, er, el) = got[:n_out], got[n_out:]
    down = [((i, j, 1), (i, j - 1, 1)) for i, j in every if j % 2 == 1]
    across = [((i, 2, 1), (i, 0, 0)) for i in range(n_az)]
    rb = [send(x, spread(k)) for k, x in enumerate(outs)]
    s1r = send(s1, swap)
    hl1, hr1 = send(er, ring(1)), send(el, ring(-1))
    pair0 = tile0 + send(tile0, down)

    tile1 = own1
    for x in rb:
        tile1 = tile1 + x
    pair1_in = send(tile1, down)
    far0 = send(pair0, across)
    near0 = send(pair0, swap)

    u_l, u_r = hl0[NV * CAX:], hr0[NV * CAX:]
    part, base, vrow = call(functools.partial(section_two_kernel, n_ax),
                            (q, q1, vel, hl1, hr1, u_l, u_r, rb[0], rb[1], s1r, sup) + react,
                            "v" * 11 + "s" * 4,
                            [shape(*q.shape), row, shape(2 * n, LANES)],
                            [pltpu.VMEM((rows, LANES), f32)] * 2)
    inlet_side = jnp.logical_and(ax == 0, plen == 0)
    dq = jnp.where(inlet_side, 0.1 * (far0 + near0), 0.0)
    pair1 = tile1 + pair1_in
    dq3 = dq.reshape(NV, n, LANES)
    far1 = send(pair1, across)
    near1 = send(jnp.where(plen == 0, dq, pair1), swap)
    dl, dr = send(dq3[:, n - 1], ring(1)), send(dq3[:, 0], ring(-1))
    out, = call(last_kernel,
                (part, base, vrow, s1, dq, near1, far1, dl, dr, hl1, hr1, u_l, u_r) + react,
                "v" * 13 + "s" * 4, [shape(*q.shape)])
    return out.reshape(NV, n, CAX, LANES).transpose(0, 2, 1, 3).reshape(1, NV, CAX, size)


def solution(mesh):
    return jax.shard_map(
        functools.partial(local, mesh.shape["az"], mesh.shape["ax"]),
        mesh=mesh,
        in_specs=(
            P("pl", None, "ax", "az"),
            P("pl", None, "ax", "az"),
            P(None, "ax", "az"),
            P(),
            P(),
            P(),
            P(),
            P(("az", "ax"), None),
            P(("az", "ax")),
            P(("az", "ax")),
        ),
        out_specs=P("pl", None, "ax", "az"),
        check_vma=False,
    )
```

time: 295 us -> 82.3 us (0.28); the launches traced: 290 us -> 81.9 us
  local copies, waits for them, and re-layouts: 96 us -> 5.14 us
  other arithmetic: 63.5 us -> 2.24 us
  matrix products: 37 us -> 0 us
  waiting for transfers between devices: 58.2 us -> 23.9 us
  Pallas kernels: 0 us -> 26.8 us
  between operations: 14.1 us -> 0.29 us
    psum x2 -> x0, waiting for transfers between devices: 56.1 us -> none  [inlet_face(): cycles_total = lax.psum(part_sum, 'ax')]
    dot_general x6 -> x0, matrix products: 37 us -> none  [the longest x2 18.9 us: reaction(): dspec = jnp.einsum('vk,k...->v...', mix, rate, precision=high)]
    slice x24 -> x3, local copies, waits for them, and re-layouts: 36.2 us -> 2.54 us  [the longest x2 2.53 us: local(): u_l, u_r = (hl0[NV * CAX:], hr0[NV * CAX:])]
    sub x4 -> x0, other arithmetic: 28.5 us -> none  [divergence(): flux = 0.5 * (vel_low * lower + vel_up * upper) - 0.5 * (upper - lower)]
    pallas_call x0 -> x4, Pallas kernels: none -> 26.8 us  [call(): pl.pallas_call(kernel, in_specs=[smem if k == 's' else vmem for k in kind...]
    ppermute x14 -> x20, waiting for transfers between devices: 0.04 us -> 23.9 us  [send(): return lax.ppermute(x, AXES, [(number(*a), number(*b)) for a, b in route])]
    another operation x7 -> x0, local copies, waits for them, and re-layouts: 15.2 us -> none  [the longest x2 11.7 us: local(): state = cells[0].reshape(NV, CAX, CAZ, NR)]
    max x4 -> x0, local copies, waits for them, and re-layouts: 12.3 us -> none  [the longest x2 11.9 us: reaction(): jnp.maximum(species, 0.0)]
  transfers between devices with their start and end apart: 18 -> 20, of which waited for: 3 -> 6; matrix products, arithmetic and copies ran while one was open for 44% -> 6% of each run, Pallas kernels for 0% -> 12%
where the time goes in v1:
time: 82.3 us; the launch traced here: 81.9 us
  Pallas kernels  26.8 us (33%)
  waiting for transfers between devices  23.9 us (29%)
  starting transfers between devices  23.6 us (29%)
  local copies, waits for them, and re-layouts  5.14 us (6%)
  other arithmetic  2.24 us (3%)
    pallas_call x4, Pallas kernels, call(): pl.pallas_call(kernel, in_specs=[smem if k == 's' else vmem for k in kind...  26.8 us
    ppermute x20, waiting for transfers between devices, send(): return lax.ppermute(x, AXES, [(number(*a), number(*b)) for a, b in route])  23.9 us
    ppermute x20, starting transfers between devices, send(): return lax.ppermute(x, AXES, [(number(*a), number(*b)) for a, b in route])  23.6 us
    unnamed x40, local copies, waits for them, and re-layouts  2.59 us
    slice x2, local copies, waits for them, and re-layouts, local(): u_l, u_r = (hl0[NV * CAX:], hr0[NV * CAX:])  2.53 us
  transfers between devices with their start and end apart: 20, of which 6 were waited for; matrix products, arithmetic and copies ran while one was open for 6% of the time, Pallas kernels for 12%

profile of v1, /device:TPU:0, one launch (start us, length us, event | category | flops | bytes accessed | tf_op | source)
XLA Modules:
  0.0 81.9 jit_solution(16485882636910497966)
XLA Ops:
  0.0 3.3 %shard_map.100 = (f32[640,128]{1,0:T(8,128)}, f32[640,128]{1,0:T(8,128)}, f32[640,128]{1,0:T(8,128)}, f32[640,128]{1,0:T(8,128)}, f32[640,128]{1,0:T(8,128)}, /*index=5*/f32[88,128]{1,0:T(8,128)}, f32[88,128]{1,0:T(8,128)}) custom-call(f32[10,512,128]{2,1,0:T(8,128)} %bitcast.24, f32[2,512,128]{2,1,0:T(8,128)} %bitcast.27, s32[8]{0:T(128)} %bitcast.35, ...), custom_call_target="tpu_custom_call" | custom-call | tf_op jit(solution)/shard_map/pallas_call | solution.py:271
  3.3 0.8 collective-permute-start.2
  4.0 2.4 %collective-permute-start.3 = (f32[640,128]{1,0:T(8,128)}, f32[640,128]{1,0:T(8,128)S(1)}, u32[]{:S(2)}, u32[]{:S(2)}) collective-permute-start(f32[640,128]{1,0:T(8,128)} %get-tuple-element.28), channel_id=1, source_target_pairs={{1,9},{3,11},{5,13},{7,15},{9,17},{11,19},{13,21},{15,23},{17,25},... | collective-permute-start | bytes 983048 | tf_op jit(solution)/shard_map/ppermute | solution.py:296
  6.5 2.5 %collective-permute-start.4 = (f32[640,128]{1,0:T(8,128)}, f32[640,128]{1,0:T(8,128)S(1)}, u32[]{:S(2)}, u32[]{:S(2)}) collective-permute-start(f32[640,128]{1,0:T(8,128)} %get-tuple-element.29), channel_id=1, source_target_pairs={{1,17},{3,19},{5,21},{7,23},{9,25},{11,27},{13,29},{15,31},{17,1},... | collective-permute-start | bytes 983048 | tf_op jit(solution)/shard_map/ppermute | solution.py:296
  9.6 1.5 %collective-permute-start = (f32[88,128]{1,0:T(8,128)}, f32[88,128]{1,0:T(8,128)S(1)}, u32[]{:S(2)}, u32[]{:S(2)}) collective-permute-start(f32[88,128]{1,0:T(8,128)} %get-tuple-element.24), channel_id=1, source_target_pairs={{0,8},{1,9},{2,10},{3,11},{4,12},{5,13},{6,14},{7,15},{8,16},{9,17... | collective-permute-start | bytes 135176 | tf_op jit(solution)/shard_map/ppermute | solution.py:296
  11.1 4.2 %collective-permute-done.hl_ref = f32[88,128]{1,0:T(8,128)S(1)} collective-permute-done((f32[88,128]{1,0:T(8,128)}, f32[88,128]{1,0:T(8,128)S(1)}, u32[]{:S(2)}, u32[]{:S(2)}) %collective-permute-start) | collective-permute-done | bytes 45088 | tf_op jit(solution)/shard_map/ppermute | solution.py:296
  15.4 1.6 %collective-permute-start.1 = (f32[88,128]{1,0:T(8,128)}, f32[88,128]{1,0:T(8,128)S(1)}, u32[]{:S(2)}, u32[]{:S(2)}) collective-permute-start(f32[88,128]{1,0:T(8,128)} %get-tuple-element.25), channel_id=1, source_target_pairs={{0,24},{1,25},{2,26},{3,27},{4,28},{5,29},{6,30},{7,31},{8,0},{9,1... | collective-permute-start | bytes 135176 | tf_op jit(solution)/shard_map/ppermute | solution.py:296
  16.9 2.7 %collective-permute-done.1.hr_ref = f32[88,128]{1,0:T(8,128)S(1)} collective-permute-done((f32[88,128]{1,0:T(8,128)}, f32[88,128]{1,0:T(8,128)S(1)}, u32[]{:S(2)}, u32[]{:S(2)}) %collective-permute-start.1) | collective-permute-done | bytes 45088 | tf_op jit(solution)/shard_map/ppermute | solution.py:296
  20.7 9.4 %shard_map.101 = (f32[640,128]{1,0:T(8,128)}, f32[640,128]{1,0:T(8,128)}, f32[640,128]{1,0:T(8,128)}, f32[10,512,128]{2,1,0:T(8,128)}, f32[640,128]{1,0:T(8,128)...) custom-call(f32[10,512,128]{2,1,0:T(8,128)} %bitcast.25, ...), custom_call_target="tpu_custom_call" | custom-call | tf_op jit(solution)/shard_map/pallas_call | solution.py:271
  30.2 0.7 collective-permute-start.8
  30.9 1.2 %collective-permute-start.9 = (f32[640,128]{1,0:T(8,128)}, f32[640,128]{1,0:T(8,128)S(1)}, u32[]{:S(2)}, u32[]{:S(2)}) collective-permute-start(f32[640,128]{1,0:T(8,128)} %get-tuple-element.35), channel_id=1, source_target_pairs={{1,17},{3,19},{5,21},{7,23},{9,25},{11,27},{13,29},{15,31},{17,1},... | collective-permute-start | bytes 983048 | tf_op jit(solution)/shard_map/ppermute | solution.py:296
  32.1 0.7 collective-permute-start.14
  32.8 0.7 collective-permute-start.11
  33.5 4.0 %collective-permute-done.8.ra_ref = f32[640,128]{1,0:T(8,128)S(1)} collective-permute-done((f32[640,128]{1,0:T(8,128)}, f32[640,128]{1,0:T(8,128)S(1)}, u32[]{:S(2)}, u32[]{:S(2)}) %collective-permute-start.8) | collective-permute-done | bytes 327712 | tf_op jit(solution)/shard_map/ppermute | solution.py:296
  37.5 3.5 %collective-permute-done.9.rb_ref = f32[640,128]{1,0:T(8,128)S(1)} collective-permute-done((f32[640,128]{1,0:T(8,128)}, f32[640,128]{1,0:T(8,128)S(1)}, u32[]{:S(2)}, u32[]{:S(2)}) %collective-permute-start.9) | collective-permute-done | bytes 327712 | tf_op jit(solution)/shard_map/ppermute | solution.py:296
  41.0 1.2 %add_add_fusion = f32[640,128]{1,0:T(8,128)S(1)} fusion(f32[640,128]{1,0:T(8,128)S(1)} %collective-permute-done.14, f32[640,128]{1,0:T(8,128)S(1)} %collective-permute-done.9.rb_ref, f32[640,128]{1,0:T(8,128)} %get-tuple-element.41, f32[640,128]{1,0:T(8,128)S(1)} %collective-permute-done.8.ra_ref), kind=kLoop, calls=%fused_computation | loop fusion | flops 245760 | bytes 1638400 | tf_op jit(solution)/shard_map/add | solution.py:343
  42.2 0.7 collective-permute-start.15
  42.9 1.0 %add.18 = f32[640,128]{1,0:T(8,128)S(1)} add(f32[640,128]{1,0:T(8,128)} %get-tuple-element.40, f32[640,128]{1,0:T(8,128)S(1)} %collective-permute-done.11) | non-fusion elementwise | flops 81920 | bytes 983040 | tf_op jit(solution)/shard_map/add | solution.py:339
  43.9 1.3 %collective-permute-start.12 = (f32[640,128]{1,0:T(8,128)S(1)}, f32[640,128]{1,0:T(8,128)S(1)}, u32[]{:S(2)}, u32[]{:S(2)}) collective-permute-start(f32[640,128]{1,0:T(8,128)S(1)} %add.18), channel_id=1, source_target_pairs={{5,0},{13,8},{21,16},{29,24}} | collective-permute-start | bytes 983048 | tf_op jit(solution)/shard_map/ppermute | solution.py:296
  45.2 1.3 %collective-permute-start.13 = (f32[640,128]{1,0:T(8,128)S(1)}, f32[640,128]{1,0:T(8,128)S(1)}, u32[]{:S(2)}, u32[]{:S(2)}) collective-permute-start(f32[640,128]{1,0:T(8,128)S(1)} %add.18), channel_id=1, source_target_pairs={{0,1},{1,0},{2,3},{3,2},{4,5},{5,4},{6,7},{7,6},{8,9},{9,8},{10,11... | collective-permute-start | bytes 983048 | tf_op jit(solution)/shard_map/ppermute | solution.py:296
  46.6 7.4 %collective-permute-done.12 = f32[640,128]{1,0:T(8,128)S(1)} collective-permute-done((f32[640,128]{1,0:T(8,128)S(1)}, f32[640,128]{1,0:T(8,128)S(1)}, u32[]{:S(2)}, u32[]{:S(2)}) %collective-permute-start.12) | collective-permute-done | bytes 327712 | tf_op jit(solution)/shard_map/ppermute | solution.py:296
  54.3 1.3 %collective-permute-start.17 = (f32[640,128]{1,0:T(8,128)S(1)}, f32[640,128]{1,0:T(8,128)S(1)}, u32[]{:S(2)}, u32[]{:S(2)}) collective-permute-start(f32[640,128]{1,0:T(8,128)S(1)} %get-tuple-element.44), channel_id=1, source_target_pairs={{5,0},{13,8},{21,16},{29,24}} | collective-permute-start | bytes 983048 | tf_op jit(solution)/shard_map/ppermute | solution.py:296
  55.6 1.9 %collective-permute-start.6 = (f32[80,128]{1,0:T(8,128)S(1)}, f32[80,128]{1,0:T(8,128)S(1)}, u32[]{:S(2)}, u32[]{:S(2)}) collective-permute-start(f32[80,128]{1,0:T(8,128)S(1)} %copy-done.18), channel_id=1, source_target_pairs={{0,8},{1,9},{2,10},{3,11},{4,12},{5,13},{6,14},{7,15},{8,16},{9,17... | collective-permute-start | bytes 122888 | tf_op jit(solution)/shard_map/ppermute | solution.py:296
  57.5 1.1 %collective-permute-start.7 = (f32[80,128]{1,0:T(8,128)S(1)}, f32[80,128]{1,0:T(8,128)S(1)}, u32[]{:S(2)}, u32[]{:S(2)}) collective-permute-start(f32[80,128]{1,0:T(8,128)S(1)} %copy-done.17), channel_id=1, source_target_pairs={{0,24},{1,25},{2,26},{3,27},{4,28},{5,29},{6,30},{7,31},{8,0},{9,1... | collective-permute-start | bytes 122888 | tf_op jit(solution)/shard_map/ppermute | solution.py:296
  58.7 2.0 %collective-permute-done.6.hl_ref = f32[80,128]{1,0:T(8,128)S(1)} collective-permute-done((f32[80,128]{1,0:T(8,128)S(1)}, f32[80,128]{1,0:T(8,128)S(1)}, u32[]{:S(2)}, u32[]{:S(2)}) %collective-permute-start.6) | collective-permute-done | bytes 40992 | tf_op jit(solution)/shard_map/ppermute | solution.py:296
  60.7 0.8 %collective-permute-start.18 = (f32[10,128]{1,0:T(8,128)S(1)}, f32[10,128]{1,0:T(8,128)S(1)}, u32[]{:S(2)}, u32[]{:S(2)}) collective-permute-start(f32[10,128]{1,0:T(8,128)S(1)} %bitcast.34), channel_id=1, source_target_pairs={{0,8},{1,9},{2,10},{3,11},{4,12},{5,13},{6,14},{7,15},{8,16},{9,17... | collective-permute-start | bytes 15368 | tf_op jit(solution)/shard_map/ppermute | solution.py:296
  61.5 2.1 %collective-permute-start.19 = (f32[10,128]{1,0:T(8,128)S(1)}, f32[10,128]{1,0:T(8,128)S(1)}, u32[]{:S(2)}, u32[]{:S(2)}) collective-permute-start(f32[10,128]{1,0:T(8,128)S(1)} %bitcast.33), channel_id=1, source_target_pairs={{0,24},{1,25},{2,26},{3,27},{4,28},{5,29},{6,30},{7,31},{8,0},{9,1... | collective-permute-start | bytes 15368 | tf_op jit(solution)/shard_map/ppermute | solution.py:296
  63.6 1.3 %slice.16.u_l_ref = f32[8,128]{1,0:T(8,128)} slice(f32[88,128]{1,0:T(8,128)} %copy-done.13), slice={[80:88], [0:128]} | slice | bytes 8192 | tf_op jit(solution)/shard_map/slice | solution.py:348
  64.9 1.3 %slice.17.u_r_ref = f32[8,128]{1,0:T(8,128)} slice(f32[88,128]{1,0:T(8,128)} %copy-done.14), slice={[80:88], [0:128]} | slice | bytes 8192 | tf_op jit(solution)/shard_map/slice | solution.py:348
  66.2 0.7 copy-done.4
  66.9 9.5 %shard_map.102 = (f32[10,512,128]{2,1,0:T(8,128)}, f32[640,128]{1,0:T(8,128)}, f32[128,128]{1,0:T(8,128)}) custom-call(f32[10,512,128]{2,1,0:T(8,128)} %bitcast.26, f32[10,512,128]{2,1,0:T(8,128)} %get-tuple-element.31.q1_ref, f32[2,512,128]{2,1,0:T(8,128)} %bitcast.29, f32[80,128]{1,0:T(8,128)} %copy-done.11, f32[80,128]{1,0:T(8,128)} %copy-done.12, ...), custom_call_target="tpu_custom_call" | custom-call | tf_op jit(solution)/shard_map/pallas_call | solution.py:271
  77.3 4.6 %shard_map.103 = f32[10,512,128]{2,1,0:T(8,128)} custom-call(f32[10,512,128]{2,1,0:T(8,128)} %get-tuple-element.37.part_ref, f32[640,128]{1,0:T(8,128)} %get-tuple-element.38.base_ref, f32[128,128]{1,0:T(8,128)} %get-tuple-element.39.row_ref, f32[640,128]{1,0:T(8,128)} %get-tuple-element.36.s1_ref, f32[640,128]{1,0:T(8,128)} %copy-done, ...), custom_call_target="tpu_custom_call" | custom-call | tf_op jit(solution)/shard_map/pallas_call | solution.py:271
  (58 shorter events, 3.1 us)
Async XLA Ops:
  3.3 16.4 %collective-permute-start.2 = (f32[640,128]{1,0:T(8,128)}, f32[640,128]{1,0:T(8,128)S(1)}, u32[]{:S(2)}, u32[]{:S(2)}) collective-permute-start(f32[640,128]{1,0:T(8,128)} %get-tuple-element.26), channel_id=1, source_target_pairs={{0,1},{1,0},{2,3},{3,2},{4,5},{5,4},{6,7},{7,6},{8,9},{9,8},{10,11... | collective-permute-start | bytes 983048 | tf_op jit(solution)/shard_map/ppermute | solution.py:296
  4.0 15.6 %collective-permute-start.3 = (f32[640,128]{1,0:T(8,128)}, f32[640,128]{1,0:T(8,128)S(1)}, u32[]{:S(2)}, u32[]{:S(2)}) collective-permute-start(f32[640,128]{1,0:T(8,128)} %get-tuple-element.28), channel_id=1, source_target_pairs={{1,9},{3,11},{5,13},{7,15},{9,17},{11,19},{13,21},{15,23},{17,25},... | collective-permute-start | bytes 983048 | tf_op jit(solution)/shard_map/ppermute | solution.py:296
  6.5 13.2 %collective-permute-start.4 = (f32[640,128]{1,0:T(8,128)}, f32[640,128]{1,0:T(8,128)S(1)}, u32[]{:S(2)}, u32[]{:S(2)}) collective-permute-start(f32[640,128]{1,0:T(8,128)} %get-tuple-element.29), channel_id=1, source_target_pairs={{1,17},{3,19},{5,21},{7,23},{9,25},{11,27},{13,29},{15,31},{17,1},... | collective-permute-start | bytes 983048 | tf_op jit(solution)/shard_map/ppermute | solution.py:296
  8.9 10.7 %collective-permute-start.5 = (f32[640,128]{1,0:T(8,128)}, f32[640,128]{1,0:T(8,128)S(1)}, u32[]{:S(2)}, u32[]{:S(2)}) collective-permute-start(f32[640,128]{1,0:T(8,128)} %get-tuple-element.30), channel_id=1, source_target_pairs={{1,25},{3,27},{5,29},{7,31},{9,1},{11,3},{13,5},{15,7},{17,9},{19,... | collective-permute-start | bytes 983048 | tf_op jit(solution)/shard_map/ppermute | solution.py:296
  9.6 5.8 %collective-permute-start = (f32[88,128]{1,0:T(8,128)}, f32[88,128]{1,0:T(8,128)S(1)}, u32[]{:S(2)}, u32[]{:S(2)}) collective-permute-start(f32[88,128]{1,0:T(8,128)} %get-tuple-element.24), channel_id=1, source_target_pairs={{0,8},{1,9},{2,10},{3,11},{4,12},{5,13},{6,14},{7,15},{8,16},{9,17... | collective-permute-start | bytes 135176 | tf_op jit(solution)/shard_map/ppermute | solution.py:296
  15.4 4.3 %copy-start.13 = (f32[88,128]{1,0:T(8,128)}, f32[88,128]{1,0:T(8,128)S(1)}, u32[]{:S(2)}) copy-start(f32[88,128]{1,0:T(8,128)S(1)} %collective-permute-done.hl_ref) | copy-start | bytes 135172
  15.4 4.3 %collective-permute-start.1 = (f32[88,128]{1,0:T(8,128)}, f32[88,128]{1,0:T(8,128)S(1)}, u32[]{:S(2)}, u32[]{:S(2)}) collective-permute-start(f32[88,128]{1,0:T(8,128)} %get-tuple-element.25), channel_id=1, source_target_pairs={{0,24},{1,25},{2,26},{3,27},{4,28},{5,29},{6,30},{7,31},{8,0},{9,1... | collective-permute-start | bytes 135176 | tf_op jit(solution)/shard_map/ppermute | solution.py:296
  19.6 0.9 %copy-start.8 = (f32[640,128]{1,0:T(8,128)}, f32[640,128]{1,0:T(8,128)S(1)}, u32[]{:S(2)}) copy-start(f32[640,128]{1,0:T(8,128)S(1)} %collective-permute-done.3.rest_0_) | copy-start | bytes 983044
  19.6 0.9 %copy-start.9 = (f32[640,128]{1,0:T(8,128)}, f32[640,128]{1,0:T(8,128)S(1)}, u32[]{:S(2)}) copy-start(f32[640,128]{1,0:T(8,128)S(1)} %collective-permute-done.4.rest_1_) | copy-start | bytes 983044
  19.7 1.1 %copy-start.10 = (f32[640,128]{1,0:T(8,128)}, f32[640,128]{1,0:T(8,128)S(1)}, u32[]{:S(2)}) copy-start(f32[640,128]{1,0:T(8,128)S(1)} %collective-permute-done.5.rest_2_) | copy-start | bytes 983044
  30.1 16.3 %copy-start.3 = (f32[640,128]{1,0:T(8,128)S(1)}, f32[640,128]{1,0:T(8,128)}, u32[]{:S(2)}) copy-start(f32[640,128]{1,0:T(8,128)} %get-tuple-element.36.s1_ref) | copy-start | bytes 983044
  30.1 25.5 %copy-start.18 = (f32[80,128]{1,0:T(8,128)S(1)}, f32[80,128]{1,0:T(8,128)}, u32[]{:S(2)}) copy-start(f32[80,128]{1,0:T(8,128)} %get-tuple-element.32) | copy-start | bytes 122884
  30.1 27.4 %copy-start.17 = (f32[80,128]{1,0:T(8,128)S(1)}, f32[80,128]{1,0:T(8,128)}, u32[]{:S(2)}) copy-start(f32[80,128]{1,0:T(8,128)} %get-tuple-element.33) | copy-start | bytes 122884
  30.2 7.3 %collective-permute-start.8 = (f32[640,128]{1,0:T(8,128)}, f32[640,128]{1,0:T(8,128)S(1)}, u32[]{:S(2)}, u32[]{:S(2)}) collective-permute-start(f32[640,128]{1,0:T(8,128)} %get-tuple-element.34), channel_id=1, source_target_pairs={{1,9},{3,11},{5,13},{7,15},{9,17},{11,19},{13,21},{15,23},{17,25},... | collective-permute-start | bytes 983048 | tf_op jit(solution)/shard_map/ppermute | solution.py:296
  30.9 10.1 %collective-permute-start.9 = (f32[640,128]{1,0:T(8,128)}, f32[640,128]{1,0:T(8,128)S(1)}, u32[]{:S(2)}, u32[]{:S(2)}) collective-permute-start(f32[640,128]{1,0:T(8,128)} %get-tuple-element.35), channel_id=1, source_target_pairs={{1,17},{3,19},{5,21},{7,23},{9,25},{11,27},{13,29},{15,31},{17,1},... | collective-permute-start | bytes 983048 | tf_op jit(solution)/shard_map/ppermute | solution.py:296
  32.1 8.9 %collective-permute-start.14 = (f32[640,128]{1,0:T(8,128)}, f32[640,128]{1,0:T(8,128)S(1)}, u32[]{:S(2)}, u32[]{:S(2)}) collective-permute-start(f32[640,128]{1,0:T(8,128)} %get-tuple-element.42), channel_id=1, source_target_pairs={{1,25},{3,27},{5,29},{7,31},{9,1},{11,3},{13,5},{15,7},{17,9},{19,... | collective-permute-start | bytes 983048 | tf_op jit(solution)/shard_map/ppermute | solution.py:296
  32.8 10.1 %collective-permute-start.11 = (f32[640,128]{1,0:T(8,128)}, f32[640,128]{1,0:T(8,128)S(1)}, u32[]{:S(2)}, u32[]{:S(2)}) collective-permute-start(f32[640,128]{1,0:T(8,128)} %get-tuple-element.40), channel_id=1, source_target_pairs={{3,1},{7,5},{11,9},{15,13},{19,17},{23,21},{27,25},{31,29}} | collective-permute-start | bytes 983048 | tf_op jit(solution)/shard_map/ppermute | solution.py:296
  37.5 28.7 %copy-start.1 = (f32[640,128]{1,0:T(8,128)}, f32[640,128]{1,0:T(8,128)S(1)}, u32[]{:S(2)}) copy-start(f32[640,128]{1,0:T(8,128)S(1)} %collective-permute-done.8.ra_ref) | copy-start | bytes 983044
  41.0 25.2 %copy-start.2 = (f32[640,128]{1,0:T(8,128)}, f32[640,128]{1,0:T(8,128)S(1)}, u32[]{:S(2)}) copy-start(f32[640,128]{1,0:T(8,128)S(1)} %collective-permute-done.9.rb_ref) | copy-start | bytes 983044
  42.2 4.4 %collective-permute-start.15 = (f32[640,128]{1,0:T(8,128)S(1)}, f32[640,128]{1,0:T(8,128)S(1)}, u32[]{:S(2)}, u32[]{:S(2)}) collective-permute-start(f32[640,128]{1,0:T(8,128)S(1)} %add_add_fusion), channel_id=1, source_target_pairs={{3,1},{7,5},{11,9},{15,13},{19,17},{23,21},{27,25},{31,29}} | collective-permute-start | bytes 983048 | tf_op jit(solution)/shard_map/ppermute | solution.py:296
  43.9 10.1 %collective-permute-start.12 = (f32[640,128]{1,0:T(8,128)S(1)}, f32[640,128]{1,0:T(8,128)S(1)}, u32[]{:S(2)}, u32[]{:S(2)}) collective-permute-start(f32[640,128]{1,0:T(8,128)S(1)} %add.18), channel_id=1, source_target_pairs={{5,0},{13,8},{21,16},{29,24}} | collective-permute-start | bytes 983048 | tf_op jit(solution)/shard_map/ppermute | solution.py:296
  45.2 8.8 %collective-permute-start.13 = (f32[640,128]{1,0:T(8,128)S(1)}, f32[640,128]{1,0:T(8,128)S(1)}, u32[]{:S(2)}, u32[]{:S(2)}) collective-permute-start(f32[640,128]{1,0:T(8,128)S(1)} %add.18), channel_id=1, source_target_pairs={{0,1},{1,0},{2,3},{3,2},{4,5},{5,4},{6,7},{7,6},{8,9},{9,8},{10,11... | collective-permute-start | bytes 983048 | tf_op jit(solution)/shard_map/ppermute | solution.py:296
  46.5 19.7 %collective-permute-start.10 = (f32[640,128]{1,0:T(8,128)S(1)}, f32[640,128]{1,0:T(8,128)S(1)}, u32[]{:S(2)}, u32[]{:S(2)}) collective-permute-start(f32[640,128]{1,0:T(8,128)S(1)} %copy-done.3), channel_id=1, source_target_pairs={{0,1},{1,0},{2,3},{3,2},{4,5},{5,4},{6,7},{7,6},{8,9},{9,8},{10,11... | collective-permute-start | bytes 983048 | tf_op jit(solution)/shard_map/ppermute | solution.py:296
  54.0 22.4 %copy-start = (f32[640,128]{1,0:T(8,128)}, f32[640,128]{1,0:T(8,128)S(1)}, u32[]{:S(2)}) copy-start(f32[640,128]{1,0:T(8,128)S(1)} %get-tuple-element.45.dq_ref) | copy-start | bytes 983044
  54.0 22.4 %collective-permute-start.16 = (f32[640,128]{1,0:T(8,128)S(1)}, f32[640,128]{1,0:T(8,128)S(1)}, u32[]{:S(2)}, u32[]{:S(2)}) collective-permute-start(f32[640,128]{1,0:T(8,128)S(1)} %get-tuple-element.43), channel_id=1, source_target_pairs={{0,1},{1,0},{2,3},{3,2},{4,5},{5,4},{6,7},{7,6},{8,9},{9,8},{10,11... | collective-permute-start | bytes 983048 | tf_op jit(solution)/shard_map/ppermute | solution.py:296
  54.3 22.1 %collective-permute-start.17 = (f32[640,128]{1,0:T(8,128)S(1)}, f32[640,128]{1,0:T(8,128)S(1)}, u32[]{:S(2)}, u32[]{:S(2)}) collective-permute-start(f32[640,128]{1,0:T(8,128)S(1)} %get-tuple-element.44), channel_id=1, source_target_pairs={{5,0},{13,8},{21,16},{29,24}} | collective-permute-start | bytes 983048 | tf_op jit(solution)/shard_map/ppermute | solution.py:296
  55.6 5.1 %collective-permute-start.6 = (f32[80,128]{1,0:T(8,128)S(1)}, f32[80,128]{1,0:T(8,128)S(1)}, u32[]{:S(2)}, u32[]{:S(2)}) collective-permute-start(f32[80,128]{1,0:T(8,128)S(1)} %copy-done.18), channel_id=1, source_target_pairs={{0,8},{1,9},{2,10},{3,11},{4,12},{5,13},{6,14},{7,15},{8,16},{9,17... | collective-permute-start | bytes 122888 | tf_op jit(solution)/shard_map/ppermute | solution.py:296
  57.5 4.0 %collective-permute-start.7 = (f32[80,128]{1,0:T(8,128)S(1)}, f32[80,128]{1,0:T(8,128)S(1)}, u32[]{:S(2)}, u32[]{:S(2)}) collective-permute-start(f32[80,128]{1,0:T(8,128)S(1)} %copy-done.17), channel_id=1, source_target_pairs={{0,24},{1,25},{2,26},{3,27},{4,28},{5,29},{6,30},{7,31},{8,0},{9,1... | collective-permute-start | bytes 122888 | tf_op jit(solution)/shard_map/ppermute | solution.py:296
  60.7 5.5 %copy-start.11 = (f32[80,128]{1,0:T(8,128)}, f32[80,128]{1,0:T(8,128)S(1)}, u32[]{:S(2)}) copy-start(f32[80,128]{1,0:T(8,128)S(1)} %collective-permute-done.6.hl_ref) | copy-start | bytes 122884
  60.7 15.7 %collective-permute-start.18 = (f32[10,128]{1,0:T(8,128)S(1)}, f32[10,128]{1,0:T(8,128)S(1)}, u32[]{:S(2)}, u32[]{:S(2)}) collective-permute-start(f32[10,128]{1,0:T(8,128)S(1)} %bitcast.34), channel_id=1, source_target_pairs={{0,8},{1,9},{2,10},{3,11},{4,12},{5,13},{6,14},{7,15},{8,16},{9,17... | collective-permute-start | bytes 15368 | tf_op jit(solution)/shard_map/ppermute | solution.py:296
  61.5 4.7 %copy-start.12 = (f32[80,128]{1,0:T(8,128)}, f32[80,128]{1,0:T(8,128)S(1)}, u32[]{:S(2)}) copy-start(f32[80,128]{1,0:T(8,128)S(1)} %collective-permute-done.7.hr_ref) | copy-start | bytes 122884
  61.5 14.9 %collective-permute-start.19 = (f32[10,128]{1,0:T(8,128)S(1)}, f32[10,128]{1,0:T(8,128)S(1)}, u32[]{:S(2)}, u32[]{:S(2)}) collective-permute-start(f32[10,128]{1,0:T(8,128)S(1)} %bitcast.33), channel_id=1, source_target_pairs={{0,24},{1,25},{2,26},{3,27},{4,28},{5,29},{6,30},{7,31},{8,0},{9,1... | collective-permute-start | bytes 15368 | tf_op jit(solution)/shard_map/ppermute | solution.py:296
  (7 other events, 4.8 us)

commit v2 on v1

v2 whole, which is shorter than its diff:
```python
import functools

import jax
import jax.numpy as jnp
from jax import lax
from jax.experimental import pallas as pl
from jax.experimental.pallas import tpu as pltpu
from jax.sharding import PartitionSpec as P

NV = 10
NS = 9
LANES = 128
CAX = 8
HALF = 64
AXES = ("az", "ax", "pl")
NJ = 4
LIMIT = 16 * 1024 * 1024

f32 = jnp.float32


def roles():
    return lax.axis_index("az"), lax.axis_index("ax"), lax.axis_index("pl")


def low_half():
    return lax.broadcasted_iota(jnp.int32, (CAX, LANES), 1) < HALF


def extract(q_ref, vel_ref, col_ref, slot_ref, open_ref, out_refs, s_ref, own_ref, n_az):
    az, ax, plen = roles()
    n = q_ref.shape[1] // CAX
    for v in range(NV):
        s_ref[pl.ds(v * n, n), :] = q_ref[v, pl.ds(0, n, stride=CAX), :]

    @pl.when(plen == 0)
    def _():
        w_low = vel_ref[1, pl.ds(0, n, stride=CAX), :]
        w_top = vel_ref[1, pl.ds(CAX - 1, n, stride=CAX), :]
        even = ax % 2 == 0

        def put(up_ref, down_ref):
            for v in range(NV):
                up_ref[pl.ds(v * n, n), :] = (1.0 + w_top) * q_ref[v, pl.ds(CAX - 1, n, stride=CAX), :]
                down_ref[pl.ds(v * n, n), :] = (1.0 - w_low) * q_ref[v, pl.ds(0, n, stride=CAX), :]

        @pl.when(even)
        def _():
            put(out_refs[0], out_refs[1])

        @pl.when(jnp.logical_not(even))
        def _():
            put(out_refs[1], out_refs[0])

    @pl.when(plen == 1)
    def _():
        refs = (own_ref,) + tuple(out_refs)
        for ref in refs:
            ref[...] = jnp.zeros_like(ref)
        blocks = n // CAX
        for b in range(blocks):
            tile = slot_ref[b]
            for shift, ref in enumerate(refs):
                here = jnp.logical_and(col_ref[b] == (az + shift) % n_az, open_ref[b] != 0)

                @pl.when(here)
                def _(ref=ref, b=b, tile=tile):
                    for v in range(NV):
                        row = pl.multiple_of(v * n + tile * CAX, CAX)
                        ref[pl.ds(row, CAX), :] += q_ref[v, pl.ds(CAX * CAX * b + CAX - 1, CAX, stride=CAX), :]


def first_kernel(n_az, n_out, q_any, vel_any, col_ref, slot_ref, open_ref, *outs):
    out_refs, (q_ref, vel_ref, s_ref, own_ref, er_ref, el_ref, sems) = outs[:n_out], outs[n_out:]
    copies = [pltpu.make_async_copy(q_any, q_ref, sems.at[0]), pltpu.make_async_copy(vel_any, vel_ref, sems.at[1])]
    for copy in copies:
        copy.start()
    for copy in copies:
        copy.wait()
    n = q_ref.shape[1] // CAX
    for v in range(NV):
        el_ref[pl.ds(v * CAX, CAX), :] = q_ref[v, pl.ds(0, CAX), :]
        er_ref[pl.ds(v * CAX, CAX), :] = q_ref[v, pl.ds((n - 1) * CAX, CAX), :]
    el_ref[pl.ds(NV * CAX, CAX), :] = vel_ref[0, pl.ds(0, CAX), :]
    er_ref[pl.ds(NV * CAX, CAX), :] = vel_ref[0, pl.ds((n - 1) * CAX, CAX), :]
    extract(q_ref, vel_ref, col_ref, slot_ref, open_ref, out_refs, s_ref, own_ref, n_az)


def source(state, mix_ref, pre_ref, act_ref, heat_ref):
    inv = 1.0 / jnp.maximum(state[NS], 0.5)
    rates = [pre_ref[k] * jnp.exp(-act_ref[k] * inv) * jnp.maximum(state[k], 0.0) for k in range(NS)]
    out = []
    for v in range(NV):
        acc = None
        for k in range(NS):
            term = (mix_ref[v, k] if v < NS else heat_ref[k]) * rates[k]
            acc = term if acc is None else acc + term
        out.append(0.2 * acc)
    return out


def boundary(state_ref, dst_ref, scale, ra_ref, rb_ref, high_refs, supply_ref, hl_ref, hr_ref, ul_ref, ur_ref, n_ax):
    _, ax, plen = roles()
    n = dst_ref.shape[1] // CAX
    even = ax % 2 == 0
    odd = jnp.logical_not(even)
    cham = plen == 0

    def add(row, rows_of):
        for v in range(NV):
            dst_ref[v, pl.ds(row, n, stride=CAX), :] += scale * rows_of(v)

    def rows(*refs):
        return lambda v: sum(ref[pl.ds(v * n, n), :] for ref in refs)

    @pl.when(plen == 1)
    def _():
        add(0, rows(supply_ref))
        add(CAX - 1, rows(*high_refs))

    @pl.when(jnp.logical_and(cham, even))
    def _():
        add(CAX - 1, rows(ra_ref))

    @pl.when(jnp.logical_and(cham, odd))
    def _():
        add(0, rows(ra_ref))

    @pl.when(jnp.logical_and(cham, jnp.logical_and(even, ax > 0)))
    def _():
        add(0, rows(rb_ref))

    @pl.when(jnp.logical_and(cham, jnp.logical_and(odd, ax < n_ax - 1)))
    def _():
        add(CAX - 1, rows(rb_ref))

    @pl.when(jnp.logical_and(cham, ax == n_ax - 1))
    def _():
        add(CAX - 1, lambda v: state_ref[v, pl.ds(CAX - 1, n, stride=CAX), :])

    left = low_half()
    al = scale + scale * pltpu.roll(ul_ref[...], HALF, 1)
    ar = scale - scale * pltpu.roll(ur_ref[...], HALF, 1)
    for v in range(NV):
        head = pltpu.roll(hl_ref[pl.ds(v * CAX, CAX), :], HALF, 1)
        tail = pltpu.roll(hr_ref[pl.ds(v * CAX, CAX), :], HALF, 1)
        dst_ref[v, pl.ds(0, CAX), :] += jnp.where(left, al * head, 0.0)
        dst_ref[v, pl.ds((n - 1) * CAX, CAX), :] += jnp.where(left, 0.0, ar * tail)


def interior(q_ref, vel_ref, mix_ref, pre_ref, act_ref, heat_ref, finish):
    n = q_ref.shape[1] // CAX
    left = low_half()
    sub = lax.broadcasted_iota(jnp.int32, (CAX, LANES), 0)
    bottom, top = sub == 0, sub == CAX - 1

    def column(ref, v, j0):
        regs = [ref[v, pl.ds(pl.multiple_of((j0 + d) * CAX, CAX), CAX), :] for d in range(NJ)]
        before = ref[v, pl.ds(pl.multiple_of(jnp.maximum(j0 - 1, 0) * CAX, CAX), CAX), :]
        after = ref[v, pl.ds(pl.multiple_of(jnp.minimum(j0 + NJ, n - 1) * CAX, CAX), CAX), :]
        before = jnp.where(j0 == 0, 0.0, before)
        after = jnp.where(j0 + NJ == n, 0.0, after)
        turned = [pltpu.roll(x, HALF, 1) for x in [before] + regs + [after]]
        lefts = [jnp.where(left, turned[d], turned[d + 1]) for d in range(NJ)]
        rights = [jnp.where(left, turned[d + 1], turned[d + 2]) for d in range(NJ)]
        return regs, lefts, rights

    def body(c, carry):
        j0 = c * NJ
        _, u_left, u_right = column(vel_ref, 0, j0)
        w = [vel_ref[1, pl.ds(pl.multiple_of((j0 + d) * CAX, CAX), CAX), :] for d in range(NJ)]
        al = [0.1 + 0.1 * x for x in u_left]
        ar = [0.1 - 0.1 * x for x in u_right]
        wu = [0.1 + 0.1 * x for x in w]
        wd = [0.1 - 0.1 * x for x in w]
        src = []
        for d in range(NJ):
            state = [q_ref[v, pl.ds(pl.multiple_of((j0 + d) * CAX, CAX), CAX), :] for v in range(NV)]
            src.append(source(state, mix_ref, pre_ref, act_ref, heat_ref))
        for v in range(NV):
            regs, lefts, rights = column(q_ref, v, j0)
            for d in range(NJ):
                below = jnp.where(bottom, 0.0, pltpu.roll(wu[d] * regs[d], 1, 0))
                above = jnp.where(top, 0.0, pltpu.roll(wd[d] * regs[d], CAX - 1, 0))
                new = (0.6 * regs[d] + src[d][v]) + (al[d] * lefts[d] + ar[d] * rights[d]) + (below + above)
                finish(j0 + d, v, new)
        return carry

    lax.fori_loop(0, n // NJ, body, 0)


def inside_one_kernel(q_ref, vel_ref, mix_ref, pre_ref, act_ref, heat_ref, out_ref):
    def finish(j, v, new):
        out_ref[v, pl.ds(pl.multiple_of(j * CAX, CAX), CAX), :] = new

    interior(q_ref, vel_ref, mix_ref, pre_ref, act_ref, heat_ref, finish)


def inside_two_kernel(q_ref, q1_ref, vel_ref, mix_ref, pre_ref, act_ref, heat_ref, out_ref):
    def finish(j, v, new):
        at = pl.ds(pl.multiple_of(j * CAX, CAX), CAX)
        out_ref[v, at, :] = 0.5 * q_ref[v, at, :] + 0.5 * new

    interior(q1_ref, vel_ref, mix_ref, pre_ref, act_ref, heat_ref, finish)


def border_one_kernel(n_az, n_ax, n_out, part_ref, q_ref, vel_ref, hl_ref, hr_ref, s_in_ref, supply_ref, own_in_ref,
                      col_ref, slot_ref, open_ref, *rest):
    got, rest = rest[:n_out], rest[n_out:]
    out_refs, (q1_ref, tile_ref, s_ref, own_ref) = rest[:n_out], rest[n_out:]
    _, _, plen = roles()
    q1_ref[...] = part_ref[...]
    boundary(q_ref, q1_ref, 0.1, got[0], got[1], (s_in_ref,), supply_ref, hl_ref, hr_ref,
             hl_ref.at[pl.ds(NV * CAX, CAX)], hr_ref.at[pl.ds(NV * CAX, CAX)], n_ax)

    @pl.when(plen == 1)
    def _():
        total = own_in_ref[...]
        for ref in got:
            total = total + ref[...]
        tile_ref[...] = total

    @pl.when(plen == 0)
    def _():
        tile_ref[...] = jnp.zeros_like(tile_ref)

    extract(q1_ref, vel_ref, col_ref, slot_ref, open_ref, out_refs, s_ref, own_ref, n_az)


def tree_kernel(n_out, tile0_ref, down0_ref, own_ref, s1_ref, *rest):
    got, (tile_ref, step_ref, core_ref) = rest[:n_out], rest[n_out:]
    _, ax, plen = roles()

    @pl.when(plen == 0)
    def _():
        core_ref[...] = s1_ref[...]
        tile_ref[...] = jnp.zeros_like(tile_ref)
        step_ref[...] = jnp.zeros_like(step_ref)

    @pl.when(plen == 1)
    def _():
        total = own_ref[...]
        for ref in got:
            total = total + ref[...]
        tile_ref[...] = total
        pair = tile0_ref[...] + down0_ref[...]
        core_ref[...] = pair
        step_ref[...] = jnp.where(ax % 2 == 1, total, pair)


def inlet_kernel(q1_ref, tile_ref, step_ref, core_ref, dq_ref, pair_ref, core_out_ref, er_ref, el_ref):
    _, ax, plen = roles()
    n = q1_ref.shape[1] // CAX
    for v in range(NV):
        el_ref[pl.ds(v * CAX, CAX), :] = q1_ref[v, pl.ds(0, CAX), :]
        er_ref[pl.ds(v * CAX, CAX), :] = q1_ref[v, pl.ds((n - 1) * CAX, CAX), :]

    @pl.when(plen == 1)
    def _():
        pair = tile_ref[...] + step_ref[...]
        pair_ref[...] = pair
        core_out_ref[...] = pair
        dq_ref[...] = jnp.zeros_like(dq_ref)

    @pl.when(jnp.logical_and(plen == 0, ax > 0))
    def _():
        pair_ref[...] = jnp.zeros_like(pair_ref)
        core_out_ref[...] = jnp.zeros_like(core_out_ref)
        dq_ref[...] = jnp.zeros_like(dq_ref)

    @pl.when(jnp.logical_and(plen == 0, ax == 0))
    def _():
        pair_ref[...] = jnp.zeros_like(pair_ref)
        dq = 0.1 * (step_ref[...] + core_ref[...])
        dq_ref[...] = dq
        core_out_ref[...] = dq
        for v in range(NV):
            el_ref[pl.ds(v * CAX, 1), :] += dq_ref[pl.ds(v * n, 1), :]
            er_ref[pl.ds(v * CAX, 1), :] += dq_ref[pl.ds(v * n + n - 1, 1), :]


def last_kernel(n_ax, part_ref, q_ref, q1_ref, vel_ref, s1_in_ref, supply_ref, ra_ref, rb_ref, dq_ref, core_ref, far_ref,
                hl_ref, hr_ref, hl0_ref, hr0_ref, mix_ref, pre_ref, act_ref, heat_ref, out_ref):
    n = out_ref.shape[1] // CAX
    _, ax, plen = roles()
    out_ref[...] = part_ref[...]
    ul_ref, ur_ref = hl0_ref.at[pl.ds(NV * CAX, CAX)], hr0_ref.at[pl.ds(NV * CAX, CAX)]
    boundary(q1_ref, out_ref, 0.05, ra_ref, rb_ref, (s1_in_ref, core_ref), supply_ref, hl_ref, hr_ref, ul_ref, ur_ref, n_ax)

    @pl.when(jnp.logical_and(ax == 0, plen == 0))
    def _():
        first = lax.broadcasted_iota(jnp.int32, (n, LANES), 0) == 0
        last = lax.broadcasted_iota(jnp.int32, (n, LANES), 0) == n - 1
        left = lax.broadcasted_iota(jnp.int32, (n, LANES), 1) < HALF

        def neighbours(x, head, tail):
            before = jnp.where(first, head, pltpu.roll(x, 1, 0))
            after = jnp.where(last, tail, pltpu.roll(x, n - 1, 0))
            mid = pltpu.roll(x, HALF, 1)
            return (jnp.where(left, pltpu.roll(before, HALF, 1), mid),
                    jnp.where(left, mid, pltpu.roll(after, HALF, 1)))

        u = vel_ref[0, pl.ds(0, n, stride=CAX), :]
        w = vel_ref[1, pl.ds(0, n, stride=CAX), :]
        w_next = vel_ref[1, pl.ds(1, n, stride=CAX), :]
        u_left, u_right = neighbours(u, ul_ref[pl.ds(0, 1), :], ur_ref[pl.ds(0, 1), :])
        state = [q1_ref[v, pl.ds(0, n, stride=CAX), :] + dq_ref[pl.ds(v * n, n), :] for v in range(NV)]
        src = source(state, mix_ref, pre_ref, act_ref, heat_ref)
        for v in range(NV):
            q_left, q_right = neighbours(state[v], hl_ref[pl.ds(v * CAX, 1), :], hr_ref[pl.ds(v * CAX, 1), :])
            inlet = core_ref[pl.ds(v * n, n), :] + far_ref[pl.ds(v * n, n), :]
            above = (1.0 - w_next) * q1_ref[v, pl.ds(1, n, stride=CAX), :]
            new = 0.6 * state[v] + 0.1 * ((1.0 + u_left) * q_left + (1.0 - u_right) * q_right + inlet + above) + src[v]
            out_ref[v, pl.ds(0, n, stride=CAX), :] = 0.5 * q_ref[v, pl.ds(0, n, stride=CAX), :] + 0.5 * new
            out_ref[v, pl.ds(1, n, stride=CAX), :] += 0.05 * ((1.0 + w) * dq_ref[pl.ds(v * n, n), :])


def shape(*dims):
    return jax.ShapeDtypeStruct(dims, f32)


def call(kernel, inputs, kinds, outs, scratch=(), cost=None):
    spaces = {"s": pltpu.SMEM, "v": pltpu.VMEM, "a": pl.ANY}
    return pl.pallas_call(
        kernel,
        in_specs=[pl.BlockSpec(memory_space=spaces[k]) for k in kinds],
        out_specs=[pl.BlockSpec(memory_space=pltpu.VMEM)] * len(outs),
        out_shape=outs,
        scratch_shapes=list(scratch),
        cost_estimate=cost,
        compiler_params=pltpu.CompilerParams(vmem_limit_bytes=LIMIT),
    )(*inputs)


def local(n_az, n_ax, cells, speeds, supply, mix, prefactor, activation, heat, inj_column, inj_slot, inj_open):
    size = cells.shape[-1]
    n = size // LANES
    rows = NV * n

    def view(array):
        k = array.shape[0]
        return array.reshape(k, CAX, n, LANES).transpose(0, 2, 1, 3).reshape(k, CAX * n, LANES)

    def number(i, j, p):
        return (i * n_ax + j) * 2 + p

    every = [(i, j) for i in range(n_az) for j in range(n_ax)]

    def send(x, route):
        return lax.ppermute(x, AXES, [(number(*a), number(*b)) for a, b in route])

    def ring(step):
        return [((i, j, p), ((i + step) % n_az, j, p)) for i, j in every for p in (0, 1)]

    swap = [((i, j, p), (i, j, 1 - p)) for i, j in every for p in (0, 1)]
    n_out = n_az - 1

    def mate(k, j):
        return j ^ 1 if k == 0 else ((j + 1) ^ 1) - 1 if 0 < j < n_ax - 1 else n_ax - 1 - j

    def spread(k):
        out = [((i, j, 1), ((i + k + 1) % n_az, j, 1)) for i, j in every]
        if k < 2:
            out += [((i, j, 0), (i, mate(k, j), 0)) for i, j in every]
        return out

    q, vel = view(cells[0]), view(speeds[0])
    sup = supply.reshape(rows, LANES)
    col, slot, opened = inj_column.reshape(-1), inj_slot, inj_open
    react = (mix, prefactor, activation, heat)
    row, edge = shape(rows, LANES), shape(NV * CAX, LANES)

    whole = shape(*q.shape)
    work = pl.CostEstimate(flops=300 * q.shape[1] * LANES, transcendentals=20 * q.shape[1] * LANES,
                           bytes_accessed=12_000_000)

    got = call(functools.partial(first_kernel, n_az, n_out), (q, vel, col, slot, opened), "aasss",
               [row] * n_out + [whole, shape(*vel.shape), row, row] + [shape((NV + 1) * CAX, LANES)] * 2,
               [pltpu.SemaphoreType.DMA((2,))])
    outs, (qv, velv, s0, own0, er, el) = got[:n_out], got[n_out:]
    hl0, hr0 = send(er, ring(1)), send(el, ring(-1))
    s0r = send(s0, swap)
    ra = [send(x, spread(k)) for k, x in enumerate(outs)]
    part, = call(inside_one_kernel, (qv, velv) + react, "vvssss", [whole], cost=work)

    got = call(functools.partial(border_one_kernel, n_az, n_ax, n_out),
               (part, qv, velv, hl0, hr0, s0r, sup, own0, col, slot, opened) + tuple(ra),
               "v" * 8 + "s" * 3 + "v" * n_out, [row] * n_out + [whole, row, row, row])
    outs, (q1, tile0, s1, own1) = got[:n_out], got[n_out:]
    down = [((i, j, 1), (i, j - 1, 1)) for i, j in every if j % 2 == 1]
    across = [((i, 2, 1), (i, 0, 0)) for i in range(n_az)]
    rb = [send(x, spread(k)) for k, x in enumerate(outs)]
    down0 = send(tile0, down)

    tile1, step, core = call(functools.partial(tree_kernel, n_out), (tile0, down0, own1, s1) + tuple(rb),
                             "v" * (4 + n_out), [row] * 3)
    step_in = send(step, down + across)
    core_in = send(core, swap)
    part, = call(inside_two_kernel, (qv, q1, velv) + react, "vvvssss", [whole], cost=work)

    dq, pair1, core2, er, el = call(inlet_kernel, (q1, tile1, step_in, core_in), "vvvv", [row] * 3 + [edge] * 2)
    core2_in = send(core2, swap)
    far1 = send(pair1, across)
    hl1, hr1 = send(er, ring(1)), send(el, ring(-1))
    out, = call(functools.partial(last_kernel, n_ax),
                (part, qv, q1, velv, core_in, sup, rb[0], rb[1], dq, core2_in, far1, hl1, hr1, hl0, hr0) + react,
                "v" * 15 + "s" * 4, [whole])
    return out.reshape(NV, n, CAX, LANES).transpose(0, 2, 1, 3).reshape(1, NV, CAX, size)


def solution(mesh):
    return jax.shard_map(
        functools.partial(local, mesh.shape["az"], mesh.shape["ax"]),
        mesh=mesh,
        in_specs=(
            P("pl", None, "ax", "az"),
            P("pl", None, "ax", "az"),
            P(None, "ax", "az"),
            P(),
            P(),
            P(),
            P(),
            P(("az", "ax"), None),
            P(("az", "ax")),
            P(("az", "ax")),
        ),
        out_specs=P("pl", None, "ax", "az"),
        check_vma=False,
    )
```

time: 82.3 us -> 64.8 us (0.79)
  Pallas kernels: 26.8 us -> 15.1 us
  waiting for transfers between devices: 23.9 us -> 19.8 us
  other arithmetic: 2.24 us -> 0 us
  starting transfers between devices: 23.6 us -> 24.5 us
    pallas_call x4 -> x7, Pallas kernels: 26.8 us -> 15.1 us  [call(): pl.pallas_call(kernel, in_specs=[pl.BlockSpec(memory_space=spaces[k]) for...]
    ppermute x20 -> x16, waiting for transfers between devices: 23.9 us -> 19.8 us  [send(): return lax.ppermute(x, AXES, [(number(*a), number(*b)) for a, b in route])]
    slice x3 -> x0, local copies, waits for them, and re-layouts: 2.54 us -> none  [the longest x2 2.53 us: local(): u_l, u_r = (hl0[NV * CAX:], hr0[NV * CAX:])]
    unnamed x40 -> x20, local copies, waits for them, and re-layouts: 2.59 us -> 4.81 us
    add x2 -> x0, other arithmetic: 2.16 us -> none  [the longest x1 1.15 us: local(): tile1 = tile1 + x]
    ppermute x20 -> x16, starting transfers between devices: 23.6 us -> 24.5 us  [send(): return lax.ppermute(x, AXES, [(number(*a), number(*b)) for a, b in route])]
  transfers between devices with their start and end apart: 20 -> 16, of which waited for: 6 -> 4; matrix products, arithmetic and copies ran while one was open for 6% -> 0% of each run, Pallas kernels for 12% -> 15%
where the time goes in v2:
time: 64.8 us; the launch traced here: 64.5 us
  starting transfers between devices  24.5 us (38%)
  waiting for transfers between devices  19.8 us (31%)
  Pallas kernels  15.1 us (23%)
  local copies, waits for them, and re-layouts  4.81 us (7%)
    ppermute x16, starting transfers between devices, send(): return lax.ppermute(x, AXES, [(number(*a), number(*b)) for a, b in route])  24.5 us
    ppermute x16, waiting for transfers between devices, send(): return lax.ppermute(x, AXES, [(number(*a), number(*b)) for a, b in route])  19.8 us
    pallas_call x7, Pallas kernels, call(): pl.pallas_call(kernel, in_specs=[pl.BlockSpec(memory_space=spaces[k]) for...  15.1 us
    unnamed x20, local copies, waits for them, and re-layouts  4.81 us
  transfers between devices with their start and end apart: 16, of which 4 were waited for; matrix products, arithmetic and copies ran while one was open for 0% of the time, Pallas kernels for 15%

profile of v2, /device:TPU:0, one launch (start us, length us, event | category | flops | bytes accessed | tf_op | source)
XLA Modules:
  0.0 64.5 jit_solution(13987839727228453322)
XLA Ops:
  0.0 1.8 %copy-done = f32[1,10,8,8192]{3,2,1,0:T(8,128)S(1)} copy-done((f32[1,10,8,8192]{3,2,1,0:T(8,128)S(1)}, f32[1,10,8,8192]{3,2,1,0:T(8,128)}, u32[]{:S(2)}) %copy-start) | copy-done | bytes 2621464
  1.8 1.0 %copy-done.2 = f32[1,2,8,8192]{3,2,1,0:T(8,128)S(1)} copy-done((f32[1,2,8,8192]{3,2,1,0:T(8,128)S(1)}, f32[1,2,8,8192]{3,2,1,0:T(8,128)}, u32[]{:S(2)}) %copy-start.2) | copy-done | bytes 524312
  2.8 0.7 %copy-done.7 = s32[8,1]{0,1:T(1,128)S(1)} copy-done((s32[8,1]{0,1:T(1,128)S(1)}, s32[8,1]{0,1:T(1,128)}, u32[]{:S(2)}) %copy-start.7) | copy-done | bytes 56
  3.5 0.7 %copy-done.8 = s32[8]{0:T(128)S(1)} copy-done((s32[8]{0:T(128)S(1)}, s32[8]{0:T(128)}, u32[]{:S(2)}) %copy-start.8) | copy-done | bytes 56
  4.1 0.7 %copy-done.9 = s32[8]{0:T(128)S(1)} copy-done((s32[8]{0:T(128)S(1)}, s32[8]{0:T(128)}, u32[]{:S(2)}) %copy-start.9) | copy-done | bytes 56
  4.8 1.0 %shard_map.100 = (f32[640,128]{1,0:T(8,128)S(1)}, f32[640,128]{1,0:T(8,128)S(1)}, f32[640,128]{1,0:T(8,128)S(1)}, f32[10,512,128]{2,1,0:T(8,128)S(1)}, f32[2,512...) custom-call(f32[10,512,128]{2,1,0:T(8,128)S(1)} %bitcast.17, ...), custom_call_target="tpu_custom_call" | custom-call | tf_op jit(solution)/shard_map/pallas_call | solution.py:324
  5.8 0.8 %collective-permute-start.2 = (f32[640,128]{1,0:T(8,128)S(1)}, f32[640,128]{1,0:T(8,128)S(1)}, u32[]{:S(2)}, u32[]{:S(2)}) collective-permute-start(f32[640,128]{1,0:T(8,128)S(1)} %get-tuple-element.33), channel_id=1, source_target_pairs={{0,1},{1,0},{2,3},{3,2},{4,5},{5,4},{6,7},{7,6},{8,9},{9,8},{10,11... | collective-permute-start | bytes 983048 | tf_op jit(solution)/shard_map/ppermute | solution.py:350
  6.7 2.4 %collective-permute-start.3 = (f32[640,128]{1,0:T(8,128)S(1)}, f32[640,128]{1,0:T(8,128)S(1)}, u32[]{:S(2)}, u32[]{:S(2)}) collective-permute-start(f32[640,128]{1,0:T(8,128)S(1)} %get-tuple-element.35), channel_id=1, source_target_pairs={{1,9},{3,11},{5,13},{7,15},{9,17},{11,19},{13,21},{15,23},{17,25},... | collective-permute-start | bytes 983048 | tf_op jit(solution)/shard_map/ppermute | solution.py:350
  9.1 2.5 %collective-permute-start.4 = (f32[640,128]{1,0:T(8,128)S(1)}, f32[640,128]{1,0:T(8,128)S(1)}, u32[]{:S(2)}, u32[]{:S(2)}) collective-permute-start(f32[640,128]{1,0:T(8,128)S(1)} %get-tuple-element.36), channel_id=1, source_target_pairs={{1,17},{3,19},{5,21},{7,23},{9,25},{11,27},{13,29},{15,31},{17,1},... | collective-permute-start | bytes 983048 | tf_op jit(solution)/shard_map/ppermute | solution.py:350
  11.6 0.7 %collective-permute-start.5 = (f32[640,128]{1,0:T(8,128)S(1)}, f32[640,128]{1,0:T(8,128)S(1)}, u32[]{:S(2)}, u32[]{:S(2)}) collective-permute-start(f32[640,128]{1,0:T(8,128)S(1)} %get-tuple-element.37), channel_id=1, source_target_pairs={{1,25},{3,27},{5,29},{7,31},{9,1},{11,3},{13,5},{15,7},{17,9},{19,... | collective-permute-start | bytes 983048 | tf_op jit(solution)/shard_map/ppermute | solution.py:350
  12.2 1.5 %collective-permute-start = (f32[88,128]{1,0:T(8,128)S(1)}, f32[88,128]{1,0:T(8,128)S(1)}, u32[]{:S(2)}, u32[]{:S(2)}) collective-permute-start(f32[88,128]{1,0:T(8,128)S(1)} %get-tuple-element.31), channel_id=1, source_target_pairs={{0,8},{1,9},{2,10},{3,11},{4,12},{5,13},{6,14},{7,15},{8,16},{9,17... | collective-permute-start | bytes 135176 | tf_op jit(solution)/shard_map/ppermute | solution.py:350
  13.7 4.0 %collective-permute-done.hl_ref.hl0_ref = f32[88,128]{1,0:T(8,128)S(1)} collective-permute-done((f32[88,128]{1,0:T(8,128)S(1)}, f32[88,128]{1,0:T(8,128)S(1)}, u32[]{:S(2)}, u32[]{:S(2)}) %collective-permute-start) | collective-permute-done | bytes 45088 | tf_op jit(solution)/shard_map/ppermute | solution.py:350
  17.8 1.5 %collective-permute-start.1 = (f32[88,128]{1,0:T(8,128)S(1)}, f32[88,128]{1,0:T(8,128)S(1)}, u32[]{:S(2)}, u32[]{:S(2)}) collective-permute-start(f32[88,128]{1,0:T(8,128)S(1)} %get-tuple-element.32), channel_id=1, source_target_pairs={{0,24},{1,25},{2,26},{3,27},{4,28},{5,29},{6,30},{7,31},{8,0},{9,1... | collective-permute-start | bytes 135176 | tf_op jit(solution)/shard_map/ppermute | solution.py:350
  19.3 4.5 %shard_map.101.part_ref = f32[10,512,128]{2,1,0:T(8,128)S(1)} custom-call(f32[10,512,128]{2,1,0:T(8,128)S(1)} %get-tuple-element.29.q_ref, f32[2,512,128]{2,1,0:T(8,128)S(1)} %get-tuple-element.30.vel_ref, f32[9,9]{1,0:T(8,128)S(1)} %copy-done.3, f32[9]{0:T(128)S(1)} %copy-done.4, f32[9]{0:T(128)S(1)} %copy-done.5, f32[9]{0:T(128)S(1)} %copy-done.6), custom_call_target="tpu_custom_call" | custom-call | flops 19660800 | bytes 12000000 | tf_op jit(solution)/shard_map/pallas_call | solution.py:324
  23.9 1.2 %shard_map.102 = (f32[640,128]{1,0:T(8,128)S(1)}, f32[640,128]{1,0:T(8,128)S(1)}, f32[640,128]{1,0:T(8,128)S(1)}, f32[10,512,128]{2,1,0:T(8,128)S(1)}, f32[640,1...) custom-call(f32[10,512,128]{2,1,0:T(8,128)S(1)} %shard_map.101.part_ref, ...), custom_call_target="tpu_custom_call" | custom-call | tf_op jit(solution)/shard_map/pallas_call | solution.py:324
  25.1 0.9 %collective-permute-start.7 = (f32[640,128]{1,0:T(8,128)S(1)}, f32[640,128]{1,0:T(8,128)S(1)}, u32[]{:S(2)}, u32[]{:S(2)}) collective-permute-start(f32[640,128]{1,0:T(8,128)S(1)} %get-tuple-element.42), channel_id=1, source_target_pairs={{1,9},{3,11},{5,13},{7,15},{9,17},{11,19},{13,21},{15,23},{17,25},... | collective-permute-start | bytes 983048 | tf_op jit(solution)/shard_map/ppermute | solution.py:350
  26.0 0.9 %collective-permute-start.8 = (f32[640,128]{1,0:T(8,128)S(1)}, f32[640,128]{1,0:T(8,128)S(1)}, u32[]{:S(2)}, u32[]{:S(2)}) collective-permute-start(f32[640,128]{1,0:T(8,128)S(1)} %get-tuple-element.43), channel_id=1, source_target_pairs={{1,17},{3,19},{5,21},{7,23},{9,25},{11,27},{13,29},{15,31},{17,1},... | collective-permute-start | bytes 983048 | tf_op jit(solution)/shard_map/ppermute | solution.py:350
  26.9 0.7 %collective-permute-start.9 = (f32[640,128]{1,0:T(8,128)S(1)}, f32[640,128]{1,0:T(8,128)S(1)}, u32[]{:S(2)}, u32[]{:S(2)}) collective-permute-start(f32[640,128]{1,0:T(8,128)S(1)} %get-tuple-element.44), channel_id=1, source_target_pairs={{1,25},{3,27},{5,29},{7,31},{9,1},{11,3},{13,5},{15,7},{17,9},{19,... | collective-permute-start | bytes 983048 | tf_op jit(solution)/shard_map/ppermute | solution.py:350
  27.6 0.7 %collective-permute-start.6 = (f32[640,128]{1,0:T(8,128)S(1)}, f32[640,128]{1,0:T(8,128)S(1)}, u32[]{:S(2)}, u32[]{:S(2)}) collective-permute-start(f32[640,128]{1,0:T(8,128)S(1)} %get-tuple-element.39.tile0_ref), channel_id=1, source_target_pairs={{3,1},{7,5},{11,9},{15,13},{19,17},{23,21},{27,25},{31,29}} | collective-permute-start | bytes 983048 | tf_op jit(solution)/shard_map/ppermute | solution.py:350
  28.2 7.5 %collective-permute-done.7.rest_0_.ra_ref = f32[640,128]{1,0:T(8,128)S(1)} collective-permute-done((f32[640,128]{1,0:T(8,128)S(1)}, f32[640,128]{1,0:T(8,128)S(1)}, u32[]{:S(2)}, u32[]{:S(2)}) %collective-permute-start.7) | collective-permute-done | bytes 327712 | tf_op jit(solution)/shard_map/ppermute | solution.py:350
  35.8 0.1 shard_map.104
  35.8 4.4 %collective-permute-start.10 = (f32[640,128]{1,0:T(8,128)S(1)}, f32[640,128]{1,0:T(8,128)S(1)}, u32[]{:S(2)}, u32[]{:S(2)}) collective-permute-start(f32[640,128]{1,0:T(8,128)S(1)} %get-tuple-element.45), channel_id=1, source_target_pairs={{0,1},{1,0},{2,3},{3,2},{4,5},{5,4},{6,7},{7,6},{8,9},{9,8},{10,11... | collective-permute-start | bytes 983048 | tf_op jit(solution)/shard_map/ppermute | solution.py:350
  40.3 1.3 %collective-permute-start.11 = (f32[640,128]{1,0:T(8,128)S(1)}, f32[640,128]{1,0:T(8,128)S(1)}, u32[]{:S(2)}, u32[]{:S(2)}) collective-permute-start(f32[640,128]{1,0:T(8,128)S(1)} %get-tuple-element.47), channel_id=1, source_target_pairs={{3,1},{7,5},{11,9},{15,13},{19,17},{23,21},{27,25},{31,29},{5,0},{... | collective-permute-start | bytes 983048 | tf_op jit(solution)/shard_map/ppermute | solution.py:350
  41.6 8.1 %collective-permute-done.11.step_ref = f32[640,128]{1,0:T(8,128)S(1)} collective-permute-done((f32[640,128]{1,0:T(8,128)S(1)}, f32[640,128]{1,0:T(8,128)S(1)}, u32[]{:S(2)}, u32[]{:S(2)}) %collective-permute-start.11) | collective-permute-done | bytes 327712 | tf_op jit(solution)/shard_map/ppermute | solution.py:350
  49.7 0.1 shard_map.105
  49.8 2.0 %collective-permute-start.12 = (f32[640,128]{1,0:T(8,128)S(1)}, f32[640,128]{1,0:T(8,128)S(1)}, u32[]{:S(2)}, u32[]{:S(2)}) collective-permute-start(f32[640,128]{1,0:T(8,128)S(1)} %get-tuple-element.49), channel_id=1, source_target_pairs={{0,1},{1,0},{2,3},{3,2},{4,5},{5,4},{6,7},{7,6},{8,9},{9,8},{10,11... | collective-permute-start | bytes 983048 | tf_op jit(solution)/shard_map/ppermute | solution.py:350
  51.8 1.3 %collective-permute-start.13 = (f32[640,128]{1,0:T(8,128)S(1)}, f32[640,128]{1,0:T(8,128)S(1)}, u32[]{:S(2)}, u32[]{:S(2)}) collective-permute-start(f32[640,128]{1,0:T(8,128)S(1)} %get-tuple-element.50), channel_id=1, source_target_pairs={{5,0},{13,8},{21,16},{29,24}} | collective-permute-start | bytes 983048 | tf_op jit(solution)/shard_map/ppermute | solution.py:350
  53.1 0.1 collective-permute-start.14
  53.1 2.9 %collective-permute-start.15 = (f32[80,128]{1,0:T(8,128)S(1)}, f32[80,128]{1,0:T(8,128)S(1)}, u32[]{:S(2)}, u32[]{:S(2)}) collective-permute-start(f32[80,128]{1,0:T(8,128)S(1)} %get-tuple-element.52), channel_id=1, source_target_pairs={{0,24},{1,25},{2,26},{3,27},{4,28},{5,29},{6,30},{7,31},{8,0},{9,1... | collective-permute-start | bytes 122888 | tf_op jit(solution)/shard_map/ppermute | solution.py:350
  56.1 4.9 %shard_map.103.part_ref = f32[10,512,128]{2,1,0:T(8,128)S(1)} custom-call(f32[10,512,128]{2,1,0:T(8,128)S(1)} %get-tuple-element.29.q_ref, f32[10,512,128]{2,1,0:T(8,128)S(1)} %get-tuple-element.38.q1_ref, f32[2,512,128]{2,1,0:T(8,128)S(1)} %get-tuple-element.30.vel_ref, f32[9,9]{1,0:T(8,128)S(1)} %copy-done.3, f32[9]{0:T(128)S(1)} %copy-done.4, ...), custom_call_target="tpu_custom_call" | custom-call | flops 19660800 | bytes 12000000 | tf_op jit(solution)/shard_map/pallas_call | solution.py:324
  61.0 0.1 collective-permute-done.13.far_ref
  61.1 3.4 %shard_map.106 = f32[10,512,128]{2,1,0:T(8,128)} custom-call(f32[10,512,128]{2,1,0:T(8,128)S(1)} %shard_map.103.part_ref, f32[10,512,128]{2,1,0:T(8,128)S(1)} %get-tuple-element.29.q_ref, f32[10,512,128]{2,1,0:T(8,128)S(1)} %get-tuple-element.38.q1_ref, f32[2,512,128]{2,1,0:T(8,128)S(1)} %get-tuple-element.30.vel_ref, ...), custom_call_target="tpu_custom_call" | custom-call | tf_op jit(solution)/shard_map/pallas_call | solution.py:324
  (27 shorter events, 0.1 us)
Async XLA Ops:
  0.0 19.3 %copy-start.6 = (f32[9]{0:T(128)S(1)}, f32[9]{0:T(128)}, u32[]{:S(2)}) copy-start(f32[9]{0:T(128)} %heat_ref.5) | copy-start | bytes 112
  0.0 19.3 %copy-start.5 = (f32[9]{0:T(128)S(1)}, f32[9]{0:T(128)}, u32[]{:S(2)}) copy-start(f32[9]{0:T(128)} %act_ref.5) | copy-start | bytes 112
  0.0 19.3 %copy-start.4 = (f32[9]{0:T(128)S(1)}, f32[9]{0:T(128)}, u32[]{:S(2)}) copy-start(f32[9]{0:T(128)} %pre_ref.5) | copy-start | bytes 112
  0.0 1.8 %copy-start = (f32[1,10,8,8192]{3,2,1,0:T(8,128)S(1)}, f32[1,10,8,8192]{3,2,1,0:T(8,128)}, u32[]{:S(2)}) copy-start(f32[1,10,8,8192]{3,2,1,0:T(8,128)} %param.10) | copy-start | bytes 7864324
  1.8 1.0 %copy-start.2 = (f32[1,2,8,8192]{3,2,1,0:T(8,128)S(1)}, f32[1,2,8,8192]{3,2,1,0:T(8,128)}, u32[]{:S(2)}) copy-start(f32[1,2,8,8192]{3,2,1,0:T(8,128)} %param.11) | copy-start | bytes 1572868
  2.8 0.7 %copy-start.7 = (s32[8,1]{0,1:T(1,128)S(1)}, s32[8,1]{0,1:T(1,128)}, u32[]{:S(2)}) copy-start(s32[8,1]{0,1:T(1,128)} %param.17) | copy-start | bytes 100
  3.5 0.7 %copy-start.8 = (s32[8]{0:T(128)S(1)}, s32[8]{0:T(128)}, u32[]{:S(2)}) copy-start(s32[8]{0:T(128)} %slot_ref.3) | copy-start | bytes 100
  4.1 0.7 %copy-start.9 = (s32[8]{0:T(128)S(1)}, s32[8]{0:T(128)}, u32[]{:S(2)}) copy-start(s32[8]{0:T(128)} %open_ref.3) | copy-start | bytes 100
  4.8 14.5 %copy-start.3 = (f32[9,9]{1,0:T(8,128)S(1)}, f32[9,9]{1,0:T(8,128)}, u32[]{:S(2)}) copy-start(f32[9,9]{1,0:T(8,128)} %mix_ref.5) | copy-start | bytes 976
  5.8 18.0 %collective-permute-start.2 = (f32[640,128]{1,0:T(8,128)S(1)}, f32[640,128]{1,0:T(8,128)S(1)}, u32[]{:S(2)}, u32[]{:S(2)}) collective-permute-start(f32[640,128]{1,0:T(8,128)S(1)} %get-tuple-element.33), channel_id=1, source_target_pairs={{0,1},{1,0},{2,3},{3,2},{4,5},{5,4},{6,7},{7,6},{8,9},{9,8},{10,11... | collective-permute-start | bytes 983048 | tf_op jit(solution)/shard_map/ppermute | solution.py:350
  6.7 17.2 %collective-permute-start.3 = (f32[640,128]{1,0:T(8,128)S(1)}, f32[640,128]{1,0:T(8,128)S(1)}, u32[]{:S(2)}, u32[]{:S(2)}) collective-permute-start(f32[640,128]{1,0:T(8,128)S(1)} %get-tuple-element.35), channel_id=1, source_target_pairs={{1,9},{3,11},{5,13},{7,15},{9,17},{11,19},{13,21},{15,23},{17,25},... | collective-permute-start | bytes 983048 | tf_op jit(solution)/shard_map/ppermute | solution.py:350
  9.1 14.8 %collective-permute-start.4 = (f32[640,128]{1,0:T(8,128)S(1)}, f32[640,128]{1,0:T(8,128)S(1)}, u32[]{:S(2)}, u32[]{:S(2)}) collective-permute-start(f32[640,128]{1,0:T(8,128)S(1)} %get-tuple-element.36), channel_id=1, source_target_pairs={{1,17},{3,19},{5,21},{7,23},{9,25},{11,27},{13,29},{15,31},{17,1},... | collective-permute-start | bytes 983048 | tf_op jit(solution)/shard_map/ppermute | solution.py:350
  11.6 12.3 %collective-permute-start.5 = (f32[640,128]{1,0:T(8,128)S(1)}, f32[640,128]{1,0:T(8,128)S(1)}, u32[]{:S(2)}, u32[]{:S(2)}) collective-permute-start(f32[640,128]{1,0:T(8,128)S(1)} %get-tuple-element.37), channel_id=1, source_target_pairs={{1,25},{3,27},{5,29},{7,31},{9,1},{11,3},{13,5},{15,7},{17,9},{19,... | collective-permute-start | bytes 983048 | tf_op jit(solution)/shard_map/ppermute | solution.py:350
  12.2 5.5 %collective-permute-start = (f32[88,128]{1,0:T(8,128)S(1)}, f32[88,128]{1,0:T(8,128)S(1)}, u32[]{:S(2)}, u32[]{:S(2)}) collective-permute-start(f32[88,128]{1,0:T(8,128)S(1)} %get-tuple-element.31), channel_id=1, source_target_pairs={{0,8},{1,9},{2,10},{3,11},{4,12},{5,13},{6,14},{7,15},{8,16},{9,17... | collective-permute-start | bytes 135176 | tf_op jit(solution)/shard_map/ppermute | solution.py:350
  17.8 6.1 %collective-permute-start.1 = (f32[88,128]{1,0:T(8,128)S(1)}, f32[88,128]{1,0:T(8,128)S(1)}, u32[]{:S(2)}, u32[]{:S(2)}) collective-permute-start(f32[88,128]{1,0:T(8,128)S(1)} %get-tuple-element.32), channel_id=1, source_target_pairs={{0,24},{1,25},{2,26},{3,27},{4,28},{5,29},{6,30},{7,31},{8,0},{9,1... | collective-permute-start | bytes 135176 | tf_op jit(solution)/shard_map/ppermute | solution.py:350
  19.3 4.6 %copy-start.1 = (f32[10,1,8192]{2,1,0:T(1,128)S(1)}, f32[10,1,8192]{2,1,0:T(1,128)}, u32[]{:S(2)}) copy-start(f32[10,1,8192]{2,1,0:T(1,128)} %param.12) | copy-start | bytes 983044
  25.1 10.6 %collective-permute-start.7 = (f32[640,128]{1,0:T(8,128)S(1)}, f32[640,128]{1,0:T(8,128)S(1)}, u32[]{:S(2)}, u32[]{:S(2)}) collective-permute-start(f32[640,128]{1,0:T(8,128)S(1)} %get-tuple-element.42), channel_id=1, source_target_pairs={{1,9},{3,11},{5,13},{7,15},{9,17},{11,19},{13,21},{15,23},{17,25},... | collective-permute-start | bytes 983048 | tf_op jit(solution)/shard_map/ppermute | solution.py:350
  26.0 9.8 %collective-permute-start.8 = (f32[640,128]{1,0:T(8,128)S(1)}, f32[640,128]{1,0:T(8,128)S(1)}, u32[]{:S(2)}, u32[]{:S(2)}) collective-permute-start(f32[640,128]{1,0:T(8,128)S(1)} %get-tuple-element.43), channel_id=1, source_target_pairs={{1,17},{3,19},{5,21},{7,23},{9,25},{11,27},{13,29},{15,31},{17,1},... | collective-permute-start | bytes 983048 | tf_op jit(solution)/shard_map/ppermute | solution.py:350
  26.9 8.9 %collective-permute-start.9 = (f32[640,128]{1,0:T(8,128)S(1)}, f32[640,128]{1,0:T(8,128)S(1)}, u32[]{:S(2)}, u32[]{:S(2)}) collective-permute-start(f32[640,128]{1,0:T(8,128)S(1)} %get-tuple-element.44), channel_id=1, source_target_pairs={{1,25},{3,27},{5,29},{7,31},{9,1},{11,3},{13,5},{15,7},{17,9},{19,... | collective-permute-start | bytes 983048 | tf_op jit(solution)/shard_map/ppermute | solution.py:350
  27.6 8.2 %collective-permute-start.6 = (f32[640,128]{1,0:T(8,128)S(1)}, f32[640,128]{1,0:T(8,128)S(1)}, u32[]{:S(2)}, u32[]{:S(2)}) collective-permute-start(f32[640,128]{1,0:T(8,128)S(1)} %get-tuple-element.39.tile0_ref), channel_id=1, source_target_pairs={{3,1},{7,5},{11,9},{15,13},{19,17},{23,21},{27,25},{31,29}} | collective-permute-start | bytes 983048 | tf_op jit(solution)/shard_map/ppermute | solution.py:350
  35.8 5.7 %collective-permute-start.10 = (f32[640,128]{1,0:T(8,128)S(1)}, f32[640,128]{1,0:T(8,128)S(1)}, u32[]{:S(2)}, u32[]{:S(2)}) collective-permute-start(f32[640,128]{1,0:T(8,128)S(1)} %get-tuple-element.45), channel_id=1, source_target_pairs={{0,1},{1,0},{2,3},{3,2},{4,5},{5,4},{6,7},{7,6},{8,9},{9,8},{10,11... | collective-permute-start | bytes 983048 | tf_op jit(solution)/shard_map/ppermute | solution.py:350
  40.3 9.4 %collective-permute-start.11 = (f32[640,128]{1,0:T(8,128)S(1)}, f32[640,128]{1,0:T(8,128)S(1)}, u32[]{:S(2)}, u32[]{:S(2)}) collective-permute-start(f32[640,128]{1,0:T(8,128)S(1)} %get-tuple-element.47), channel_id=1, source_target_pairs={{3,1},{7,5},{11,9},{15,13},{19,17},{23,21},{27,25},{31,29},{5,0},{... | collective-permute-start | bytes 983048 | tf_op jit(solution)/shard_map/ppermute | solution.py:350
  49.8 11.2 %collective-permute-start.12 = (f32[640,128]{1,0:T(8,128)S(1)}, f32[640,128]{1,0:T(8,128)S(1)}, u32[]{:S(2)}, u32[]{:S(2)}) collective-permute-start(f32[640,128]{1,0:T(8,128)S(1)} %get-tuple-element.49), channel_id=1, source_target_pairs={{0,1},{1,0},{2,3},{3,2},{4,5},{5,4},{6,7},{7,6},{8,9},{9,8},{10,11... | collective-permute-start | bytes 983048 | tf_op jit(solution)/shard_map/ppermute | solution.py:350
  51.8 9.3 %collective-permute-start.13 = (f32[640,128]{1,0:T(8,128)S(1)}, f32[640,128]{1,0:T(8,128)S(1)}, u32[]{:S(2)}, u32[]{:S(2)}) collective-permute-start(f32[640,128]{1,0:T(8,128)S(1)} %get-tuple-element.50), channel_id=1, source_target_pairs={{5,0},{13,8},{21,16},{29,24}} | collective-permute-start | bytes 983048 | tf_op jit(solution)/shard_map/ppermute | solution.py:350
  53.1 7.8 %collective-permute-start.14 = (f32[80,128]{1,0:T(8,128)S(1)}, f32[80,128]{1,0:T(8,128)S(1)}, u32[]{:S(2)}, u32[]{:S(2)}) collective-permute-start(f32[80,128]{1,0:T(8,128)S(1)} %get-tuple-element.51), channel_id=1, source_target_pairs={{0,8},{1,9},{2,10},{3,11},{4,12},{5,13},{6,14},{7,15},{8,16},{9,17... | collective-permute-start | bytes 122888 | tf_op jit(solution)/shard_map/ppermute | solution.py:350
  53.1 7.8 %collective-permute-start.15 = (f32[80,128]{1,0:T(8,128)S(1)}, f32[80,128]{1,0:T(8,128)S(1)}, u32[]{:S(2)}, u32[]{:S(2)}) collective-permute-start(f32[80,128]{1,0:T(8,128)S(1)} %get-tuple-element.52), channel_id=1, source_target_pairs={{0,24},{1,25},{2,26},{3,27},{4,28},{5,29},{6,30},{7,31},{8,0},{9,1... | collective-permute-start | bytes 122888 | tf_op jit(solution)/shard_map/ppermute | solution.py:350

commit v3 on v2

v3 whole, which is shorter than its diff:
```python
import functools

import jax
import jax.numpy as jnp
from jax import lax
from jax.experimental import pallas as pl
from jax.experimental.pallas import tpu as pltpu
from jax.sharding import PartitionSpec as P

NV = 10
NS = 9
LANES = 128
CAX = 8
HALF = 64
AXES = ("az", "ax", "pl")
NJ = 4
LOG2E = 1.4426950408889634
LIMIT = 16 * 1024 * 1024

f32 = jnp.float32


def roles():
    return lax.axis_index("az"), lax.axis_index("ax"), lax.axis_index("pl")


def low_half():
    return lax.broadcasted_iota(jnp.int32, (CAX, LANES), 1) < HALF


def extract(q_ref, vel_ref, col_ref, slot_ref, open_ref, out_refs, s_ref, own_ref, n_az):
    az, ax, plen = roles()
    n = q_ref.shape[1] // CAX
    for v in range(NV):
        s_ref[pl.ds(v * n, n), :] = q_ref[v, pl.ds(0, n, stride=CAX), :]

    @pl.when(plen == 0)
    def _():
        w_low = vel_ref[1, pl.ds(0, n, stride=CAX), :]
        w_top = vel_ref[1, pl.ds(CAX - 1, n, stride=CAX), :]
        even = ax % 2 == 0

        def put(up_ref, down_ref):
            for v in range(NV):
                up_ref[pl.ds(v * n, n), :] = (1.0 + w_top) * q_ref[v, pl.ds(CAX - 1, n, stride=CAX), :]
                down_ref[pl.ds(v * n, n), :] = (1.0 - w_low) * q_ref[v, pl.ds(0, n, stride=CAX), :]

        @pl.when(even)
        def _():
            put(out_refs[0], out_refs[1])

        @pl.when(jnp.logical_not(even))
        def _():
            put(out_refs[1], out_refs[0])

    @pl.when(plen == 1)
    def _():
        refs = (own_ref,) + tuple(out_refs)
        for ref in refs:
            ref[...] = jnp.zeros_like(ref)
        blocks = n // CAX
        for b in range(blocks):
            tile = slot_ref[b]
            for shift, ref in enumerate(refs):
                here = jnp.logical_and(col_ref[b] == (az + shift) % n_az, open_ref[b] != 0)

                @pl.when(here)
                def _(ref=ref, b=b, tile=tile):
                    for v in range(NV):
                        row = pl.multiple_of(v * n + tile * CAX, CAX)
                        ref[pl.ds(row, CAX), :] += q_ref[v, pl.ds(CAX * CAX * b + CAX - 1, CAX, stride=CAX), :]


def edge_kernel(q_any, vel_any, er_ref, el_ref, q_l, q_r, sems):
    n = q_any.shape[1] // CAX
    ends = [(q_l, el_ref, 0), (q_r, er_ref, (n - 1) * CAX)]
    copies = []
    for k, (q_ref, e_ref, at) in enumerate(ends):
        copies.append(pltpu.make_async_copy(q_any.at[:, pl.ds(at, CAX)], q_ref, sems.at[2 * k]))
        copies.append(pltpu.make_async_copy(vel_any.at[0, pl.ds(at, CAX)], e_ref.at[pl.ds(NV * CAX, CAX)], sems.at[2 * k + 1]))
    for copy in copies:
        copy.start()
    for copy in copies:
        copy.wait()
    for q_ref, e_ref, _ in ends:
        for v in range(NV):
            e_ref[pl.ds(v * CAX, CAX), :] = q_ref[v]


def first_kernel(n_az, n_out, q_any, vel_any, col_any, slot_any, open_any, *outs):
    out_refs, rest = outs[:n_out], outs[n_out:]
    q_ref, vel_ref, s_ref, own_ref, col_ref, slot_ref, open_ref, sems = rest
    pairs = [(vel_any, vel_ref), (col_any, col_ref), (slot_any, slot_ref), (open_any, open_ref)]
    pairs += [(q_any.at[pl.ds(v, 2)], q_ref.at[pl.ds(v, 2)]) for v in range(0, NV, 2)]
    copies = [pltpu.make_async_copy(x, y, sems.at[k]) for k, (x, y) in enumerate(pairs)]
    for copy in copies:
        copy.start()
    for copy in copies:
        copy.wait()
    extract(q_ref, vel_ref, col_ref, slot_ref, open_ref, out_refs, s_ref, own_ref, n_az)


def source(state, mix_ref, pre_ref, act_ref, heat_ref):
    inv = 1.0 / jnp.maximum(state[NS], 0.5)
    rates = [pre_ref[k] * jnp.exp(-act_ref[k] * inv) * jnp.maximum(state[k], 0.0) for k in range(NS)]
    out = []
    for v in range(NV):
        acc = None
        for k in range(NS):
            term = (mix_ref[v, k] if v < NS else heat_ref[k]) * rates[k]
            acc = term if acc is None else acc + term
        out.append(0.2 * acc)
    return out


def fill_ghosts(state_ref, lo_ref, hi_ref, ra_ref, rb_ref, high_refs, supply_ref, n_ax):
    _, ax, plen = roles()
    n = state_ref.shape[1] // CAX
    even = ax % 2 == 0
    odd = jnp.logical_not(even)
    cham = plen == 0

    @pl.when(plen == 1)
    def _():
        lo_ref[...] = supply_ref[...]
        hi_ref[...] = sum(ref[...] for ref in high_refs)

    @pl.when(jnp.logical_and(cham, even))
    def _():
        hi_ref[...] = ra_ref[...]

    @pl.when(jnp.logical_and(cham, odd))
    def _():
        lo_ref[...] = ra_ref[...]

    @pl.when(jnp.logical_and(cham, ax == 0))
    def _():
        lo_ref[...] = jnp.zeros_like(lo_ref)

    @pl.when(jnp.logical_and(cham, jnp.logical_and(even, ax > 0)))
    def _():
        lo_ref[...] = rb_ref[...]

    @pl.when(jnp.logical_and(cham, jnp.logical_and(odd, ax < n_ax - 1)))
    def _():
        hi_ref[...] = rb_ref[...]

    @pl.when(jnp.logical_and(cham, ax == n_ax - 1))
    def _():
        for v in range(NV):
            hi_ref[pl.ds(v * n, n), :] = state_ref[v, pl.ds(CAX - 1, n, stride=CAX), :]


def add_border(v, dst_ref, scale, lo_ref, hi_ref, hl_ref, hr_ref, ul_ref, ur_ref):
    n = dst_ref.shape[1] // CAX
    left = low_half()
    dst_ref[v, pl.ds(0, n, stride=CAX), :] += scale * lo_ref[pl.ds(v * n, n), :]
    dst_ref[v, pl.ds(CAX - 1, n, stride=CAX), :] += scale * hi_ref[pl.ds(v * n, n), :]
    al = scale + scale * pltpu.roll(ul_ref[...], HALF, 1)
    ar = scale - scale * pltpu.roll(ur_ref[...], HALF, 1)
    head = pltpu.roll(hl_ref[pl.ds(v * CAX, CAX), :], HALF, 1)
    tail = pltpu.roll(hr_ref[pl.ds(v * CAX, CAX), :], HALF, 1)
    dst_ref[v, pl.ds(0, CAX), :] += jnp.where(left, al * head, 0.0)
    dst_ref[v, pl.ds((n - 1) * CAX, CAX), :] += jnp.where(left, 0.0, ar * tail)


def mixing(a_ref, scale, mix_ref, pre_ref, heat_ref):
    width = NV * CAX
    col = lax.broadcasted_iota(jnp.int32, (CAX, 3 * width), 1)
    row = lax.broadcasted_iota(jnp.int32, (CAX, 3 * width), 0)
    inner = col % width
    species, lane = inner // CAX, inner % CAX
    for v in range(NV):
        block = jnp.zeros((CAX, 3 * width), f32)
        for k in range(NS):
            value = (0.2 * scale) * pre_ref[k] * (mix_ref[v, k] if v < NS else heat_ref[k])
            block = jnp.where(species == k, value, block)
        block = jnp.where(lane == row, block, 0.0)
        high = block.astype(jnp.bfloat16).astype(f32)
        a_ref[pl.ds(v * CAX, CAX), :] = jnp.where(col // width == 1, block - high, high)


def interior(q_ref, vel_ref, a_ref, scale, mix_ref, pre_ref, act_ref, heat_ref, finish):
    n = q_ref.shape[1] // CAX
    left = low_half()
    sub = lax.broadcasted_iota(jnp.int32, (CAX, LANES), 0)
    bottom, top = sub == 0, sub == CAX - 1
    mixing(a_ref, scale, mix_ref, pre_ref, heat_ref)
    a = a_ref[...].astype(jnp.bfloat16)
    power = [act_ref[k] * (-LOG2E) for k in range(NS)]
    c = 0.1 * scale

    def reg(ref, v, j):
        return ref[v, pl.ds(pl.multiple_of(j * CAX, CAX), CAX), :]

    def column(ref, v, j0):
        regs = [reg(ref, v, j0 + d) for d in range(NJ)]
        before = jnp.where(j0 == 0, 0.0, reg(ref, v, jnp.maximum(j0 - 1, 0)))
        after = jnp.where(j0 + NJ == n, 0.0, reg(ref, v, jnp.minimum(j0 + NJ, n - 1)))
        turned = [pltpu.roll(x, HALF, 1) for x in [before] + regs + [after]]
        lefts = [jnp.where(left, turned[d], turned[d + 1]) for d in range(NJ)]
        rights = [jnp.where(left, turned[d + 1], turned[d + 2]) for d in range(NJ)]
        return regs, lefts, rights

    def body(step, carry):
        j0 = step * NJ
        rates = []
        for d in range(NJ):
            inv = 1.0 / jnp.maximum(reg(q_ref, NS, j0 + d), 0.5)
            some = [jnp.exp2(power[k] * inv) * jnp.maximum(reg(q_ref, k, j0 + d), 0.0) for k in range(NS)]
            rates.append(jnp.concatenate(some + [jnp.zeros((CAX, LANES), f32)], axis=0))
        rate = jnp.concatenate(rates, axis=1)
        high = rate.astype(jnp.bfloat16)
        low = (rate - high.astype(f32)).astype(jnp.bfloat16)
        src = jnp.dot(a, jnp.concatenate([high, high, low], axis=0), preferred_element_type=f32)
        _, u_left, u_right = column(vel_ref, 0, j0)
        w = [reg(vel_ref, 1, j0 + d) for d in range(NJ)]
        al = [c + c * x for x in u_left]
        ar = [c - c * x for x in u_right]
        wu = [jnp.where(bottom, 0.0, c + c * pltpu.roll(x, 1, 0)) for x in w]
        wd = [jnp.where(top, 0.0, c - c * pltpu.roll(x, CAX - 1, 0)) for x in w]
        for v in range(NV):
            regs, lefts, rights = column(q_ref, v, j0)
            for d in range(NJ):
                vertical = wu[d] * pltpu.roll(regs[d], 1, 0) + wd[d] * pltpu.roll(regs[d], CAX - 1, 0)
                new = (0.6 * scale) * regs[d] + src[v * CAX:(v + 1) * CAX, d * LANES:(d + 1) * LANES]
                finish(j0 + d, v, new + (al[d] * lefts[d] + ar[d] * rights[d]) + vertical)
        return carry

    lax.fori_loop(0, n // NJ, body, 0)


def inside_one_kernel(q_ref, vel_ref, mix_ref, pre_ref, act_ref, heat_ref, out_ref, a_ref):
    def finish(j, v, new):
        out_ref[v, pl.ds(pl.multiple_of(j * CAX, CAX), CAX), :] = new

    interior(q_ref, vel_ref, a_ref, 1.0, mix_ref, pre_ref, act_ref, heat_ref, finish)


def inside_two_kernel(q_ref, q1_ref, vel_ref, mix_ref, pre_ref, act_ref, heat_ref, out_ref, er_ref, el_ref, a_ref):
    n = q_ref.shape[1] // CAX
    for v in range(NV):
        el_ref[pl.ds(v * CAX, CAX), :] = q1_ref[v, pl.ds(0, CAX), :]
        er_ref[pl.ds(v * CAX, CAX), :] = q1_ref[v, pl.ds((n - 1) * CAX, CAX), :]

    def finish(j, v, new):
        at = pl.ds(pl.multiple_of(j * CAX, CAX), CAX)
        out_ref[v, at, :] = 0.5 * q_ref[v, at, :] + new

    interior(q1_ref, vel_ref, a_ref, 0.5, mix_ref, pre_ref, act_ref, heat_ref, finish)


def border_one_kernel(n_az, n_ax, n_out, s_in_ref, *rest):
    late, rest = rest[:n_out - 2], rest[n_out - 2:]
    hl_ref, hr_ref, part_ref, q_ref, vel_ref, supply_ref, own_in_ref, col_ref, slot_ref, open_ref = rest[2:12]
    got, rest = rest[:2] + late, rest[12:]
    out_refs, (q1_ref, tile_ref, s_ref, own_ref, lo_ref, hi_ref) = rest[:n_out], rest[n_out:]
    _, _, plen = roles()
    fill_ghosts(q_ref, lo_ref, hi_ref, got[0], got[1], (s_in_ref,), supply_ref, n_ax)
    for v in range(NV):
        q1_ref[v] = part_ref[v]
        add_border(v, q1_ref, 0.1, lo_ref, hi_ref, hl_ref, hr_ref,
                   hl_ref.at[pl.ds(NV * CAX, CAX)], hr_ref.at[pl.ds(NV * CAX, CAX)])

    @pl.when(plen == 1)
    def _():
        total = own_in_ref[...]
        for ref in got:
            total = total + ref[...]
        tile_ref[...] = total

    @pl.when(plen == 0)
    def _():
        tile_ref[...] = jnp.zeros_like(tile_ref)

    extract(q1_ref, vel_ref, col_ref, slot_ref, open_ref, out_refs, s_ref, own_ref, n_az)


def tree_kernel(n_out, tile0_ref, down0_ref, own_ref, s1_ref, row_ref, *rest):
    got, (tile_ref, step_ref, core_ref) = rest[:n_out], rest[n_out:]
    _, ax, plen = roles()

    @pl.when(plen == 0)
    def _():
        core_ref[...] = s1_ref[...]
        tile_ref[...] = jnp.zeros_like(tile_ref)
        step_ref[...] = row_ref[...]

    @pl.when(plen == 1)
    def _():
        total = own_ref[...]
        for ref in got:
            total = total + ref[...]
        tile_ref[...] = total
        pair = tile0_ref[...] + down0_ref[...]
        core_ref[...] = pair
        step_ref[...] = jnp.where(ax % 2 == 1, total, pair)


def inlet_kernel(er_in_ref, el_in_ref, tile_ref, step_ref, core_ref, dq_ref, pair_ref, core_out_ref, er_ref, el_ref):
    _, ax, plen = roles()
    n = dq_ref.shape[0] // NV
    er_ref[...] = er_in_ref[...]
    el_ref[...] = el_in_ref[...]

    @pl.when(plen == 1)
    def _():
        pair = tile_ref[...] + step_ref[...]
        pair_ref[...] = pair
        core_out_ref[...] = pair
        dq_ref[...] = jnp.zeros_like(dq_ref)

    @pl.when(jnp.logical_and(plen == 0, ax > 0))
    def _():
        pair_ref[...] = jnp.zeros_like(pair_ref)
        core_out_ref[...] = jnp.zeros_like(core_out_ref)
        dq_ref[...] = jnp.zeros_like(dq_ref)

    @pl.when(jnp.logical_and(plen == 0, ax == 0))
    def _():
        pair_ref[...] = jnp.zeros_like(pair_ref)
        dq = 0.1 * (step_ref[...] + core_ref[...])
        dq_ref[...] = dq
        core_out_ref[...] = dq
        for v in range(NV):
            el_ref[pl.ds(v * CAX, 1), :] += dq_ref[pl.ds(v * n, 1), :]
            er_ref[pl.ds(v * CAX, 1), :] += dq_ref[pl.ds(v * n + n - 1, 1), :]


def last_kernel(n_ax, part_ref, q_ref, q1_ref, vel_ref, s1_in_ref, supply_ref, ra_ref, rb_ref, dq_ref, core_ref, far_ref,
                hl_ref, hr_ref, hl0_ref, hr0_ref, mix_ref, pre_ref, act_ref, heat_ref, out_any,
                out_ref, row_ref, lo_ref, hi_ref, sems):
    n = out_ref.shape[1] // CAX
    _, ax, plen = roles()
    inlet_side = jnp.logical_and(ax == 0, plen == 0)
    ul_ref, ur_ref = hl0_ref.at[pl.ds(NV * CAX, CAX)], hr0_ref.at[pl.ds(NV * CAX, CAX)]
    fill_ghosts(q1_ref, lo_ref, hi_ref, ra_ref, rb_ref, (s1_in_ref, core_ref), supply_ref, n_ax)

    @pl.when(inlet_side)
    def _():
        first = lax.broadcasted_iota(jnp.int32, (n, LANES), 0) == 0
        last = lax.broadcasted_iota(jnp.int32, (n, LANES), 0) == n - 1
        left = lax.broadcasted_iota(jnp.int32, (n, LANES), 1) < HALF

        def neighbours(x, head, tail):
            before = jnp.where(first, head, pltpu.roll(x, 1, 0))
            after = jnp.where(last, tail, pltpu.roll(x, n - 1, 0))
            mid = pltpu.roll(x, HALF, 1)
            return (jnp.where(left, pltpu.roll(before, HALF, 1), mid),
                    jnp.where(left, mid, pltpu.roll(after, HALF, 1)))

        u = vel_ref[0, pl.ds(0, n, stride=CAX), :]
        w_next = vel_ref[1, pl.ds(1, n, stride=CAX), :]
        u_left, u_right = neighbours(u, ul_ref[pl.ds(0, 1), :], ur_ref[pl.ds(0, 1), :])
        state = [q1_ref[v, pl.ds(0, n, stride=CAX), :] + dq_ref[pl.ds(v * n, n), :] for v in range(NV)]
        src = source(state, mix_ref, pre_ref, act_ref, heat_ref)
        for v in range(NV):
            q_left, q_right = neighbours(state[v], hl_ref[pl.ds(v * CAX, 1), :], hr_ref[pl.ds(v * CAX, 1), :])
            inlet = core_ref[pl.ds(v * n, n), :] + far_ref[pl.ds(v * n, n), :]
            above = (1.0 - w_next) * q1_ref[v, pl.ds(1, n, stride=CAX), :]
            new = 0.6 * state[v] + 0.1 * ((1.0 + u_left) * q_left + (1.0 - u_right) * q_right + inlet + above) + src[v]
            row_ref[pl.ds(v * n, n), :] = 0.5 * q_ref[v, pl.ds(0, n, stride=CAX), :] + 0.5 * new

    copies = []
    for v in range(NV):
        out_ref[v] = part_ref[v]
        add_border(v, out_ref, 0.05, lo_ref, hi_ref, hl_ref, hr_ref, ul_ref, ur_ref)

        @pl.when(inlet_side)
        def _(v=v):
            w = vel_ref[1, pl.ds(0, n, stride=CAX), :]
            out_ref[v, pl.ds(0, n, stride=CAX), :] = row_ref[pl.ds(v * n, n), :]
            out_ref[v, pl.ds(1, n, stride=CAX), :] += 0.05 * ((1.0 + w) * dq_ref[pl.ds(v * n, n), :])

        copies.append(pltpu.make_async_copy(out_ref.at[v], out_any.at[v], sems.at[v]))
        copies[-1].start()
    for copy in copies:
        copy.wait()


def shape(*dims):
    return jax.ShapeDtypeStruct(dims, f32)


def call(kernel, inputs, kinds, outs, scratch=(), cost=None, to=pltpu.VMEM):
    spaces = {"s": pltpu.SMEM, "v": pltpu.VMEM, "h": pltpu.HBM}
    return pl.pallas_call(
        kernel,
        in_specs=[pl.BlockSpec(memory_space=spaces[k]) for k in kinds],
        out_specs=[pl.BlockSpec(memory_space=to)] * len(outs),
        out_shape=outs,
        scratch_shapes=list(scratch),
        cost_estimate=cost,
        compiler_params=pltpu.CompilerParams(vmem_limit_bytes=LIMIT),
    )(*inputs)


def local(n_az, n_ax, cells, speeds, supply, mix, prefactor, activation, heat, inj_column, inj_slot, inj_open):
    size = cells.shape[-1]
    n = size // LANES
    rows = NV * n

    def view(array):
        k = array.shape[0]
        return array.reshape(k, CAX, n, LANES).transpose(0, 2, 1, 3).reshape(k, CAX * n, LANES)

    def number(i, j, p):
        return (i * n_ax + j) * 2 + p

    every = [(i, j) for i in range(n_az) for j in range(n_ax)]

    def send(x, route):
        return lax.ppermute(x, AXES, [(number(*a), number(*b)) for a, b in route])

    def ring(step):
        return [((i, j, p), ((i + step) % n_az, j, p)) for i, j in every for p in (0, 1)]

    swap = [((i, j, p), (i, j, 1 - p)) for i, j in every for p in (0, 1)]
    n_out = n_az - 1

    def mate(k, j):
        return j ^ 1 if k == 0 else ((j + 1) ^ 1) - 1 if 0 < j < n_ax - 1 else n_ax - 1 - j

    def spread(k):
        out = [((i, j, 1), ((i + k + 1) % n_az, j, 1)) for i, j in every]
        if k < 2:
            out += [((i, j, 0), (i, mate(k, j), 0)) for i, j in every]
        return out

    q, vel = view(cells[0]), view(speeds[0])
    sup = supply.reshape(rows, LANES)
    col, slot, opened = inj_column.reshape(-1), inj_slot, inj_open
    react = (mix, prefactor, activation, heat)
    row, edge = shape(rows, LANES), shape(NV * CAX, LANES)

    whole = shape(*q.shape)
    work = pl.CostEstimate(flops=300 * q.shape[1] * LANES, transcendentals=20 * q.shape[1] * LANES,
                           bytes_accessed=12_000_000)

    raw = tuple(pltpu.with_memory_space_constraint(x, pltpu.HBM) for x in (q, vel, col, slot, opened))
    er, el = call(edge_kernel, raw[:2], "hh", [shape((NV + 1) * CAX, LANES)] * 2,
                  [pltpu.VMEM((NV, CAX, LANES), f32)] * 2 + [pltpu.SemaphoreType.DMA((4,))])
    hl0, hr0 = send(er, ring(1)), send(el, ring(-1))
    got = call(functools.partial(first_kernel, n_az, n_out), raw, "hhhhh",
               [row] * n_out + [whole, shape(*vel.shape), row, row],
               [pltpu.SMEM(col.shape, jnp.int32)] * 3 + [pltpu.SemaphoreType.DMA((4 + NV // 2,))])
    outs, (qv, velv, s0, own0) = got[:n_out], got[n_out:]
    s0r = send(s0, swap)
    late = [send(outs[k], spread(k)) for k in range(2, n_out)]
    ra = [send(outs[0], spread(0))]
    after, hl0, hr0 = lax.optimization_barrier((outs[1], hl0, hr0))
    ra.append(send(after, spread(1)))
    matrix = pltpu.VMEM((NV * CAX, 3 * NV * CAX), f32)
    part, = call(inside_one_kernel, (qv, velv) + react, "vvssss", [whole], [matrix], cost=work)

    got = call(functools.partial(border_one_kernel, n_az, n_ax, n_out),
               (s0r, *late, *ra, hl0, hr0, part, qv, velv, sup, own0, col, slot, opened),
               "v" * (n_out + 8) + "s" * 3, [row] * n_out + [whole, row, row, row],
               [pltpu.VMEM((rows, LANES), f32)] * 2)
    outs, (q1, tile0, s1, own1) = got[:n_out], got[n_out:]
    down = [((i, j, 1), (i, j - 1, 1)) for i, j in every if j % 2 == 1]
    across = [((i, 2, 1), (i, 0, 0)) for i in range(n_az)]
    inner = [((i, j, 0), (i, mate(1, j), 0)) for i, j in every if 0 < j < n_ax - 1]
    rb = [send(outs[k], [(x, y) for x, y in spread(k) if k == 0 or x[2] == 1]) for k in range(n_out)]
    down0 = send(tile0, down)

    tile1, step, core = call(functools.partial(tree_kernel, n_out), (tile0, down0, own1, s1, outs[1]) + tuple(rb),
                             "v" * (5 + n_out), [row] * 3)
    step_in = send(step, down + across + inner)
    core_in = send(core, swap)
    part, er, el = call(inside_two_kernel, (qv, q1, velv) + react, "vvvssss", [whole, edge, edge], [matrix], cost=work)

    dq, pair1, core2, er, el = call(inlet_kernel, (er, el, tile1, step_in, core_in), "vvvvv", [row] * 3 + [edge] * 2)
    far1 = send(pair1, across)
    core2_in = send(core2, swap)
    hl1, hr1 = send(er, ring(1)), send(el, ring(-1))
    out, = call(functools.partial(last_kernel, n_ax),
                (part, qv, q1, velv, core_in, sup, rb[0], step_in, dq, core2_in, far1, hl1, hr1, hl0, hr0) + react,
                "v" * 15 + "s" * 4, [whole],
                [pltpu.VMEM(q.shape, f32)] + [pltpu.VMEM((rows, LANES), f32)] * 3 + [pltpu.SemaphoreType.DMA((NV,))],
                to=pltpu.HBM)
    return out.reshape(NV, n, CAX, LANES).transpose(0, 2, 1, 3).reshape(1, NV, CAX, size)


def solution(mesh):
    return jax.shard_map(
        functools.partial(local, mesh.shape["az"], mesh.shape["ax"]),
        mesh=mesh,
        in_specs=(
            P("pl", None, "ax", "az"),
            P("pl", None, "ax", "az"),
            P(None, "ax", "az"),
            P(),
            P(),
            P(),
            P(),
            P(("az", "ax"), None),
            P(("az", "ax")),
            P(("az", "ax")),
        ),
        out_specs=P("pl", None, "ax", "az"),
        check_vma=False,
    )
```

time: 64.8 us -> 60.8 us (0.938)
  local copies, waits for them, and re-layouts: 4.81 us -> 0.04 us
  Pallas kernels: 15.1 us -> 16.2 us
    unnamed x20 -> x16, local copies, waits for them, and re-layouts: 4.81 us -> 0.04 us
    pallas_call x7 -> x8, Pallas kernels: 15.1 us -> 16.2 us  [call(): pl.pallas_call(kernel, in_specs=[pl.BlockSpec(memory_space=spaces[k]) for...]
  transfers between devices with their start and end apart: 16 -> 16, of which waited for: 4 -> 6; matrix products, arithmetic and copies ran while one was open for 0% -> 0% of each run, Pallas kernels for 15% -> 18%
where the time goes in v3:
time: 60.8 us; the launch traced here: 60.5 us
  starting transfers between devices  24.6 us (40%)
  waiting for transfers between devices  19.5 us (32%)
  Pallas kernels  16.2 us (27%)
    ppermute x16, starting transfers between devices, send(): return lax.ppermute(x, AXES, [(number(*a), number(*b)) for a, b in route])  24.6 us
    ppermute x16, waiting for transfers between devices, send(): return lax.ppermute(x, AXES, [(number(*a), number(*b)) for a, b in route])  19.5 us
    pallas_call x8, Pallas kernels, call(): pl.pallas_call(kernel, in_specs=[pl.BlockSpec(memory_space=spaces[k]) for...  16.2 us
  transfers between devices with their start and end apart: 16, of which 6 were waited for; matrix products, arithmetic and copies ran while one was open for 0% of the time, Pallas kernels for 18%

profile of v3, /device:TPU:0, one launch (start us, length us, event | category | flops | bytes accessed | tf_op | source)
XLA Modules:
  0.0 60.5 jit_solution(5207196385509664396)
XLA Ops:
  0.0 0.9 %shard_map.101 = (f32[88,128]{1,0:T(8,128)S(1)}, f32[88,128]{1,0:T(8,128)S(1)}) custom-call(f32[10,512,128]{2,1,0:T(8,128)} %bitcast.21, f32[2,512,128]{2,1,0:T(8,128)} %bitcast.23), custom_call_target="tpu_custom_call" | custom-call | tf_op jit(solution)/shard_map/pallas_call | solution.py:387
  0.9 3.0 %collective-permute-start.3 = (f32[88,128]{1,0:T(8,128)S(1)}, f32[88,128]{1,0:T(8,128)S(1)}, u32[]{:S(2)}, u32[]{:S(2)}) collective-permute-start(f32[88,128]{1,0:T(8,128)S(1)} %get-tuple-element.40), channel_id=1, source_target_pairs={{0,8},{1,9},{2,10},{3,11},{4,12},{5,13},{6,14},{7,15},{8,16},{9,17... | collective-permute-start | bytes 135176 | tf_op jit(solution)/shard_map/ppermute | solution.py:413
  3.9 1.0 %collective-permute-start.4 = (f32[88,128]{1,0:T(8,128)S(1)}, f32[88,128]{1,0:T(8,128)S(1)}, u32[]{:S(2)}, u32[]{:S(2)}) collective-permute-start(f32[88,128]{1,0:T(8,128)S(1)} %get-tuple-element.41), channel_id=1, source_target_pairs={{0,24},{1,25},{2,26},{3,27},{4,28},{5,29},{6,30},{7,31},{8,0},{9,1... | collective-permute-start | bytes 135176 | tf_op jit(solution)/shard_map/ppermute | solution.py:413
  4.9 2.1 %shard_map.100 = (f32[640,128]{1,0:T(8,128)S(1)}, f32[640,128]{1,0:T(8,128)S(1)}, f32[640,128]{1,0:T(8,128)S(1)}, f32[10,512,128]{2,1,0:T(8,128)S(1)}, f32[2,512...) custom-call(f32[10,512,128]{2,1,0:T(8,128)} %bitcast.22, f32[2,512,128]{2,1,0:T(8,128)} %bitcast.24, ...), custom_call_target="tpu_custom_call" | custom-call | tf_op jit(solution)/shard_map/pallas_call | solution.py:387
  7.1 0.1 collective-permute-start
  7.2 0.7 %collective-permute-start.1 = (f32[640,128]{1,0:T(8,128)S(1)}, f32[640,128]{1,0:T(8,128)S(1)}, u32[]{:S(2)}, u32[]{:S(2)}) collective-permute-start(f32[640,128]{1,0:T(8,128)S(1)} %get-tuple-element.37), channel_id=1, source_target_pairs={{1,25},{3,27},{5,29},{7,31},{9,1},{11,3},{13,5},{15,7},{17,9},{19,... | collective-permute-start | bytes 983048 | tf_op jit(solution)/shard_map/ppermute | solution.py:413
  7.8 2.0 %collective-permute-start.2 = (f32[640,128]{1,0:T(8,128)S(1)}, f32[640,128]{1,0:T(8,128)S(1)}, u32[]{:S(2)}, u32[]{:S(2)}) collective-permute-start(f32[640,128]{1,0:T(8,128)S(1)} %get-tuple-element.38), channel_id=1, source_target_pairs={{1,9},{3,11},{5,13},{7,15},{9,17},{11,19},{13,21},{15,23},{17,25},... | collective-permute-start | bytes 983048 | tf_op jit(solution)/shard_map/ppermute | solution.py:413
  9.9 2.5 %collective-permute-start.5 = (f32[640,128]{1,0:T(8,128)S(1)}, f32[640,128]{1,0:T(8,128)S(1)}, u32[]{:S(2)}, u32[]{:S(2)}) collective-permute-start(f32[640,128]{1,0:T(8,128)S(1)} %get-tuple-element.42), channel_id=1, source_target_pairs={{1,17},{3,19},{5,21},{7,23},{9,25},{11,27},{13,29},{15,31},{17,1},... | collective-permute-start | bytes 983048 | tf_op jit(solution)/shard_map/ppermute | solution.py:413
  12.4 0.0 copy-start.6
  12.4 0.0 copy-start.7
  12.4 4.2 %shard_map.102.rest_5_ = f32[10,512,128]{2,1,0:T(8,128)S(1)} custom-call(f32[10,512,128]{2,1,0:T(8,128)S(1)} %get-tuple-element.35.q_ref.rest_6_, f32[2,512,128]{2,1,0:T(8,128)S(1)} %get-tuple-element.45.vel_ref.rest_7_, f32[9,9]{1,0:T(8,128)S(1)} %copy-done.1, f32[9]{0:T(128)S(1)} %copy-done.2, f32[9]{0:T(128)S(1)} %copy-done.3, f32[9]{0:T(128)S(1)} %copy-done.4), custom_call_target="tpu_custom_call" | custom-call | flops 19660800 | bytes 12000000 | tf_op jit(solution)/shard_map/pallas_call | solution.py:387
  16.7 4.3 %collective-permute-done.5.rest_2_ = f32[640,128]{1,0:T(8,128)S(1)} collective-permute-done((f32[640,128]{1,0:T(8,128)S(1)}, f32[640,128]{1,0:T(8,128)S(1)}, u32[]{:S(2)}, u32[]{:S(2)}) %collective-permute-start.5) | collective-permute-done | bytes 327712 | tf_op jit(solution)/shard_map/ppermute | solution.py:413
  21.0 1.3 %shard_map.103 = (f32[640,128]{1,0:T(8,128)S(1)}, f32[640,128]{1,0:T(8,128)S(1)}, f32[640,128]{1,0:T(8,128)S(1)}, f32[10,512,128]{2,1,0:T(8,128)S(1)}, f32[640,1...) custom-call(f32[640,128]{1,0:T(8,128)S(1)} %collective-permute-done.s_in_ref, ...), custom_call_target="tpu_custom_call" | custom-call | tf_op jit(solution)/shard_map/pallas_call | solution.py:387
  22.4 0.6 %collective-permute-start.7 = (f32[640,128]{1,0:T(8,128)S(1)}, f32[640,128]{1,0:T(8,128)S(1)}, u32[]{:S(2)}, u32[]{:S(2)}) collective-permute-start(f32[640,128]{1,0:T(8,128)S(1)} %get-tuple-element.53), channel_id=1, source_target_pairs={{1,9},{3,11},{5,13},{7,15},{9,17},{11,19},{13,21},{15,23},{17,25},... | collective-permute-start | bytes 983048 | tf_op jit(solution)/shard_map/ppermute | solution.py:413
  23.0 0.7 %collective-permute-start.9 = (f32[640,128]{1,0:T(8,128)S(1)}, f32[640,128]{1,0:T(8,128)S(1)}, u32[]{:S(2)}, u32[]{:S(2)}) collective-permute-start(f32[640,128]{1,0:T(8,128)S(1)} %get-tuple-element.54), channel_id=1, source_target_pairs={{1,25},{3,27},{5,29},{7,31},{9,1},{11,3},{13,5},{15,7},{17,9},{19,... | collective-permute-start | bytes 983048 | tf_op jit(solution)/shard_map/ppermute | solution.py:413
  23.7 0.7 %collective-permute-start.6 = (f32[640,128]{1,0:T(8,128)S(1)}, f32[640,128]{1,0:T(8,128)S(1)}, u32[]{:S(2)}, u32[]{:S(2)}) collective-permute-start(f32[640,128]{1,0:T(8,128)S(1)} %get-tuple-element.49.tile0_ref), channel_id=1, source_target_pairs={{3,1},{7,5},{11,9},{15,13},{19,17},{23,21},{27,25},{31,29}} | collective-permute-start | bytes 983048 | tf_op jit(solution)/shard_map/ppermute | solution.py:413
  24.4 0.7 %collective-permute-start.8 = (f32[640,128]{1,0:T(8,128)S(1)}, f32[640,128]{1,0:T(8,128)S(1)}, u32[]{:S(2)}, u32[]{:S(2)}) collective-permute-start(f32[640,128]{1,0:T(8,128)S(1)} %get-tuple-element.52.row_ref), channel_id=1, source_target_pairs={{1,17},{3,19},{5,21},{7,23},{9,25},{11,27},{13,29},{15,31},{17,1},... | collective-permute-start | bytes 983048 | tf_op jit(solution)/shard_map/ppermute | solution.py:413
  25.1 4.4 %collective-permute-done.7.rest_0_.ra_ref = f32[640,128]{1,0:T(8,128)S(1)} collective-permute-done((f32[640,128]{1,0:T(8,128)S(1)}, f32[640,128]{1,0:T(8,128)S(1)}, u32[]{:S(2)}, u32[]{:S(2)}) %collective-permute-start.7) | collective-permute-done | bytes 327712 | tf_op jit(solution)/shard_map/ppermute | solution.py:413
  29.5 0.1 shard_map.105
  29.6 6.9 %collective-permute-start.10 = (f32[640,128]{1,0:T(8,128)S(1)}, f32[640,128]{1,0:T(8,128)S(1)}, u32[]{:S(2)}, u32[]{:S(2)}) collective-permute-start(f32[640,128]{1,0:T(8,128)S(1)} %get-tuple-element.55), channel_id=1, source_target_pairs={{0,1},{1,0},{2,3},{3,2},{4,5},{5,4},{6,7},{7,6},{8,9},{9,8},{10,11... | collective-permute-start | bytes 983048 | tf_op jit(solution)/shard_map/ppermute | solution.py:413
  36.5 1.3 %collective-permute-start.11 = (f32[640,128]{1,0:T(8,128)S(1)}, f32[640,128]{1,0:T(8,128)S(1)}, u32[]{:S(2)}, u32[]{:S(2)}) collective-permute-start(f32[640,128]{1,0:T(8,128)S(1)} %get-tuple-element.56), channel_id=1, source_target_pairs={{3,1},{7,5},{11,9},{15,13},{19,17},{23,21},{27,25},{31,29},{5,0},{... | collective-permute-start | bytes 983048 | tf_op jit(solution)/shard_map/ppermute | solution.py:413
  37.8 4.4 %shard_map.104 = (f32[10,512,128]{2,1,0:T(8,128)S(1)}, f32[80,128]{1,0:T(8,128)S(1)}, f32[80,128]{1,0:T(8,128)S(1)}) custom-call(f32[10,512,128]{2,1,0:T(8,128)S(1)} %get-tuple-element.35.q_ref.rest_6_, f32[10,512,128]{2,1,0:T(8,128)S(1)} %get-tuple-element.47.q1_ref, f32[2,512,128]{2,1,0:T(8,128)S(1)} %get-tuple-element.45.vel_ref.rest_7_, ...), custom_call_target="tpu_custom_call" | custom-call | flops 19660800 | bytes 12000000 | tf_op jit(solution)/shard_map/pallas_call | solution.py:387
  42.2 5.7 %collective-permute-done.11.step_ref.rb_ref = f32[640,128]{1,0:T(8,128)S(1)} collective-permute-done((f32[640,128]{1,0:T(8,128)S(1)}, f32[640,128]{1,0:T(8,128)S(1)}, u32[]{:S(2)}, u32[]{:S(2)}) %collective-permute-start.11) | collective-permute-done | bytes 327712 | tf_op jit(solution)/shard_map/ppermute | solution.py:413
  47.8 0.1 shard_map.106
  47.9 0.2 collective-permute-start.12
  48.1 1.3 %collective-permute-start.13 = (f32[640,128]{1,0:T(8,128)S(1)}, f32[640,128]{1,0:T(8,128)S(1)}, u32[]{:S(2)}, u32[]{:S(2)}) collective-permute-start(f32[640,128]{1,0:T(8,128)S(1)} %get-tuple-element.62), channel_id=1, source_target_pairs={{5,0},{13,8},{21,16},{29,24}} | collective-permute-start | bytes 983048 | tf_op jit(solution)/shard_map/ppermute | solution.py:413
  49.4 2.5 %collective-permute-start.14 = (f32[80,128]{1,0:T(8,128)S(1)}, f32[80,128]{1,0:T(8,128)S(1)}, u32[]{:S(2)}, u32[]{:S(2)}) collective-permute-start(f32[80,128]{1,0:T(8,128)S(1)} %get-tuple-element.63), channel_id=1, source_target_pairs={{0,8},{1,9},{2,10},{3,11},{4,12},{5,13},{6,14},{7,15},{8,16},{9,17... | collective-permute-start | bytes 122888 | tf_op jit(solution)/shard_map/ppermute | solution.py:413
  51.9 0.5 collective-permute-start.15
  52.4 2.3 %collective-permute-done.14.hl_ref = f32[80,128]{1,0:T(8,128)S(1)} collective-permute-done((f32[80,128]{1,0:T(8,128)S(1)}, f32[80,128]{1,0:T(8,128)S(1)}, u32[]{:S(2)}, u32[]{:S(2)}) %collective-permute-start.14) | collective-permute-done | bytes 40992 | tf_op jit(solution)/shard_map/ppermute | solution.py:413
  54.7 1.2 %collective-permute-done.15.hr_ref = f32[80,128]{1,0:T(8,128)S(1)} collective-permute-done((f32[80,128]{1,0:T(8,128)S(1)}, f32[80,128]{1,0:T(8,128)S(1)}, u32[]{:S(2)}, u32[]{:S(2)}) %collective-permute-start.15) | collective-permute-done | bytes 40992 | tf_op jit(solution)/shard_map/ppermute | solution.py:413
  55.9 1.5 %collective-permute-done.13.far_ref = f32[640,128]{1,0:T(8,128)S(1)} collective-permute-done((f32[640,128]{1,0:T(8,128)S(1)}, f32[640,128]{1,0:T(8,128)S(1)}, u32[]{:S(2)}, u32[]{:S(2)}) %collective-permute-start.13) | collective-permute-done | bytes 327712 | tf_op jit(solution)/shard_map/ppermute | solution.py:413
  57.4 3.1 %shard_map.107 = f32[10,512,128]{2,1,0:T(8,128)} custom-call(f32[10,512,128]{2,1,0:T(8,128)S(1)} %get-tuple-element.48.part_ref, f32[10,512,128]{2,1,0:T(8,128)S(1)} %get-tuple-element.35.q_ref.rest_6_, f32[10,512,128]{2,1,0:T(8,128)S(1)} %get-tuple-element.47.q1_ref, f32[2,512,128]{2,1,0:T(8,128)S(1)} %get-tuple-element.45.vel_ref.rest_7_, ...), custom_call_target="tpu_custom_call" | custom-call | tf_op jit(solution)/shard_map/pallas_call | solution.py:387
  (24 shorter events, 0.1 us)
Async XLA Ops:
  0.0 12.4 %copy-start.1 = (f32[9,9]{1,0:T(8,128)S(1)}, f32[9,9]{1,0:T(8,128)}, u32[]{:S(2)}) copy-start(f32[9,9]{1,0:T(8,128)} %mix_ref.5) | copy-start | bytes 976
  0.0 12.4 %copy-start.2 = (f32[9]{0:T(128)S(1)}, f32[9]{0:T(128)}, u32[]{:S(2)}) copy-start(f32[9]{0:T(128)} %pre_ref.5) | copy-start | bytes 112
  0.0 12.4 %copy-start.3 = (f32[9]{0:T(128)S(1)}, f32[9]{0:T(128)}, u32[]{:S(2)}) copy-start(f32[9]{0:T(128)} %act_ref.5) | copy-start | bytes 112
  0.0 12.4 %copy-start.4 = (f32[9]{0:T(128)S(1)}, f32[9]{0:T(128)}, u32[]{:S(2)}) copy-start(f32[9]{0:T(128)} %heat_ref.5) | copy-start | bytes 112
  0.9 9.0 %collective-permute-start.3 = (f32[88,128]{1,0:T(8,128)S(1)}, f32[88,128]{1,0:T(8,128)S(1)}, u32[]{:S(2)}, u32[]{:S(2)}) collective-permute-start(f32[88,128]{1,0:T(8,128)S(1)} %get-tuple-element.40), channel_id=1, source_target_pairs={{0,8},{1,9},{2,10},{3,11},{4,12},{5,13},{6,14},{7,15},{8,16},{9,17... | collective-permute-start | bytes 135176 | tf_op jit(solution)/shard_map/ppermute | solution.py:413
  3.9 6.0 %collective-permute-start.4 = (f32[88,128]{1,0:T(8,128)S(1)}, f32[88,128]{1,0:T(8,128)S(1)}, u32[]{:S(2)}, u32[]{:S(2)}) collective-permute-start(f32[88,128]{1,0:T(8,128)S(1)} %get-tuple-element.41), channel_id=1, source_target_pairs={{0,24},{1,25},{2,26},{3,27},{4,28},{5,29},{6,30},{7,31},{8,0},{9,1... | collective-permute-start | bytes 135176 | tf_op jit(solution)/shard_map/ppermute | solution.py:413
  7.1 9.6 %collective-permute-start = (f32[640,128]{1,0:T(8,128)S(1)}, f32[640,128]{1,0:T(8,128)S(1)}, u32[]{:S(2)}, u32[]{:S(2)}) collective-permute-start(f32[640,128]{1,0:T(8,128)S(1)} %get-tuple-element.36), channel_id=1, source_target_pairs={{0,1},{1,0},{2,3},{3,2},{4,5},{5,4},{6,7},{7,6},{8,9},{9,8},{10,11... | collective-permute-start | bytes 983048 | tf_op jit(solution)/shard_map/ppermute | solution.py:413
  7.2 9.5 %collective-permute-start.1 = (f32[640,128]{1,0:T(8,128)S(1)}, f32[640,128]{1,0:T(8,128)S(1)}, u32[]{:S(2)}, u32[]{:S(2)}) collective-permute-start(f32[640,128]{1,0:T(8,128)S(1)} %get-tuple-element.37), channel_id=1, source_target_pairs={{1,25},{3,27},{5,29},{7,31},{9,1},{11,3},{13,5},{15,7},{17,9},{19,... | collective-permute-start | bytes 983048 | tf_op jit(solution)/shard_map/ppermute | solution.py:413
  7.8 8.8 %collective-permute-start.2 = (f32[640,128]{1,0:T(8,128)S(1)}, f32[640,128]{1,0:T(8,128)S(1)}, u32[]{:S(2)}, u32[]{:S(2)}) collective-permute-start(f32[640,128]{1,0:T(8,128)S(1)} %get-tuple-element.38), channel_id=1, source_target_pairs={{1,9},{3,11},{5,13},{7,15},{9,17},{11,19},{13,21},{15,23},{17,25},... | collective-permute-start | bytes 983048 | tf_op jit(solution)/shard_map/ppermute | solution.py:413
  9.9 11.1 %collective-permute-start.5 = (f32[640,128]{1,0:T(8,128)S(1)}, f32[640,128]{1,0:T(8,128)S(1)}, u32[]{:S(2)}, u32[]{:S(2)}) collective-permute-start(f32[640,128]{1,0:T(8,128)S(1)} %get-tuple-element.42), channel_id=1, source_target_pairs={{1,17},{3,19},{5,21},{7,23},{9,25},{11,27},{13,29},{15,31},{17,1},... | collective-permute-start | bytes 983048 | tf_op jit(solution)/shard_map/ppermute | solution.py:413
  12.4 8.6 %copy-start = (f32[10,1,8192]{2,1,0:T(1,128)S(1)}, f32[10,1,8192]{2,1,0:T(1,128)}, u32[]{:S(2)}) copy-start(f32[10,1,8192]{2,1,0:T(1,128)} %param.12) | copy-start | bytes 983044
  12.4 8.6 %copy-start.5 = (s32[8,1]{0,1:T(1,128)S(1)}, s32[8,1]{0,1:T(1,128)}, u32[]{:S(2)}) copy-start(s32[8,1]{0,1:T(1,128)} %param.17) | copy-start | bytes 100
  12.4 8.6 %copy-start.6 = (s32[8]{0:T(128)S(1)}, s32[8]{0:T(128)}, u32[]{:S(2)}) copy-start(s32[8]{0:T(128)} %rest_11_.1) | copy-start | bytes 100
  12.4 8.6 %copy-start.7 = (s32[8]{0:T(128)S(1)}, s32[8]{0:T(128)}, u32[]{:S(2)}) copy-start(s32[8]{0:T(128)} %rest_12_.1) | copy-start | bytes 100
  22.4 7.1 %collective-permute-start.7 = (f32[640,128]{1,0:T(8,128)S(1)}, f32[640,128]{1,0:T(8,128)S(1)}, u32[]{:S(2)}, u32[]{:S(2)}) collective-permute-start(f32[640,128]{1,0:T(8,128)S(1)} %get-tuple-element.53), channel_id=1, source_target_pairs={{1,9},{3,11},{5,13},{7,15},{9,17},{11,19},{13,21},{15,23},{17,25},... | collective-permute-start | bytes 983048 | tf_op jit(solution)/shard_map/ppermute | solution.py:413
  23.0 6.5 %collective-permute-start.9 = (f32[640,128]{1,0:T(8,128)S(1)}, f32[640,128]{1,0:T(8,128)S(1)}, u32[]{:S(2)}, u32[]{:S(2)}) collective-permute-start(f32[640,128]{1,0:T(8,128)S(1)} %get-tuple-element.54), channel_id=1, source_target_pairs={{1,25},{3,27},{5,29},{7,31},{9,1},{11,3},{13,5},{15,7},{17,9},{19,... | collective-permute-start | bytes 983048 | tf_op jit(solution)/shard_map/ppermute | solution.py:413
  23.7 5.8 %collective-permute-start.6 = (f32[640,128]{1,0:T(8,128)S(1)}, f32[640,128]{1,0:T(8,128)S(1)}, u32[]{:S(2)}, u32[]{:S(2)}) collective-permute-start(f32[640,128]{1,0:T(8,128)S(1)} %get-tuple-element.49.tile0_ref), channel_id=1, source_target_pairs={{3,1},{7,5},{11,9},{15,13},{19,17},{23,21},{27,25},{31,29}} | collective-permute-start | bytes 983048 | tf_op jit(solution)/shard_map/ppermute | solution.py:413
  24.4 5.1 %collective-permute-start.8 = (f32[640,128]{1,0:T(8,128)S(1)}, f32[640,128]{1,0:T(8,128)S(1)}, u32[]{:S(2)}, u32[]{:S(2)}) collective-permute-start(f32[640,128]{1,0:T(8,128)S(1)} %get-tuple-element.52.row_ref), channel_id=1, source_target_pairs={{1,17},{3,19},{5,21},{7,23},{9,25},{11,27},{13,29},{15,31},{17,1},... | collective-permute-start | bytes 983048 | tf_op jit(solution)/shard_map/ppermute | solution.py:413
  29.6 12.5 %collective-permute-start.10 = (f32[640,128]{1,0:T(8,128)S(1)}, f32[640,128]{1,0:T(8,128)S(1)}, u32[]{:S(2)}, u32[]{:S(2)}) collective-permute-start(f32[640,128]{1,0:T(8,128)S(1)} %get-tuple-element.55), channel_id=1, source_target_pairs={{0,1},{1,0},{2,3},{3,2},{4,5},{5,4},{6,7},{7,6},{8,9},{9,8},{10,11... | collective-permute-start | bytes 983048 | tf_op jit(solution)/shard_map/ppermute | solution.py:413
  36.5 11.3 %collective-permute-start.11 = (f32[640,128]{1,0:T(8,128)S(1)}, f32[640,128]{1,0:T(8,128)S(1)}, u32[]{:S(2)}, u32[]{:S(2)}) collective-permute-start(f32[640,128]{1,0:T(8,128)S(1)} %get-tuple-element.56), channel_id=1, source_target_pairs={{3,1},{7,5},{11,9},{15,13},{19,17},{23,21},{27,25},{31,29},{5,0},{... | collective-permute-start | bytes 983048 | tf_op jit(solution)/shard_map/ppermute | solution.py:413
  47.9 7.9 %collective-permute-start.12 = (f32[640,128]{1,0:T(8,128)S(1)}, f32[640,128]{1,0:T(8,128)S(1)}, u32[]{:S(2)}, u32[]{:S(2)}) collective-permute-start(f32[640,128]{1,0:T(8,128)S(1)} %get-tuple-element.61), channel_id=1, source_target_pairs={{0,1},{1,0},{2,3},{3,2},{4,5},{5,4},{6,7},{7,6},{8,9},{9,8},{10,11... | collective-permute-start | bytes 983048 | tf_op jit(solution)/shard_map/ppermute | solution.py:413
  48.1 9.3 %collective-permute-start.13 = (f32[640,128]{1,0:T(8,128)S(1)}, f32[640,128]{1,0:T(8,128)S(1)}, u32[]{:S(2)}, u32[]{:S(2)}) collective-permute-start(f32[640,128]{1,0:T(8,128)S(1)} %get-tuple-element.62), channel_id=1, source_target_pairs={{5,0},{13,8},{21,16},{29,24}} | collective-permute-start | bytes 983048 | tf_op jit(solution)/shard_map/ppermute | solution.py:413
  49.4 5.3 %collective-permute-start.14 = (f32[80,128]{1,0:T(8,128)S(1)}, f32[80,128]{1,0:T(8,128)S(1)}, u32[]{:S(2)}, u32[]{:S(2)}) collective-permute-start(f32[80,128]{1,0:T(8,128)S(1)} %get-tuple-element.63), channel_id=1, source_target_pairs={{0,8},{1,9},{2,10},{3,11},{4,12},{5,13},{6,14},{7,15},{8,16},{9,17... | collective-permute-start | bytes 122888 | tf_op jit(solution)/shard_map/ppermute | solution.py:413
  51.9 4.0 %collective-permute-start.15 = (f32[80,128]{1,0:T(8,128)S(1)}, f32[80,128]{1,0:T(8,128)S(1)}, u32[]{:S(2)}, u32[]{:S(2)}) collective-permute-start(f32[80,128]{1,0:T(8,128)S(1)} %get-tuple-element.64), channel_id=1, source_target_pairs={{0,24},{1,25},{2,26},{3,27},{4,28},{5,29},{6,30},{7,31},{8,0},{9,1... | collective-permute-start | bytes 122888 | tf_op jit(solution)/shard_map/ppermute | solution.py:413

commit v4 on v3

v4 whole, which is shorter than its diff:
```python
import functools

import jax
import jax.numpy as jnp
from jax import lax
from jax.experimental import pallas as pl
from jax.experimental.pallas import tpu as pltpu
from jax.sharding import PartitionSpec as P

NV = 10
NS = 9
LANES = 128
CAX = 8
HALF = 64
AXES = ("az", "ax", "pl")
NJ = 4
EXT = 16
LOG2E = 1.4426950408889634
LIMIT = 16 * 1024 * 1024

f32 = jnp.float32


def roles():
    return lax.axis_index("az"), lax.axis_index("ax"), lax.axis_index("pl")


def low_half():
    return lax.broadcasted_iota(jnp.int32, (CAX, LANES), 1) < HALF


def block(q_ref, v, b):
    return q_ref[v, pl.ds(CAX * CAX * b + CAX - 1, CAX, stride=CAX), :]


def axial_rows(q_ref, vel_ref, first_mate, second_mate):
    _, ax, _ = roles()
    n = q_ref.shape[1] // CAX

    def up(v, at, size):
        rows = pl.ds(CAX * at + CAX - 1, size, stride=CAX)
        return (1.0 + vel_ref[1, rows, :]) * q_ref[v, rows, :]

    def down(v, at, size):
        rows = pl.ds(CAX * at, size, stride=CAX)
        return (1.0 - vel_ref[1, rows, :]) * q_ref[v, rows, :]

    def put(refs, value):
        size = NV * n // len(refs)
        step = min(n, size) if size % n == 0 or n % size == 0 else n // 2
        for k in range(NV * n // step):
            at = k * step
            refs[at // size][pl.ds(at % size, step), :] = value(at // n, at % n, step)

    @pl.when(ax % 2 == 0)
    def _():
        put(first_mate, up)
        put(second_mate, down)

    @pl.when(ax % 2 == 1)
    def _():
        put(first_mate, down)
        put(second_mate, up)


def edges(q_ref, er_ref, el_ref):
    n = q_ref.shape[1] // CAX
    for v in range(NV):
        el_ref[pl.ds(v * CAX, CAX), :] = q_ref[v, pl.ds(0, CAX), :]
        er_ref[pl.ds(v * CAX, CAX), :] = q_ref[v, pl.ds((n - 1) * CAX, CAX), :]


def first_kernel(n_az, n_out, q_any, vel_any, col_any, slot_any, open_any, *outs):
    out_refs, rest = outs[:n_out], outs[n_out:]
    q_ref, vel_ref, s_ref, own_ref, er_ref, el_ref, col_ref, slot_ref, open_ref, sems = rest
    pairs = [(vel_any, vel_ref), (col_any, col_ref), (slot_any, slot_ref), (open_any, open_ref)]
    pairs += [(q_any.at[pl.ds(v, 2)], q_ref.at[pl.ds(v, 2)]) for v in range(0, NV, 2)]
    copies = [pltpu.make_async_copy(x, y, sems.at[k]) for k, (x, y) in enumerate(pairs)]
    for copy in copies:
        copy.start()
    for copy in copies:
        copy.wait()
    az, _, plen = roles()
    n = q_ref.shape[1] // CAX
    rows = NV * n
    edges(q_ref, er_ref, el_ref)
    el_ref[pl.ds(NV * CAX, CAX), :] = vel_ref[0, pl.ds(0, CAX), :]
    er_ref[pl.ds(NV * CAX, CAX), :] = vel_ref[0, pl.ds((n - 1) * CAX, CAX), :]
    for v in range(NV):
        s_ref[pl.ds(v * n, n), :] = q_ref[v, pl.ds(0, n, stride=CAX), :]

    @pl.when(plen == 0)
    def _():
        axial_rows(q_ref, vel_ref, out_refs[:1], out_refs[1:2])

    @pl.when(plen == 1)
    def _():
        sub = lax.broadcasted_iota(jnp.int32, (CAX, LANES), 0)
        left = lax.broadcasted_iota(jnp.int32, (1, LANES), 1) < HALF
        blocks = n // CAX
        for shift, ref in enumerate((own_ref,) + tuple(out_refs)):
            ref[pl.ds(0, rows + EXT), :] = jnp.zeros((rows + EXT, LANES), f32)
            table = jnp.full((CAX, LANES), -1.0, f32)
            used = jnp.int32(0)
            for b in range(blocks):
                tile, opened = slot_ref[b], open_ref[b] != 0
                ahead = (col_ref[b] - az - shift + 2 * n_az) % n_az
                here = jnp.logical_and(ahead == 0, opened)
                table = jnp.where(sub == jnp.where(here, used, CAX), tile.astype(f32), table)
                used = used + here.astype(jnp.int32)

                @pl.when(here)
                def _(ref=ref, b=b, tile=tile):
                    for v in range(NV):
                        at = pl.ds(pl.multiple_of(v * n + tile * CAX, CAX), CAX)
                        ref[at, :] += block(q_ref, v, b)

                @pl.when(jnp.logical_and(opened, jnp.logical_and(ahead == 1, tile == 0)))
                def _(ref=ref, b=b):
                    for v in range(NV):
                        cell = q_ref[v, pl.ds(CAX * CAX * b + CAX - 1, 1), :]
                        ref[pl.ds(rows + v, 1), :] += jnp.where(left, cell, 0.0)

                @pl.when(jnp.logical_and(opened, jnp.logical_and(ahead == n_az - 1, tile == blocks - 1)))
                def _(ref=ref, b=b):
                    for v in range(NV):
                        cell = q_ref[v, pl.ds(CAX * CAX * (b + 1) - 1, 1), :]
                        ref[pl.ds(rows + v, 1), :] += jnp.where(left, 0.0, cell)

            if shift > 0:
                ref[pl.ds(rows + EXT, CAX), :] = table


def source(state, mix_ref, pre_ref, act_ref, heat_ref):
    inv = 1.0 / jnp.maximum(state[NS], 0.5)
    rates = [pre_ref[k] * jnp.exp(-act_ref[k] * inv) * jnp.maximum(state[k], 0.0) for k in range(NS)]
    out = []
    for v in range(NV):
        acc = None
        for k in range(NS):
            term = (mix_ref[v, k] if v < NS else heat_ref[k]) * rates[k]
            acc = term if acc is None else acc + term
        out.append(0.2 * acc)
    return out


def fill_ghosts(state_ref, lo_ref, hi_ref, ra_refs, rb_ref, high_ref, supply_ref, n_ax):
    _, ax, plen = roles()
    n = state_ref.shape[1] // CAX
    even = ax % 2 == 0
    odd = jnp.logical_not(even)
    cham = plen == 0

    def put(ref):
        size = ref.shape[0] // len(ra_refs)
        for k, part in enumerate(ra_refs):
            ref[pl.ds(k * size, size), :] = part[pl.ds(0, size), :]

    @pl.when(plen == 1)
    def _():
        lo_ref[...] = supply_ref[...]
        hi_ref[...] = high_ref[pl.ds(0, hi_ref.shape[0]), :]

    @pl.when(jnp.logical_and(cham, even))
    def _():
        put(hi_ref)

    @pl.when(jnp.logical_and(cham, odd))
    def _():
        put(lo_ref)

    @pl.when(jnp.logical_and(cham, ax == 0))
    def _():
        lo_ref[...] = jnp.zeros_like(lo_ref)

    @pl.when(jnp.logical_and(cham, jnp.logical_and(even, ax > 0)))
    def _():
        lo_ref[...] = rb_ref[pl.ds(0, lo_ref.shape[0]), :]

    @pl.when(jnp.logical_and(cham, jnp.logical_and(odd, ax < n_ax - 1)))
    def _():
        hi_ref[...] = rb_ref[pl.ds(0, hi_ref.shape[0]), :]

    @pl.when(jnp.logical_and(cham, ax == n_ax - 1))
    def _():
        for v in range(NV):
            hi_ref[pl.ds(v * n, n), :] = state_ref[v, pl.ds(CAX - 1, n, stride=CAX), :]


def add_border(v, dst_ref, scale, lo_ref, hi_ref, hl_ref, hr_ref, ul_ref, ur_ref):
    n = dst_ref.shape[1] // CAX
    left = low_half()
    dst_ref[v, pl.ds(0, n, stride=CAX), :] += scale * lo_ref[pl.ds(v * n, n), :]
    dst_ref[v, pl.ds(CAX - 1, n, stride=CAX), :] += scale * hi_ref[pl.ds(v * n, n), :]
    al = scale + scale * pltpu.roll(ul_ref[...], HALF, 1)
    ar = scale - scale * pltpu.roll(ur_ref[...], HALF, 1)
    head = pltpu.roll(hl_ref[pl.ds(v * CAX, CAX), :], HALF, 1)
    tail = pltpu.roll(hr_ref[pl.ds(v * CAX, CAX), :], HALF, 1)
    dst_ref[v, pl.ds(0, CAX), :] += jnp.where(left, al * head, 0.0)
    dst_ref[v, pl.ds((n - 1) * CAX, CAX), :] += jnp.where(left, 0.0, ar * tail)


def mixing(a_ref, scale, mix_ref, pre_ref, heat_ref):
    width = NV * CAX
    col = lax.broadcasted_iota(jnp.int32, (CAX, 3 * width), 1)
    row = lax.broadcasted_iota(jnp.int32, (CAX, 3 * width), 0)
    inner = col % width
    species, lane = inner // CAX, inner % CAX
    for v in range(NV):
        block = jnp.zeros((CAX, 3 * width), f32)
        for k in range(NS):
            value = (0.2 * scale) * pre_ref[k] * (mix_ref[v, k] if v < NS else heat_ref[k])
            block = jnp.where(species == k, value, block)
        block = jnp.where(lane == row, block, 0.0)
        high = block.astype(jnp.bfloat16).astype(f32)
        a_ref[pl.ds(v * CAX, CAX), :] = jnp.where(col // width == 1, block - high, high)


def interior(q_ref, vel_ref, a_ref, scale, mix_ref, pre_ref, act_ref, heat_ref, finish):
    n = q_ref.shape[1] // CAX
    left = low_half()
    sub = lax.broadcasted_iota(jnp.int32, (CAX, LANES), 0)
    bottom, top = sub == 0, sub == CAX - 1
    mixing(a_ref, scale, mix_ref, pre_ref, heat_ref)
    a = a_ref[...].astype(jnp.bfloat16)
    power = [act_ref[k] * (-LOG2E) for k in range(NS)]
    c = 0.1 * scale

    def reg(ref, v, j):
        return ref[v, pl.ds(pl.multiple_of(j * CAX, CAX), CAX), :]

    def column(ref, v, j0):
        regs = [reg(ref, v, j0 + d) for d in range(NJ)]
        before = jnp.where(j0 == 0, 0.0, reg(ref, v, jnp.maximum(j0 - 1, 0)))
        after = jnp.where(j0 + NJ == n, 0.0, reg(ref, v, jnp.minimum(j0 + NJ, n - 1)))
        turned = [pltpu.roll(x, HALF, 1) for x in [before] + regs + [after]]
        lefts = [jnp.where(left, turned[d], turned[d + 1]) for d in range(NJ)]
        rights = [jnp.where(left, turned[d + 1], turned[d + 2]) for d in range(NJ)]
        return regs, lefts, rights

    def body(step, carry):
        j0 = step * NJ
        rates = []
        for d in range(NJ):
            inv = 1.0 / jnp.maximum(reg(q_ref, NS, j0 + d), 0.5)
            some = [jnp.exp2(power[k] * inv) * jnp.maximum(reg(q_ref, k, j0 + d), 0.0) for k in range(NS)]
            rates.append(jnp.concatenate(some + [jnp.zeros((CAX, LANES), f32)], axis=0))
        rate = jnp.concatenate(rates, axis=1)
        high = rate.astype(jnp.bfloat16)
        low = (rate - high.astype(f32)).astype(jnp.bfloat16)
        src = jnp.dot(a, jnp.concatenate([high, high, low], axis=0), preferred_element_type=f32)
        _, u_left, u_right = column(vel_ref, 0, j0)
        w = [reg(vel_ref, 1, j0 + d) for d in range(NJ)]
        al = [c + c * x for x in u_left]
        ar = [c - c * x for x in u_right]
        wu = [jnp.where(bottom, 0.0, c + c * pltpu.roll(x, 1, 0)) for x in w]
        wd = [jnp.where(top, 0.0, c - c * pltpu.roll(x, CAX - 1, 0)) for x in w]
        for v in range(NV):
            regs, lefts, rights = column(q_ref, v, j0)
            for d in range(NJ):
                vertical = wu[d] * pltpu.roll(regs[d], 1, 0) + wd[d] * pltpu.roll(regs[d], CAX - 1, 0)
                new = (0.6 * scale) * regs[d] + src[v * CAX:(v + 1) * CAX, d * LANES:(d + 1) * LANES]
                finish(j0 + d, v, new + (al[d] * lefts[d] + ar[d] * rights[d]) + vertical)
        return carry

    lax.fori_loop(0, n // NJ, body, 0)


def inside_one_kernel(q_ref, vel_ref, mix_ref, pre_ref, act_ref, heat_ref, out_ref, a_ref):
    def finish(j, v, new):
        out_ref[v, pl.ds(pl.multiple_of(j * CAX, CAX), CAX), :] = new

    interior(q_ref, vel_ref, a_ref, 1.0, mix_ref, pre_ref, act_ref, heat_ref, finish)


def inside_two_kernel(q_ref, q1_ref, vel_ref, mix_ref, pre_ref, act_ref, heat_ref, out_ref, a_ref):
    def finish(j, v, new):
        at = pl.ds(pl.multiple_of(j * CAX, CAX), CAX)
        out_ref[v, at, :] = 0.5 * q_ref[v, at, :] + new

    interior(q1_ref, vel_ref, a_ref, 0.5, mix_ref, pre_ref, act_ref, heat_ref, finish)


def border_one_kernel(n_az, n_ax, n_out, cap, s_in_ref, *rest):
    got, rest = rest[:n_out], rest[n_out:]
    hl_ref, hr_ref, part_ref, q_ref, vel_ref, supply_ref, own_in_ref, col_ref, slot_ref, open_ref = rest[:10]
    out_refs, rest = rest[10:10 + n_out], rest[10 + n_out:]
    q1_ref, tile_ref, s_ref, z_ref, own_ref, er_ref, el_ref, lo_ref, hi_ref = rest
    az, _, plen = roles()
    n = q_ref.shape[1] // CAX
    rows = NV * n
    fill_ghosts(q_ref, lo_ref, hi_ref, got[:1], got[1], s_in_ref, supply_ref, n_ax)
    for v in range(NV):
        q1_ref[v] = part_ref[v]
        add_border(v, q1_ref, 0.1, lo_ref, hi_ref, hl_ref, hr_ref,
                   hl_ref.at[pl.ds(NV * CAX, CAX)], hr_ref.at[pl.ds(NV * CAX, CAX)])
    edges(q1_ref, er_ref, el_ref)

    @pl.when(plen == 0)
    def _():
        tile_ref[...] = jnp.zeros_like(tile_ref)
        for v in range(NV):
            s_ref[pl.ds(v * n, n), :] = q1_ref[v, pl.ds(0, n, stride=CAX), :]
        axial_rows(q1_ref, vel_ref, out_refs[:CAX // cap], (z_ref,))

    @pl.when(plen == 1)
    def _():
        total = own_in_ref[...]
        for ref in got:
            total = total + ref[pl.ds(0, rows + EXT), :]
        tile_ref[...] = total
        own_ref[...] = jnp.zeros_like(own_ref)
        used = [jnp.int32(0)] * n_out
        for b in range(n // CAX):
            tile = slot_ref[b]
            ahead = (col_ref[b] - az + n_az) % n_az
            opened = open_ref[b] != 0

            @pl.when(jnp.logical_and(opened, ahead == 0))
            def _(b=b, tile=tile):
                for v in range(NV):
                    at = pl.ds(pl.multiple_of(v * n + tile * CAX, CAX), CAX)
                    own_ref[at, :] += block(q1_ref, v, b)

            for k, ref in enumerate(out_refs):
                here = jnp.logical_and(opened, ahead == k + 1)

                @pl.when(here)
                def _(ref=ref, b=b, slot=used[k]):
                    for v in range(NV):
                        at = pl.ds(pl.multiple_of((slot * NV + v) * CAX, CAX), CAX)
                        ref[at, :] = block(q1_ref, v, b)

                used[k] = used[k] + here.astype(jnp.int32)


def tree_kernel(n_out, cap, tile0_ref, down0_ref, own_ref, s1_ref, z_ref, *rest):
    got, tables, (tile_ref, step_ref, core_ref) = rest[:n_out], rest[n_out:2 * n_out], rest[2 * n_out:]
    _, ax, plen = roles()
    rows = own_ref.shape[0]
    n = rows // NV

    @pl.when(plen == 0)
    def _():
        core_ref[pl.ds(0, rows), :] = s1_ref[...]
        step_ref[pl.ds(0, rows), :] = z_ref[...]
        core_ref[pl.ds(rows, EXT), :] = jnp.zeros((EXT, LANES), f32)
        step_ref[pl.ds(rows, EXT), :] = jnp.zeros((EXT, LANES), f32)
        tile_ref[...] = jnp.zeros_like(tile_ref)

    @pl.when(plen == 1)
    def _():
        core_ref[...] = tile0_ref[...] + down0_ref[...]
        slots = [(k, m) for k in range(n_out) for m in range(cap)]
        named = [jnp.broadcast_to(tables[k][pl.ds(rows + EXT + m, 1), :], (CAX, LANES)) for k, m in slots]
        for v in range(NV):
            blocks = [got[k][pl.ds((m * NV + v) * CAX, CAX), :] for k, m in slots]
            for t in range(n // CAX):
                at = pl.ds(v * n + t * CAX, CAX)
                total = own_ref[at, :]
                for name, value in zip(named, blocks):
                    total = total + jnp.where(name == t, value, 0.0)
                tile_ref[at, :] = total

        @pl.when(ax % 2 == 1)
        def _():
            step_ref[pl.ds(0, rows), :] = tile_ref[...]
            step_ref[pl.ds(rows, EXT), :] = jnp.zeros((EXT, LANES), f32)

        @pl.when(ax % 2 == 0)
        def _():
            step_ref[...] = core_ref[...]


def inlet_kernel(tile_ref, step_ref, core_ref, dq_ref, pair_ref, core_out_ref):
    _, ax, plen = roles()
    rows = tile_ref.shape[0]

    @pl.when(plen == 1)
    def _():
        pair = tile_ref[...] + step_ref[pl.ds(0, rows), :]
        pair_ref[...] = pair
        core_out_ref[...] = pair
        dq_ref[...] = jnp.zeros_like(dq_ref)

    @pl.when(jnp.logical_and(plen == 0, ax > 0))
    def _():
        pair_ref[...] = jnp.zeros_like(pair_ref)
        core_out_ref[...] = jnp.zeros_like(core_out_ref)
        dq_ref[...] = jnp.zeros_like(dq_ref)

    @pl.when(jnp.logical_and(plen == 0, ax == 0))
    def _():
        pair_ref[...] = jnp.zeros_like(pair_ref)
        dq_ref[...] = 0.1 * (step_ref[...] + core_ref[...])
        core_out_ref[...] = dq_ref[pl.ds(0, rows), :]


def border_two_kernel(n_ax, n_z, part_ref, q_ref, q1_ref, vel_ref, core_ref, supply_ref, step_ref, dq_ref, hl_ref, hr_ref,
                      hl0_ref, hr0_ref, *rest):
    ra_refs, rest = rest[:n_z], rest[n_z:]
    mix_ref, pre_ref, act_ref, heat_ref, out_any, keep_ref, out_ref, lo_ref, hi_ref, sems = rest
    n = out_ref.shape[1] // CAX
    rows = NV * n
    _, ax, plen = roles()
    inlet_side = jnp.logical_and(ax == 0, plen == 0)
    ul_ref, ur_ref = hl0_ref.at[pl.ds(NV * CAX, CAX)], hr0_ref.at[pl.ds(NV * CAX, CAX)]
    fill_ghosts(q1_ref, lo_ref, hi_ref, ra_refs, step_ref, core_ref, supply_ref, n_ax)

    @pl.when(inlet_side)
    def _():
        first = lax.broadcasted_iota(jnp.int32, (n, LANES), 0) == 0
        last = lax.broadcasted_iota(jnp.int32, (n, LANES), 0) == n - 1
        left = lax.broadcasted_iota(jnp.int32, (n, LANES), 1) < HALF

        def neighbours(x, head, tail):
            before = jnp.where(first, head, pltpu.roll(x, 1, 0))
            after = jnp.where(last, tail, pltpu.roll(x, n - 1, 0))
            mid = pltpu.roll(x, HALF, 1)
            return (jnp.where(left, pltpu.roll(before, HALF, 1), mid),
                    jnp.where(left, mid, pltpu.roll(after, HALF, 1)))

        u = vel_ref[0, pl.ds(0, n, stride=CAX), :]
        w_next = vel_ref[1, pl.ds(1, n, stride=CAX), :]
        u_left, u_right = neighbours(u, ul_ref[pl.ds(0, 1), :], ur_ref[pl.ds(0, 1), :])
        state = [q1_ref[v, pl.ds(0, n, stride=CAX), :] + dq_ref[pl.ds(v * n, n), :] for v in range(NV)]
        src = source(state, mix_ref, pre_ref, act_ref, heat_ref)
        for v in range(NV):
            beside = dq_ref[pl.ds(rows + v, 1), :]
            q_left, q_right = neighbours(state[v], hl_ref[pl.ds(v * CAX, 1), :] + beside, hr_ref[pl.ds(v * CAX, 1), :] + beside)
            above = (1.0 - w_next) * q1_ref[v, pl.ds(1, n, stride=CAX), :]
            new = 0.6 * state[v] + 0.1 * ((1.0 + u_left) * q_left + (1.0 - u_right) * q_right + above) + src[v]
            keep_ref[pl.ds(v * n, n), :] = 0.5 * q_ref[v, pl.ds(0, n, stride=CAX), :] + 0.5 * new

    copies = []
    for v in range(NV):
        out_ref[v] = part_ref[v]
        add_border(v, out_ref, 0.05, lo_ref, hi_ref, hl_ref, hr_ref, ul_ref, ur_ref)

        @pl.when(inlet_side)
        def _(v=v):
            w = vel_ref[1, pl.ds(0, n, stride=CAX), :]
            out_ref[v, pl.ds(1, n, stride=CAX), :] += 0.05 * ((1.0 + w) * dq_ref[pl.ds(v * n, n), :])

        @pl.when(plen == 1)
        def _(v=v):
            keep_ref[pl.ds(v * n, n), :] = out_ref[v, pl.ds(CAX - 1, n, stride=CAX), :]

        copies.append(pltpu.make_async_copy(out_ref.at[v], out_any.at[v], sems.at[v]))
        copies[-1].start()
    for copy in copies:
        copy.wait()


def last_kernel(in_any, keep_ref, core_ref, far_ref, out_any, row_ref, sem):
    _, ax, plen = roles()
    n = keep_ref.shape[0] // NV

    def patch(at, value):
        for v in range(NV):
            row_ref[v, :, 0, :] = value(pl.ds(v * n, n))
        copy = pltpu.make_async_copy(row_ref, out_any.at[:, :, pl.ds(at, 1), :], sem)
        copy.start()
        copy.wait()

    @pl.when(jnp.logical_and(ax == 0, plen == 0))
    def _():
        patch(0, lambda at: keep_ref[at, :] + 0.05 * (core_ref[at, :] + far_ref[at, :]))

    @pl.when(jnp.logical_and(ax == 0, plen == 1))
    def _():
        patch(CAX - 1, lambda at: keep_ref[at, :] + 0.05 * core_ref[at, :])


def shape(*dims):
    return jax.ShapeDtypeStruct(dims, f32)


SPACES = {"s": pltpu.SMEM, "v": pltpu.VMEM, "h": pltpu.HBM}


def call(kernel, inputs, kinds, outs, scratch=(), cost=None, to=None, aliases=None):
    return pl.pallas_call(
        kernel,
        in_specs=[pl.BlockSpec(memory_space=SPACES[k]) for k in kinds],
        out_specs=[pl.BlockSpec(memory_space=SPACES[k]) for k in (to or "v" * len(outs))],
        out_shape=outs,
        scratch_shapes=list(scratch),
        cost_estimate=cost,
        input_output_aliases=aliases or {},
        compiler_params=pltpu.CompilerParams(vmem_limit_bytes=LIMIT),
    )(*inputs)


def local(n_az, n_ax, cells, speeds, supply, mix, prefactor, activation, heat, inj_column, inj_slot, inj_open):
    size = cells.shape[-1]
    n = size // LANES
    rows = NV * n

    def view(array):
        k = array.shape[0]
        return array.reshape(k, CAX, n, LANES).transpose(0, 2, 1, 3).reshape(k, CAX * n, LANES)

    def number(i, j, p):
        return (i * n_ax + j) * 2 + p

    every = [(i, j) for i in range(n_az) for j in range(n_ax)]

    def send(x, route):
        return lax.ppermute(x, AXES, [(number(*a), number(*b)) for a, b in route])

    def ring(step):
        return [((i, j, p), ((i + step) % n_az, j, p)) for i, j in every for p in (0, 1)]

    swap = [((i, j, p), (i, j, 1 - p)) for i, j in every for p in (0, 1)]
    n_out = n_az - 1

    def mate(k, j):
        return j ^ 1 if k == 0 else ((j + 1) ^ 1) - 1 if 0 < j < n_ax - 1 else n_ax - 1 - j

    cap = CAX // 4 if n_az > 4 else CAX // 2
    pieces = CAX // cap

    def dense(k):
        out = [((i, j, 1), ((i + k + 1) % n_az, j, 1)) for i, j in every]
        if k < 2:
            out += [((i, j, 0), (i, mate(k, j), 0)) for i, j in every]
        return out

    def compact(k):
        out = [((i, j, 1), ((i + k + 1) % n_az, j, 1)) for i, j in every]
        if k < pieces:
            return out + [((i, j, 0), (i, mate(0, j), 0)) for i, j in every]
        return out + [((i, j, 0), ((i + k + 1) % n_az, j, 0)) for i, j in every]

    q, vel = view(cells[0]), view(speeds[0])
    sup = supply.reshape(rows, LANES)
    col, slot, opened = inj_column.reshape(-1), inj_slot, inj_open
    react = (mix, prefactor, activation, heat)
    row, edge = shape(rows, LANES), shape(NV * CAX, LANES)

    whole = shape(*q.shape)
    work = pl.CostEstimate(flops=300 * q.shape[1] * LANES, transcendentals=20 * q.shape[1] * LANES,
                           bytes_accessed=12_000_000)

    raw = tuple(pltpu.with_memory_space_constraint(x, pltpu.HBM) for x in (q, vel, col, slot, opened))
    wide, edge0 = shape(rows + EXT, LANES), shape((NV + 1) * CAX, LANES)
    got = call(functools.partial(first_kernel, n_az, n_out), raw, "hhhhh",
               [shape(rows + EXT + CAX, LANES)] * n_out + [whole, shape(*vel.shape), row, wide, edge0, edge0],
               [pltpu.SMEM(col.shape, jnp.int32)] * 3 + [pltpu.SemaphoreType.DMA((4 + NV // 2,))])
    outs, (qv, velv, s0, own0, er, el) = got[:n_out], got[n_out:]
    ra = [send(x, dense(k)) for k, x in enumerate(outs)]
    s0r = send(s0, swap)
    hl0 = send(er, ring(1))
    el, s0r = lax.optimization_barrier((el, s0r))
    hr0 = send(el, ring(-1))
    matrix = pltpu.VMEM((NV * CAX, 3 * NV * CAX), f32)
    part, = call(inside_one_kernel, (qv, velv) + react, "vvssss", [whole], [matrix], cost=work)

    got = call(functools.partial(border_one_kernel, n_az, n_ax, n_out, cap),
               (s0r, *ra, hl0, hr0, part, qv, velv, sup, own0, col, slot, opened),
               "v" * (n_out + 8) + "s" * 3,
               [shape(cap * NV * CAX, LANES)] * n_out + [whole, wide, row, row, row, edge, edge],
               [pltpu.VMEM((rows, LANES), f32)] * 2)
    outs, (q1, tile0, s1, z1, own1, er, el) = got[:n_out], got[n_out:]
    down = [((i, j, 1), (i, j - 1, 1)) for i, j in every if j % 2 == 1]
    across = [((i, 2, 1), (i, 0, 0)) for i in range(n_az)]
    inner = [((i, j, 0), (i, mate(1, j), 0)) for i, j in every if 0 < j < n_ax - 1]
    rb = [send(x, compact(k)) for k, x in enumerate(outs)]
    down0 = send(tile0, down)

    tile1, step, core = call(functools.partial(tree_kernel, n_out, cap), (tile0, down0, own1, s1, z1, *rb, *ra),
                             "v" * (5 + 2 * n_out), [row, wide, wide])
    step_in = send(step, down + across + inner)
    core_in = send(core, swap)
    hl1, hr1 = send(er, ring(1)), send(el, ring(-1))
    part, = call(inside_two_kernel, (qv, q1, velv) + react, "vvvssss", [whole], [matrix], cost=work)
    part, tile1, hl1, hr1 = lax.optimization_barrier((part, tile1, hl1, hr1))

    dq, pair1, core2 = call(inlet_kernel, (tile1, step_in, core_in), "vvv", [wide, row, row])
    far1 = send(pair1, across)
    core2_in = send(core2, swap)
    out, keep = call(functools.partial(border_two_kernel, n_ax, pieces),
                     (part, qv, q1, velv, core_in, sup, step_in, dq, hl1, hr1, hl0, hr0, *rb[:pieces]) + react,
                     "v" * (12 + pieces) + "s" * 4, [whole, row],
                     [pltpu.VMEM(q.shape, f32)] + [pltpu.VMEM((rows, LANES), f32)] * 2 + [pltpu.SemaphoreType.DMA((NV,))],
                     cost=work, to="hv")
    out, = call(last_kernel, (out.reshape(NV, n, CAX, LANES), keep, core2_in, far1), "hvvv", [shape(NV, n, CAX, LANES)],
                [pltpu.VMEM((NV, n, 1, LANES), f32), pltpu.SemaphoreType.DMA(())], to="h", aliases={0: 0})
    return out.transpose(0, 2, 1, 3).reshape(1, NV, CAX, size)


def solution(mesh):
    return jax.shard_map(
        functools.partial(local, mesh.shape["az"], mesh.shape["ax"]),
        mesh=mesh,
        in_specs=(
            P("pl", None, "ax", "az"),
            P("pl", None, "ax", "az"),
            P(None, "ax", "az"),
            P(),
            P(),
            P(),
            P(),
            P(("az", "ax"), None),
            P(("az", "ax")),
            P(("az", "ax")),
        ),
        out_specs=P("pl", None, "ax", "az"),
        check_vma=False,
    )
```

time: 60.8 us -> 53.9 us (0.89)
  waiting for transfers between devices: 19.5 us -> 15.9 us
  starting transfers between devices: 24.6 us -> 21.3 us
    ppermute x16, waiting for transfers between devices: 19.5 us -> 15.9 us  [send(): return lax.ppermute(x, AXES, [(number(*a), number(*b)) for a, b in route])]
    ppermute x16, starting transfers between devices: 24.6 us -> 21.3 us  [send(): return lax.ppermute(x, AXES, [(number(*a), number(*b)) for a, b in route])]
  transfers between devices with their start and end apart: 16 -> 16, of which waited for: 6 -> 5; matrix products, arithmetic and copies ran while one was open for 0% -> 0% of each run, Pallas kernels for 18% -> 22%
where the time goes in v4:
time: 53.9 us; the launch traced here: 53.8 us
  starting transfers between devices  21.3 us (40%)
  Pallas kernels  16.3 us (30%)
  waiting for transfers between devices  15.9 us (29%)
    ppermute x16, starting transfers between devices, send(): return lax.ppermute(x, AXES, [(number(*a), number(*b)) for a, b in route])  21.3 us
    pallas_call x8, Pallas kernels, call(): pl.pallas_call(kernel, in_specs=[pl.BlockSpec(memory_space=SPACES[k]) for...  16.3 us
    ppermute x16, waiting for transfers between devices, send(): return lax.ppermute(x, AXES, [(number(*a), number(*b)) for a, b in route])  15.9 us
  transfers between devices with their start and end apart: 16, of which 5 were waited for; matrix products, arithmetic and copies ran while one was open for 0% of the time, Pallas kernels for 22%

profile of v4, /device:TPU:0, one launch (start us, length us, event | category | flops | bytes accessed | tf_op | source)
XLA Modules:
  0.0 53.8 jit_solution(18221404835637635529)
XLA Ops:
  0.0 2.3 %shard_map.100 = (f32[664,128]{1,0:T(8,128)S(1)}, f32[664,128]{1,0:T(8,128)S(1)}, f32[664,128]{1,0:T(8,128)S(1)}, f32[10,512,128]{2,1,0:T(8,128)S(1)}, f32[2,512...) custom-call(f32[10,512,128]{2,1,0:T(8,128)} %bitcast.20, ...), custom_call_target="tpu_custom_call" | custom-call | tf_op jit(solution)/shard_map/pallas_call | solution.py:483
  2.3 1.3 %collective-permute-start = (f32[640,128]{1,0:T(8,128)S(1)}, f32[640,128]{1,0:T(8,128)S(1)}, u32[]{:S(2)}, u32[]{:S(2)}) collective-permute-start(f32[640,128]{1,0:T(8,128)S(1)} %get-tuple-element.40), channel_id=1, source_target_pairs={{0,1},{1,0},{2,3},{3,2},{4,5},{5,4},{6,7},{7,6},{8,9},{9,8},{10,11... | collective-permute-start | bytes 983048 | tf_op jit(solution)/shard_map/ppermute | solution.py:510
  3.6 2.4 %collective-permute-start.1 = (f32[664,128]{1,0:T(8,128)S(1)}, f32[664,128]{1,0:T(8,128)S(1)}, u32[]{:S(2)}, u32[]{:S(2)}) collective-permute-start(f32[664,128]{1,0:T(8,128)S(1)} %get-tuple-element.42), channel_id=1, source_target_pairs={{1,9},{3,11},{5,13},{7,15},{9,17},{11,19},{13,21},{15,23},{17,25},... | collective-permute-start | bytes 1019912 | tf_op jit(solution)/shard_map/ppermute | solution.py:510
  6.0 2.5 %collective-permute-start.2 = (f32[664,128]{1,0:T(8,128)S(1)}, f32[664,128]{1,0:T(8,128)S(1)}, u32[]{:S(2)}, u32[]{:S(2)}) collective-permute-start(f32[664,128]{1,0:T(8,128)S(1)} %get-tuple-element.43), channel_id=1, source_target_pairs={{1,17},{3,19},{5,21},{7,23},{9,25},{11,27},{13,29},{15,31},{17,1},... | collective-permute-start | bytes 1019912 | tf_op jit(solution)/shard_map/ppermute | solution.py:510
  8.4 0.7 %collective-permute-start.3 = (f32[664,128]{1,0:T(8,128)S(1)}, f32[664,128]{1,0:T(8,128)S(1)}, u32[]{:S(2)}, u32[]{:S(2)}) collective-permute-start(f32[664,128]{1,0:T(8,128)S(1)} %get-tuple-element.44), channel_id=1, source_target_pairs={{1,25},{3,27},{5,29},{7,31},{9,1},{11,3},{13,5},{15,7},{17,9},{19,... | collective-permute-start | bytes 1019912 | tf_op jit(solution)/shard_map/ppermute | solution.py:510
  9.1 1.6 %collective-permute-start.4 = (f32[88,128]{1,0:T(8,128)S(1)}, f32[88,128]{1,0:T(8,128)S(1)}, u32[]{:S(2)}, u32[]{:S(2)}) collective-permute-start(f32[88,128]{1,0:T(8,128)S(1)} %get-tuple-element.45), channel_id=1, source_target_pairs={{0,8},{1,9},{2,10},{3,11},{4,12},{5,13},{6,14},{7,15},{8,16},{9,17... | collective-permute-start | bytes 135176 | tf_op jit(solution)/shard_map/ppermute | solution.py:510
  10.7 1.4 %collective-permute-start.5 = (f32[88,128]{1,0:T(8,128)S(1)}, f32[88,128]{1,0:T(8,128)S(1)}, u32[]{:S(2)}, u32[]{:S(2)}) collective-permute-start(f32[88,128]{1,0:T(8,128)S(1)} %get-tuple-element.46), channel_id=1, source_target_pairs={{0,24},{1,25},{2,26},{3,27},{4,28},{5,29},{6,30},{7,31},{8,0},{9,1... | collective-permute-start | bytes 135176 | tf_op jit(solution)/shard_map/ppermute | solution.py:510
  12.1 0.0 copy-start
  12.1 0.0 copy-start.5
  12.1 0.0 copy-start.6
  12.2 4.2 %shard_map.101.rest_5_ = f32[10,512,128]{2,1,0:T(8,128)S(1)} custom-call(f32[10,512,128]{2,1,0:T(8,128)S(1)} %get-tuple-element.38.q_ref.rest_6_, f32[2,512,128]{2,1,0:T(8,128)S(1)} %get-tuple-element.47.vel_ref.rest_7_, f32[9,9]{1,0:T(8,128)S(1)} %copy-done.1, f32[9]{0:T(128)S(1)} %copy-done.2, f32[9]{0:T(128)S(1)} %copy-done.3, f32[9]{0:T(128)S(1)} %copy-done.4), custom_call_target="tpu_custom_call" | custom-call | flops 19660800 | bytes 12000000 | tf_op jit(solution)/shard_map/pallas_call | solution.py:483
  16.4 1.0 %collective-permute-done.2.rest_1_.rest_4_ = f32[664,128]{1,0:T(8,128)S(1)} collective-permute-done((f32[664,128]{1,0:T(8,128)S(1)}, f32[664,128]{1,0:T(8,128)S(1)}, u32[]{:S(2)}, u32[]{:S(2)}) %collective-permute-start.2) | collective-permute-done | bytes 340000 | tf_op jit(solution)/shard_map/ppermute | solution.py:510
  17.4 1.4 %shard_map.102 = (f32[320,128]{1,0:T(8,128)S(1)}, f32[320,128]{1,0:T(8,128)S(1)}, f32[320,128]{1,0:T(8,128)S(1)}, f32[10,512,128]{2,1,0:T(8,128)S(1)}, f32[656,1...) custom-call(f32[640,128]{1,0:T(8,128)S(1)} %collective-permute-done., ...), custom_call_target="tpu_custom_call" | custom-call | tf_op jit(solution)/shard_map/pallas_call | solution.py:483
  18.8 0.7 %collective-permute-start.6 = (f32[656,128]{1,0:T(8,128)S(1)}, f32[656,128]{1,0:T(8,128)S(1)}, u32[]{:S(2)}, u32[]{:S(2)}) collective-permute-start(f32[656,128]{1,0:T(8,128)S(1)} %get-tuple-element.50.tile0_ref), channel_id=1, source_target_pairs={{3,1},{7,5},{11,9},{15,13},{19,17},{23,21},{27,25},{31,29}} | collective-permute-start | bytes 1007624 | tf_op jit(solution)/shard_map/ppermute | solution.py:510
  19.5 0.6 %collective-permute-start.7 = (f32[320,128]{1,0:T(8,128)S(1)}, f32[320,128]{1,0:T(8,128)S(1)}, u32[]{:S(2)}, u32[]{:S(2)}) collective-permute-start(f32[320,128]{1,0:T(8,128)S(1)} %get-tuple-element.54), channel_id=1, source_target_pairs={{1,9},{3,11},{5,13},{7,15},{9,17},{11,19},{13,21},{15,23},{17,25},... | collective-permute-start | bytes 491528 | tf_op jit(solution)/shard_map/ppermute | solution.py:510
  20.1 1.4 %collective-permute-start.8 = (f32[320,128]{1,0:T(8,128)S(1)}, f32[320,128]{1,0:T(8,128)S(1)}, u32[]{:S(2)}, u32[]{:S(2)}) collective-permute-start(f32[320,128]{1,0:T(8,128)S(1)} %get-tuple-element.55), channel_id=1, source_target_pairs={{1,17},{3,19},{5,21},{7,23},{9,25},{11,27},{13,29},{15,31},{17,1},... | collective-permute-start | bytes 491528 | tf_op jit(solution)/shard_map/ppermute | solution.py:510
  21.6 2.5 %collective-permute-start.9 = (f32[320,128]{1,0:T(8,128)S(1)}, f32[320,128]{1,0:T(8,128)S(1)}, u32[]{:S(2)}, u32[]{:S(2)}) collective-permute-start(f32[320,128]{1,0:T(8,128)S(1)} %get-tuple-element.56), channel_id=1, source_target_pairs={{1,25},{3,27},{5,29},{7,31},{9,1},{11,3},{13,5},{15,7},{17,9},{19,... | collective-permute-start | bytes 491528 | tf_op jit(solution)/shard_map/ppermute | solution.py:510
  24.0 2.3 %collective-permute-done.7.rest_0_ = f32[320,128]{1,0:T(8,128)S(1)} collective-permute-done((f32[320,128]{1,0:T(8,128)S(1)}, f32[320,128]{1,0:T(8,128)S(1)}, u32[]{:S(2)}, u32[]{:S(2)}) %collective-permute-start.7) | collective-permute-done | bytes 163872 | tf_op jit(solution)/shard_map/ppermute | solution.py:510
  26.3 3.5 %collective-permute-done.8.rest_1_ = f32[320,128]{1,0:T(8,128)S(1)} collective-permute-done((f32[320,128]{1,0:T(8,128)S(1)}, f32[320,128]{1,0:T(8,128)S(1)}, u32[]{:S(2)}, u32[]{:S(2)}) %collective-permute-start.8) | collective-permute-done | bytes 163872 | tf_op jit(solution)/shard_map/ppermute | solution.py:510
  29.8 0.1 shard_map.104
  29.9 0.7 %collective-permute-start.12 = (f32[656,128]{1,0:T(8,128)S(1)}, f32[656,128]{1,0:T(8,128)S(1)}, u32[]{:S(2)}, u32[]{:S(2)}) collective-permute-start(f32[656,128]{1,0:T(8,128)S(1)} %get-tuple-element.61), channel_id=1, source_target_pairs={{0,1},{1,0},{2,3},{3,2},{4,5},{5,4},{6,7},{7,6},{8,9},{9,8},{10,11... | collective-permute-start | bytes 1007624 | tf_op jit(solution)/shard_map/ppermute | solution.py:510
  30.5 1.3 %collective-permute-start.13 = (f32[656,128]{1,0:T(8,128)S(1)}, f32[656,128]{1,0:T(8,128)S(1)}, u32[]{:S(2)}, u32[]{:S(2)}) collective-permute-start(f32[656,128]{1,0:T(8,128)S(1)} %get-tuple-element.62), channel_id=1, source_target_pairs={{3,1},{7,5},{11,9},{15,13},{19,17},{23,21},{27,25},{31,29},{5,0},{... | collective-permute-start | bytes 1007624 | tf_op jit(solution)/shard_map/ppermute | solution.py:510
  31.8 1.6 %collective-permute-start.10 = (f32[80,128]{1,0:T(8,128)S(1)}, f32[80,128]{1,0:T(8,128)S(1)}, u32[]{:S(2)}, u32[]{:S(2)}) collective-permute-start(f32[80,128]{1,0:T(8,128)S(1)} %get-tuple-element.58), channel_id=1, source_target_pairs={{0,8},{1,9},{2,10},{3,11},{4,12},{5,13},{6,14},{7,15},{8,16},{9,17... | collective-permute-start | bytes 122888 | tf_op jit(solution)/shard_map/ppermute | solution.py:510
  33.4 1.4 %collective-permute-start.11 = (f32[80,128]{1,0:T(8,128)S(1)}, f32[80,128]{1,0:T(8,128)S(1)}, u32[]{:S(2)}, u32[]{:S(2)}) collective-permute-start(f32[80,128]{1,0:T(8,128)S(1)} %get-tuple-element.59), channel_id=1, source_target_pairs={{0,24},{1,25},{2,26},{3,27},{4,28},{5,29},{6,30},{7,31},{8,0},{9,1... | collective-permute-start | bytes 122888 | tf_op jit(solution)/shard_map/ppermute | solution.py:510
  34.8 4.4 %shard_map.103.part_ref = f32[10,512,128]{2,1,0:T(8,128)S(1)} custom-call(f32[10,512,128]{2,1,0:T(8,128)S(1)} %get-tuple-element.38.q_ref.rest_6_, f32[10,512,128]{2,1,0:T(8,128)S(1)} %get-tuple-element.49.q1_ref, f32[2,512,128]{2,1,0:T(8,128)S(1)} %get-tuple-element.47.vel_ref.rest_7_, f32[9,9]{1,0:T(8,128)S(1)} %copy-done.1, f32[9]{0:T(128)S(1)} %copy-done.2, ...), custom_call_target="tpu_custom_call" | custom-call | flops 19660800 | bytes 12000000 | tf_op jit(solution)/shard_map/pallas_call | solution.py:483
  39.2 4.2 %collective-permute-done.13.step_ref = f32[656,128]{1,0:T(8,128)S(1)} collective-permute-done((f32[656,128]{1,0:T(8,128)S(1)}, f32[656,128]{1,0:T(8,128)S(1)}, u32[]{:S(2)}, u32[]{:S(2)}) %collective-permute-start.13) | collective-permute-done | bytes 335904 | tf_op jit(solution)/shard_map/ppermute | solution.py:510
  43.4 0.1 shard_map.105
  43.5 0.1 collective-permute-start.14
  43.5 1.3 %collective-permute-start.15 = (f32[640,128]{1,0:T(8,128)S(1)}, f32[640,128]{1,0:T(8,128)S(1)}, u32[]{:S(2)}, u32[]{:S(2)}) collective-permute-start(f32[640,128]{1,0:T(8,128)S(1)} %get-tuple-element.70), channel_id=1, source_target_pairs={{5,0},{13,8},{21,16},{29,24}} | collective-permute-start | bytes 983048 | tf_op jit(solution)/shard_map/ppermute | solution.py:510
  44.8 3.0 %shard_map.106 = (f32[10,512,128]{2,1,0:T(8,128)}, f32[640,128]{1,0:T(8,128)S(1)}) custom-call(f32[10,512,128]{2,1,0:T(8,128)S(1)} %shard_map.103.part_ref, f32[10,512,128]{2,1,0:T(8,128)S(1)} %get-tuple-element.38.q_ref.rest_6_, f32[10,512,128]{2,1,0:T(8,128)S(1)} %get-tuple-element.49.q1_ref, f32[2,512,128]{2,1,0:T(8,128)S(1)} %get-tuple-element.47.vel_ref.rest_7_, ...), custom_call_target="tpu_custom_call" | custom-call | flops 19660800 | bytes 12000000 | tf_op jit(solution)/shard_map/pallas_call | solution.py:483
  47.9 5.0 %collective-permute-done.15.far_ref = f32[640,128]{1,0:T(8,128)S(1)} collective-permute-done((f32[640,128]{1,0:T(8,128)S(1)}, f32[640,128]{1,0:T(8,128)S(1)}, u32[]{:S(2)}, u32[]{:S(2)}) %collective-permute-start.15) | collective-permute-done | bytes 327712 | tf_op jit(solution)/shard_map/ppermute | solution.py:510
  52.8 1.0 %shard_map.107 = f32[10,64,8,128]{3,2,1,0:T(8,128)} custom-call(f32[10,64,8,128]{3,2,1,0:T(8,128)} %bitcast.21, f32[640,128]{1,0:T(8,128)S(1)} %get-tuple-element.68.keep_ref, f32[640,128]{1,0:T(8,128)S(1)} %collective-permute-done.14.core_ref, f32[640,128]{1,0:T(8,128)S(1)} %collective-permute-done.15.far_ref), custom_call_target="tpu_custom_call", output_to_operand_aliasing={{}: (0, {})} | custom-call | tf_op jit(solution)/shard_map/pallas_call | solution.py:483
  (24 shorter events, 0.1 us)
Async XLA Ops:
  0.0 12.1 %copy-start.4 = (f32[9]{0:T(128)S(1)}, f32[9]{0:T(128)}, u32[]{:S(2)}) copy-start(f32[9]{0:T(128)} %rest_5_.1) | copy-start | bytes 112
  0.0 12.1 %copy-start.3 = (f32[9]{0:T(128)S(1)}, f32[9]{0:T(128)}, u32[]{:S(2)}) copy-start(f32[9]{0:T(128)} %rest_4_.1) | copy-start | bytes 112
  0.0 12.1 %copy-start.2 = (f32[9]{0:T(128)S(1)}, f32[9]{0:T(128)}, u32[]{:S(2)}) copy-start(f32[9]{0:T(128)} %rest_3_.1) | copy-start | bytes 112
  0.0 12.1 %copy-start.1 = (f32[9,9]{1,0:T(8,128)S(1)}, f32[9,9]{1,0:T(8,128)}, u32[]{:S(2)}) copy-start(f32[9,9]{1,0:T(8,128)} %rest_2_.1) | copy-start | bytes 976
  2.3 8.4 %collective-permute-start = (f32[640,128]{1,0:T(8,128)S(1)}, f32[640,128]{1,0:T(8,128)S(1)}, u32[]{:S(2)}, u32[]{:S(2)}) collective-permute-start(f32[640,128]{1,0:T(8,128)S(1)} %get-tuple-element.40), channel_id=1, source_target_pairs={{0,1},{1,0},{2,3},{3,2},{4,5},{5,4},{6,7},{7,6},{8,9},{9,8},{10,11... | collective-permute-start | bytes 983048 | tf_op jit(solution)/shard_map/ppermute | solution.py:510
  3.6 12.8 %collective-permute-start.1 = (f32[664,128]{1,0:T(8,128)S(1)}, f32[664,128]{1,0:T(8,128)S(1)}, u32[]{:S(2)}, u32[]{:S(2)}) collective-permute-start(f32[664,128]{1,0:T(8,128)S(1)} %get-tuple-element.42), channel_id=1, source_target_pairs={{1,9},{3,11},{5,13},{7,15},{9,17},{11,19},{13,21},{15,23},{17,25},... | collective-permute-start | bytes 1019912 | tf_op jit(solution)/shard_map/ppermute | solution.py:510
  6.0 11.4 %collective-permute-start.2 = (f32[664,128]{1,0:T(8,128)S(1)}, f32[664,128]{1,0:T(8,128)S(1)}, u32[]{:S(2)}, u32[]{:S(2)}) collective-permute-start(f32[664,128]{1,0:T(8,128)S(1)} %get-tuple-element.43), channel_id=1, source_target_pairs={{1,17},{3,19},{5,21},{7,23},{9,25},{11,27},{13,29},{15,31},{17,1},... | collective-permute-start | bytes 1019912 | tf_op jit(solution)/shard_map/ppermute | solution.py:510
  8.4 8.9 %collective-permute-start.3 = (f32[664,128]{1,0:T(8,128)S(1)}, f32[664,128]{1,0:T(8,128)S(1)}, u32[]{:S(2)}, u32[]{:S(2)}) collective-permute-start(f32[664,128]{1,0:T(8,128)S(1)} %get-tuple-element.44), channel_id=1, source_target_pairs={{1,25},{3,27},{5,29},{7,31},{9,1},{11,3},{13,5},{15,7},{17,9},{19,... | collective-permute-start | bytes 1019912 | tf_op jit(solution)/shard_map/ppermute | solution.py:510
  9.1 7.3 %collective-permute-start.4 = (f32[88,128]{1,0:T(8,128)S(1)}, f32[88,128]{1,0:T(8,128)S(1)}, u32[]{:S(2)}, u32[]{:S(2)}) collective-permute-start(f32[88,128]{1,0:T(8,128)S(1)} %get-tuple-element.45), channel_id=1, source_target_pairs={{0,8},{1,9},{2,10},{3,11},{4,12},{5,13},{6,14},{7,15},{8,16},{9,17... | collective-permute-start | bytes 135176 | tf_op jit(solution)/shard_map/ppermute | solution.py:510
  10.7 6.7 %collective-permute-start.5 = (f32[88,128]{1,0:T(8,128)S(1)}, f32[88,128]{1,0:T(8,128)S(1)}, u32[]{:S(2)}, u32[]{:S(2)}) collective-permute-start(f32[88,128]{1,0:T(8,128)S(1)} %get-tuple-element.46), channel_id=1, source_target_pairs={{0,24},{1,25},{2,26},{3,27},{4,28},{5,29},{6,30},{7,31},{8,0},{9,1... | collective-permute-start | bytes 135176 | tf_op jit(solution)/shard_map/ppermute | solution.py:510
  12.1 5.3 %copy-start = (f32[10,1,8192]{2,1,0:T(1,128)S(1)}, f32[10,1,8192]{2,1,0:T(1,128)}, u32[]{:S(2)}) copy-start(f32[10,1,8192]{2,1,0:T(1,128)} %param.12) | copy-start | bytes 983044
  12.1 5.3 %copy-start.5 = (s32[8,1]{0,1:T(1,128)S(1)}, s32[8,1]{0,1:T(1,128)}, u32[]{:S(2)}) copy-start(s32[8,1]{0,1:T(1,128)} %param.17) | copy-start | bytes 100
  12.1 5.3 %copy-start.6 = (s32[8]{0:T(128)S(1)}, s32[8]{0:T(128)}, u32[]{:S(2)}) copy-start(s32[8]{0:T(128)} %rest_11_.1) | copy-start | bytes 100
  12.1 5.3 %copy-start.7 = (s32[8]{0:T(128)S(1)}, s32[8]{0:T(128)}, u32[]{:S(2)}) copy-start(s32[8]{0:T(128)} %rest_12_.1) | copy-start | bytes 100
  18.8 11.0 %collective-permute-start.6 = (f32[656,128]{1,0:T(8,128)S(1)}, f32[656,128]{1,0:T(8,128)S(1)}, u32[]{:S(2)}, u32[]{:S(2)}) collective-permute-start(f32[656,128]{1,0:T(8,128)S(1)} %get-tuple-element.50.tile0_ref), channel_id=1, source_target_pairs={{3,1},{7,5},{11,9},{15,13},{19,17},{23,21},{27,25},{31,29}} | collective-permute-start | bytes 1007624 | tf_op jit(solution)/shard_map/ppermute | solution.py:510
  19.5 6.8 %collective-permute-start.7 = (f32[320,128]{1,0:T(8,128)S(1)}, f32[320,128]{1,0:T(8,128)S(1)}, u32[]{:S(2)}, u32[]{:S(2)}) collective-permute-start(f32[320,128]{1,0:T(8,128)S(1)} %get-tuple-element.54), channel_id=1, source_target_pairs={{1,9},{3,11},{5,13},{7,15},{9,17},{11,19},{13,21},{15,23},{17,25},... | collective-permute-start | bytes 491528 | tf_op jit(solution)/shard_map/ppermute | solution.py:510
  20.1 9.7 %collective-permute-start.8 = (f32[320,128]{1,0:T(8,128)S(1)}, f32[320,128]{1,0:T(8,128)S(1)}, u32[]{:S(2)}, u32[]{:S(2)}) collective-permute-start(f32[320,128]{1,0:T(8,128)S(1)} %get-tuple-element.55), channel_id=1, source_target_pairs={{1,17},{3,19},{5,21},{7,23},{9,25},{11,27},{13,29},{15,31},{17,1},... | collective-permute-start | bytes 491528 | tf_op jit(solution)/shard_map/ppermute | solution.py:510
  21.6 8.2 %collective-permute-start.9 = (f32[320,128]{1,0:T(8,128)S(1)}, f32[320,128]{1,0:T(8,128)S(1)}, u32[]{:S(2)}, u32[]{:S(2)}) collective-permute-start(f32[320,128]{1,0:T(8,128)S(1)} %get-tuple-element.56), channel_id=1, source_target_pairs={{1,25},{3,27},{5,29},{7,31},{9,1},{11,3},{13,5},{15,7},{17,9},{19,... | collective-permute-start | bytes 491528 | tf_op jit(solution)/shard_map/ppermute | solution.py:510
  29.9 9.3 %collective-permute-start.12 = (f32[656,128]{1,0:T(8,128)S(1)}, f32[656,128]{1,0:T(8,128)S(1)}, u32[]{:S(2)}, u32[]{:S(2)}) collective-permute-start(f32[656,128]{1,0:T(8,128)S(1)} %get-tuple-element.61), channel_id=1, source_target_pairs={{0,1},{1,0},{2,3},{3,2},{4,5},{5,4},{6,7},{7,6},{8,9},{9,8},{10,11... | collective-permute-start | bytes 1007624 | tf_op jit(solution)/shard_map/ppermute | solution.py:510
  30.5 12.8 %collective-permute-start.13 = (f32[656,128]{1,0:T(8,128)S(1)}, f32[656,128]{1,0:T(8,128)S(1)}, u32[]{:S(2)}, u32[]{:S(2)}) collective-permute-start(f32[656,128]{1,0:T(8,128)S(1)} %get-tuple-element.62), channel_id=1, source_target_pairs={{3,1},{7,5},{11,9},{15,13},{19,17},{23,21},{27,25},{31,29},{5,0},{... | collective-permute-start | bytes 1007624 | tf_op jit(solution)/shard_map/ppermute | solution.py:510
  31.8 7.4 %collective-permute-start.10 = (f32[80,128]{1,0:T(8,128)S(1)}, f32[80,128]{1,0:T(8,128)S(1)}, u32[]{:S(2)}, u32[]{:S(2)}) collective-permute-start(f32[80,128]{1,0:T(8,128)S(1)} %get-tuple-element.58), channel_id=1, source_target_pairs={{0,8},{1,9},{2,10},{3,11},{4,12},{5,13},{6,14},{7,15},{8,16},{9,17... | collective-permute-start | bytes 122888 | tf_op jit(solution)/shard_map/ppermute | solution.py:510
  33.4 5.8 %collective-permute-start.11 = (f32[80,128]{1,0:T(8,128)S(1)}, f32[80,128]{1,0:T(8,128)S(1)}, u32[]{:S(2)}, u32[]{:S(2)}) collective-permute-start(f32[80,128]{1,0:T(8,128)S(1)} %get-tuple-element.59), channel_id=1, source_target_pairs={{0,24},{1,25},{2,26},{3,27},{4,28},{5,29},{6,30},{7,31},{8,0},{9,1... | collective-permute-start | bytes 122888 | tf_op jit(solution)/shard_map/ppermute | solution.py:510
  43.5 4.4 %collective-permute-start.14 = (f32[640,128]{1,0:T(8,128)S(1)}, f32[640,128]{1,0:T(8,128)S(1)}, u32[]{:S(2)}, u32[]{:S(2)}) collective-permute-start(f32[640,128]{1,0:T(8,128)S(1)} %get-tuple-element.69), channel_id=1, source_target_pairs={{0,1},{1,0},{2,3},{3,2},{4,5},{5,4},{6,7},{7,6},{8,9},{9,8},{10,11... | collective-permute-start | bytes 983048 | tf_op jit(solution)/shard_map/ppermute | solution.py:510
  43.5 9.3 %collective-permute-start.15 = (f32[640,128]{1,0:T(8,128)S(1)}, f32[640,128]{1,0:T(8,128)S(1)}, u32[]{:S(2)}, u32[]{:S(2)}) collective-permute-start(f32[640,128]{1,0:T(8,128)S(1)} %get-tuple-element.70), channel_id=1, source_target_pairs={{5,0},{13,8},{21,16},{29,24}} | collective-permute-start | bytes 983048 | tf_op jit(solution)/shard_map/ppermute | solution.py:510

commit v5 on v4

--- a/solution.py
+++ b/solution.py
@@ -334,23 +334,18 @@
                 used[k] = used[k] + here.astype(jnp.int32)
 
 
-def tree_kernel(n_out, cap, tile0_ref, down0_ref, own_ref, s1_ref, z_ref, *rest):
-    got, tables, (tile_ref, step_ref, core_ref) = rest[:n_out], rest[n_out:2 * n_out], rest[2 * n_out:]
-    _, ax, plen = roles()
+def tile_kernel(n_out, cap, own_ref, z_ref, *rest):
+    got, tables, (step_ref,) = rest[:n_out], rest[n_out:2 * n_out], rest[2 * n_out:]
+    _, _, plen = roles()
     rows = own_ref.shape[0]
     n = rows // NV
 
     @pl.when(plen == 0)
     def _():
-        core_ref[pl.ds(0, rows), :] = s1_ref[...]
-        step_ref[pl.ds(0, rows), :] = z_ref[...]
-        core_ref[pl.ds(rows, EXT), :] = jnp.zeros((EXT, LANES), f32)
-        step_ref[pl.ds(rows, EXT), :] = jnp.zeros((EXT, LANES), f32)
-        tile_ref[...] = jnp.zeros_like(tile_ref)
+        step_ref[...] = z_ref[...]
 
     @pl.when(plen == 1)
     def _():
-        core_ref[...] = tile0_ref[...] + down0_ref[...]
         slots = [(k, m) for k in range(n_out) for m in range(cap)]
         named = [jnp.broadcast_to(tables[k][pl.ds(rows + EXT + m, 1), :], (CAX, LANES)) for k, m in slots]
         for v in range(NV):
@@ -360,40 +355,41 @@
                 total = own_ref[at, :]
                 for name, value in zip(named, blocks):
                     total = total + jnp.where(name == t, value, 0.0)
-                tile_ref[at, :] = total
-
-        @pl.when(ax % 2 == 1)
-        def _():
-            step_ref[pl.ds(0, rows), :] = tile_ref[...]
-            step_ref[pl.ds(rows, EXT), :] = jnp.zeros((EXT, LANES), f32)
-
-        @pl.when(ax % 2 == 0)
-        def _():
-            step_ref[...] = core_ref[...]
-
-
-def inlet_kernel(tile_ref, step_ref, core_ref, dq_ref, pair_ref, core_out_ref):
+                step_ref[at, :] = total
+
+
+def pair_kernel(tile_ref, down_ref, s1_ref, core_ref):
+    _, _, plen = roles()
+    rows = s1_ref.shape[0]
+
+    @pl.when(plen == 0)
+    def _():
+        core_ref[pl.ds(0, rows), :] = s1_ref[...]
+        core_ref[pl.ds(rows, EXT), :] = jnp.zeros((EXT, LANES), f32)
+
+    @pl.when(plen == 1)
+    def _():
+        core_ref[...] = tile_ref[...] + down_ref[...]
+
+
+def add_kernel(x_ref, y_ref, out_ref):
+    out_ref[...] = x_ref[...] + y_ref[...]
+
+
+def inlet_kernel(pair_ref, far_ref, core_ref, dq_ref, out_ref):
     _, ax, plen = roles()
-    rows = tile_ref.shape[0]
-
-    @pl.when(plen == 1)
-    def _():
-        pair = tile_ref[...] + step_ref[pl.ds(0, rows), :]
-        pair_ref[...] = pair
-        core_out_ref[...] = pair
+    rows = out_ref.shape[0]
+    inlet_side = jnp.logical_and(plen == 0, ax == 0)
+
+    @pl.when(inlet_side)
+    def _():
+        dq_ref[...] = 0.1 * (far_ref[...] + core_ref[...])
+        out_ref[...] = dq_ref[pl.ds(0, rows), :]
+
+    @pl.when(jnp.logical_not(inlet_side))
+    def _():
         dq_ref[...] = jnp.zeros_like(dq_ref)
-
-    @pl.when(jnp.logical_and(plen == 0, ax > 0))
-    def _():
-        pair_ref[...] = jnp.zeros_like(pair_ref)
-        core_out_ref[...] = jnp.zeros_like(core_out_ref)
-        dq_ref[...] = jnp.zeros_like(dq_ref)
-
-    @pl.when(jnp.logical_and(plen == 0, ax == 0))
-    def _():
-        pair_ref[...] = jnp.zeros_like(pair_ref)
-        dq_ref[...] = 0.1 * (step_ref[...] + core_ref[...])
-        core_out_ref[...] = dq_ref[pl.ds(0, rows), :]
+        out_ref[...] = pair_ref[...]
 
 
 def border_two_kernel(n_ax, n_z, part_ref, q_ref, q1_ref, vel_ref, core_ref, supply_ref, step_ref, dq_ref, hl_ref, hr_ref,
@@ -569,16 +565,20 @@
     rb = [send(x, compact(k)) for k, x in enumerate(outs)]
     down0 = send(tile0, down)
 
-    tile1, step, core = call(functools.partial(tree_kernel, n_out, cap), (tile0, down0, own1, s1, z1, *rb, *ra),
-                             "v" * (5 + 2 * n_out), [row, wide, wide])
-    step_in = send(step, down + across + inner)
+    step, = call(functools.partial(tile_kernel, n_out, cap), (own1, z1, *rb, *ra), "v" * (2 + 2 * n_out), [row])
+    step_in = send(step, down + inner)
+    er, el, step = lax.optimization_barrier((er, el, step))
+    hl1, hr1 = send(er, ring(1)), send(el, ring(-1))
+    core, = call(pair_kernel, (tile0, down0, s1), "vvv", [wide])
+    far0 = send(core, across)
     core_in = send(core, swap)
-    hl1, hr1 = send(er, ring(1)), send(el, ring(-1))
+    pair1, = call(add_kernel, (step, step_in), "vv", [row])
+    far1 = send(pair1, across)
+    q1, pair1 = lax.optimization_barrier((q1, pair1))
     part, = call(inside_two_kernel, (qv, q1, velv) + react, "vvvssss", [whole], [matrix], cost=work)
-    part, tile1, hl1, hr1 = lax.optimization_barrier((part, tile1, hl1, hr1))
-
-    dq, pair1, core2 = call(inlet_kernel, (tile1, step_in, core_in), "vvv", [wide, row, row])
-    far1 = send(pair1, across)
+    part, pair1, hl1, hr1 = lax.optimization_barrier((part, pair1, hl1, hr1))
+
+    dq, core2 = call(inlet_kernel, (pair1, far0, core_in), "vvv", [wide, row])
     core2_in = send(core2, swap)
     out, keep = call(functools.partial(border_two_kernel, n_ax, pieces),
                      (part, qv, q1, velv, core_in, sup, step_in, dq, hl1, hr1, hl0, hr0, *rb[:pieces]) + react,

time: 53.9 us -> 50.6 us (0.939)
  waiting for transfers between devices: 15.9 us -> 0.99 us
  starting transfers between devices: 21.3 us -> 32.8 us
    ppermute x16 -> x17, waiting for transfers between devices: 15.9 us -> 0.99 us  [send(): return lax.ppermute(x, AXES, [(number(*a), number(*b)) for a, b in route])]
    ppermute x16 -> x17, starting transfers between devices: 21.3 us -> 32.8 us  [send(): return lax.ppermute(x, AXES, [(number(*a), number(*b)) for a, b in route])]
    pallas_call x8 -> x10, Pallas kernels: 16.3 us -> 16.4 us  [call(): pl.pallas_call(kernel, in_specs=[pl.BlockSpec(memory_space=SPACES[k]) for...]
  transfers between devices with their start and end apart: 16 -> 17, of which waited for: 5 -> 1; matrix products, arithmetic and copies ran while one was open for 0% -> 0% of each run, Pallas kernels for 22% -> 23%
where the time goes in v5:
time: 50.6 us; the launch traced here: 50.5 us
  starting transfers between devices  32.8 us (65%)
  Pallas kernels  16.4 us (32%)
  waiting for transfers between devices  0.99 us (2%)
    ppermute x17, starting transfers between devices, send(): return lax.ppermute(x, AXES, [(number(*a), number(*b)) for a, b in route])  32.8 us
    pallas_call x10, Pallas kernels, call(): pl.pallas_call(kernel, in_specs=[pl.BlockSpec(memory_space=SPACES[k]) for...  16.4 us
  transfers between devices with their start and end apart: 17, of which 1 were waited for; matrix products, arithmetic and copies ran while one was open for 0% of the time, Pallas kernels for 23%

profile of v5, /device:TPU:0, one launch (start us, length us, event | category | flops | bytes accessed | tf_op | source)
XLA Modules:
  0.0 50.5 jit_solution(15487518114143923713)
XLA Ops:
  0.0 2.3 %shard_map.100 = (f32[664,128]{1,0:T(8,128)S(1)}, f32[664,128]{1,0:T(8,128)S(1)}, f32[664,128]{1,0:T(8,128)S(1)}, f32[10,512,128]{2,1,0:T(8,128)S(1)}, f32[2,512...) custom-call(f32[10,512,128]{2,1,0:T(8,128)} %bitcast.20, ...), custom_call_target="tpu_custom_call" | custom-call | tf_op jit(solution)/shard_map/pallas_call | solution.py:479
  2.3 1.3 %collective-permute-start = (f32[640,128]{1,0:T(8,128)S(1)}, f32[640,128]{1,0:T(8,128)S(1)}, u32[]{:S(2)}, u32[]{:S(2)}) collective-permute-start(f32[640,128]{1,0:T(8,128)S(1)} %get-tuple-element.41), channel_id=1, source_target_pairs={{0,1},{1,0},{2,3},{3,2},{4,5},{5,4},{6,7},{7,6},{8,9},{9,8},{10,11... | collective-permute-start | bytes 983048 | tf_op jit(solution)/shard_map/ppermute | solution.py:506
  3.6 2.4 %collective-permute-start.1 = (f32[664,128]{1,0:T(8,128)S(1)}, f32[664,128]{1,0:T(8,128)S(1)}, u32[]{:S(2)}, u32[]{:S(2)}) collective-permute-start(f32[664,128]{1,0:T(8,128)S(1)} %get-tuple-element.43), channel_id=1, source_target_pairs={{1,9},{3,11},{5,13},{7,15},{9,17},{11,19},{13,21},{15,23},{17,25},... | collective-permute-start | bytes 1019912 | tf_op jit(solution)/shard_map/ppermute | solution.py:506
  6.0 2.5 %collective-permute-start.2 = (f32[664,128]{1,0:T(8,128)S(1)}, f32[664,128]{1,0:T(8,128)S(1)}, u32[]{:S(2)}, u32[]{:S(2)}) collective-permute-start(f32[664,128]{1,0:T(8,128)S(1)} %get-tuple-element.44), channel_id=1, source_target_pairs={{1,17},{3,19},{5,21},{7,23},{9,25},{11,27},{13,29},{15,31},{17,1},... | collective-permute-start | bytes 1019912 | tf_op jit(solution)/shard_map/ppermute | solution.py:506
  8.4 0.7 %collective-permute-start.3 = (f32[664,128]{1,0:T(8,128)S(1)}, f32[664,128]{1,0:T(8,128)S(1)}, u32[]{:S(2)}, u32[]{:S(2)}) collective-permute-start(f32[664,128]{1,0:T(8,128)S(1)} %get-tuple-element.45), channel_id=1, source_target_pairs={{1,25},{3,27},{5,29},{7,31},{9,1},{11,3},{13,5},{15,7},{17,9},{19,... | collective-permute-start | bytes 1019912 | tf_op jit(solution)/shard_map/ppermute | solution.py:506
  9.1 1.6 %collective-permute-start.4 = (f32[88,128]{1,0:T(8,128)S(1)}, f32[88,128]{1,0:T(8,128)S(1)}, u32[]{:S(2)}, u32[]{:S(2)}) collective-permute-start(f32[88,128]{1,0:T(8,128)S(1)} %get-tuple-element.46), channel_id=1, source_target_pairs={{0,8},{1,9},{2,10},{3,11},{4,12},{5,13},{6,14},{7,15},{8,16},{9,17... | collective-permute-start | bytes 135176 | tf_op jit(solution)/shard_map/ppermute | solution.py:506
  10.7 1.4 %collective-permute-start.5 = (f32[88,128]{1,0:T(8,128)S(1)}, f32[88,128]{1,0:T(8,128)S(1)}, u32[]{:S(2)}, u32[]{:S(2)}) collective-permute-start(f32[88,128]{1,0:T(8,128)S(1)} %get-tuple-element.47), channel_id=1, source_target_pairs={{0,24},{1,25},{2,26},{3,27},{4,28},{5,29},{6,30},{7,31},{8,0},{9,1... | collective-permute-start | bytes 135176 | tf_op jit(solution)/shard_map/ppermute | solution.py:506
  12.1 0.0 copy-start
  12.1 0.0 copy-start.5
  12.1 0.0 copy-start.6
  12.1 0.0 copy-start.7
  12.1 4.2 %shard_map.101.rest_5_ = f32[10,512,128]{2,1,0:T(8,128)S(1)} custom-call(f32[10,512,128]{2,1,0:T(8,128)S(1)} %get-tuple-element.39.q_ref.rest_6_, f32[2,512,128]{2,1,0:T(8,128)S(1)} %get-tuple-element.48.vel_ref.rest_7_, f32[9,9]{1,0:T(8,128)S(1)} %copy-done.1, f32[9]{0:T(128)S(1)} %copy-done.2, f32[9]{0:T(128)S(1)} %copy-done.3, f32[9]{0:T(128)S(1)} %copy-done.4), custom_call_target="tpu_custom_call" | custom-call | flops 19660800 | bytes 12000000 | tf_op jit(solution)/shard_map/pallas_call | solution.py:479
  16.4 0.0 collective-permute-done.4.rest_3_.hl0_ref
  16.4 1.0 %collective-permute-done.2.rest_1_.rest_4_ = f32[664,128]{1,0:T(8,128)S(1)} collective-permute-done((f32[664,128]{1,0:T(8,128)S(1)}, f32[664,128]{1,0:T(8,128)S(1)}, u32[]{:S(2)}, u32[]{:S(2)}) %collective-permute-start.2) | collective-permute-done | bytes 340000 | tf_op jit(solution)/shard_map/ppermute | solution.py:506
  17.4 0.0 collective-permute-done.3.rest_2_.rest_5_
  17.4 1.4 %shard_map.102 = (f32[320,128]{1,0:T(8,128)S(1)}, f32[320,128]{1,0:T(8,128)S(1)}, f32[320,128]{1,0:T(8,128)S(1)}, f32[10,512,128]{2,1,0:T(8,128)S(1)}, f32[656,1...) custom-call(f32[640,128]{1,0:T(8,128)S(1)} %collective-permute-done., ...), custom_call_target="tpu_custom_call" | custom-call | tf_op jit(solution)/shard_map/pallas_call | solution.py:479
  18.8 0.7 %collective-permute-start.12 = (f32[656,128]{1,0:T(8,128)S(1)}, f32[656,128]{1,0:T(8,128)S(1)}, u32[]{:S(2)}, u32[]{:S(2)}) collective-permute-start(f32[656,128]{1,0:T(8,128)S(1)} %get-tuple-element.64.tile_ref), channel_id=1, source_target_pairs={{3,1},{7,5},{11,9},{15,13},{19,17},{23,21},{27,25},{31,29}} | collective-permute-start | bytes 1007624 | tf_op jit(solution)/shard_map/ppermute | solution.py:506
  19.5 0.6 %collective-permute-start.6 = (f32[320,128]{1,0:T(8,128)S(1)}, f32[320,128]{1,0:T(8,128)S(1)}, u32[]{:S(2)}, u32[]{:S(2)}) collective-permute-start(f32[320,128]{1,0:T(8,128)S(1)} %get-tuple-element.55), channel_id=1, source_target_pairs={{1,9},{3,11},{5,13},{7,15},{9,17},{11,19},{13,21},{15,23},{17,25},... | collective-permute-start | bytes 491528 | tf_op jit(solution)/shard_map/ppermute | solution.py:506
  20.1 1.4 %collective-permute-start.7 = (f32[320,128]{1,0:T(8,128)S(1)}, f32[320,128]{1,0:T(8,128)S(1)}, u32[]{:S(2)}, u32[]{:S(2)}) collective-permute-start(f32[320,128]{1,0:T(8,128)S(1)} %get-tuple-element.56), channel_id=1, source_target_pairs={{1,17},{3,19},{5,21},{7,23},{9,25},{11,27},{13,29},{15,31},{17,1},... | collective-permute-start | bytes 491528 | tf_op jit(solution)/shard_map/ppermute | solution.py:506
  21.6 2.5 %collective-permute-start.8 = (f32[320,128]{1,0:T(8,128)S(1)}, f32[320,128]{1,0:T(8,128)S(1)}, u32[]{:S(2)}, u32[]{:S(2)}) collective-permute-start(f32[320,128]{1,0:T(8,128)S(1)} %get-tuple-element.57), channel_id=1, source_target_pairs={{1,25},{3,27},{5,29},{7,31},{9,1},{11,3},{13,5},{15,7},{17,9},{19,... | collective-permute-start | bytes 491528 | tf_op jit(solution)/shard_map/ppermute | solution.py:506
  24.0 0.0 collective-permute-done.12.down_ref
  24.1 1.3 %collective-permute-start.14 = (f32[656,128]{1,0:T(8,128)S(1)}, f32[656,128]{1,0:T(8,128)S(1)}, u32[]{:S(2)}, u32[]{:S(2)}) collective-permute-start(f32[656,128]{1,0:T(8,128)S(1)} %shard_map.106), channel_id=1, source_target_pairs={{5,0},{13,8},{21,16},{29,24}} | collective-permute-start | bytes 1007624 | tf_op jit(solution)/shard_map/ppermute | solution.py:506
  25.4 5.5 %collective-permute-start.13 = (f32[656,128]{1,0:T(8,128)S(1)}, f32[656,128]{1,0:T(8,128)S(1)}, u32[]{:S(2)}, u32[]{:S(2)}) collective-permute-start(f32[656,128]{1,0:T(8,128)S(1)} %shard_map.106), channel_id=1, source_target_pairs={{0,1},{1,0},{2,3},{3,2},{4,5},{5,4},{6,7},{7,6},{8,9},{9,8},{10,11... | collective-permute-start | bytes 1007624 | tf_op jit(solution)/shard_map/ppermute | solution.py:506
  30.9 0.7 %collective-permute-start.9 = (f32[640,128]{1,0:T(8,128)S(1)}, f32[640,128]{1,0:T(8,128)S(1)}, u32[]{:S(2)}, u32[]{:S(2)}) collective-permute-start(f32[640,128]{1,0:T(8,128)S(1)} %shard_map.103.x_ref), channel_id=1, source_target_pairs={{3,1},{7,5},{11,9},{15,13},{19,17},{23,21},{27,25},{31,29},{2,4},{... | collective-permute-start | bytes 983048 | tf_op jit(solution)/shard_map/ppermute | solution.py:506
  31.6 1.6 %collective-permute-start.10 = (f32[80,128]{1,0:T(8,128)S(1)}, f32[80,128]{1,0:T(8,128)S(1)}, u32[]{:S(2)}, u32[]{:S(2)}) collective-permute-start(f32[80,128]{1,0:T(8,128)S(1)} %get-tuple-element.61), channel_id=1, source_target_pairs={{0,8},{1,9},{2,10},{3,11},{4,12},{5,13},{6,14},{7,15},{8,16},{9,17... | collective-permute-start | bytes 122888 | tf_op jit(solution)/shard_map/ppermute | solution.py:506
  33.1 1.4 %collective-permute-start.11 = (f32[80,128]{1,0:T(8,128)S(1)}, f32[80,128]{1,0:T(8,128)S(1)}, u32[]{:S(2)}, u32[]{:S(2)}) collective-permute-start(f32[80,128]{1,0:T(8,128)S(1)} %get-tuple-element.62), channel_id=1, source_target_pairs={{0,24},{1,25},{2,26},{3,27},{4,28},{5,29},{6,30},{7,31},{8,0},{9,1... | collective-permute-start | bytes 122888 | tf_op jit(solution)/shard_map/ppermute | solution.py:506
  34.6 1.3 %collective-permute-start.16 = (f32[640,128]{1,0:T(8,128)S(1)}, f32[640,128]{1,0:T(8,128)S(1)}, u32[]{:S(2)}, u32[]{:S(2)}) collective-permute-start(f32[640,128]{1,0:T(8,128)S(1)} %shard_map.104.pair_ref), channel_id=1, source_target_pairs={{5,0},{13,8},{21,16},{29,24}} | collective-permute-start | bytes 983048 | tf_op jit(solution)/shard_map/ppermute | solution.py:506
  35.9 4.4 %shard_map.105.part_ref = f32[10,512,128]{2,1,0:T(8,128)S(1)} custom-call(f32[10,512,128]{2,1,0:T(8,128)S(1)} %get-tuple-element.39.q_ref.rest_6_, f32[10,512,128]{2,1,0:T(8,128)S(1)} %get-tuple-element.59.q1_ref, f32[2,512,128]{2,1,0:T(8,128)S(1)} %get-tuple-element.48.vel_ref.rest_7_, f32[9,9]{1,0:T(8,128)S(1)} %copy-done.1, f32[9]{0:T(128)S(1)} %copy-done.2, ...), custom_call_target="tpu_custom_call" | custom-call | flops 19660800 | bytes 12000000 | tf_op jit(solution)/shard_map/pallas_call | solution.py:479
  40.3 0.1 shard_map.107
  40.4 6.1 %collective-permute-start.15 = (f32[640,128]{1,0:T(8,128)S(1)}, f32[640,128]{1,0:T(8,128)S(1)}, u32[]{:S(2)}, u32[]{:S(2)}) collective-permute-start(f32[640,128]{1,0:T(8,128)S(1)} %get-tuple-element.72), channel_id=1, source_target_pairs={{0,1},{1,0},{2,3},{3,2},{4,5},{5,4},{6,7},{7,6},{8,9},{9,8},{10,11... | collective-permute-start | bytes 983048 | tf_op jit(solution)/shard_map/ppermute | solution.py:506
  46.5 3.0 %shard_map.108 = (f32[10,512,128]{2,1,0:T(8,128)}, f32[640,128]{1,0:T(8,128)S(1)}) custom-call(f32[10,512,128]{2,1,0:T(8,128)S(1)} %shard_map.105.part_ref, f32[10,512,128]{2,1,0:T(8,128)S(1)} %get-tuple-element.39.q_ref.rest_6_, f32[10,512,128]{2,1,0:T(8,128)S(1)} %get-tuple-element.59.q1_ref, f32[2,512,128]{2,1,0:T(8,128)S(1)} %get-tuple-element.48.vel_ref.rest_7_, ...), custom_call_target="tpu_custom_call" | custom-call | flops 19660800 | bytes 12000000 | tf_op jit(solution)/shard_map/pallas_call | solution.py:479
  49.5 1.0 %shard_map.109 = f32[10,64,8,128]{3,2,1,0:T(8,128)} custom-call(f32[10,64,8,128]{3,2,1,0:T(8,128)} %bitcast.21, f32[640,128]{1,0:T(8,128)S(1)} %get-tuple-element.71.keep_ref, f32[640,128]{1,0:T(8,128)S(1)} %collective-permute-done.15.core_ref, f32[640,128]{1,0:T(8,128)S(1)} %collective-permute-done.16.far_ref), custom_call_target="tpu_custom_call", output_to_operand_aliasing={{}: (0, {})} | custom-call | tf_op jit(solution)/shard_map/pallas_call | solution.py:479
  (28 shorter events, 0.2 us)
Async XLA Ops:
  0.0 12.1 %copy-start.4 = (f32[9]{0:T(128)S(1)}, f32[9]{0:T(128)}, u32[]{:S(2)}) copy-start(f32[9]{0:T(128)} %rest_5_.1) | copy-start | bytes 112
  0.0 12.1 %copy-start.3 = (f32[9]{0:T(128)S(1)}, f32[9]{0:T(128)}, u32[]{:S(2)}) copy-start(f32[9]{0:T(128)} %rest_4_.1) | copy-start | bytes 112
  0.0 12.1 %copy-start.2 = (f32[9]{0:T(128)S(1)}, f32[9]{0:T(128)}, u32[]{:S(2)}) copy-start(f32[9]{0:T(128)} %rest_3_.1) | copy-start | bytes 112
  0.0 12.1 %copy-start.1 = (f32[9,9]{1,0:T(8,128)S(1)}, f32[9,9]{1,0:T(8,128)}, u32[]{:S(2)}) copy-start(f32[9,9]{1,0:T(8,128)} %rest_2_.1) | copy-start | bytes 976
  2.3 8.4 %collective-permute-start = (f32[640,128]{1,0:T(8,128)S(1)}, f32[640,128]{1,0:T(8,128)S(1)}, u32[]{:S(2)}, u32[]{:S(2)}) collective-permute-start(f32[640,128]{1,0:T(8,128)S(1)} %get-tuple-element.41), channel_id=1, source_target_pairs={{0,1},{1,0},{2,3},{3,2},{4,5},{5,4},{6,7},{7,6},{8,9},{9,8},{10,11... | collective-permute-start | bytes 983048 | tf_op jit(solution)/shard_map/ppermute | solution.py:506
  3.6 12.8 %collective-permute-start.1 = (f32[664,128]{1,0:T(8,128)S(1)}, f32[664,128]{1,0:T(8,128)S(1)}, u32[]{:S(2)}, u32[]{:S(2)}) collective-permute-start(f32[664,128]{1,0:T(8,128)S(1)} %get-tuple-element.43), channel_id=1, source_target_pairs={{1,9},{3,11},{5,13},{7,15},{9,17},{11,19},{13,21},{15,23},{17,25},... | collective-permute-start | bytes 1019912 | tf_op jit(solution)/shard_map/ppermute | solution.py:506
  6.0 11.4 %collective-permute-start.2 = (f32[664,128]{1,0:T(8,128)S(1)}, f32[664,128]{1,0:T(8,128)S(1)}, u32[]{:S(2)}, u32[]{:S(2)}) collective-permute-start(f32[664,128]{1,0:T(8,128)S(1)} %get-tuple-element.44), channel_id=1, source_target_pairs={{1,17},{3,19},{5,21},{7,23},{9,25},{11,27},{13,29},{15,31},{17,1},... | collective-permute-start | bytes 1019912 | tf_op jit(solution)/shard_map/ppermute | solution.py:506
  8.4 8.9 %collective-permute-start.3 = (f32[664,128]{1,0:T(8,128)S(1)}, f32[664,128]{1,0:T(8,128)S(1)}, u32[]{:S(2)}, u32[]{:S(2)}) collective-permute-start(f32[664,128]{1,0:T(8,128)S(1)} %get-tuple-element.45), channel_id=1, source_target_pairs={{1,25},{3,27},{5,29},{7,31},{9,1},{11,3},{13,5},{15,7},{17,9},{19,... | collective-permute-start | bytes 1019912 | tf_op jit(solution)/shard_map/ppermute | solution.py:506
  9.1 7.3 %collective-permute-start.4 = (f32[88,128]{1,0:T(8,128)S(1)}, f32[88,128]{1,0:T(8,128)S(1)}, u32[]{:S(2)}, u32[]{:S(2)}) collective-permute-start(f32[88,128]{1,0:T(8,128)S(1)} %get-tuple-element.46), channel_id=1, source_target_pairs={{0,8},{1,9},{2,10},{3,11},{4,12},{5,13},{6,14},{7,15},{8,16},{9,17... | collective-permute-start | bytes 135176 | tf_op jit(solution)/shard_map/ppermute | solution.py:506
  10.7 6.7 %collective-permute-start.5 = (f32[88,128]{1,0:T(8,128)S(1)}, f32[88,128]{1,0:T(8,128)S(1)}, u32[]{:S(2)}, u32[]{:S(2)}) collective-permute-start(f32[88,128]{1,0:T(8,128)S(1)} %get-tuple-element.47), channel_id=1, source_target_pairs={{0,24},{1,25},{2,26},{3,27},{4,28},{5,29},{6,30},{7,31},{8,0},{9,1... | collective-permute-start | bytes 135176 | tf_op jit(solution)/shard_map/ppermute | solution.py:506
  12.1 5.3 %copy-start = (f32[10,1,8192]{2,1,0:T(1,128)S(1)}, f32[10,1,8192]{2,1,0:T(1,128)}, u32[]{:S(2)}) copy-start(f32[10,1,8192]{2,1,0:T(1,128)} %param.12) | copy-start | bytes 983044
  12.1 5.3 %copy-start.5 = (s32[8,1]{0,1:T(1,128)S(1)}, s32[8,1]{0,1:T(1,128)}, u32[]{:S(2)}) copy-start(s32[8,1]{0,1:T(1,128)} %param.17) | copy-start | bytes 100
  12.1 5.3 %copy-start.6 = (s32[8]{0:T(128)S(1)}, s32[8]{0:T(128)}, u32[]{:S(2)}) copy-start(s32[8]{0:T(128)} %rest_11_.1) | copy-start | bytes 100
  12.1 5.3 %copy-start.7 = (s32[8]{0:T(128)S(1)}, s32[8]{0:T(128)}, u32[]{:S(2)}) copy-start(s32[8]{0:T(128)} %rest_12_.1) | copy-start | bytes 100
  18.8 5.3 %collective-permute-start.12 = (f32[656,128]{1,0:T(8,128)S(1)}, f32[656,128]{1,0:T(8,128)S(1)}, u32[]{:S(2)}, u32[]{:S(2)}) collective-permute-start(f32[656,128]{1,0:T(8,128)S(1)} %get-tuple-element.64.tile_ref), channel_id=1, source_target_pairs={{3,1},{7,5},{11,9},{15,13},{19,17},{23,21},{27,25},{31,29}} | collective-permute-start | bytes 1007624 | tf_op jit(solution)/shard_map/ppermute | solution.py:506
  19.5 11.4 %collective-permute-start.6 = (f32[320,128]{1,0:T(8,128)S(1)}, f32[320,128]{1,0:T(8,128)S(1)}, u32[]{:S(2)}, u32[]{:S(2)}) collective-permute-start(f32[320,128]{1,0:T(8,128)S(1)} %get-tuple-element.55), channel_id=1, source_target_pairs={{1,9},{3,11},{5,13},{7,15},{9,17},{11,19},{13,21},{15,23},{17,25},... | collective-permute-start | bytes 491528 | tf_op jit(solution)/shard_map/ppermute | solution.py:506
  20.1 10.7 %collective-permute-start.7 = (f32[320,128]{1,0:T(8,128)S(1)}, f32[320,128]{1,0:T(8,128)S(1)}, u32[]{:S(2)}, u32[]{:S(2)}) collective-permute-start(f32[320,128]{1,0:T(8,128)S(1)} %get-tuple-element.56), channel_id=1, source_target_pairs={{1,17},{3,19},{5,21},{7,23},{9,25},{11,27},{13,29},{15,31},{17,1},... | collective-permute-start | bytes 491528 | tf_op jit(solution)/shard_map/ppermute | solution.py:506
  21.6 9.3 %collective-permute-start.8 = (f32[320,128]{1,0:T(8,128)S(1)}, f32[320,128]{1,0:T(8,128)S(1)}, u32[]{:S(2)}, u32[]{:S(2)}) collective-permute-start(f32[320,128]{1,0:T(8,128)S(1)} %get-tuple-element.57), channel_id=1, source_target_pairs={{1,25},{3,27},{5,29},{7,31},{9,1},{11,3},{13,5},{15,7},{17,9},{19,... | collective-permute-start | bytes 491528 | tf_op jit(solution)/shard_map/ppermute | solution.py:506
  24.1 16.2 %collective-permute-start.14 = (f32[656,128]{1,0:T(8,128)S(1)}, f32[656,128]{1,0:T(8,128)S(1)}, u32[]{:S(2)}, u32[]{:S(2)}) collective-permute-start(f32[656,128]{1,0:T(8,128)S(1)} %shard_map.106), channel_id=1, source_target_pairs={{5,0},{13,8},{21,16},{29,24}} | collective-permute-start | bytes 1007624 | tf_op jit(solution)/shard_map/ppermute | solution.py:506
  25.4 14.9 %collective-permute-start.13 = (f32[656,128]{1,0:T(8,128)S(1)}, f32[656,128]{1,0:T(8,128)S(1)}, u32[]{:S(2)}, u32[]{:S(2)}) collective-permute-start(f32[656,128]{1,0:T(8,128)S(1)} %shard_map.106), channel_id=1, source_target_pairs={{0,1},{1,0},{2,3},{3,2},{4,5},{5,4},{6,7},{7,6},{8,9},{9,8},{10,11... | collective-permute-start | bytes 1007624 | tf_op jit(solution)/shard_map/ppermute | solution.py:506
  30.9 3.7 %collective-permute-start.9 = (f32[640,128]{1,0:T(8,128)S(1)}, f32[640,128]{1,0:T(8,128)S(1)}, u32[]{:S(2)}, u32[]{:S(2)}) collective-permute-start(f32[640,128]{1,0:T(8,128)S(1)} %shard_map.103.x_ref), channel_id=1, source_target_pairs={{3,1},{7,5},{11,9},{15,13},{19,17},{23,21},{27,25},{31,29},{2,4},{... | collective-permute-start | bytes 983048 | tf_op jit(solution)/shard_map/ppermute | solution.py:506
  31.6 8.7 %collective-permute-start.10 = (f32[80,128]{1,0:T(8,128)S(1)}, f32[80,128]{1,0:T(8,128)S(1)}, u32[]{:S(2)}, u32[]{:S(2)}) collective-permute-start(f32[80,128]{1,0:T(8,128)S(1)} %get-tuple-element.61), channel_id=1, source_target_pairs={{0,8},{1,9},{2,10},{3,11},{4,12},{5,13},{6,14},{7,15},{8,16},{9,17... | collective-permute-start | bytes 122888 | tf_op jit(solution)/shard_map/ppermute | solution.py:506
  33.1 7.1 %collective-permute-start.11 = (f32[80,128]{1,0:T(8,128)S(1)}, f32[80,128]{1,0:T(8,128)S(1)}, u32[]{:S(2)}, u32[]{:S(2)}) collective-permute-start(f32[80,128]{1,0:T(8,128)S(1)} %get-tuple-element.62), channel_id=1, source_target_pairs={{0,24},{1,25},{2,26},{3,27},{4,28},{5,29},{6,30},{7,31},{8,0},{9,1... | collective-permute-start | bytes 122888 | tf_op jit(solution)/shard_map/ppermute | solution.py:506
  34.6 14.9 %collective-permute-start.16 = (f32[640,128]{1,0:T(8,128)S(1)}, f32[640,128]{1,0:T(8,128)S(1)}, u32[]{:S(2)}, u32[]{:S(2)}) collective-permute-start(f32[640,128]{1,0:T(8,128)S(1)} %shard_map.104.pair_ref), channel_id=1, source_target_pairs={{5,0},{13,8},{21,16},{29,24}} | collective-permute-start | bytes 983048 | tf_op jit(solution)/shard_map/ppermute | solution.py:506
  40.4 9.1 %collective-permute-start.15 = (f32[640,128]{1,0:T(8,128)S(1)}, f32[640,128]{1,0:T(8,128)S(1)}, u32[]{:S(2)}, u32[]{:S(2)}) collective-permute-start(f32[640,128]{1,0:T(8,128)S(1)} %get-tuple-element.72), channel_id=1, source_target_pairs={{0,1},{1,0},{2,3},{3,2},{4,5},{5,4},{6,7},{7,6},{8,9},{9,8},{10,11... | collective-permute-start | bytes 983048 | tf_op jit(solution)/shard_map/ppermute | solution.py:506

commit v6 on v5

--- a/solution.py
+++ b/solution.py
@@ -13,7 +13,7 @@
 CAX = 8
 HALF = 64
 AXES = ("az", "ax", "pl")
-NJ = 4
+NJ = 8
 EXT = 16
 LOG2E = 1.4426950408889634
 LIMIT = 16 * 1024 * 1024
@@ -70,27 +70,41 @@
         er_ref[pl.ds(v * CAX, CAX), :] = q_ref[v, pl.ds((n - 1) * CAX, CAX), :]
 
 
-def first_kernel(n_az, n_out, q_any, vel_any, col_any, slot_any, open_any, *outs):
+def first_kernel(n_az, n_out, q_any, vel_any, col_any, slot_any, open_any, mix_any, pre_any, act_any, heat_any, *outs):
     out_refs, rest = outs[:n_out], outs[n_out:]
-    q_ref, vel_ref, s_ref, own_ref, er_ref, el_ref, col_ref, slot_ref, open_ref, sems = rest
-    pairs = [(vel_any, vel_ref), (col_any, col_ref), (slot_any, slot_ref), (open_any, open_ref)]
+    (q_ref, vel_ref, s_ref, own_ref, er_ref, el_ref, a_ref, power_ref,
+     col_ref, slot_ref, open_ref, mix_ref, pre_ref, act_ref, heat_ref, sems) = rest
+    pairs = [(mix_any, mix_ref), (pre_any, pre_ref), (act_any, act_ref), (heat_any, heat_ref),
+             (col_any, col_ref), (slot_any, slot_ref), (open_any, open_ref), (vel_any, vel_ref)]
+    small = len(pairs) - 1
     pairs += [(q_any.at[pl.ds(v, 2)], q_ref.at[pl.ds(v, 2)]) for v in range(0, NV, 2)]
     copies = [pltpu.make_async_copy(x, y, sems.at[k]) for k, (x, y) in enumerate(pairs)]
-    for copy in copies:
+    for copy in copies[small:] + copies[:small]:
         copy.start()
-    for copy in copies:
-        copy.wait()
     az, _, plen = roles()
     n = q_ref.shape[1] // CAX
     rows = NV * n
+
+    @pl.when(plen == 1)
+    def _():
+        for ref in (own_ref,) + tuple(out_refs):
+            ref[pl.ds(0, rows + EXT), :] = jnp.zeros((rows + EXT, LANES), f32)
+
+    for copy in copies[:small]:
+        copy.wait()
+    mixing(a_ref, mix_ref, pre_ref, heat_ref)
+    for k in range(NS):
+        power_ref[pl.ds(k * CAX, CAX), :] = jnp.full((CAX, LANES), act_ref[k] * (-LOG2E), f32)
+    for copy in copies[small:]:
+        copy.wait()
     edges(q_ref, er_ref, el_ref)
     el_ref[pl.ds(NV * CAX, CAX), :] = vel_ref[0, pl.ds(0, CAX), :]
     er_ref[pl.ds(NV * CAX, CAX), :] = vel_ref[0, pl.ds((n - 1) * CAX, CAX), :]
-    for v in range(NV):
-        s_ref[pl.ds(v * n, n), :] = q_ref[v, pl.ds(0, n, stride=CAX), :]
 
     @pl.when(plen == 0)
     def _():
+        for v in range(NV):
+            s_ref[pl.ds(v * n, n), :] = q_ref[v, pl.ds(0, n, stride=CAX), :]
         axial_rows(q_ref, vel_ref, out_refs[:1], out_refs[1:2])
 
     @pl.when(plen == 1)
@@ -98,16 +112,16 @@
         sub = lax.broadcasted_iota(jnp.int32, (CAX, LANES), 0)
         left = lax.broadcasted_iota(jnp.int32, (1, LANES), 1) < HALF
         blocks = n // CAX
-        for shift, ref in enumerate((own_ref,) + tuple(out_refs)):
-            ref[pl.ds(0, rows + EXT), :] = jnp.zeros((rows + EXT, LANES), f32)
-            table = jnp.full((CAX, LANES), -1.0, f32)
-            used = jnp.int32(0)
-            for b in range(blocks):
-                tile, opened = slot_ref[b], open_ref[b] != 0
-                ahead = (col_ref[b] - az - shift + 2 * n_az) % n_az
-                here = jnp.logical_and(ahead == 0, opened)
-                table = jnp.where(sub == jnp.where(here, used, CAX), tile.astype(f32), table)
-                used = used + here.astype(jnp.int32)
+        refs = (own_ref,) + tuple(out_refs)
+        tables = [jnp.full((CAX, LANES), -1.0, f32)] * n_az
+        used = [jnp.int32(0)] * n_az
+        for b in range(blocks):
+            tile, opened = slot_ref[b], open_ref[b] != 0
+            ahead = (col_ref[b] - az + n_az) % n_az
+            for shift, ref in enumerate(refs):
+                here = jnp.logical_and(ahead == shift, opened)
+                tables[shift] = jnp.where(sub == jnp.where(here, used[shift], CAX), tile.astype(f32), tables[shift])
+                used[shift] = used[shift] + here.astype(jnp.int32)
 
                 @pl.when(here)
                 def _(ref=ref, b=b, tile=tile):
@@ -115,33 +129,21 @@
                         at = pl.ds(pl.multiple_of(v * n + tile * CAX, CAX), CAX)
                         ref[at, :] += block(q_ref, v, b)
 
-                @pl.when(jnp.logical_and(opened, jnp.logical_and(ahead == 1, tile == 0)))
-                def _(ref=ref, b=b):
-                    for v in range(NV):
-                        cell = q_ref[v, pl.ds(CAX * CAX * b + CAX - 1, 1), :]
-                        ref[pl.ds(rows + v, 1), :] += jnp.where(left, cell, 0.0)
-
-                @pl.when(jnp.logical_and(opened, jnp.logical_and(ahead == n_az - 1, tile == blocks - 1)))
-                def _(ref=ref, b=b):
-                    for v in range(NV):
-                        cell = q_ref[v, pl.ds(CAX * CAX * (b + 1) - 1, 1), :]
-                        ref[pl.ds(rows + v, 1), :] += jnp.where(left, 0.0, cell)
-
-            if shift > 0:
-                ref[pl.ds(rows + EXT, CAX), :] = table
-
-
-def source(state, mix_ref, pre_ref, act_ref, heat_ref):
-    inv = 1.0 / jnp.maximum(state[NS], 0.5)
-    rates = [pre_ref[k] * jnp.exp(-act_ref[k] * inv) * jnp.maximum(state[k], 0.0) for k in range(NS)]
-    out = []
-    for v in range(NV):
-        acc = None
-        for k in range(NS):
-            term = (mix_ref[v, k] if v < NS else heat_ref[k]) * rates[k]
-            acc = term if acc is None else acc + term
-        out.append(0.2 * acc)
-    return out
+            def beside(end, step, row, keep_left, b=b, tile=tile, opened=opened, ahead=ahead):
+                @pl.when(jnp.logical_and(opened, tile == end))
+                def _():
+                    for shift, ref in enumerate(refs):
+                        @pl.when(ahead == (shift + step) % n_az)
+                        def _(ref=ref):
+                            for v in range(NV):
+                                cell = q_ref[v, pl.ds(row, 1), :]
+                                cell = jnp.where(left, cell, 0.0) if keep_left else jnp.where(left, 0.0, cell)
+                                ref[pl.ds(rows + v, 1), :] += cell
+
+            beside(0, 1, CAX * CAX * b + CAX - 1, True)
+            beside(blocks - 1, n_az - 1, CAX * CAX * (b + 1) - 1, False)
+        for ref, table in zip(out_refs, tables[1:]):
+            ref[pl.ds(rows + EXT, CAX), :] = table
 
 
 def fill_ghosts(state_ref, lo_ref, hi_ref, ra_refs, rb_ref, high_ref, supply_ref, n_ax):
@@ -200,7 +202,7 @@
     dst_ref[v, pl.ds((n - 1) * CAX, CAX), :] += jnp.where(left, 0.0, ar * tail)
 
 
-def mixing(a_ref, scale, mix_ref, pre_ref, heat_ref):
+def mixing(a_ref, mix_ref, pre_ref, heat_ref):
     width = NV * CAX
     col = lax.broadcasted_iota(jnp.int32, (CAX, 3 * width), 1)
     row = lax.broadcasted_iota(jnp.int32, (CAX, 3 * width), 0)
@@ -209,21 +211,31 @@
     for v in range(NV):
         block = jnp.zeros((CAX, 3 * width), f32)
         for k in range(NS):
-            value = (0.2 * scale) * pre_ref[k] * (mix_ref[v, k] if v < NS else heat_ref[k])
+            value = 0.2 * pre_ref[k] * (mix_ref[v, k] if v < NS else heat_ref[k])
             block = jnp.where(species == k, value, block)
         block = jnp.where(lane == row, block, 0.0)
         high = block.astype(jnp.bfloat16).astype(f32)
         a_ref[pl.ds(v * CAX, CAX), :] = jnp.where(col // width == 1, block - high, high)
 
 
-def interior(q_ref, vel_ref, a_ref, scale, mix_ref, pre_ref, act_ref, heat_ref, finish):
+def reactions(states, a, power_ref):
+    rates = []
+    for state in states:
+        inv = 1.0 / jnp.maximum(state[NS], 0.5)
+        some = [jnp.exp2(power_ref[pl.ds(k * CAX, CAX), :] * inv) * jnp.maximum(state[k], 0.0) for k in range(NS)]
+        rates.append(jnp.concatenate(some + [jnp.zeros((CAX, LANES), f32)], axis=0))
+    rate = jnp.concatenate(rates, axis=1)
+    high = rate.astype(jnp.bfloat16)
+    low = (rate - high.astype(f32)).astype(jnp.bfloat16)
+    return jnp.dot(a, jnp.concatenate([high, high, low], axis=0), preferred_element_type=f32)
+
+
+def interior(q_ref, vel_ref, a_ref, power_ref, scale, finish):
     n = q_ref.shape[1] // CAX
     left = low_half()
     sub = lax.broadcasted_iota(jnp.int32, (CAX, LANES), 0)
     bottom, top = sub == 0, sub == CAX - 1
-    mixing(a_ref, scale, mix_ref, pre_ref, heat_ref)
-    a = a_ref[...].astype(jnp.bfloat16)
-    power = [act_ref[k] * (-LOG2E) for k in range(NS)]
+    a = (scale * a_ref[...]).astype(jnp.bfloat16)
     c = 0.1 * scale
 
     def reg(ref, v, j):
@@ -240,15 +252,7 @@
 
     def body(step, carry):
         j0 = step * NJ
-        rates = []
-        for d in range(NJ):
-            inv = 1.0 / jnp.maximum(reg(q_ref, NS, j0 + d), 0.5)
-            some = [jnp.exp2(power[k] * inv) * jnp.maximum(reg(q_ref, k, j0 + d), 0.0) for k in range(NS)]
-            rates.append(jnp.concatenate(some + [jnp.zeros((CAX, LANES), f32)], axis=0))
-        rate = jnp.concatenate(rates, axis=1)
-        high = rate.astype(jnp.bfloat16)
-        low = (rate - high.astype(f32)).astype(jnp.bfloat16)
-        src = jnp.dot(a, jnp.concatenate([high, high, low], axis=0), preferred_element_type=f32)
+        src = reactions([[reg(q_ref, v, j0 + d) for v in range(NV)] for d in range(NJ)], a, power_ref)
         _, u_left, u_right = column(vel_ref, 0, j0)
         w = [reg(vel_ref, 1, j0 + d) for d in range(NJ)]
         al = [c + c * x for x in u_left]
@@ -266,26 +270,31 @@
     lax.fori_loop(0, n // NJ, body, 0)
 
 
-def inside_one_kernel(q_ref, vel_ref, mix_ref, pre_ref, act_ref, heat_ref, out_ref, a_ref):
+def inside_one_kernel(q_ref, vel_ref, a_ref, power_ref, out_ref):
     def finish(j, v, new):
         out_ref[v, pl.ds(pl.multiple_of(j * CAX, CAX), CAX), :] = new
 
-    interior(q_ref, vel_ref, a_ref, 1.0, mix_ref, pre_ref, act_ref, heat_ref, finish)
-
-
-def inside_two_kernel(q_ref, q1_ref, vel_ref, mix_ref, pre_ref, act_ref, heat_ref, out_ref, a_ref):
+    interior(q_ref, vel_ref, a_ref, power_ref, 1.0, finish)
+
+
+def inside_two_kernel(q_ref, q1_ref, vel_ref, a_ref, power_ref, out_ref):
     def finish(j, v, new):
         at = pl.ds(pl.multiple_of(j * CAX, CAX), CAX)
         out_ref[v, at, :] = 0.5 * q_ref[v, at, :] + new
 
-    interior(q1_ref, vel_ref, a_ref, 0.5, mix_ref, pre_ref, act_ref, heat_ref, finish)
+    interior(q1_ref, vel_ref, a_ref, power_ref, 0.5, finish)
 
 
 def border_one_kernel(n_az, n_ax, n_out, cap, s_in_ref, *rest):
     got, rest = rest[:n_out], rest[n_out:]
-    hl_ref, hr_ref, part_ref, q_ref, vel_ref, supply_ref, own_in_ref, col_ref, slot_ref, open_ref = rest[:10]
+    hl_ref, hr_ref, part_ref, q_ref, vel_ref, supply_ref, own_in_ref, col_any, slot_any, open_any = rest[:10]
     out_refs, rest = rest[10:10 + n_out], rest[10 + n_out:]
-    q1_ref, tile_ref, s_ref, z_ref, own_ref, er_ref, el_ref, lo_ref, hi_ref = rest
+    (q1_ref, tile_ref, s_ref, z_ref, own_ref, er_ref, el_ref, lo_ref, hi_ref,
+     col_ref, slot_ref, open_ref, sems) = rest
+    pairs = [(col_any, col_ref), (slot_any, slot_ref), (open_any, open_ref)]
+    copies = [pltpu.make_async_copy(x, y, sems.at[k]) for k, (x, y) in enumerate(pairs)]
+    for copy in copies:
+        copy.start()
     az, _, plen = roles()
     n = q_ref.shape[1] // CAX
     rows = NV * n
@@ -295,6 +304,8 @@
         add_border(v, q1_ref, 0.1, lo_ref, hi_ref, hl_ref, hr_ref,
                    hl_ref.at[pl.ds(NV * CAX, CAX)], hr_ref.at[pl.ds(NV * CAX, CAX)])
     edges(q1_ref, er_ref, el_ref)
+    for copy in copies:
+        copy.wait()
 
     @pl.when(plen == 0)
     def _():
@@ -395,7 +406,7 @@
 def border_two_kernel(n_ax, n_z, part_ref, q_ref, q1_ref, vel_ref, core_ref, supply_ref, step_ref, dq_ref, hl_ref, hr_ref,
                       hl0_ref, hr0_ref, *rest):
     ra_refs, rest = rest[:n_z], rest[n_z:]
-    mix_ref, pre_ref, act_ref, heat_ref, out_any, keep_ref, out_ref, lo_ref, hi_ref, sems = rest
+    a_ref, power_ref, out_any, keep_ref, out_ref, lo_ref, hi_ref, sems = rest
     n = out_ref.shape[1] // CAX
     rows = NV * n
     _, ax, plen = roles()
@@ -420,12 +431,15 @@
         w_next = vel_ref[1, pl.ds(1, n, stride=CAX), :]
         u_left, u_right = neighbours(u, ul_ref[pl.ds(0, 1), :], ur_ref[pl.ds(0, 1), :])
         state = [q1_ref[v, pl.ds(0, n, stride=CAX), :] + dq_ref[pl.ds(v * n, n), :] for v in range(NV)]
-        src = source(state, mix_ref, pre_ref, act_ref, heat_ref)
+        parts = [[x[d * CAX:(d + 1) * CAX] for x in state] for d in range(n // CAX)]
+        src = reactions(parts, a_ref[...].astype(jnp.bfloat16), power_ref)
         for v in range(NV):
             beside = dq_ref[pl.ds(rows + v, 1), :]
             q_left, q_right = neighbours(state[v], hl_ref[pl.ds(v * CAX, 1), :] + beside, hr_ref[pl.ds(v * CAX, 1), :] + beside)
             above = (1.0 - w_next) * q1_ref[v, pl.ds(1, n, stride=CAX), :]
-            new = 0.6 * state[v] + 0.1 * ((1.0 + u_left) * q_left + (1.0 - u_right) * q_right + above) + src[v]
+            mixed = src[v * CAX:(v + 1) * CAX]
+            mixed = jnp.concatenate([mixed[:, d * LANES:(d + 1) * LANES] for d in range(n // CAX)], axis=0)
+            new = 0.6 * state[v] + 0.1 * ((1.0 + u_left) * q_left + (1.0 - u_right) * q_right + above) + mixed
             keep_ref[pl.ds(v * n, n), :] = 0.5 * q_ref[v, pl.ds(0, n, stride=CAX), :] + 0.5 * new
 
     copies = []
@@ -539,25 +553,27 @@
     work = pl.CostEstimate(flops=300 * q.shape[1] * LANES, transcendentals=20 * q.shape[1] * LANES,
                            bytes_accessed=12_000_000)
 
-    raw = tuple(pltpu.with_memory_space_constraint(x, pltpu.HBM) for x in (q, vel, col, slot, opened))
+    raw = tuple(pltpu.with_memory_space_constraint(x, pltpu.HBM) for x in (q, vel, col, slot, opened) + react)
     wide, edge0 = shape(rows + EXT, LANES), shape((NV + 1) * CAX, LANES)
-    got = call(functools.partial(first_kernel, n_az, n_out), raw, "hhhhh",
-               [shape(rows + EXT + CAX, LANES)] * n_out + [whole, shape(*vel.shape), row, wide, edge0, edge0],
-               [pltpu.SMEM(col.shape, jnp.int32)] * 3 + [pltpu.SemaphoreType.DMA((4 + NV // 2,))])
-    outs, (qv, velv, s0, own0, er, el) = got[:n_out], got[n_out:]
+    got = call(functools.partial(first_kernel, n_az, n_out), raw, "h" * 9,
+               [shape(rows + EXT + CAX, LANES)] * n_out + [whole, shape(*vel.shape), row, wide, edge0, edge0,
+                                                         shape(NV * CAX, 3 * NV * CAX), shape(NS * CAX, LANES)],
+               [pltpu.SMEM(col.shape, jnp.int32)] * 3 + [pltpu.SMEM(x.shape, f32) for x in react]
+               + [pltpu.SemaphoreType.DMA((8 + NV // 2,))])
+    outs, (qv, velv, s0, own0, er, el, matrix, power) = got[:n_out], got[n_out:]
     ra = [send(x, dense(k)) for k, x in enumerate(outs)]
     s0r = send(s0, swap)
     hl0 = send(er, ring(1))
     el, s0r = lax.optimization_barrier((el, s0r))
     hr0 = send(el, ring(-1))
-    matrix = pltpu.VMEM((NV * CAX, 3 * NV * CAX), f32)
-    part, = call(inside_one_kernel, (qv, velv) + react, "vvssss", [whole], [matrix], cost=work)
+    part, = call(inside_one_kernel, (qv, velv, matrix, power), "vvvv", [whole], cost=work)
 
     got = call(functools.partial(border_one_kernel, n_az, n_ax, n_out, cap),
                (s0r, *ra, hl0, hr0, part, qv, velv, sup, own0, col, slot, opened),
-               "v" * (n_out + 8) + "s" * 3,
+               "v" * (n_out + 11),
                [shape(cap * NV * CAX, LANES)] * n_out + [whole, wide, row, row, row, edge, edge],
-               [pltpu.VMEM((rows, LANES), f32)] * 2)
+               [pltpu.VMEM((rows, LANES), f32)] * 2 + [pltpu.SMEM(col.shape, jnp.int32)] * 3
+               + [pltpu.SemaphoreType.DMA((3,))])
     outs, (q1, tile0, s1, z1, own1, er, el) = got[:n_out], got[n_out:]
     down = [((i, j, 1), (i, j - 1, 1)) for i, j in every if j % 2 == 1]
     across = [((i, 2, 1), (i, 0, 0)) for i in range(n_az)]
@@ -565,6 +581,8 @@
     rb = [send(x, compact(k)) for k, x in enumerate(outs)]
     down0 = send(tile0, down)
 
+    part, = call(inside_two_kernel, (qv, q1, velv, matrix, power), "vvvvv", [whole], cost=work)
+    part, own1, s1 = lax.optimization_barrier((part, own1, s1))
     step, = call(functools.partial(tile_kernel, n_out, cap), (own1, z1, *rb, *ra), "v" * (2 + 2 * n_out), [row])
     step_in = send(step, down + inner)
     er, el, step = lax.optimization_barrier((er, el, step))
@@ -574,15 +592,13 @@
     core_in = send(core, swap)
     pair1, = call(add_kernel, (step, step_in), "vv", [row])
     far1 = send(pair1, across)
-    q1, pair1 = lax.optimization_barrier((q1, pair1))
-    part, = call(inside_two_kernel, (qv, q1, velv) + react, "vvvssss", [whole], [matrix], cost=work)
-    part, pair1, hl1, hr1 = lax.optimization_barrier((part, pair1, hl1, hr1))
+    pair1, hl1, hr1 = lax.optimization_barrier((pair1, hl1, hr1))
 
     dq, core2 = call(inlet_kernel, (pair1, far0, core_in), "vvv", [wide, row])
     core2_in = send(core2, swap)
     out, keep = call(functools.partial(border_two_kernel, n_ax, pieces),
-                     (part, qv, q1, velv, core_in, sup, step_in, dq, hl1, hr1, hl0, hr0, *rb[:pieces]) + react,
-                     "v" * (12 + pieces) + "s" * 4, [whole, row],
+                     (part, qv, q1, velv, core_in, sup, step_in, dq, hl1, hr1, hl0, hr0, *rb[:pieces], matrix, power),
+                     "v" * (14 + pieces), [whole, row],
                      [pltpu.VMEM(q.shape, f32)] + [pltpu.VMEM((rows, LANES), f32)] * 2 + [pltpu.SemaphoreType.DMA((NV,))],
                      cost=work, to="hv")
     out, = call(last_kernel, (out.reshape(NV, n, CAX, LANES), keep, core2_in, far1), "hvvv", [shape(NV, n, CAX, LANES)],

time: 50.6 us -> 47.8 us (0.945)
  waiting for transfers between devices: 0.99 us -> 8.97 us
  starting transfers between devices: 32.8 us -> 26.7 us
  Pallas kernels: 16.4 us -> 11.7 us
    ppermute x17, waiting for transfers between devices: 0.99 us -> 8.97 us  [send(): return lax.ppermute(x, AXES, [(number(*a), number(*b)) for a, b in route])]
    ppermute x17, starting transfers between devices: 32.8 us -> 26.7 us  [send(): return lax.ppermute(x, AXES, [(number(*a), number(*b)) for a, b in route])]
    pallas_call x10, Pallas kernels: 16.4 us -> 11.7 us  [call(): pl.pallas_call(kernel, in_specs=[pl.BlockSpec(memory_space=SPACES[k]) for...]
  transfers between devices with their start and end apart: 17 -> 17, of which waited for: 1 -> 6; matrix products, arithmetic and copies ran while one was open for 0% -> 0% of each run, Pallas kernels for 23% -> 16%
where the time goes in v6:
time: 47.8 us; the launch traced here: 47.6 us
  starting transfers between devices  26.7 us (56%)
  Pallas kernels  11.7 us (24%)
  waiting for transfers between devices  8.97 us (19%)
    ppermute x17, starting transfers between devices, send(): return lax.ppermute(x, AXES, [(number(*a), number(*b)) for a, b in route])  26.7 us
    pallas_call x10, Pallas kernels, call(): pl.pallas_call(kernel, in_specs=[pl.BlockSpec(memory_space=SPACES[k]) for...  11.7 us
    ppermute x17, waiting for transfers between devices, send(): return lax.ppermute(x, AXES, [(number(*a), number(*b)) for a, b in route])  8.97 us
  transfers between devices with their start and end apart: 17, of which 6 were waited for; matrix products, arithmetic and copies ran while one was open for 0% of the time, Pallas kernels for 16%

profile of v6, /device:TPU:0, one launch (start us, length us, event | category | flops | bytes accessed | tf_op | source)
XLA Modules:
  0.0 47.6 jit_solution(9225527536161771352)
XLA Ops:
  0.0 2.2 %shard_map.100 = (f32[664,128]{1,0:T(8,128)S(1)}, f32[664,128]{1,0:T(8,128)S(1)}, f32[664,128]{1,0:T(8,128)S(1)}, f32[10,512,128]{2,1,0:T(8,128)S(1)}, f32[2,512...) custom-call(f32[10,512,128]{2,1,0:T(8,128)} %bitcast.20, ...), custom_call_target="tpu_custom_call" | custom-call | tf_op jit(solution)/shard_map/pallas_call | solution.py:493
  2.3 0.7 %collective-permute-start = (f32[640,128]{1,0:T(8,128)S(1)}, f32[640,128]{1,0:T(8,128)S(1)}, u32[]{:S(2)}, u32[]{:S(2)}) collective-permute-start(f32[640,128]{1,0:T(8,128)S(1)} %get-tuple-element.43), channel_id=1, source_target_pairs={{0,1},{1,0},{2,3},{3,2},{4,5},{5,4},{6,7},{7,6},{8,9},{9,8},{10,11... | collective-permute-start | bytes 983048 | tf_op jit(solution)/shard_map/ppermute | solution.py:520
  2.9 2.5 %collective-permute-start.1 = (f32[664,128]{1,0:T(8,128)S(1)}, f32[664,128]{1,0:T(8,128)S(1)}, u32[]{:S(2)}, u32[]{:S(2)}) collective-permute-start(f32[664,128]{1,0:T(8,128)S(1)} %get-tuple-element.45), channel_id=1, source_target_pairs={{1,9},{3,11},{5,13},{7,15},{9,17},{11,19},{13,21},{15,23},{17,25},... | collective-permute-start | bytes 1019912 | tf_op jit(solution)/shard_map/ppermute | solution.py:520
  5.4 2.5 %collective-permute-start.2 = (f32[664,128]{1,0:T(8,128)S(1)}, f32[664,128]{1,0:T(8,128)S(1)}, u32[]{:S(2)}, u32[]{:S(2)}) collective-permute-start(f32[664,128]{1,0:T(8,128)S(1)} %get-tuple-element.46), channel_id=1, source_target_pairs={{1,17},{3,19},{5,21},{7,23},{9,25},{11,27},{13,29},{15,31},{17,1},... | collective-permute-start | bytes 1019912 | tf_op jit(solution)/shard_map/ppermute | solution.py:520
  7.9 0.7 %collective-permute-start.3 = (f32[664,128]{1,0:T(8,128)S(1)}, f32[664,128]{1,0:T(8,128)S(1)}, u32[]{:S(2)}, u32[]{:S(2)}) collective-permute-start(f32[664,128]{1,0:T(8,128)S(1)} %get-tuple-element.47), channel_id=1, source_target_pairs={{1,25},{3,27},{5,29},{7,31},{9,1},{11,3},{13,5},{15,7},{17,9},{19,... | collective-permute-start | bytes 1019912 | tf_op jit(solution)/shard_map/ppermute | solution.py:520
  8.6 1.5 %collective-permute-start.4 = (f32[88,128]{1,0:T(8,128)S(1)}, f32[88,128]{1,0:T(8,128)S(1)}, u32[]{:S(2)}, u32[]{:S(2)}) collective-permute-start(f32[88,128]{1,0:T(8,128)S(1)} %get-tuple-element.48), channel_id=1, source_target_pairs={{0,8},{1,9},{2,10},{3,11},{4,12},{5,13},{6,14},{7,15},{8,16},{9,17... | collective-permute-start | bytes 135176 | tf_op jit(solution)/shard_map/ppermute | solution.py:520
  10.1 0.0 collective-permute-done.s_in_ref
  10.1 1.4 %collective-permute-start.5 = (f32[88,128]{1,0:T(8,128)S(1)}, f32[88,128]{1,0:T(8,128)S(1)}, u32[]{:S(2)}, u32[]{:S(2)}) collective-permute-start(f32[88,128]{1,0:T(8,128)S(1)} %get-tuple-element.49), channel_id=1, source_target_pairs={{0,24},{1,25},{2,26},{3,27},{4,28},{5,29},{6,30},{7,31},{8,0},{9,1... | collective-permute-start | bytes 135176 | tf_op jit(solution)/shard_map/ppermute | solution.py:520
  11.6 2.5 %shard_map.101.rest_5_ = f32[10,512,128]{2,1,0:T(8,128)S(1)} custom-call(f32[10,512,128]{2,1,0:T(8,128)S(1)} %get-tuple-element.41.q_ref.rest_6_, f32[2,512,128]{2,1,0:T(8,128)S(1)} %get-tuple-element.50.vel_ref.rest_7_, f32[80,240]{1,0:T(8,128)S(1)} %get-tuple-element.51.a_ref.rest_2_, f32[72,128]{1,0:T(8,128)S(1)} %get-tuple-element.52.power_ref.rest_3_), custom_call_target="tpu_custom_call" | custom-call | flops 19660800 | bytes 12000000 | tf_op jit(solution)/shard_map/pallas_call | solution.py:493
  14.0 0.1 collective-permute-done.4.rest_3_.hl0_ref
  14.1 2.7 %collective-permute-done.2.rest_1_.rest_4_ = f32[664,128]{1,0:T(8,128)S(1)} collective-permute-done((f32[664,128]{1,0:T(8,128)S(1)}, f32[664,128]{1,0:T(8,128)S(1)}, u32[]{:S(2)}, u32[]{:S(2)}) %collective-permute-start.2) | collective-permute-done | bytes 340000 | tf_op jit(solution)/shard_map/ppermute | solution.py:520
  16.9 0.9 %shard_map.102 = (f32[320,128]{1,0:T(8,128)S(1)}, f32[320,128]{1,0:T(8,128)S(1)}, f32[320,128]{1,0:T(8,128)S(1)}, f32[10,512,128]{2,1,0:T(8,128)S(1)}, f32[656,1...) custom-call(f32[640,128]{1,0:T(8,128)S(1)} %collective-permute-done., ...), custom_call_target="tpu_custom_call" | custom-call | tf_op jit(solution)/shard_map/pallas_call | solution.py:493
  17.7 0.7 %collective-permute-start.6 = (f32[656,128]{1,0:T(8,128)S(1)}, f32[656,128]{1,0:T(8,128)S(1)}, u32[]{:S(2)}, u32[]{:S(2)}) collective-permute-start(f32[656,128]{1,0:T(8,128)S(1)} %get-tuple-element.58.tile_ref), channel_id=1, source_target_pairs={{3,1},{7,5},{11,9},{15,13},{19,17},{23,21},{27,25},{31,29}} | collective-permute-start | bytes 1007624 | tf_op jit(solution)/shard_map/ppermute | solution.py:520
  18.4 0.6 %collective-permute-start.8 = (f32[320,128]{1,0:T(8,128)S(1)}, f32[320,128]{1,0:T(8,128)S(1)}, u32[]{:S(2)}, u32[]{:S(2)}) collective-permute-start(f32[320,128]{1,0:T(8,128)S(1)} %get-tuple-element.62), channel_id=1, source_target_pairs={{1,9},{3,11},{5,13},{7,15},{9,17},{11,19},{13,21},{15,23},{17,25},... | collective-permute-start | bytes 491528 | tf_op jit(solution)/shard_map/ppermute | solution.py:520
  19.1 1.4 %collective-permute-start.9 = (f32[320,128]{1,0:T(8,128)S(1)}, f32[320,128]{1,0:T(8,128)S(1)}, u32[]{:S(2)}, u32[]{:S(2)}) collective-permute-start(f32[320,128]{1,0:T(8,128)S(1)} %get-tuple-element.63), channel_id=1, source_target_pairs={{1,17},{3,19},{5,21},{7,23},{9,25},{11,27},{13,29},{15,31},{17,1},... | collective-permute-start | bytes 491528 | tf_op jit(solution)/shard_map/ppermute | solution.py:520
  20.5 2.4 %collective-permute-start.10 = (f32[320,128]{1,0:T(8,128)S(1)}, f32[320,128]{1,0:T(8,128)S(1)}, u32[]{:S(2)}, u32[]{:S(2)}) collective-permute-start(f32[320,128]{1,0:T(8,128)S(1)} %get-tuple-element.64), channel_id=1, source_target_pairs={{1,25},{3,27},{5,29},{7,31},{9,1},{11,3},{13,5},{15,7},{17,9},{19,... | collective-permute-start | bytes 491528 | tf_op jit(solution)/shard_map/ppermute | solution.py:520
  23.0 2.8 %shard_map.103.part_ref = f32[10,512,128]{2,1,0:T(8,128)S(1)} custom-call(f32[10,512,128]{2,1,0:T(8,128)S(1)} %get-tuple-element.41.q_ref.rest_6_, f32[10,512,128]{2,1,0:T(8,128)S(1)} %get-tuple-element.54.q1_ref, f32[2,512,128]{2,1,0:T(8,128)S(1)} %get-tuple-element.50.vel_ref.rest_7_, f32[80,240]{1,0:T(8,128)S(1)} %get-tuple-element.51.a_ref.rest_2_, ...), custom_call_target="tpu_custom_call" | custom-call | flops 19660800 | bytes 12000000 | tf_op jit(solution)/shard_map/pallas_call | solution.py:493
  25.8 0.0 collective-permute-done.6.down_ref
  25.8 1.3 %collective-permute-start.14 = (f32[656,128]{1,0:T(8,128)S(1)}, f32[656,128]{1,0:T(8,128)S(1)}, u32[]{:S(2)}, u32[]{:S(2)}) collective-permute-start(f32[656,128]{1,0:T(8,128)S(1)} %shard_map.104), channel_id=1, source_target_pairs={{5,0},{13,8},{21,16},{29,24}} | collective-permute-start | bytes 1007624 | tf_op jit(solution)/shard_map/ppermute | solution.py:520
  27.1 2.7 %collective-permute-start.7 = (f32[656,128]{1,0:T(8,128)S(1)}, f32[656,128]{1,0:T(8,128)S(1)}, u32[]{:S(2)}, u32[]{:S(2)}) collective-permute-start(f32[656,128]{1,0:T(8,128)S(1)} %shard_map.104), channel_id=1, source_target_pairs={{0,1},{1,0},{2,3},{3,2},{4,5},{5,4},{6,7},{7,6},{8,9},{9,8},{10,11... | collective-permute-start | bytes 1007624 | tf_op jit(solution)/shard_map/ppermute | solution.py:520
  29.8 0.7 %collective-permute-start.11 = (f32[640,128]{1,0:T(8,128)S(1)}, f32[640,128]{1,0:T(8,128)S(1)}, u32[]{:S(2)}, u32[]{:S(2)}) collective-permute-start(f32[640,128]{1,0:T(8,128)S(1)} %shard_map.105.x_ref), channel_id=1, source_target_pairs={{3,1},{7,5},{11,9},{15,13},{19,17},{23,21},{27,25},{31,29},{2,4},{... | collective-permute-start | bytes 983048 | tf_op jit(solution)/shard_map/ppermute | solution.py:520
  30.5 1.5 %collective-permute-start.12 = (f32[80,128]{1,0:T(8,128)S(1)}, f32[80,128]{1,0:T(8,128)S(1)}, u32[]{:S(2)}, u32[]{:S(2)}) collective-permute-start(f32[80,128]{1,0:T(8,128)S(1)} %get-tuple-element.68), channel_id=1, source_target_pairs={{0,8},{1,9},{2,10},{3,11},{4,12},{5,13},{6,14},{7,15},{8,16},{9,17... | collective-permute-start | bytes 122888 | tf_op jit(solution)/shard_map/ppermute | solution.py:520
  32.1 1.4 %collective-permute-start.13 = (f32[80,128]{1,0:T(8,128)S(1)}, f32[80,128]{1,0:T(8,128)S(1)}, u32[]{:S(2)}, u32[]{:S(2)}) collective-permute-start(f32[80,128]{1,0:T(8,128)S(1)} %get-tuple-element.69), channel_id=1, source_target_pairs={{0,24},{1,25},{2,26},{3,27},{4,28},{5,29},{6,30},{7,31},{8,0},{9,1... | collective-permute-start | bytes 122888 | tf_op jit(solution)/shard_map/ppermute | solution.py:520
  33.5 1.3 %collective-permute-start.16 = (f32[640,128]{1,0:T(8,128)S(1)}, f32[640,128]{1,0:T(8,128)S(1)}, u32[]{:S(2)}, u32[]{:S(2)}) collective-permute-start(f32[640,128]{1,0:T(8,128)S(1)} %shard_map.106.pair_ref), channel_id=1, source_target_pairs={{5,0},{13,8},{21,16},{29,24}} | collective-permute-start | bytes 983048 | tf_op jit(solution)/shard_map/ppermute | solution.py:520
  34.8 1.1 %collective-permute-done.12.hl_ref = f32[80,128]{1,0:T(8,128)S(1)} collective-permute-done((f32[80,128]{1,0:T(8,128)S(1)}, f32[80,128]{1,0:T(8,128)S(1)}, u32[]{:S(2)}, u32[]{:S(2)}) %collective-permute-start.12) | collective-permute-done | bytes 40992 | tf_op jit(solution)/shard_map/ppermute | solution.py:520
  35.9 1.0 %collective-permute-done.13.hr_ref = f32[80,128]{1,0:T(8,128)S(1)} collective-permute-done((f32[80,128]{1,0:T(8,128)S(1)}, f32[80,128]{1,0:T(8,128)S(1)}, u32[]{:S(2)}, u32[]{:S(2)}) %collective-permute-start.13) | collective-permute-done | bytes 40992 | tf_op jit(solution)/shard_map/ppermute | solution.py:520
  36.9 0.7 %collective-permute-done.14.far_ref = f32[656,128]{1,0:T(8,128)S(1)} collective-permute-done((f32[656,128]{1,0:T(8,128)S(1)}, f32[656,128]{1,0:T(8,128)S(1)}, u32[]{:S(2)}, u32[]{:S(2)}) %collective-permute-start.14) | collective-permute-done | bytes 335904 | tf_op jit(solution)/shard_map/ppermute | solution.py:520
  37.6 0.1 shard_map.107
  37.7 3.4 %collective-permute-start.15 = (f32[640,128]{1,0:T(8,128)S(1)}, f32[640,128]{1,0:T(8,128)S(1)}, u32[]{:S(2)}, u32[]{:S(2)}) collective-permute-start(f32[640,128]{1,0:T(8,128)S(1)} %get-tuple-element.76), channel_id=1, source_target_pairs={{0,1},{1,0},{2,3},{3,2},{4,5},{5,4},{6,7},{7,6},{8,9},{9,8},{10,11... | collective-permute-start | bytes 983048 | tf_op jit(solution)/shard_map/ppermute | solution.py:520
  41.0 2.2 %shard_map.108 = (f32[10,512,128]{2,1,0:T(8,128)}, f32[640,128]{1,0:T(8,128)S(1)}) custom-call(f32[10,512,128]{2,1,0:T(8,128)S(1)} %shard_map.103.part_ref, f32[10,512,128]{2,1,0:T(8,128)S(1)} %get-tuple-element.41.q_ref.rest_6_, f32[10,512,128]{2,1,0:T(8,128)S(1)} %get-tuple-element.54.q1_ref, f32[2,512,128]{2,1,0:T(8,128)S(1)} %get-tuple-element.50.vel_ref.rest_7_, ...), custom_call_target="tpu_custom_call" | custom-call | flops 19660800 | bytes 12000000 | tf_op jit(solution)/shard_map/pallas_call | solution.py:493
  43.3 3.4 %collective-permute-done.16.far_ref = f32[640,128]{1,0:T(8,128)S(1)} collective-permute-done((f32[640,128]{1,0:T(8,128)S(1)}, f32[640,128]{1,0:T(8,128)S(1)}, u32[]{:S(2)}, u32[]{:S(2)}) %collective-permute-start.16) | collective-permute-done | bytes 327712 | tf_op jit(solution)/shard_map/ppermute | solution.py:520
  46.7 0.9 %shard_map.109 = f32[10,64,8,128]{3,2,1,0:T(8,128)} custom-call(f32[10,64,8,128]{3,2,1,0:T(8,128)} %bitcast.21, f32[640,128]{1,0:T(8,128)S(1)} %get-tuple-element.75.keep_ref, f32[640,128]{1,0:T(8,128)S(1)} %collective-permute-done.15.core_ref, f32[640,128]{1,0:T(8,128)S(1)} %collective-permute-done.16.far_ref), custom_call_target="tpu_custom_call", output_to_operand_aliasing={{}: (0, {})} | custom-call | tf_op jit(solution)/shard_map/pallas_call | solution.py:493
  (20 shorter events, 0.1 us)
Async XLA Ops:
  2.3 7.9 %collective-permute-start = (f32[640,128]{1,0:T(8,128)S(1)}, f32[640,128]{1,0:T(8,128)S(1)}, u32[]{:S(2)}, u32[]{:S(2)}) collective-permute-start(f32[640,128]{1,0:T(8,128)S(1)} %get-tuple-element.43), channel_id=1, source_target_pairs={{0,1},{1,0},{2,3},{3,2},{4,5},{5,4},{6,7},{7,6},{8,9},{9,8},{10,11... | collective-permute-start | bytes 983048 | tf_op jit(solution)/shard_map/ppermute | solution.py:520
  2.9 11.2 %collective-permute-start.1 = (f32[664,128]{1,0:T(8,128)S(1)}, f32[664,128]{1,0:T(8,128)S(1)}, u32[]{:S(2)}, u32[]{:S(2)}) collective-permute-start(f32[664,128]{1,0:T(8,128)S(1)} %get-tuple-element.45), channel_id=1, source_target_pairs={{1,9},{3,11},{5,13},{7,15},{9,17},{11,19},{13,21},{15,23},{17,25},... | collective-permute-start | bytes 1019912 | tf_op jit(solution)/shard_map/ppermute | solution.py:520
  5.4 11.4 %collective-permute-start.2 = (f32[664,128]{1,0:T(8,128)S(1)}, f32[664,128]{1,0:T(8,128)S(1)}, u32[]{:S(2)}, u32[]{:S(2)}) collective-permute-start(f32[664,128]{1,0:T(8,128)S(1)} %get-tuple-element.46), channel_id=1, source_target_pairs={{1,17},{3,19},{5,21},{7,23},{9,25},{11,27},{13,29},{15,31},{17,1},... | collective-permute-start | bytes 1019912 | tf_op jit(solution)/shard_map/ppermute | solution.py:520
  7.9 8.9 %collective-permute-start.3 = (f32[664,128]{1,0:T(8,128)S(1)}, f32[664,128]{1,0:T(8,128)S(1)}, u32[]{:S(2)}, u32[]{:S(2)}) collective-permute-start(f32[664,128]{1,0:T(8,128)S(1)} %get-tuple-element.47), channel_id=1, source_target_pairs={{1,25},{3,27},{5,29},{7,31},{9,1},{11,3},{13,5},{15,7},{17,9},{19,... | collective-permute-start | bytes 1019912 | tf_op jit(solution)/shard_map/ppermute | solution.py:520
  8.6 5.5 %collective-permute-start.4 = (f32[88,128]{1,0:T(8,128)S(1)}, f32[88,128]{1,0:T(8,128)S(1)}, u32[]{:S(2)}, u32[]{:S(2)}) collective-permute-start(f32[88,128]{1,0:T(8,128)S(1)} %get-tuple-element.48), channel_id=1, source_target_pairs={{0,8},{1,9},{2,10},{3,11},{4,12},{5,13},{6,14},{7,15},{8,16},{9,17... | collective-permute-start | bytes 135176 | tf_op jit(solution)/shard_map/ppermute | solution.py:520
  10.1 6.7 %collective-permute-start.5 = (f32[88,128]{1,0:T(8,128)S(1)}, f32[88,128]{1,0:T(8,128)S(1)}, u32[]{:S(2)}, u32[]{:S(2)}) collective-permute-start(f32[88,128]{1,0:T(8,128)S(1)} %get-tuple-element.49), channel_id=1, source_target_pairs={{0,24},{1,25},{2,26},{3,27},{4,28},{5,29},{6,30},{7,31},{8,0},{9,1... | collective-permute-start | bytes 135176 | tf_op jit(solution)/shard_map/ppermute | solution.py:520
  11.5 5.3 %copy-start = (f32[10,1,8192]{2,1,0:T(1,128)S(1)}, f32[10,1,8192]{2,1,0:T(1,128)}, u32[]{:S(2)}) copy-start(f32[10,1,8192]{2,1,0:T(1,128)} %param.12) | copy-start | bytes 983044
  11.5 5.3 %copy-start.1 = (s32[8,1]{0,1:T(1,128)S(1)}, s32[8,1]{0,1:T(1,128)}, u32[]{:S(2)}) copy-start(s32[8,1]{0,1:T(1,128)} %param.17) | copy-start | bytes 100
  11.5 5.3 %copy-start.2 = (s32[8]{0:T(128)S(1)}, s32[8]{0:T(128)}, u32[]{:S(2)}) copy-start(s32[8]{0:T(128)} %rest_11_.1) | copy-start | bytes 100
  11.5 5.3 %copy-start.3 = (s32[8]{0:T(128)S(1)}, s32[8]{0:T(128)}, u32[]{:S(2)}) copy-start(s32[8]{0:T(128)} %rest_12_.1) | copy-start | bytes 100
  17.7 8.0 %collective-permute-start.6 = (f32[656,128]{1,0:T(8,128)S(1)}, f32[656,128]{1,0:T(8,128)S(1)}, u32[]{:S(2)}, u32[]{:S(2)}) collective-permute-start(f32[656,128]{1,0:T(8,128)S(1)} %get-tuple-element.58.tile_ref), channel_id=1, source_target_pairs={{3,1},{7,5},{11,9},{15,13},{19,17},{23,21},{27,25},{31,29}} | collective-permute-start | bytes 1007624 | tf_op jit(solution)/shard_map/ppermute | solution.py:520
  18.4 11.4 %collective-permute-start.8 = (f32[320,128]{1,0:T(8,128)S(1)}, f32[320,128]{1,0:T(8,128)S(1)}, u32[]{:S(2)}, u32[]{:S(2)}) collective-permute-start(f32[320,128]{1,0:T(8,128)S(1)} %get-tuple-element.62), channel_id=1, source_target_pairs={{1,9},{3,11},{5,13},{7,15},{9,17},{11,19},{13,21},{15,23},{17,25},... | collective-permute-start | bytes 491528 | tf_op jit(solution)/shard_map/ppermute | solution.py:520
  19.1 10.7 %collective-permute-start.9 = (f32[320,128]{1,0:T(8,128)S(1)}, f32[320,128]{1,0:T(8,128)S(1)}, u32[]{:S(2)}, u32[]{:S(2)}) collective-permute-start(f32[320,128]{1,0:T(8,128)S(1)} %get-tuple-element.63), channel_id=1, source_target_pairs={{1,17},{3,19},{5,21},{7,23},{9,25},{11,27},{13,29},{15,31},{17,1},... | collective-permute-start | bytes 491528 | tf_op jit(solution)/shard_map/ppermute | solution.py:520
  20.5 9.3 %collective-permute-start.10 = (f32[320,128]{1,0:T(8,128)S(1)}, f32[320,128]{1,0:T(8,128)S(1)}, u32[]{:S(2)}, u32[]{:S(2)}) collective-permute-start(f32[320,128]{1,0:T(8,128)S(1)} %get-tuple-element.64), channel_id=1, source_target_pairs={{1,25},{3,27},{5,29},{7,31},{9,1},{11,3},{13,5},{15,7},{17,9},{19,... | collective-permute-start | bytes 491528 | tf_op jit(solution)/shard_map/ppermute | solution.py:520
  25.8 11.7 %collective-permute-start.14 = (f32[656,128]{1,0:T(8,128)S(1)}, f32[656,128]{1,0:T(8,128)S(1)}, u32[]{:S(2)}, u32[]{:S(2)}) collective-permute-start(f32[656,128]{1,0:T(8,128)S(1)} %shard_map.104), channel_id=1, source_target_pairs={{5,0},{13,8},{21,16},{29,24}} | collective-permute-start | bytes 1007624 | tf_op jit(solution)/shard_map/ppermute | solution.py:520
  27.1 10.4 %collective-permute-start.7 = (f32[656,128]{1,0:T(8,128)S(1)}, f32[656,128]{1,0:T(8,128)S(1)}, u32[]{:S(2)}, u32[]{:S(2)}) collective-permute-start(f32[656,128]{1,0:T(8,128)S(1)} %shard_map.104), channel_id=1, source_target_pairs={{0,1},{1,0},{2,3},{3,2},{4,5},{5,4},{6,7},{7,6},{8,9},{9,8},{10,11... | collective-permute-start | bytes 1007624 | tf_op jit(solution)/shard_map/ppermute | solution.py:520
  29.8 3.7 %collective-permute-start.11 = (f32[640,128]{1,0:T(8,128)S(1)}, f32[640,128]{1,0:T(8,128)S(1)}, u32[]{:S(2)}, u32[]{:S(2)}) collective-permute-start(f32[640,128]{1,0:T(8,128)S(1)} %shard_map.105.x_ref), channel_id=1, source_target_pairs={{3,1},{7,5},{11,9},{15,13},{19,17},{23,21},{27,25},{31,29},{2,4},{... | collective-permute-start | bytes 983048 | tf_op jit(solution)/shard_map/ppermute | solution.py:520
  30.5 5.4 %collective-permute-start.12 = (f32[80,128]{1,0:T(8,128)S(1)}, f32[80,128]{1,0:T(8,128)S(1)}, u32[]{:S(2)}, u32[]{:S(2)}) collective-permute-start(f32[80,128]{1,0:T(8,128)S(1)} %get-tuple-element.68), channel_id=1, source_target_pairs={{0,8},{1,9},{2,10},{3,11},{4,12},{5,13},{6,14},{7,15},{8,16},{9,17... | collective-permute-start | bytes 122888 | tf_op jit(solution)/shard_map/ppermute | solution.py:520
  32.1 4.8 %collective-permute-start.13 = (f32[80,128]{1,0:T(8,128)S(1)}, f32[80,128]{1,0:T(8,128)S(1)}, u32[]{:S(2)}, u32[]{:S(2)}) collective-permute-start(f32[80,128]{1,0:T(8,128)S(1)} %get-tuple-element.69), channel_id=1, source_target_pairs={{0,24},{1,25},{2,26},{3,27},{4,28},{5,29},{6,30},{7,31},{8,0},{9,1... | collective-permute-start | bytes 122888 | tf_op jit(solution)/shard_map/ppermute | solution.py:520
  33.5 13.1 %collective-permute-start.16 = (f32[640,128]{1,0:T(8,128)S(1)}, f32[640,128]{1,0:T(8,128)S(1)}, u32[]{:S(2)}, u32[]{:S(2)}) collective-permute-start(f32[640,128]{1,0:T(8,128)S(1)} %shard_map.106.pair_ref), channel_id=1, source_target_pairs={{5,0},{13,8},{21,16},{29,24}} | collective-permute-start | bytes 983048 | tf_op jit(solution)/shard_map/ppermute | solution.py:520
  37.7 9.0 %collective-permute-start.15 = (f32[640,128]{1,0:T(8,128)S(1)}, f32[640,128]{1,0:T(8,128)S(1)}, u32[]{:S(2)}, u32[]{:S(2)}) collective-permute-start(f32[640,128]{1,0:T(8,128)S(1)} %get-tuple-element.76), channel_id=1, source_target_pairs={{0,1},{1,0},{2,3},{3,2},{4,5},{5,4},{6,7},{7,6},{8,9},{9,8},{10,11... | collective-permute-start | bytes 983048 | tf_op jit(solution)/shard_map/ppermute | solution.py:520

commit v7 on v6

--- a/solution.py
+++ b/solution.py
@@ -70,7 +70,7 @@
         er_ref[pl.ds(v * CAX, CAX), :] = q_ref[v, pl.ds((n - 1) * CAX, CAX), :]
 
 
-def first_kernel(n_az, n_out, q_any, vel_any, col_any, slot_any, open_any, mix_any, pre_any, act_any, heat_any, *outs):
+def first_kernel(n_az, n_out, pieces, q_any, vel_any, col_any, slot_any, open_any, mix_any, pre_any, act_any, heat_any, *outs):
     out_refs, rest = outs[:n_out], outs[n_out:]
     (q_ref, vel_ref, s_ref, own_ref, er_ref, el_ref, a_ref, power_ref,
      col_ref, slot_ref, open_ref, mix_ref, pre_ref, act_ref, heat_ref, sems) = rest
@@ -84,11 +84,15 @@
     az, _, plen = roles()
     n = q_ref.shape[1] // CAX
     rows = NV * n
+    refs = (own_ref,) + tuple(out_refs)
+    beside_at = [rows] + [ref.shape[0] - CAX - EXT for ref in out_refs]
 
     @pl.when(plen == 1)
     def _():
-        for ref in (own_ref,) + tuple(out_refs):
-            ref[pl.ds(0, rows + EXT), :] = jnp.zeros((rows + EXT, LANES), f32)
+        for ref in (own_ref, out_refs[0]):
+            ref[pl.ds(0, rows), :] = jnp.zeros((rows, LANES), f32)
+        for ref, at in zip(refs, beside_at):
+            ref[pl.ds(at, EXT), :] = jnp.zeros((EXT, LANES), f32)
 
     for copy in copies[:small]:
         copy.wait()
@@ -105,14 +109,13 @@
     def _():
         for v in range(NV):
             s_ref[pl.ds(v * n, n), :] = q_ref[v, pl.ds(0, n, stride=CAX), :]
-        axial_rows(q_ref, vel_ref, out_refs[:1], out_refs[1:2])
+        axial_rows(q_ref, vel_ref, out_refs[:1], out_refs[1:1 + pieces])
 
     @pl.when(plen == 1)
     def _():
         sub = lax.broadcasted_iota(jnp.int32, (CAX, LANES), 0)
         left = lax.broadcasted_iota(jnp.int32, (1, LANES), 1) < HALF
         blocks = n // CAX
-        refs = (own_ref,) + tuple(out_refs)
         tables = [jnp.full((CAX, LANES), -1.0, f32)] * n_az
         used = [jnp.int32(0)] * n_az
         for b in range(blocks):
@@ -121,41 +124,46 @@
             for shift, ref in enumerate(refs):
                 here = jnp.logical_and(ahead == shift, opened)
                 tables[shift] = jnp.where(sub == jnp.where(here, used[shift], CAX), tile.astype(f32), tables[shift])
+
+                @pl.when(here)
+                def _(ref=ref, b=b, tile=tile, shift=shift, slot=used[shift]):
+                    for v in range(NV):
+                        if shift < 2:
+                            at = pl.ds(pl.multiple_of(v * n + tile * CAX, CAX), CAX)
+                            ref[at, :] += block(q_ref, v, b)
+                        else:
+                            at = pl.ds(pl.multiple_of((slot * NV + v) * CAX, CAX), CAX)
+                            ref[at, :] = block(q_ref, v, b)
+
                 used[shift] = used[shift] + here.astype(jnp.int32)
-
-                @pl.when(here)
-                def _(ref=ref, b=b, tile=tile):
-                    for v in range(NV):
-                        at = pl.ds(pl.multiple_of(v * n + tile * CAX, CAX), CAX)
-                        ref[at, :] += block(q_ref, v, b)
 
             def beside(end, step, row, keep_left, b=b, tile=tile, opened=opened, ahead=ahead):
                 @pl.when(jnp.logical_and(opened, tile == end))
                 def _():
                     for shift, ref in enumerate(refs):
                         @pl.when(ahead == (shift + step) % n_az)
-                        def _(ref=ref):
+                        def _(ref=ref, at=beside_at[shift]):
                             for v in range(NV):
                                 cell = q_ref[v, pl.ds(row, 1), :]
                                 cell = jnp.where(left, cell, 0.0) if keep_left else jnp.where(left, 0.0, cell)
-                                ref[pl.ds(rows + v, 1), :] += cell
+                                ref[pl.ds(at + v, 1), :] += cell
 
             beside(0, 1, CAX * CAX * b + CAX - 1, True)
             beside(blocks - 1, n_az - 1, CAX * CAX * (b + 1) - 1, False)
         for ref, table in zip(out_refs, tables[1:]):
-            ref[pl.ds(rows + EXT, CAX), :] = table
-
-
-def fill_ghosts(state_ref, lo_ref, hi_ref, ra_refs, rb_ref, high_ref, supply_ref, n_ax):
+            ref[pl.ds(ref.shape[0] - CAX, CAX), :] = table
+
+
+def fill_ghosts(state_ref, lo_ref, hi_ref, ra_refs, rb_refs, high_ref, supply_ref, n_ax):
     _, ax, plen = roles()
     n = state_ref.shape[1] // CAX
     even = ax % 2 == 0
     odd = jnp.logical_not(even)
     cham = plen == 0
 
-    def put(ref):
-        size = ref.shape[0] // len(ra_refs)
-        for k, part in enumerate(ra_refs):
+    def put(ref, parts):
+        size = ref.shape[0] // len(parts)
+        for k, part in enumerate(parts):
             ref[pl.ds(k * size, size), :] = part[pl.ds(0, size), :]
 
     @pl.when(plen == 1)
@@ -165,11 +173,11 @@
 
     @pl.when(jnp.logical_and(cham, even))
     def _():
-        put(hi_ref)
+        put(hi_ref, ra_refs)
 
     @pl.when(jnp.logical_and(cham, odd))
     def _():
-        put(lo_ref)
+        put(lo_ref, ra_refs)
 
     @pl.when(jnp.logical_and(cham, ax == 0))
     def _():
@@ -177,11 +185,11 @@
 
     @pl.when(jnp.logical_and(cham, jnp.logical_and(even, ax > 0)))
     def _():
-        lo_ref[...] = rb_ref[pl.ds(0, lo_ref.shape[0]), :]
+        put(lo_ref, rb_refs)
 
     @pl.when(jnp.logical_and(cham, jnp.logical_and(odd, ax < n_ax - 1)))
     def _():
-        hi_ref[...] = rb_ref[pl.ds(0, hi_ref.shape[0]), :]
+        put(hi_ref, rb_refs)
 
     @pl.when(jnp.logical_and(cham, ax == n_ax - 1))
     def _():
@@ -285,11 +293,24 @@
     interior(q1_ref, vel_ref, a_ref, power_ref, 0.5, finish)
 
 
+def gather_slots(dst_ref, base, got, tables, cap):
+    slots = [(k, m) for k in range(len(got)) for m in range(cap)]
+    named = [jnp.broadcast_to(tables[k][pl.ds(tables[k].shape[0] - CAX + m, 1), :], (CAX, LANES)) for k, m in slots]
+    for v in range(NV):
+        blocks = [got[k][pl.ds((m * NV + v) * CAX, CAX), :] for k, m in slots]
+        for t in range(CAX):
+            at = pl.ds((v * CAX + t) * CAX, CAX)
+            total = base(at)
+            for name, value in zip(named, blocks):
+                total = total + jnp.where(name == t, value, 0.0)
+            dst_ref[at, :] = total
+
+
 def border_one_kernel(n_az, n_ax, n_out, cap, s_in_ref, *rest):
     got, rest = rest[:n_out], rest[n_out:]
     hl_ref, hr_ref, part_ref, q_ref, vel_ref, supply_ref, own_in_ref, col_any, slot_any, open_any = rest[:10]
     out_refs, rest = rest[10:10 + n_out], rest[10 + n_out:]
-    (q1_ref, tile_ref, s_ref, z_ref, own_ref, er_ref, el_ref, lo_ref, hi_ref,
+    (q1_ref, core_ref, z_ref, own_ref, er_ref, el_ref, lo_ref, hi_ref,
      col_ref, slot_ref, open_ref, sems) = rest
     pairs = [(col_any, col_ref), (slot_any, slot_ref), (open_any, open_ref)]
     copies = [pltpu.make_async_copy(x, y, sems.at[k]) for k, (x, y) in enumerate(pairs)]
@@ -298,7 +319,7 @@
     az, _, plen = roles()
     n = q_ref.shape[1] // CAX
     rows = NV * n
-    fill_ghosts(q_ref, lo_ref, hi_ref, got[:1], got[1], s_in_ref, supply_ref, n_ax)
+    fill_ghosts(q_ref, lo_ref, hi_ref, got[:1], got[1:1 + CAX // cap], s_in_ref, supply_ref, n_ax)
     for v in range(NV):
         q1_ref[v] = part_ref[v]
         add_border(v, q1_ref, 0.1, lo_ref, hi_ref, hl_ref, hr_ref,
@@ -309,17 +330,18 @@
 
     @pl.when(plen == 0)
     def _():
-        tile_ref[...] = jnp.zeros_like(tile_ref)
+        core_ref[pl.ds(rows, EXT), :] = jnp.zeros((EXT, LANES), f32)
         for v in range(NV):
-            s_ref[pl.ds(v * n, n), :] = q1_ref[v, pl.ds(0, n, stride=CAX), :]
+            core_ref[pl.ds(v * n, n), :] = q1_ref[v, pl.ds(0, n, stride=CAX), :]
         axial_rows(q1_ref, vel_ref, out_refs[:CAX // cap], (z_ref,))
 
     @pl.when(plen == 1)
     def _():
-        total = own_in_ref[...]
+        gather_slots(core_ref, lambda at: own_in_ref[at, :] + got[0][at, :], got[1:], got[1:], cap)
+        beside = own_in_ref[pl.ds(rows, EXT), :]
         for ref in got:
-            total = total + ref[pl.ds(0, rows + EXT), :]
-        tile_ref[...] = total
+            beside = beside + ref[pl.ds(ref.shape[0] - CAX - EXT, EXT), :]
+        core_ref[pl.ds(rows, EXT), :] = beside
         own_ref[...] = jnp.zeros_like(own_ref)
         used = [jnp.int32(0)] * n_out
         for b in range(n // CAX):
@@ -348,8 +370,6 @@
 def tile_kernel(n_out, cap, own_ref, z_ref, *rest):
     got, tables, (step_ref,) = rest[:n_out], rest[n_out:2 * n_out], rest[2 * n_out:]
     _, _, plen = roles()
-    rows = own_ref.shape[0]
-    n = rows // NV
 
     @pl.when(plen == 0)
     def _():
@@ -357,44 +377,21 @@
 
     @pl.when(plen == 1)
     def _():
-        slots = [(k, m) for k in range(n_out) for m in range(cap)]
-        named = [jnp.broadcast_to(tables[k][pl.ds(rows + EXT + m, 1), :], (CAX, LANES)) for k, m in slots]
-        for v in range(NV):
-            blocks = [got[k][pl.ds((m * NV + v) * CAX, CAX), :] for k, m in slots]
-            for t in range(n // CAX):
-                at = pl.ds(v * n + t * CAX, CAX)
-                total = own_ref[at, :]
-                for name, value in zip(named, blocks):
-                    total = total + jnp.where(name == t, value, 0.0)
-                step_ref[at, :] = total
-
-
-def pair_kernel(tile_ref, down_ref, s1_ref, core_ref):
-    _, _, plen = roles()
-    rows = s1_ref.shape[0]
-
-    @pl.when(plen == 0)
-    def _():
-        core_ref[pl.ds(0, rows), :] = s1_ref[...]
-        core_ref[pl.ds(rows, EXT), :] = jnp.zeros((EXT, LANES), f32)
-
-    @pl.when(plen == 1)
-    def _():
-        core_ref[...] = tile_ref[...] + down_ref[...]
+        gather_slots(step_ref, lambda at: own_ref[at, :], got, tables, cap)
 
 
 def add_kernel(x_ref, y_ref, out_ref):
     out_ref[...] = x_ref[...] + y_ref[...]
 
 
-def inlet_kernel(pair_ref, far_ref, core_ref, dq_ref, out_ref):
+def inlet_kernel(pair_ref, far_ref, near_ref, dq_ref, out_ref):
     _, ax, plen = roles()
     rows = out_ref.shape[0]
     inlet_side = jnp.logical_and(plen == 0, ax == 0)
 
     @pl.when(inlet_side)
     def _():
-        dq_ref[...] = 0.1 * (far_ref[...] + core_ref[...])
+        dq_ref[...] = 0.1 * (far_ref[...] + near_ref[...])
         out_ref[...] = dq_ref[pl.ds(0, rows), :]
 
     @pl.when(jnp.logical_not(inlet_side))
@@ -412,7 +409,7 @@
     _, ax, plen = roles()
     inlet_side = jnp.logical_and(ax == 0, plen == 0)
     ul_ref, ur_ref = hl0_ref.at[pl.ds(NV * CAX, CAX)], hr0_ref.at[pl.ds(NV * CAX, CAX)]
-    fill_ghosts(q1_ref, lo_ref, hi_ref, ra_refs, step_ref, core_ref, supply_ref, n_ax)
+    fill_ghosts(q1_ref, lo_ref, hi_ref, ra_refs, (step_ref,), core_ref, supply_ref, n_ax)
 
     @pl.when(inlet_side)
     def _():
@@ -531,11 +528,11 @@
     cap = CAX // 4 if n_az > 4 else CAX // 2
     pieces = CAX // cap
 
-    def dense(k):
+    def first(k):
         out = [((i, j, 1), ((i + k + 1) % n_az, j, 1)) for i, j in every]
-        if k < 2:
-            out += [((i, j, 0), (i, mate(k, j), 0)) for i, j in every]
-        return out
+        if k <= pieces:
+            return out + [((i, j, 0), (i, mate(min(k, 1), j), 0)) for i, j in every]
+        return out + [((i, j, 0), ((i + k + 1) % n_az, j, 0)) for i, j in every]
 
     def compact(k):
         out = [((i, j, 1), ((i + k + 1) % n_az, j, 1)) for i, j in every]
@@ -555,13 +552,13 @@
 
     raw = tuple(pltpu.with_memory_space_constraint(x, pltpu.HBM) for x in (q, vel, col, slot, opened) + react)
     wide, edge0 = shape(rows + EXT, LANES), shape((NV + 1) * CAX, LANES)
-    got = call(functools.partial(first_kernel, n_az, n_out), raw, "h" * 9,
-               [shape(rows + EXT + CAX, LANES)] * n_out + [whole, shape(*vel.shape), row, wide, edge0, edge0,
+    got = call(functools.partial(first_kernel, n_az, n_out, pieces), raw, "h" * 9,
+               [shape(rows + EXT + CAX, LANES)] + [shape(cap * NV * CAX + EXT + CAX, LANES)] * (n_out - 1) + [whole, shape(*vel.shape), row, wide, edge0, edge0,
                                                          shape(NV * CAX, 3 * NV * CAX), shape(NS * CAX, LANES)],
                [pltpu.SMEM(col.shape, jnp.int32)] * 3 + [pltpu.SMEM(x.shape, f32) for x in react]
                + [pltpu.SemaphoreType.DMA((8 + NV // 2,))])
     outs, (qv, velv, s0, own0, er, el, matrix, power) = got[:n_out], got[n_out:]
-    ra = [send(x, dense(k)) for k, x in enumerate(outs)]
+    ra = [send(x, first(k)) for k, x in enumerate(outs)]
     s0r = send(s0, swap)
     hl0 = send(er, ring(1))
     el, s0r = lax.optimization_barrier((el, s0r))
@@ -571,30 +568,30 @@
     got = call(functools.partial(border_one_kernel, n_az, n_ax, n_out, cap),
                (s0r, *ra, hl0, hr0, part, qv, velv, sup, own0, col, slot, opened),
                "v" * (n_out + 11),
-               [shape(cap * NV * CAX, LANES)] * n_out + [whole, wide, row, row, row, edge, edge],
+               [shape(cap * NV * CAX, LANES)] * n_out + [whole, wide, row, row, edge, edge],
                [pltpu.VMEM((rows, LANES), f32)] * 2 + [pltpu.SMEM(col.shape, jnp.int32)] * 3
                + [pltpu.SemaphoreType.DMA((3,))])
-    outs, (q1, tile0, s1, z1, own1, er, el) = got[:n_out], got[n_out:]
+    outs, (q1, core, z1, own1, er, el) = got[:n_out], got[n_out:]
     down = [((i, j, 1), (i, j - 1, 1)) for i, j in every if j % 2 == 1]
     across = [((i, 2, 1), (i, 0, 0)) for i in range(n_az)]
     inner = [((i, j, 0), (i, mate(1, j), 0)) for i, j in every if 0 < j < n_ax - 1]
     rb = [send(x, compact(k)) for k, x in enumerate(outs)]
-    down0 = send(tile0, down)
+    core_in = send(core, swap)
+    down0 = send(core, [((i, j, 1), (i, j - 1, 0)) for i, j in every if j % 2 == 1])
 
     part, = call(inside_two_kernel, (qv, q1, velv, matrix, power), "vvvvv", [whole], cost=work)
-    part, own1, s1 = lax.optimization_barrier((part, own1, s1))
+    part, own1 = lax.optimization_barrier((part, own1))
     step, = call(functools.partial(tile_kernel, n_out, cap), (own1, z1, *rb, *ra), "v" * (2 + 2 * n_out), [row])
     step_in = send(step, down + inner)
-    er, el, step = lax.optimization_barrier((er, el, step))
+    er, el, core_in, step = lax.optimization_barrier((er, el, core_in, step))
     hl1, hr1 = send(er, ring(1)), send(el, ring(-1))
-    core, = call(pair_kernel, (tile0, down0, s1), "vvv", [wide])
-    far0 = send(core, across)
-    core_in = send(core, swap)
+    pair0, = call(add_kernel, (core_in, down0), "vv", [wide])
+    far0 = send(pair0, [((i, 2, 0), (i, 0, 0)) for i in range(n_az)])
     pair1, = call(add_kernel, (step, step_in), "vv", [row])
     far1 = send(pair1, across)
     pair1, hl1, hr1 = lax.optimization_barrier((pair1, hl1, hr1))
 
-    dq, core2 = call(inlet_kernel, (pair1, far0, core_in), "vvv", [wide, row])
+    dq, core2 = call(inlet_kernel, (pair1, far0, pair0), "vvv", [wide, row])
     core2_in = send(core2, swap)
     out, keep = call(functools.partial(border_two_kernel, n_ax, pieces),
                      (part, qv, q1, velv, core_in, sup, step_in, dq, hl1, hr1, hl0, hr0, *rb[:pieces], matrix, power),

time: 47.8 us -> 48.1 us (level)
  waiting for transfers between devices: 8.97 us -> 12.8 us
  starting transfers between devices: 26.7 us -> 23.2 us
    ppermute x17, waiting for transfers between devices: 8.97 us -> 12.8 us  [send(): return lax.ppermute(x, AXES, [(number(*a), number(*b)) for a, b in route])]
    ppermute x17, starting transfers between devices: 26.7 us -> 23.2 us  [send(): return lax.ppermute(x, AXES, [(number(*a), number(*b)) for a, b in route])]
  transfers between devices with their start and end apart: 17 -> 17, of which waited for: 6 -> 7; matrix products, arithmetic and copies ran while one was open for 0% -> 0% of each run, Pallas kernels for 16% -> 16%
where the time goes in v7:
time: 48.1 us; the launch traced here: 48 us
  starting transfers between devices  23.2 us (48%)
  waiting for transfers between devices  12.8 us (27%)
  Pallas kernels  11.7 us (24%)
    ppermute x17, starting transfers between devices, send(): return lax.ppermute(x, AXES, [(number(*a), number(*b)) for a, b in route])  23.2 us
    ppermute x17, waiting for transfers between devices, send(): return lax.ppermute(x, AXES, [(number(*a), number(*b)) for a, b in route])  12.8 us
    pallas_call x10, Pallas kernels, call(): pl.pallas_call(kernel, in_specs=[pl.BlockSpec(memory_space=SPACES[k]) for...  11.7 us
  transfers between devices with their start and end apart: 17, of which 7 were waited for; matrix products, arithmetic and copies ran while one was open for 0% of the time, Pallas kernels for 16%

profile of v7, /device:TPU:0, one launch (start us, length us, event | category | flops | bytes accessed | tf_op | source)
XLA Modules:
  0.0 48.0 jit_solution(13257459217716110054)
XLA Ops:
  0.0 2.2 %shard_map.100 = (f32[664,128]{1,0:T(8,128)S(1)}, f32[344,128]{1,0:T(8,128)S(1)}, f32[344,128]{1,0:T(8,128)S(1)}, f32[10,512,128]{2,1,0:T(8,128)S(1)}, f32[2,512...) custom-call(f32[10,512,128]{2,1,0:T(8,128)} %bitcast.20, ...), custom_call_target="tpu_custom_call" | custom-call | tf_op jit(solution)/shard_map/pallas_call | solution.py:490
  2.3 0.7 %collective-permute-start = (f32[640,128]{1,0:T(8,128)S(1)}, f32[640,128]{1,0:T(8,128)S(1)}, u32[]{:S(2)}, u32[]{:S(2)}) collective-permute-start(f32[640,128]{1,0:T(8,128)S(1)} %get-tuple-element.42), channel_id=1, source_target_pairs={{0,1},{1,0},{2,3},{3,2},{4,5},{5,4},{6,7},{7,6},{8,9},{9,8},{10,11... | collective-permute-start | bytes 983048 | tf_op jit(solution)/shard_map/ppermute | solution.py:517
  3.0 2.4 %collective-permute-start.1 = (f32[664,128]{1,0:T(8,128)S(1)}, f32[664,128]{1,0:T(8,128)S(1)}, u32[]{:S(2)}, u32[]{:S(2)}) collective-permute-start(f32[664,128]{1,0:T(8,128)S(1)} %get-tuple-element.44), channel_id=1, source_target_pairs={{1,9},{3,11},{5,13},{7,15},{9,17},{11,19},{13,21},{15,23},{17,25},... | collective-permute-start | bytes 1019912 | tf_op jit(solution)/shard_map/ppermute | solution.py:517
  5.4 2.5 %collective-permute-start.2 = (f32[344,128]{1,0:T(8,128)S(1)}, f32[344,128]{1,0:T(8,128)S(1)}, u32[]{:S(2)}, u32[]{:S(2)}) collective-permute-start(f32[344,128]{1,0:T(8,128)S(1)} %get-tuple-element.45), channel_id=1, source_target_pairs={{1,17},{3,19},{5,21},{7,23},{9,25},{11,27},{13,29},{15,31},{17,1},... | collective-permute-start | bytes 528392 | tf_op jit(solution)/shard_map/ppermute | solution.py:517
  7.9 1.3 %collective-permute-start.3 = (f32[344,128]{1,0:T(8,128)S(1)}, f32[344,128]{1,0:T(8,128)S(1)}, u32[]{:S(2)}, u32[]{:S(2)}) collective-permute-start(f32[344,128]{1,0:T(8,128)S(1)} %get-tuple-element.46), channel_id=1, source_target_pairs={{1,25},{3,27},{5,29},{7,31},{9,1},{11,3},{13,5},{15,7},{17,9},{19,... | collective-permute-start | bytes 528392 | tf_op jit(solution)/shard_map/ppermute | solution.py:517
  9.2 1.5 %collective-permute-start.4 = (f32[88,128]{1,0:T(8,128)S(1)}, f32[88,128]{1,0:T(8,128)S(1)}, u32[]{:S(2)}, u32[]{:S(2)}) collective-permute-start(f32[88,128]{1,0:T(8,128)S(1)} %get-tuple-element.47), channel_id=1, source_target_pairs={{0,8},{1,9},{2,10},{3,11},{4,12},{5,13},{6,14},{7,15},{8,16},{9,17... | collective-permute-start | bytes 135176 | tf_op jit(solution)/shard_map/ppermute | solution.py:517
  10.7 1.4 %collective-permute-start.5 = (f32[88,128]{1,0:T(8,128)S(1)}, f32[88,128]{1,0:T(8,128)S(1)}, u32[]{:S(2)}, u32[]{:S(2)}) collective-permute-start(f32[88,128]{1,0:T(8,128)S(1)} %get-tuple-element.48), channel_id=1, source_target_pairs={{0,24},{1,25},{2,26},{3,27},{4,28},{5,29},{6,30},{7,31},{8,0},{9,1... | collective-permute-start | bytes 135176 | tf_op jit(solution)/shard_map/ppermute | solution.py:517
  12.2 2.5 %shard_map.101.rest_5_ = f32[10,512,128]{2,1,0:T(8,128)S(1)} custom-call(f32[10,512,128]{2,1,0:T(8,128)S(1)} %get-tuple-element.40.q_ref.rest_6_, f32[2,512,128]{2,1,0:T(8,128)S(1)} %get-tuple-element.49.vel_ref.rest_7_, f32[80,240]{1,0:T(8,128)S(1)} %get-tuple-element.50.a_ref.rest_2_, f32[72,128]{1,0:T(8,128)S(1)} %get-tuple-element.51.power_ref.rest_3_), custom_call_target="tpu_custom_call" | custom-call | flops 19660800 | bytes 12000000 | tf_op jit(solution)/shard_map/pallas_call | solution.py:490
  14.6 0.4 collective-permute-done.2.rest_1_.rest_4_
  15.0 1.9 %collective-permute-done.3.rest_2_.rest_5_ = f32[344,128]{1,0:T(8,128)S(1)} collective-permute-done((f32[344,128]{1,0:T(8,128)S(1)}, f32[344,128]{1,0:T(8,128)S(1)}, u32[]{:S(2)}, u32[]{:S(2)}) %collective-permute-start.3) | collective-permute-done | bytes 176160 | tf_op jit(solution)/shard_map/ppermute | solution.py:517
  17.0 0.9 %shard_map.102 = (f32[320,128]{1,0:T(8,128)S(1)}, f32[320,128]{1,0:T(8,128)S(1)}, f32[320,128]{1,0:T(8,128)S(1)}, f32[10,512,128]{2,1,0:T(8,128)S(1)}, f32[656,1...) custom-call(f32[640,128]{1,0:T(8,128)S(1)} %collective-permute-done., ...), custom_call_target="tpu_custom_call" | custom-call | tf_op jit(solution)/shard_map/pallas_call | solution.py:490
  17.9 0.1 collective-permute-start.6
  17.9 1.3 %collective-permute-start.13 = (f32[656,128]{1,0:T(8,128)S(1)}, f32[656,128]{1,0:T(8,128)S(1)}, u32[]{:S(2)}, u32[]{:S(2)}) collective-permute-start(f32[656,128]{1,0:T(8,128)S(1)} %get-tuple-element.58), channel_id=1, source_target_pairs={{3,0},{7,4},{11,8},{15,12},{19,16},{23,20},{27,24},{31,28}} | collective-permute-start | bytes 1007624 | tf_op jit(solution)/shard_map/ppermute | solution.py:517
  19.2 0.3 collective-permute-start.7
  19.5 1.8 %collective-permute-start.8 = (f32[320,128]{1,0:T(8,128)S(1)}, f32[320,128]{1,0:T(8,128)S(1)}, u32[]{:S(2)}, u32[]{:S(2)}) collective-permute-start(f32[320,128]{1,0:T(8,128)S(1)} %get-tuple-element.62), channel_id=1, source_target_pairs={{1,17},{3,19},{5,21},{7,23},{9,25},{11,27},{13,29},{15,31},{17,1},... | collective-permute-start | bytes 491528 | tf_op jit(solution)/shard_map/ppermute | solution.py:517
  21.3 2.4 %collective-permute-start.9 = (f32[320,128]{1,0:T(8,128)S(1)}, f32[320,128]{1,0:T(8,128)S(1)}, u32[]{:S(2)}, u32[]{:S(2)}) collective-permute-start(f32[320,128]{1,0:T(8,128)S(1)} %get-tuple-element.63), channel_id=1, source_target_pairs={{1,25},{3,27},{5,29},{7,31},{9,1},{11,3},{13,5},{15,7},{17,9},{19,... | collective-permute-start | bytes 491528 | tf_op jit(solution)/shard_map/ppermute | solution.py:517
  23.8 2.8 %shard_map.103.part_ref = f32[10,512,128]{2,1,0:T(8,128)S(1)} custom-call(f32[10,512,128]{2,1,0:T(8,128)S(1)} %get-tuple-element.40.q_ref.rest_6_, f32[10,512,128]{2,1,0:T(8,128)S(1)} %get-tuple-element.53.q1_ref, f32[2,512,128]{2,1,0:T(8,128)S(1)} %get-tuple-element.49.vel_ref.rest_7_, f32[80,240]{1,0:T(8,128)S(1)} %get-tuple-element.50.a_ref.rest_2_, ...), custom_call_target="tpu_custom_call" | custom-call | flops 19660800 | bytes 12000000 | tf_op jit(solution)/shard_map/pallas_call | solution.py:490
  26.6 3.3 %collective-permute-done.8.rest_1_ = f32[320,128]{1,0:T(8,128)S(1)} collective-permute-done((f32[320,128]{1,0:T(8,128)S(1)}, f32[320,128]{1,0:T(8,128)S(1)}, u32[]{:S(2)}, u32[]{:S(2)}) %collective-permute-start.8) | collective-permute-done | bytes 163872 | tf_op jit(solution)/shard_map/ppermute | solution.py:517
  29.9 0.0 collective-permute-done.13.y_ref
  30.0 1.3 %collective-permute-start.14 = (f32[656,128]{1,0:T(8,128)S(1)}, f32[656,128]{1,0:T(8,128)S(1)}, u32[]{:S(2)}, u32[]{:S(2)}) collective-permute-start(f32[656,128]{1,0:T(8,128)S(1)} %shard_map.106.near_ref), channel_id=1, source_target_pairs={{4,0},{12,8},{20,16},{28,24}} | collective-permute-start | bytes 1007624 | tf_op jit(solution)/shard_map/ppermute | solution.py:517
  31.3 0.7 %collective-permute-start.10 = (f32[640,128]{1,0:T(8,128)S(1)}, f32[640,128]{1,0:T(8,128)S(1)}, u32[]{:S(2)}, u32[]{:S(2)}) collective-permute-start(f32[640,128]{1,0:T(8,128)S(1)} %shard_map.104.x_ref), channel_id=1, source_target_pairs={{3,1},{7,5},{11,9},{15,13},{19,17},{23,21},{27,25},{31,29},{2,4},{... | collective-permute-start | bytes 983048 | tf_op jit(solution)/shard_map/ppermute | solution.py:517
  32.0 1.5 %collective-permute-start.11 = (f32[80,128]{1,0:T(8,128)S(1)}, f32[80,128]{1,0:T(8,128)S(1)}, u32[]{:S(2)}, u32[]{:S(2)}) collective-permute-start(f32[80,128]{1,0:T(8,128)S(1)} %get-tuple-element.66), channel_id=1, source_target_pairs={{0,8},{1,9},{2,10},{3,11},{4,12},{5,13},{6,14},{7,15},{8,16},{9,17... | collective-permute-start | bytes 122888 | tf_op jit(solution)/shard_map/ppermute | solution.py:517
  33.5 1.4 %collective-permute-start.12 = (f32[80,128]{1,0:T(8,128)S(1)}, f32[80,128]{1,0:T(8,128)S(1)}, u32[]{:S(2)}, u32[]{:S(2)}) collective-permute-start(f32[80,128]{1,0:T(8,128)S(1)} %get-tuple-element.67), channel_id=1, source_target_pairs={{0,24},{1,25},{2,26},{3,27},{4,28},{5,29},{6,30},{7,31},{8,0},{9,1... | collective-permute-start | bytes 122888 | tf_op jit(solution)/shard_map/ppermute | solution.py:517
  35.0 1.3 %collective-permute-start.16 = (f32[640,128]{1,0:T(8,128)S(1)}, f32[640,128]{1,0:T(8,128)S(1)}, u32[]{:S(2)}, u32[]{:S(2)}) collective-permute-start(f32[640,128]{1,0:T(8,128)S(1)} %shard_map.105.pair_ref), channel_id=1, source_target_pairs={{5,0},{13,8},{21,16},{29,24}} | collective-permute-start | bytes 983048 | tf_op jit(solution)/shard_map/ppermute | solution.py:517
  36.3 0.6 %collective-permute-done.11.hl_ref = f32[80,128]{1,0:T(8,128)S(1)} collective-permute-done((f32[80,128]{1,0:T(8,128)S(1)}, f32[80,128]{1,0:T(8,128)S(1)}, u32[]{:S(2)}, u32[]{:S(2)}) %collective-permute-start.11) | collective-permute-done | bytes 40992 | tf_op jit(solution)/shard_map/ppermute | solution.py:517
  36.9 0.6 %collective-permute-done.12.hr_ref = f32[80,128]{1,0:T(8,128)S(1)} collective-permute-done((f32[80,128]{1,0:T(8,128)S(1)}, f32[80,128]{1,0:T(8,128)S(1)}, u32[]{:S(2)}, u32[]{:S(2)}) %collective-permute-start.12) | collective-permute-done | bytes 40992 | tf_op jit(solution)/shard_map/ppermute | solution.py:517
  37.5 2.5 %collective-permute-done.14.far_ref = f32[656,128]{1,0:T(8,128)S(1)} collective-permute-done((f32[656,128]{1,0:T(8,128)S(1)}, f32[656,128]{1,0:T(8,128)S(1)}, u32[]{:S(2)}, u32[]{:S(2)}) %collective-permute-start.14) | collective-permute-done | bytes 335904 | tf_op jit(solution)/shard_map/ppermute | solution.py:517
  40.0 0.1 shard_map.107
  40.1 1.2 %collective-permute-start.15 = (f32[640,128]{1,0:T(8,128)S(1)}, f32[640,128]{1,0:T(8,128)S(1)}, u32[]{:S(2)}, u32[]{:S(2)}) collective-permute-start(f32[640,128]{1,0:T(8,128)S(1)} %get-tuple-element.74), channel_id=1, source_target_pairs={{0,1},{1,0},{2,3},{3,2},{4,5},{5,4},{6,7},{7,6},{8,9},{9,8},{10,11... | collective-permute-start | bytes 983048 | tf_op jit(solution)/shard_map/ppermute | solution.py:517
  41.3 2.2 %shard_map.108 = (f32[10,512,128]{2,1,0:T(8,128)}, f32[640,128]{1,0:T(8,128)S(1)}) custom-call(f32[10,512,128]{2,1,0:T(8,128)S(1)} %shard_map.103.part_ref, f32[10,512,128]{2,1,0:T(8,128)S(1)} %get-tuple-element.40.q_ref.rest_6_, f32[10,512,128]{2,1,0:T(8,128)S(1)} %get-tuple-element.53.q1_ref, f32[2,512,128]{2,1,0:T(8,128)S(1)} %get-tuple-element.49.vel_ref.rest_7_, ...), custom_call_target="tpu_custom_call" | custom-call | flops 19660800 | bytes 12000000 | tf_op jit(solution)/shard_map/pallas_call | solution.py:490
  43.6 3.5 %collective-permute-done.16.far_ref = f32[640,128]{1,0:T(8,128)S(1)} collective-permute-done((f32[640,128]{1,0:T(8,128)S(1)}, f32[640,128]{1,0:T(8,128)S(1)}, u32[]{:S(2)}, u32[]{:S(2)}) %collective-permute-start.16) | collective-permute-done | bytes 327712 | tf_op jit(solution)/shard_map/ppermute | solution.py:517
  47.0 0.9 %shard_map.109 = f32[10,64,8,128]{3,2,1,0:T(8,128)} custom-call(f32[10,64,8,128]{3,2,1,0:T(8,128)} %bitcast.21, f32[640,128]{1,0:T(8,128)S(1)} %get-tuple-element.73.keep_ref, f32[640,128]{1,0:T(8,128)S(1)} %collective-permute-done.15.core_ref, f32[640,128]{1,0:T(8,128)S(1)} %collective-permute-done.16.far_ref), custom_call_target="tpu_custom_call", output_to_operand_aliasing={{}: (0, {})} | custom-call | tf_op jit(solution)/shard_map/pallas_call | solution.py:490
  (20 shorter events, 0.1 us)
Async XLA Ops:
  2.3 8.5 %collective-permute-start = (f32[640,128]{1,0:T(8,128)S(1)}, f32[640,128]{1,0:T(8,128)S(1)}, u32[]{:S(2)}, u32[]{:S(2)}) collective-permute-start(f32[640,128]{1,0:T(8,128)S(1)} %get-tuple-element.42), channel_id=1, source_target_pairs={{0,1},{1,0},{2,3},{3,2},{4,5},{5,4},{6,7},{7,6},{8,9},{9,8},{10,11... | collective-permute-start | bytes 983048 | tf_op jit(solution)/shard_map/ppermute | solution.py:517
  3.0 14.0 %collective-permute-start.1 = (f32[664,128]{1,0:T(8,128)S(1)}, f32[664,128]{1,0:T(8,128)S(1)}, u32[]{:S(2)}, u32[]{:S(2)}) collective-permute-start(f32[664,128]{1,0:T(8,128)S(1)} %get-tuple-element.44), channel_id=1, source_target_pairs={{1,9},{3,11},{5,13},{7,15},{9,17},{11,19},{13,21},{15,23},{17,25},... | collective-permute-start | bytes 1019912 | tf_op jit(solution)/shard_map/ppermute | solution.py:517
  5.4 9.6 %collective-permute-start.2 = (f32[344,128]{1,0:T(8,128)S(1)}, f32[344,128]{1,0:T(8,128)S(1)}, u32[]{:S(2)}, u32[]{:S(2)}) collective-permute-start(f32[344,128]{1,0:T(8,128)S(1)} %get-tuple-element.45), channel_id=1, source_target_pairs={{1,17},{3,19},{5,21},{7,23},{9,25},{11,27},{13,29},{15,31},{17,1},... | collective-permute-start | bytes 528392 | tf_op jit(solution)/shard_map/ppermute | solution.py:517
  7.9 9.1 %collective-permute-start.3 = (f32[344,128]{1,0:T(8,128)S(1)}, f32[344,128]{1,0:T(8,128)S(1)}, u32[]{:S(2)}, u32[]{:S(2)}) collective-permute-start(f32[344,128]{1,0:T(8,128)S(1)} %get-tuple-element.46), channel_id=1, source_target_pairs={{1,25},{3,27},{5,29},{7,31},{9,1},{11,3},{13,5},{15,7},{17,9},{19,... | collective-permute-start | bytes 528392 | tf_op jit(solution)/shard_map/ppermute | solution.py:517
  9.2 5.4 %collective-permute-start.4 = (f32[88,128]{1,0:T(8,128)S(1)}, f32[88,128]{1,0:T(8,128)S(1)}, u32[]{:S(2)}, u32[]{:S(2)}) collective-permute-start(f32[88,128]{1,0:T(8,128)S(1)} %get-tuple-element.47), channel_id=1, source_target_pairs={{0,8},{1,9},{2,10},{3,11},{4,12},{5,13},{6,14},{7,15},{8,16},{9,17... | collective-permute-start | bytes 135176 | tf_op jit(solution)/shard_map/ppermute | solution.py:517
  10.7 6.2 %collective-permute-start.5 = (f32[88,128]{1,0:T(8,128)S(1)}, f32[88,128]{1,0:T(8,128)S(1)}, u32[]{:S(2)}, u32[]{:S(2)}) collective-permute-start(f32[88,128]{1,0:T(8,128)S(1)} %get-tuple-element.48), channel_id=1, source_target_pairs={{0,24},{1,25},{2,26},{3,27},{4,28},{5,29},{6,30},{7,31},{8,0},{9,1... | collective-permute-start | bytes 135176 | tf_op jit(solution)/shard_map/ppermute | solution.py:517
  12.2 4.8 %copy-start = (f32[10,1,8192]{2,1,0:T(1,128)S(1)}, f32[10,1,8192]{2,1,0:T(1,128)}, u32[]{:S(2)}) copy-start(f32[10,1,8192]{2,1,0:T(1,128)} %param.12) | copy-start | bytes 983044
  12.2 4.8 %copy-start.1 = (s32[8,1]{0,1:T(1,128)S(1)}, s32[8,1]{0,1:T(1,128)}, u32[]{:S(2)}) copy-start(s32[8,1]{0,1:T(1,128)} %param.17) | copy-start | bytes 100
  12.2 4.8 %copy-start.2 = (s32[8]{0:T(128)S(1)}, s32[8]{0:T(128)}, u32[]{:S(2)}) copy-start(s32[8]{0:T(128)} %rest_11_.1) | copy-start | bytes 100
  12.2 4.8 %copy-start.3 = (s32[8]{0:T(128)S(1)}, s32[8]{0:T(128)}, u32[]{:S(2)}) copy-start(s32[8]{0:T(128)} %rest_12_.1) | copy-start | bytes 100
  17.9 12.0 %collective-permute-start.6 = (f32[656,128]{1,0:T(8,128)S(1)}, f32[656,128]{1,0:T(8,128)S(1)}, u32[]{:S(2)}, u32[]{:S(2)}) collective-permute-start(f32[656,128]{1,0:T(8,128)S(1)} %get-tuple-element.58), channel_id=1, source_target_pairs={{0,1},{1,0},{2,3},{3,2},{4,5},{5,4},{6,7},{7,6},{8,9},{9,8},{10,11... | collective-permute-start | bytes 1007624 | tf_op jit(solution)/shard_map/ppermute | solution.py:517
  17.9 12.0 %collective-permute-start.13 = (f32[656,128]{1,0:T(8,128)S(1)}, f32[656,128]{1,0:T(8,128)S(1)}, u32[]{:S(2)}, u32[]{:S(2)}) collective-permute-start(f32[656,128]{1,0:T(8,128)S(1)} %get-tuple-element.58), channel_id=1, source_target_pairs={{3,0},{7,4},{11,8},{15,12},{19,16},{23,20},{27,24},{31,28}} | collective-permute-start | bytes 1007624 | tf_op jit(solution)/shard_map/ppermute | solution.py:517
  19.2 7.3 %collective-permute-start.7 = (f32[320,128]{1,0:T(8,128)S(1)}, f32[320,128]{1,0:T(8,128)S(1)}, u32[]{:S(2)}, u32[]{:S(2)}) collective-permute-start(f32[320,128]{1,0:T(8,128)S(1)} %get-tuple-element.61), channel_id=1, source_target_pairs={{1,9},{3,11},{5,13},{7,15},{9,17},{11,19},{13,21},{15,23},{17,25},... | collective-permute-start | bytes 491528 | tf_op jit(solution)/shard_map/ppermute | solution.py:517
  19.5 10.3 %collective-permute-start.8 = (f32[320,128]{1,0:T(8,128)S(1)}, f32[320,128]{1,0:T(8,128)S(1)}, u32[]{:S(2)}, u32[]{:S(2)}) collective-permute-start(f32[320,128]{1,0:T(8,128)S(1)} %get-tuple-element.62), channel_id=1, source_target_pairs={{1,17},{3,19},{5,21},{7,23},{9,25},{11,27},{13,29},{15,31},{17,1},... | collective-permute-start | bytes 491528 | tf_op jit(solution)/shard_map/ppermute | solution.py:517
  21.3 8.6 %collective-permute-start.9 = (f32[320,128]{1,0:T(8,128)S(1)}, f32[320,128]{1,0:T(8,128)S(1)}, u32[]{:S(2)}, u32[]{:S(2)}) collective-permute-start(f32[320,128]{1,0:T(8,128)S(1)} %get-tuple-element.63), channel_id=1, source_target_pairs={{1,25},{3,27},{5,29},{7,31},{9,1},{11,3},{13,5},{15,7},{17,9},{19,... | collective-permute-start | bytes 491528 | tf_op jit(solution)/shard_map/ppermute | solution.py:517
  30.0 10.1 %collective-permute-start.14 = (f32[656,128]{1,0:T(8,128)S(1)}, f32[656,128]{1,0:T(8,128)S(1)}, u32[]{:S(2)}, u32[]{:S(2)}) collective-permute-start(f32[656,128]{1,0:T(8,128)S(1)} %shard_map.106.near_ref), channel_id=1, source_target_pairs={{4,0},{12,8},{20,16},{28,24}} | collective-permute-start | bytes 1007624 | tf_op jit(solution)/shard_map/ppermute | solution.py:517
  31.3 3.7 %collective-permute-start.10 = (f32[640,128]{1,0:T(8,128)S(1)}, f32[640,128]{1,0:T(8,128)S(1)}, u32[]{:S(2)}, u32[]{:S(2)}) collective-permute-start(f32[640,128]{1,0:T(8,128)S(1)} %shard_map.104.x_ref), channel_id=1, source_target_pairs={{3,1},{7,5},{11,9},{15,13},{19,17},{23,21},{27,25},{31,29},{2,4},{... | collective-permute-start | bytes 983048 | tf_op jit(solution)/shard_map/ppermute | solution.py:517
  32.0 5.0 %collective-permute-start.11 = (f32[80,128]{1,0:T(8,128)S(1)}, f32[80,128]{1,0:T(8,128)S(1)}, u32[]{:S(2)}, u32[]{:S(2)}) collective-permute-start(f32[80,128]{1,0:T(8,128)S(1)} %get-tuple-element.66), channel_id=1, source_target_pairs={{0,8},{1,9},{2,10},{3,11},{4,12},{5,13},{6,14},{7,15},{8,16},{9,17... | collective-permute-start | bytes 122888 | tf_op jit(solution)/shard_map/ppermute | solution.py:517
  33.5 4.0 %collective-permute-start.12 = (f32[80,128]{1,0:T(8,128)S(1)}, f32[80,128]{1,0:T(8,128)S(1)}, u32[]{:S(2)}, u32[]{:S(2)}) collective-permute-start(f32[80,128]{1,0:T(8,128)S(1)} %get-tuple-element.67), channel_id=1, source_target_pairs={{0,24},{1,25},{2,26},{3,27},{4,28},{5,29},{6,30},{7,31},{8,0},{9,1... | collective-permute-start | bytes 122888 | tf_op jit(solution)/shard_map/ppermute | solution.py:517
  35.0 12.0 %collective-permute-start.16 = (f32[640,128]{1,0:T(8,128)S(1)}, f32[640,128]{1,0:T(8,128)S(1)}, u32[]{:S(2)}, u32[]{:S(2)}) collective-permute-start(f32[640,128]{1,0:T(8,128)S(1)} %shard_map.105.pair_ref), channel_id=1, source_target_pairs={{5,0},{13,8},{21,16},{29,24}} | collective-permute-start | bytes 983048 | tf_op jit(solution)/shard_map/ppermute | solution.py:517
  40.1 6.9 %collective-permute-start.15 = (f32[640,128]{1,0:T(8,128)S(1)}, f32[640,128]{1,0:T(8,128)S(1)}, u32[]{:S(2)}, u32[]{:S(2)}) collective-permute-start(f32[640,128]{1,0:T(8,128)S(1)} %get-tuple-element.74), channel_id=1, source_target_pairs={{0,1},{1,0},{2,3},{3,2},{4,5},{5,4},{6,7},{7,6},{8,9},{9,8},{10,11... | collective-permute-start | bytes 983048 | tf_op jit(solution)/shard_map/ppermute | solution.py:517

commit v8 on v7

--- a/solution.py
+++ b/solution.py
@@ -380,8 +380,8 @@
         gather_slots(step_ref, lambda at: own_ref[at, :], got, tables, cap)
 
 
-def add_kernel(x_ref, y_ref, out_ref):
-    out_ref[...] = x_ref[...] + y_ref[...]
+def add_kernel(*refs):
+    refs[-1][...] = sum(ref[...] for ref in refs[:-1])
 
 
 def inlet_kernel(pair_ref, far_ref, near_ref, dq_ref, out_ref):
@@ -530,9 +530,10 @@
 
     def first(k):
         out = [((i, j, 1), ((i + k + 1) % n_az, j, 1)) for i, j in every]
-        if k <= pieces:
-            return out + [((i, j, 0), (i, mate(min(k, 1), j), 0)) for i, j in every]
-        return out + [((i, j, 0), ((i + k + 1) % n_az, j, 0)) for i, j in every]
+        for i, j in every:
+            along = k == 0 or (k <= pieces and 0 < j < n_ax - 1)
+            out.append(((i, j, 0), (i, mate(min(k, 1), j), 0) if along else ((i + k + 1) % n_az, j, 0)))
+        return out
 
     def compact(k):
         out = [((i, j, 1), ((i + k + 1) % n_az, j, 1)) for i, j in every]
@@ -577,16 +578,17 @@
     inner = [((i, j, 0), (i, mate(1, j), 0)) for i, j in every if 0 < j < n_ax - 1]
     rb = [send(x, compact(k)) for k, x in enumerate(outs)]
     core_in = send(core, swap)
-    down0 = send(core, [((i, j, 1), (i, j - 1, 0)) for i, j in every if j % 2 == 1])
+    down0 = send(core, [((i, 2, 1), (i, 1, 0)) for i in range(n_az)])
 
     part, = call(inside_two_kernel, (qv, q1, velv, matrix, power), "vvvvv", [whole], cost=work)
-    part, own1 = lax.optimization_barrier((part, own1))
+    part, own1, late, rb = lax.optimization_barrier((part, own1, core, rb))
+    down1 = send(late, [((i, 3, 1), (i, 1, 0)) for i in range(n_az)])
     step, = call(functools.partial(tile_kernel, n_out, cap), (own1, z1, *rb, *ra), "v" * (2 + 2 * n_out), [row])
     step_in = send(step, down + inner)
     er, el, core_in, step = lax.optimization_barrier((er, el, core_in, step))
     hl1, hr1 = send(er, ring(1)), send(el, ring(-1))
-    pair0, = call(add_kernel, (core_in, down0), "vv", [wide])
-    far0 = send(pair0, [((i, 2, 0), (i, 0, 0)) for i in range(n_az)])
+    pair0, = call(add_kernel, (core_in, down0, down1), "vvv", [wide])
+    far0 = send(pair0, [((i, 1, 0), (i, 0, 0)) for i in range(n_az)])
     pair1, = call(add_kernel, (step, step_in), "vv", [row])
     far1 = send(pair1, across)
     pair1, hl1, hr1 = lax.optimization_barrier((pair1, hl1, hr1))

time: 48.1 us -> 50.8 us (1.056)
  waiting for transfers between devices: 12.8 us -> 17.3 us
  starting transfers between devices: 23.2 us -> 21.3 us
    ppermute x17 -> x18, waiting for transfers between devices: 12.8 us -> 17.3 us  [send(): return lax.ppermute(x, AXES, [(number(*a), number(*b)) for a, b in route])]
    ppermute x17 -> x18, starting transfers between devices: 23.2 us -> 21.3 us  [send(): return lax.ppermute(x, AXES, [(number(*a), number(*b)) for a, b in route])]
  transfers between devices with their start and end apart: 17 -> 18, of which waited for: 7 -> 8; matrix products, arithmetic and copies ran while one was open for 0% -> 0% of each run, Pallas kernels for 16% -> 15%
where the time goes in v8:
time: 50.8 us; the launch traced here: 50.6 us
  starting transfers between devices  21.3 us (42%)
  waiting for transfers between devices  17.3 us (34%)
  Pallas kernels  11.8 us (23%)
    ppermute x18, starting transfers between devices, send(): return lax.ppermute(x, AXES, [(number(*a), number(*b)) for a, b in route])  21.3 us
    ppermute x18, waiting for transfers between devices, send(): return lax.ppermute(x, AXES, [(number(*a), number(*b)) for a, b in route])  17.3 us
    pallas_call x10, Pallas kernels, call(): pl.pallas_call(kernel, in_specs=[pl.BlockSpec(memory_space=SPACES[k]) for...  11.8 us
  transfers between devices with their start and end apart: 18, of which 8 were waited for; matrix products, arithmetic and copies ran while one was open for 0% of the time, Pallas kernels for 15%

profile of v8, /device:TPU:0, one launch (start us, length us, event | category | flops | bytes accessed | tf_op | source)
XLA Modules:
  0.0 50.6 jit_solution(978728301650417269)
XLA Ops:
  0.0 2.2 %shard_map.100 = (f32[664,128]{1,0:T(8,128)S(1)}, f32[344,128]{1,0:T(8,128)S(1)}, f32[344,128]{1,0:T(8,128)S(1)}, f32[10,512,128]{2,1,0:T(8,128)S(1)}, f32[2,512...) custom-call(f32[10,512,128]{2,1,0:T(8,128)} %bitcast.20, ...), custom_call_target="tpu_custom_call" | custom-call | tf_op jit(solution)/shard_map/pallas_call | solution.py:490
  2.3 0.7 %collective-permute-start = (f32[640,128]{1,0:T(8,128)S(1)}, f32[640,128]{1,0:T(8,128)S(1)}, u32[]{:S(2)}, u32[]{:S(2)}) collective-permute-start(f32[640,128]{1,0:T(8,128)S(1)} %get-tuple-element.46), channel_id=1, source_target_pairs={{0,1},{1,0},{2,3},{3,2},{4,5},{5,4},{6,7},{7,6},{8,9},{9,8},{10,11... | collective-permute-start | bytes 983048 | tf_op jit(solution)/shard_map/ppermute | solution.py:517
  3.0 2.4 %collective-permute-start.1 = (f32[664,128]{1,0:T(8,128)S(1)}, f32[664,128]{1,0:T(8,128)S(1)}, u32[]{:S(2)}, u32[]{:S(2)}) collective-permute-start(f32[664,128]{1,0:T(8,128)S(1)} %get-tuple-element.48), channel_id=1, source_target_pairs={{1,9},{3,11},{5,13},{7,15},{9,17},{11,19},{13,21},{15,23},{17,25},... | collective-permute-start | bytes 1019912 | tf_op jit(solution)/shard_map/ppermute | solution.py:517
  5.4 1.5 %collective-permute-start.2 = (f32[344,128]{1,0:T(8,128)S(1)}, f32[344,128]{1,0:T(8,128)S(1)}, u32[]{:S(2)}, u32[]{:S(2)}) collective-permute-start(f32[344,128]{1,0:T(8,128)S(1)} %get-tuple-element.49), channel_id=1, source_target_pairs={{1,17},{3,19},{5,21},{7,23},{9,25},{11,27},{13,29},{15,31},{17,1},... | collective-permute-start | bytes 528392 | tf_op jit(solution)/shard_map/ppermute | solution.py:517
  6.9 1.5 %collective-permute-start.3 = (f32[344,128]{1,0:T(8,128)S(1)}, f32[344,128]{1,0:T(8,128)S(1)}, u32[]{:S(2)}, u32[]{:S(2)}) collective-permute-start(f32[344,128]{1,0:T(8,128)S(1)} %get-tuple-element.50), channel_id=1, source_target_pairs={{1,25},{3,27},{5,29},{7,31},{9,1},{11,3},{13,5},{15,7},{17,9},{19,... | collective-permute-start | bytes 528392 | tf_op jit(solution)/shard_map/ppermute | solution.py:517
  8.4 0.6 %collective-permute-start.4 = (f32[88,128]{1,0:T(8,128)S(1)}, f32[88,128]{1,0:T(8,128)S(1)}, u32[]{:S(2)}, u32[]{:S(2)}) collective-permute-start(f32[88,128]{1,0:T(8,128)S(1)} %get-tuple-element.51), channel_id=1, source_target_pairs={{0,8},{1,9},{2,10},{3,11},{4,12},{5,13},{6,14},{7,15},{8,16},{9,17... | collective-permute-start | bytes 135176 | tf_op jit(solution)/shard_map/ppermute | solution.py:517
  9.0 2.4 %collective-permute-start.5 = (f32[88,128]{1,0:T(8,128)S(1)}, f32[88,128]{1,0:T(8,128)S(1)}, u32[]{:S(2)}, u32[]{:S(2)}) collective-permute-start(f32[88,128]{1,0:T(8,128)S(1)} %get-tuple-element.52), channel_id=1, source_target_pairs={{0,24},{1,25},{2,26},{3,27},{4,28},{5,29},{6,30},{7,31},{8,0},{9,1... | collective-permute-start | bytes 135176 | tf_op jit(solution)/shard_map/ppermute | solution.py:517
  11.3 2.5 %shard_map.101.rest_5_ = f32[10,512,128]{2,1,0:T(8,128)S(1)} custom-call(f32[10,512,128]{2,1,0:T(8,128)S(1)} %get-tuple-element.44.q_ref.rest_6_, f32[2,512,128]{2,1,0:T(8,128)S(1)} %get-tuple-element.53.vel_ref.rest_7_, f32[80,240]{1,0:T(8,128)S(1)} %get-tuple-element.54.a_ref.rest_2_, f32[72,128]{1,0:T(8,128)S(1)} %get-tuple-element.55.power_ref.rest_3_), custom_call_target="tpu_custom_call" | custom-call | flops 19660800 | bytes 12000000 | tf_op jit(solution)/shard_map/pallas_call | solution.py:490
  13.8 1.4 %collective-permute-done.4.rest_3_.hl0_ref = f32[88,128]{1,0:T(8,128)S(1)} collective-permute-done((f32[88,128]{1,0:T(8,128)S(1)}, f32[88,128]{1,0:T(8,128)S(1)}, u32[]{:S(2)}, u32[]{:S(2)}) %collective-permute-start.4) | collective-permute-done | bytes 45088 | tf_op jit(solution)/shard_map/ppermute | solution.py:517
  15.2 0.2 collective-permute-done.2.rest_1_.rest_4_
  15.5 0.8 %collective-permute-done.5.rest_4_.hr0_ref = f32[88,128]{1,0:T(8,128)S(1)} collective-permute-done((f32[88,128]{1,0:T(8,128)S(1)}, f32[88,128]{1,0:T(8,128)S(1)}, u32[]{:S(2)}, u32[]{:S(2)}) %collective-permute-start.5) | collective-permute-done | bytes 45088 | tf_op jit(solution)/shard_map/ppermute | solution.py:517
  16.3 0.9 %shard_map.102 = (f32[320,128]{1,0:T(8,128)S(1)}, f32[320,128]{1,0:T(8,128)S(1)}, f32[320,128]{1,0:T(8,128)S(1)}, f32[10,512,128]{2,1,0:T(8,128)S(1)}, f32[656,1...) custom-call(f32[640,128]{1,0:T(8,128)S(1)} %collective-permute-done., ...), custom_call_target="tpu_custom_call" | custom-call | tf_op jit(solution)/shard_map/pallas_call | solution.py:490
  17.2 2.0 %collective-permute-start.7 = (f32[320,128]{1,0:T(8,128)S(1)}, f32[320,128]{1,0:T(8,128)S(1)}, u32[]{:S(2)}, u32[]{:S(2)}) collective-permute-start(f32[320,128]{1,0:T(8,128)S(1)} %get-tuple-element.61), channel_id=1, source_target_pairs={{1,17},{3,19},{5,21},{7,23},{9,25},{11,27},{13,29},{15,31},{17,1},... | collective-permute-start | bytes 491528 | tf_op jit(solution)/shard_map/ppermute | solution.py:517
  19.2 2.4 %collective-permute-start.8 = (f32[320,128]{1,0:T(8,128)S(1)}, f32[320,128]{1,0:T(8,128)S(1)}, u32[]{:S(2)}, u32[]{:S(2)}) collective-permute-start(f32[320,128]{1,0:T(8,128)S(1)} %get-tuple-element.62), channel_id=1, source_target_pairs={{1,25},{3,27},{5,29},{7,31},{9,1},{11,3},{13,5},{15,7},{17,9},{19,... | collective-permute-start | bytes 491528 | tf_op jit(solution)/shard_map/ppermute | solution.py:517
  21.6 0.7 %collective-permute-start.13 = (f32[656,128]{1,0:T(8,128)S(1)}, f32[656,128]{1,0:T(8,128)S(1)}, u32[]{:S(2)}, u32[]{:S(2)}) collective-permute-start(f32[656,128]{1,0:T(8,128)S(1)} %get-tuple-element.76), channel_id=1, source_target_pairs={{5,2},{13,10},{21,18},{29,26}} | collective-permute-start | bytes 1007624 | tf_op jit(solution)/shard_map/ppermute | solution.py:517
  22.3 0.1 collective-permute-start.9
  22.4 2.8 %shard_map.103.part_ref = f32[10,512,128]{2,1,0:T(8,128)S(1)} custom-call(f32[10,512,128]{2,1,0:T(8,128)S(1)} %get-tuple-element.44.q_ref.rest_6_, f32[10,512,128]{2,1,0:T(8,128)S(1)} %get-tuple-element.57.q1_ref, f32[2,512,128]{2,1,0:T(8,128)S(1)} %get-tuple-element.53.vel_ref.rest_7_, f32[80,240]{1,0:T(8,128)S(1)} %get-tuple-element.54.a_ref.rest_2_, ...), custom_call_target="tpu_custom_call" | custom-call | flops 19660800 | bytes 12000000 | tf_op jit(solution)/shard_map/pallas_call | solution.py:490
  25.2 1.4 %collective-permute-done.8.rest_2_ = f32[320,128]{1,0:T(8,128)S(1)} collective-permute-done((f32[320,128]{1,0:T(8,128)S(1)}, f32[320,128]{1,0:T(8,128)S(1)}, u32[]{:S(2)}, u32[]{:S(2)}) %collective-permute-start.8) | collective-permute-done | bytes 163872 | tf_op jit(solution)/shard_map/ppermute | solution.py:517
  26.7 0.7 %collective-permute-start.14 = (f32[656,128]{1,0:T(8,128)S(1)}, f32[656,128]{1,0:T(8,128)S(1)}, u32[]{:S(2)}, u32[]{:S(2)}) collective-permute-start(f32[656,128]{1,0:T(8,128)S(1)} %get-tuple-element.76), channel_id=1, source_target_pairs={{7,2},{15,10},{23,18},{31,26}} | collective-permute-start | bytes 1007624 | tf_op jit(solution)/shard_map/ppermute | solution.py:517
  27.5 1.3 %collective-permute-start.15 = (f32[656,128]{1,0:T(8,128)S(1)}, f32[656,128]{1,0:T(8,128)S(1)}, u32[]{:S(2)}, u32[]{:S(2)}) collective-permute-start(f32[656,128]{1,0:T(8,128)S(1)} %shard_map.106.near_ref), channel_id=1, source_target_pairs={{2,0},{10,8},{18,16},{26,24}} | collective-permute-start | bytes 1007624 | tf_op jit(solution)/shard_map/ppermute | solution.py:517
  28.8 0.7 %collective-permute-start.10 = (f32[640,128]{1,0:T(8,128)S(1)}, f32[640,128]{1,0:T(8,128)S(1)}, u32[]{:S(2)}, u32[]{:S(2)}) collective-permute-start(f32[640,128]{1,0:T(8,128)S(1)} %shard_map.104.refs_0_), channel_id=1, source_target_pairs={{3,1},{7,5},{11,9},{15,13},{19,17},{23,21},{27,25},{31,29},{2,4},{... | collective-permute-start | bytes 983048 | tf_op jit(solution)/shard_map/ppermute | solution.py:517
  29.5 1.7 %collective-permute-start.11 = (f32[80,128]{1,0:T(8,128)S(1)}, f32[80,128]{1,0:T(8,128)S(1)}, u32[]{:S(2)}, u32[]{:S(2)}) collective-permute-start(f32[80,128]{1,0:T(8,128)S(1)} %get-tuple-element.73), channel_id=1, source_target_pairs={{0,8},{1,9},{2,10},{3,11},{4,12},{5,13},{6,14},{7,15},{8,16},{9,17... | collective-permute-start | bytes 122888 | tf_op jit(solution)/shard_map/ppermute | solution.py:517
  31.2 1.2 %collective-permute-start.12 = (f32[80,128]{1,0:T(8,128)S(1)}, f32[80,128]{1,0:T(8,128)S(1)}, u32[]{:S(2)}, u32[]{:S(2)}) collective-permute-start(f32[80,128]{1,0:T(8,128)S(1)} %get-tuple-element.74), channel_id=1, source_target_pairs={{0,24},{1,25},{2,26},{3,27},{4,28},{5,29},{6,30},{7,31},{8,0},{9,1... | collective-permute-start | bytes 122888 | tf_op jit(solution)/shard_map/ppermute | solution.py:517
  32.5 1.3 %collective-permute-start.17 = (f32[640,128]{1,0:T(8,128)S(1)}, f32[640,128]{1,0:T(8,128)S(1)}, u32[]{:S(2)}, u32[]{:S(2)}) collective-permute-start(f32[640,128]{1,0:T(8,128)S(1)} %shard_map.105.pair_ref), channel_id=1, source_target_pairs={{5,0},{13,8},{21,16},{29,24}} | collective-permute-start | bytes 983048 | tf_op jit(solution)/shard_map/ppermute | solution.py:517
  33.8 0.9 %collective-permute-done.11.hl_ref = f32[80,128]{1,0:T(8,128)S(1)} collective-permute-done((f32[80,128]{1,0:T(8,128)S(1)}, f32[80,128]{1,0:T(8,128)S(1)}, u32[]{:S(2)}, u32[]{:S(2)}) %collective-permute-start.11) | collective-permute-done | bytes 40992 | tf_op jit(solution)/shard_map/ppermute | solution.py:517
  34.7 0.5 %collective-permute-done.12.hr_ref = f32[80,128]{1,0:T(8,128)S(1)} collective-permute-done((f32[80,128]{1,0:T(8,128)S(1)}, f32[80,128]{1,0:T(8,128)S(1)}, u32[]{:S(2)}, u32[]{:S(2)}) %collective-permute-start.12) | collective-permute-done | bytes 40992 | tf_op jit(solution)/shard_map/ppermute | solution.py:517
  35.2 7.6 %collective-permute-done.15.far_ref = f32[656,128]{1,0:T(8,128)S(1)} collective-permute-done((f32[656,128]{1,0:T(8,128)S(1)}, f32[656,128]{1,0:T(8,128)S(1)}, u32[]{:S(2)}, u32[]{:S(2)}) %collective-permute-start.15) | collective-permute-done | bytes 335904 | tf_op jit(solution)/shard_map/ppermute | solution.py:517
  42.8 0.1 shard_map.107
  42.9 0.1 collective-permute-start.16
  42.9 2.3 %shard_map.108 = (f32[10,512,128]{2,1,0:T(8,128)}, f32[640,128]{1,0:T(8,128)S(1)}) custom-call(f32[10,512,128]{2,1,0:T(8,128)S(1)} %shard_map.103.part_ref, f32[10,512,128]{2,1,0:T(8,128)S(1)} %get-tuple-element.44.q_ref.rest_6_, f32[10,512,128]{2,1,0:T(8,128)S(1)} %get-tuple-element.57.q1_ref, f32[2,512,128]{2,1,0:T(8,128)S(1)} %get-tuple-element.53.vel_ref.rest_7_, ...), custom_call_target="tpu_custom_call" | custom-call | flops 19660800 | bytes 12000000 | tf_op jit(solution)/shard_map/pallas_call | solution.py:490
  45.2 4.4 %collective-permute-done.17.far_ref = f32[640,128]{1,0:T(8,128)S(1)} collective-permute-done((f32[640,128]{1,0:T(8,128)S(1)}, f32[640,128]{1,0:T(8,128)S(1)}, u32[]{:S(2)}, u32[]{:S(2)}) %collective-permute-start.17) | collective-permute-done | bytes 327712 | tf_op jit(solution)/shard_map/ppermute | solution.py:517
  49.6 0.9 %shard_map.109 = f32[10,64,8,128]{3,2,1,0:T(8,128)} custom-call(f32[10,64,8,128]{3,2,1,0:T(8,128)} %bitcast.21, f32[640,128]{1,0:T(8,128)S(1)} %get-tuple-element.81.keep_ref, f32[640,128]{1,0:T(8,128)S(1)} %collective-permute-done.16.core_ref, f32[640,128]{1,0:T(8,128)S(1)} %collective-permute-done.17.far_ref), custom_call_target="tpu_custom_call", output_to_operand_aliasing={{}: (0, {})} | custom-call | tf_op jit(solution)/shard_map/pallas_call | solution.py:490
  (22 shorter events, 0.2 us)
Async XLA Ops:
  2.3 6.7 %collective-permute-start = (f32[640,128]{1,0:T(8,128)S(1)}, f32[640,128]{1,0:T(8,128)S(1)}, u32[]{:S(2)}, u32[]{:S(2)}) collective-permute-start(f32[640,128]{1,0:T(8,128)S(1)} %get-tuple-element.46), channel_id=1, source_target_pairs={{0,1},{1,0},{2,3},{3,2},{4,5},{5,4},{6,7},{7,6},{8,9},{9,8},{10,11... | collective-permute-start | bytes 983048 | tf_op jit(solution)/shard_map/ppermute | solution.py:517
  3.0 12.5 %collective-permute-start.1 = (f32[664,128]{1,0:T(8,128)S(1)}, f32[664,128]{1,0:T(8,128)S(1)}, u32[]{:S(2)}, u32[]{:S(2)}) collective-permute-start(f32[664,128]{1,0:T(8,128)S(1)} %get-tuple-element.48), channel_id=1, source_target_pairs={{1,9},{3,11},{5,13},{7,15},{9,17},{11,19},{13,21},{15,23},{17,25},... | collective-permute-start | bytes 1019912 | tf_op jit(solution)/shard_map/ppermute | solution.py:517
  5.4 10.1 %collective-permute-start.2 = (f32[344,128]{1,0:T(8,128)S(1)}, f32[344,128]{1,0:T(8,128)S(1)}, u32[]{:S(2)}, u32[]{:S(2)}) collective-permute-start(f32[344,128]{1,0:T(8,128)S(1)} %get-tuple-element.49), channel_id=1, source_target_pairs={{1,17},{3,19},{5,21},{7,23},{9,25},{11,27},{13,29},{15,31},{17,1},... | collective-permute-start | bytes 528392 | tf_op jit(solution)/shard_map/ppermute | solution.py:517
  6.9 8.5 %collective-permute-start.3 = (f32[344,128]{1,0:T(8,128)S(1)}, f32[344,128]{1,0:T(8,128)S(1)}, u32[]{:S(2)}, u32[]{:S(2)}) collective-permute-start(f32[344,128]{1,0:T(8,128)S(1)} %get-tuple-element.50), channel_id=1, source_target_pairs={{1,25},{3,27},{5,29},{7,31},{9,1},{11,3},{13,5},{15,7},{17,9},{19,... | collective-permute-start | bytes 528392 | tf_op jit(solution)/shard_map/ppermute | solution.py:517
  8.4 6.8 %collective-permute-start.4 = (f32[88,128]{1,0:T(8,128)S(1)}, f32[88,128]{1,0:T(8,128)S(1)}, u32[]{:S(2)}, u32[]{:S(2)}) collective-permute-start(f32[88,128]{1,0:T(8,128)S(1)} %get-tuple-element.51), channel_id=1, source_target_pairs={{0,8},{1,9},{2,10},{3,11},{4,12},{5,13},{6,14},{7,15},{8,16},{9,17... | collective-permute-start | bytes 135176 | tf_op jit(solution)/shard_map/ppermute | solution.py:517
  9.0 7.3 %collective-permute-start.5 = (f32[88,128]{1,0:T(8,128)S(1)}, f32[88,128]{1,0:T(8,128)S(1)}, u32[]{:S(2)}, u32[]{:S(2)}) collective-permute-start(f32[88,128]{1,0:T(8,128)S(1)} %get-tuple-element.52), channel_id=1, source_target_pairs={{0,24},{1,25},{2,26},{3,27},{4,28},{5,29},{6,30},{7,31},{8,0},{9,1... | collective-permute-start | bytes 135176 | tf_op jit(solution)/shard_map/ppermute | solution.py:517
  11.3 4.9 %copy-start = (f32[10,1,8192]{2,1,0:T(1,128)S(1)}, f32[10,1,8192]{2,1,0:T(1,128)}, u32[]{:S(2)}) copy-start(f32[10,1,8192]{2,1,0:T(1,128)} %param.12) | copy-start | bytes 983044
  11.3 4.9 %copy-start.1 = (s32[8,1]{0,1:T(1,128)S(1)}, s32[8,1]{0,1:T(1,128)}, u32[]{:S(2)}) copy-start(s32[8,1]{0,1:T(1,128)} %param.17) | copy-start | bytes 100
  11.3 4.9 %copy-start.2 = (s32[8]{0:T(128)S(1)}, s32[8]{0:T(128)}, u32[]{:S(2)}) copy-start(s32[8]{0:T(128)} %rest_11_.1) | copy-start | bytes 100
  11.3 4.9 %copy-start.3 = (s32[8]{0:T(128)S(1)}, s32[8]{0:T(128)}, u32[]{:S(2)}) copy-start(s32[8]{0:T(128)} %rest_12_.1) | copy-start | bytes 100
  17.2 8.1 %collective-permute-start.6 = (f32[320,128]{1,0:T(8,128)S(1)}, f32[320,128]{1,0:T(8,128)S(1)}, u32[]{:S(2)}, u32[]{:S(2)}) collective-permute-start(f32[320,128]{1,0:T(8,128)S(1)} %get-tuple-element.60), channel_id=1, source_target_pairs={{1,9},{3,11},{5,13},{7,15},{9,17},{11,19},{13,21},{15,23},{17,25},... | collective-permute-start | bytes 491528 | tf_op jit(solution)/shard_map/ppermute | solution.py:517
  17.2 8.0 %collective-permute-start.7 = (f32[320,128]{1,0:T(8,128)S(1)}, f32[320,128]{1,0:T(8,128)S(1)}, u32[]{:S(2)}, u32[]{:S(2)}) collective-permute-start(f32[320,128]{1,0:T(8,128)S(1)} %get-tuple-element.61), channel_id=1, source_target_pairs={{1,17},{3,19},{5,21},{7,23},{9,25},{11,27},{13,29},{15,31},{17,1},... | collective-permute-start | bytes 491528 | tf_op jit(solution)/shard_map/ppermute | solution.py:517
  19.2 7.4 %collective-permute-start.8 = (f32[320,128]{1,0:T(8,128)S(1)}, f32[320,128]{1,0:T(8,128)S(1)}, u32[]{:S(2)}, u32[]{:S(2)}) collective-permute-start(f32[320,128]{1,0:T(8,128)S(1)} %get-tuple-element.62), channel_id=1, source_target_pairs={{1,25},{3,27},{5,29},{7,31},{9,1},{11,3},{13,5},{15,7},{17,9},{19,... | collective-permute-start | bytes 491528 | tf_op jit(solution)/shard_map/ppermute | solution.py:517
  21.6 5.8 %collective-permute-start.13 = (f32[656,128]{1,0:T(8,128)S(1)}, f32[656,128]{1,0:T(8,128)S(1)}, u32[]{:S(2)}, u32[]{:S(2)}) collective-permute-start(f32[656,128]{1,0:T(8,128)S(1)} %get-tuple-element.76), channel_id=1, source_target_pairs={{5,2},{13,10},{21,18},{29,26}} | collective-permute-start | bytes 1007624 | tf_op jit(solution)/shard_map/ppermute | solution.py:517
  22.3 5.1 %collective-permute-start.9 = (f32[656,128]{1,0:T(8,128)S(1)}, f32[656,128]{1,0:T(8,128)S(1)}, u32[]{:S(2)}, u32[]{:S(2)}) collective-permute-start(f32[656,128]{1,0:T(8,128)S(1)} %get-tuple-element.76), channel_id=1, source_target_pairs={{0,1},{1,0},{2,3},{3,2},{4,5},{5,4},{6,7},{7,6},{8,9},{9,8},{10,11... | collective-permute-start | bytes 1007624 | tf_op jit(solution)/shard_map/ppermute | solution.py:517
  26.7 0.7 %collective-permute-start.14 = (f32[656,128]{1,0:T(8,128)S(1)}, f32[656,128]{1,0:T(8,128)S(1)}, u32[]{:S(2)}, u32[]{:S(2)}) collective-permute-start(f32[656,128]{1,0:T(8,128)S(1)} %get-tuple-element.76), channel_id=1, source_target_pairs={{7,2},{15,10},{23,18},{31,26}} | collective-permute-start | bytes 1007624 | tf_op jit(solution)/shard_map/ppermute | solution.py:517
  27.5 15.3 %collective-permute-start.15 = (f32[656,128]{1,0:T(8,128)S(1)}, f32[656,128]{1,0:T(8,128)S(1)}, u32[]{:S(2)}, u32[]{:S(2)}) collective-permute-start(f32[656,128]{1,0:T(8,128)S(1)} %shard_map.106.near_ref), channel_id=1, source_target_pairs={{2,0},{10,8},{18,16},{26,24}} | collective-permute-start | bytes 1007624 | tf_op jit(solution)/shard_map/ppermute | solution.py:517
  28.8 3.7 %collective-permute-start.10 = (f32[640,128]{1,0:T(8,128)S(1)}, f32[640,128]{1,0:T(8,128)S(1)}, u32[]{:S(2)}, u32[]{:S(2)}) collective-permute-start(f32[640,128]{1,0:T(8,128)S(1)} %shard_map.104.refs_0_), channel_id=1, source_target_pairs={{3,1},{7,5},{11,9},{15,13},{19,17},{23,21},{27,25},{31,29},{2,4},{... | collective-permute-start | bytes 983048 | tf_op jit(solution)/shard_map/ppermute | solution.py:517
  29.5 5.2 %collective-permute-start.11 = (f32[80,128]{1,0:T(8,128)S(1)}, f32[80,128]{1,0:T(8,128)S(1)}, u32[]{:S(2)}, u32[]{:S(2)}) collective-permute-start(f32[80,128]{1,0:T(8,128)S(1)} %get-tuple-element.73), channel_id=1, source_target_pairs={{0,8},{1,9},{2,10},{3,11},{4,12},{5,13},{6,14},{7,15},{8,16},{9,17... | collective-permute-start | bytes 122888 | tf_op jit(solution)/shard_map/ppermute | solution.py:517
  31.2 4.0 %collective-permute-start.12 = (f32[80,128]{1,0:T(8,128)S(1)}, f32[80,128]{1,0:T(8,128)S(1)}, u32[]{:S(2)}, u32[]{:S(2)}) collective-permute-start(f32[80,128]{1,0:T(8,128)S(1)} %get-tuple-element.74), channel_id=1, source_target_pairs={{0,24},{1,25},{2,26},{3,27},{4,28},{5,29},{6,30},{7,31},{8,0},{9,1... | collective-permute-start | bytes 122888 | tf_op jit(solution)/shard_map/ppermute | solution.py:517
  32.5 17.1 %collective-permute-start.17 = (f32[640,128]{1,0:T(8,128)S(1)}, f32[640,128]{1,0:T(8,128)S(1)}, u32[]{:S(2)}, u32[]{:S(2)}) collective-permute-start(f32[640,128]{1,0:T(8,128)S(1)} %shard_map.105.pair_ref), channel_id=1, source_target_pairs={{5,0},{13,8},{21,16},{29,24}} | collective-permute-start | bytes 983048 | tf_op jit(solution)/shard_map/ppermute | solution.py:517
  42.9 6.7 %collective-permute-start.16 = (f32[640,128]{1,0:T(8,128)S(1)}, f32[640,128]{1,0:T(8,128)S(1)}, u32[]{:S(2)}, u32[]{:S(2)}) collective-permute-start(f32[640,128]{1,0:T(8,128)S(1)} %get-tuple-element.82), channel_id=1, source_target_pairs={{0,1},{1,0},{2,3},{3,2},{4,5},{5,4},{6,7},{7,6},{8,9},{9,8},{10,11... | collective-permute-start | bytes 983048 | tf_op jit(solution)/shard_map/ppermute | solution.py:517

commit v9 on v8

--- a/solution.py
+++ b/solution.py
@@ -23,6 +23,10 @@
 
 def roles():
     return lax.axis_index("az"), lax.axis_index("ax"), lax.axis_index("pl")
+
+
+def shifts_of(n_az):
+    return [n_az // 2] + [s for s in range(1, n_az) if s != n_az // 2]
 
 
 def low_half():
@@ -85,6 +89,7 @@
     n = q_ref.shape[1] // CAX
     rows = NV * n
     refs = (own_ref,) + tuple(out_refs)
+    turns = [0] + shifts_of(n_az)
     beside_at = [rows] + [ref.shape[0] - CAX - EXT for ref in out_refs]
 
     @pl.when(plen == 1)
@@ -121,8 +126,8 @@
         for b in range(blocks):
             tile, opened = slot_ref[b], open_ref[b] != 0
             ahead = (col_ref[b] - az + n_az) % n_az
-            for shift, ref in enumerate(refs):
-                here = jnp.logical_and(ahead == shift, opened)
+            for shift, (turn, ref) in enumerate(zip(turns, refs)):
+                here = jnp.logical_and(ahead == turn, opened)
                 tables[shift] = jnp.where(sub == jnp.where(here, used[shift], CAX), tile.astype(f32), tables[shift])
 
                 @pl.when(here)
@@ -140,8 +145,8 @@
             def beside(end, step, row, keep_left, b=b, tile=tile, opened=opened, ahead=ahead):
                 @pl.when(jnp.logical_and(opened, tile == end))
                 def _():
-                    for shift, ref in enumerate(refs):
-                        @pl.when(ahead == (shift + step) % n_az)
+                    for shift, (turn, ref) in enumerate(zip(turns, refs)):
+                        @pl.when(ahead == (turn + step) % n_az)
                         def _(ref=ref, at=beside_at[shift]):
                             for v in range(NV):
                                 cell = q_ref[v, pl.ds(row, 1), :]
@@ -356,7 +361,7 @@
                     own_ref[at, :] += block(q1_ref, v, b)
 
             for k, ref in enumerate(out_refs):
-                here = jnp.logical_and(opened, ahead == k + 1)
+                here = jnp.logical_and(opened, ahead == shifts_of(n_az)[k])
 
                 @pl.when(here)
                 def _(ref=ref, b=b, slot=used[k]):
@@ -528,18 +533,22 @@
     cap = CAX // 4 if n_az > 4 else CAX // 2
     pieces = CAX // cap
 
+    shifts = shifts_of(n_az)
+
     def first(k):
-        out = [((i, j, 1), ((i + k + 1) % n_az, j, 1)) for i, j in every]
+        out = [((i, j, 1), ((i + shifts[k]) % n_az, j, 1)) for i, j in every]
         for i, j in every:
-            along = k == 0 or (k <= pieces and 0 < j < n_ax - 1)
-            out.append(((i, j, 0), (i, mate(min(k, 1), j), 0) if along else ((i + k + 1) % n_az, j, 0)))
+            inside = 0 < j < n_ax - 1
+            if k == 0 or (k <= pieces and (inside or k % 2 == 0)):
+                to = (i, mate(min(k, 1), j), 0)
+            else:
+                to = (i ^ 1, j, 0)
+            out.append(((i, j, 0), to))
         return out
 
     def compact(k):
-        out = [((i, j, 1), ((i + k + 1) % n_az, j, 1)) for i, j in every]
-        if k < pieces:
-            return out + [((i, j, 0), (i, mate(0, j), 0)) for i, j in every]
-        return out + [((i, j, 0), ((i + k + 1) % n_az, j, 0)) for i, j in every]
+        out = [((i, j, 1), ((i + shifts[k]) % n_az, j, 1)) for i, j in every]
+        return out + [((i, j, 0), (i, mate(0, j), 0) if k < pieces else (i ^ 1, j, 0)) for i, j in every]
 
     q, vel = view(cells[0]), view(speeds[0])
     sup = supply.reshape(rows, LANES)
@@ -578,11 +587,11 @@
     inner = [((i, j, 0), (i, mate(1, j), 0)) for i, j in every if 0 < j < n_ax - 1]
     rb = [send(x, compact(k)) for k, x in enumerate(outs)]
     core_in = send(core, swap)
-    down0 = send(core, [((i, 2, 1), (i, 1, 0)) for i in range(n_az)])
+    down0 = send(core, [((i, 3, 1), (i, 1, 0)) for i in range(n_az)])
 
     part, = call(inside_two_kernel, (qv, q1, velv, matrix, power), "vvvvv", [whole], cost=work)
     part, own1, late, rb = lax.optimization_barrier((part, own1, core, rb))
-    down1 = send(late, [((i, 3, 1), (i, 1, 0)) for i in range(n_az)])
+    down1 = send(late, [((i, 2, 1), (i, 1, 0)) for i in range(n_az)])
     step, = call(functools.partial(tile_kernel, n_out, cap), (own1, z1, *rb, *ra), "v" * (2 + 2 * n_out), [row])
     step_in = send(step, down + inner)
     er, el, core_in, step = lax.optimization_barrier((er, el, core_in, step))

time: 50.8 us -> 49.3 us (0.970)
  waiting for transfers between devices: 17.3 us -> 15.4 us
    ppermute x18, waiting for transfers between devices: 17.3 us -> 15.4 us  [send(): return lax.ppermute(x, AXES, [(number(*a), number(*b)) for a, b in route])]
  transfers between devices with their start and end apart: 18 -> 18, of which waited for: 8 -> 8; matrix products, arithmetic and copies ran while one was open for 0% -> 0% of each run, Pallas kernels for 15% -> 16%
where the time goes in v9:
time: 49.3 us; the launch traced here: 49.1 us
  starting transfers between devices  21.7 us (44%)
  waiting for transfers between devices  15.4 us (31%)
  Pallas kernels  11.8 us (24%)
    ppermute x18, starting transfers between devices, send(): return lax.ppermute(x, AXES, [(number(*a), number(*b)) for a, b in route])  21.7 us
    ppermute x18, waiting for transfers between devices, send(): return lax.ppermute(x, AXES, [(number(*a), number(*b)) for a, b in route])  15.4 us
    pallas_call x10, Pallas kernels, call(): pl.pallas_call(kernel, in_specs=[pl.BlockSpec(memory_space=SPACES[k]) for...  11.8 us
  transfers between devices with their start and end apart: 18, of which 8 were waited for; matrix products, arithmetic and copies ran while one was open for 0% of the time, Pallas kernels for 16%

profile of v9, /device:TPU:0, one launch (start us, length us, event | category | flops | bytes accessed | tf_op | source)
XLA Modules:
  0.0 49.1 jit_solution(12794987278721078320)
XLA Ops:
  0.0 2.2 %shard_map.100 = (f32[664,128]{1,0:T(8,128)S(1)}, f32[344,128]{1,0:T(8,128)S(1)}, f32[344,128]{1,0:T(8,128)S(1)}, f32[10,512,128]{2,1,0:T(8,128)S(1)}, f32[2,512...) custom-call(f32[10,512,128]{2,1,0:T(8,128)} %bitcast.20, ...), custom_call_target="tpu_custom_call" | custom-call | tf_op jit(solution)/shard_map/pallas_call | solution.py:495
  2.3 0.7 %collective-permute-start = (f32[640,128]{1,0:T(8,128)S(1)}, f32[640,128]{1,0:T(8,128)S(1)}, u32[]{:S(2)}, u32[]{:S(2)}) collective-permute-start(f32[640,128]{1,0:T(8,128)S(1)} %get-tuple-element.46), channel_id=1, source_target_pairs={{0,1},{1,0},{2,3},{3,2},{4,5},{5,4},{6,7},{7,6},{8,9},{9,8},{10,11... | collective-permute-start | bytes 983048 | tf_op jit(solution)/shard_map/ppermute | solution.py:522
  2.9 2.5 %collective-permute-start.1 = (f32[664,128]{1,0:T(8,128)S(1)}, f32[664,128]{1,0:T(8,128)S(1)}, u32[]{:S(2)}, u32[]{:S(2)}) collective-permute-start(f32[664,128]{1,0:T(8,128)S(1)} %get-tuple-element.48), channel_id=1, source_target_pairs={{1,17},{3,19},{5,21},{7,23},{9,25},{11,27},{13,29},{15,31},{17,1},... | collective-permute-start | bytes 1019912 | tf_op jit(solution)/shard_map/ppermute | solution.py:522
  5.4 1.5 %collective-permute-start.2 = (f32[344,128]{1,0:T(8,128)S(1)}, f32[344,128]{1,0:T(8,128)S(1)}, u32[]{:S(2)}, u32[]{:S(2)}) collective-permute-start(f32[344,128]{1,0:T(8,128)S(1)} %get-tuple-element.49), channel_id=1, source_target_pairs={{1,9},{3,11},{5,13},{7,15},{9,17},{11,19},{13,21},{15,23},{17,25},... | collective-permute-start | bytes 528392 | tf_op jit(solution)/shard_map/ppermute | solution.py:522
  6.9 2.5 %collective-permute-start.3 = (f32[344,128]{1,0:T(8,128)S(1)}, f32[344,128]{1,0:T(8,128)S(1)}, u32[]{:S(2)}, u32[]{:S(2)}) collective-permute-start(f32[344,128]{1,0:T(8,128)S(1)} %get-tuple-element.50), channel_id=1, source_target_pairs={{1,25},{3,27},{5,29},{7,31},{9,1},{11,3},{13,5},{15,7},{17,9},{19,... | collective-permute-start | bytes 528392 | tf_op jit(solution)/shard_map/ppermute | solution.py:522
  9.4 0.5 %collective-permute-start.4 = (f32[88,128]{1,0:T(8,128)S(1)}, f32[88,128]{1,0:T(8,128)S(1)}, u32[]{:S(2)}, u32[]{:S(2)}) collective-permute-start(f32[88,128]{1,0:T(8,128)S(1)} %get-tuple-element.51), channel_id=1, source_target_pairs={{0,8},{1,9},{2,10},{3,11},{4,12},{5,13},{6,14},{7,15},{8,16},{9,17... | collective-permute-start | bytes 135176 | tf_op jit(solution)/shard_map/ppermute | solution.py:522
  9.9 2.4 %collective-permute-start.5 = (f32[88,128]{1,0:T(8,128)S(1)}, f32[88,128]{1,0:T(8,128)S(1)}, u32[]{:S(2)}, u32[]{:S(2)}) collective-permute-start(f32[88,128]{1,0:T(8,128)S(1)} %get-tuple-element.52), channel_id=1, source_target_pairs={{0,24},{1,25},{2,26},{3,27},{4,28},{5,29},{6,30},{7,31},{8,0},{9,1... | collective-permute-start | bytes 135176 | tf_op jit(solution)/shard_map/ppermute | solution.py:522
  12.3 2.4 %shard_map.101.rest_5_ = f32[10,512,128]{2,1,0:T(8,128)S(1)} custom-call(f32[10,512,128]{2,1,0:T(8,128)S(1)} %get-tuple-element.44.q_ref.rest_6_, f32[2,512,128]{2,1,0:T(8,128)S(1)} %get-tuple-element.53.vel_ref.rest_7_, f32[80,240]{1,0:T(8,128)S(1)} %get-tuple-element.54.a_ref.rest_2_, f32[72,128]{1,0:T(8,128)S(1)} %get-tuple-element.55.power_ref.rest_3_), custom_call_target="tpu_custom_call" | custom-call | flops 19660800 | bytes 12000000 | tf_op jit(solution)/shard_map/pallas_call | solution.py:495
  14.8 0.1 collective-permute-done.4.rest_3_.hl0_ref
  14.9 0.2 collective-permute-done.3.rest_2_.rest_5_
  15.1 0.4 collective-permute-done.5.rest_4_.hr0_ref
  15.5 0.9 %shard_map.102 = (f32[320,128]{1,0:T(8,128)S(1)}, f32[320,128]{1,0:T(8,128)S(1)}, f32[320,128]{1,0:T(8,128)S(1)}, f32[10,512,128]{2,1,0:T(8,128)S(1)}, f32[656,1...) custom-call(f32[640,128]{1,0:T(8,128)S(1)} %collective-permute-done., ...), custom_call_target="tpu_custom_call" | custom-call | tf_op jit(solution)/shard_map/pallas_call | solution.py:495
  16.4 0.5 %collective-permute-start.6 = (f32[320,128]{1,0:T(8,128)S(1)}, f32[320,128]{1,0:T(8,128)S(1)}, u32[]{:S(2)}, u32[]{:S(2)}) collective-permute-start(f32[320,128]{1,0:T(8,128)S(1)} %get-tuple-element.60), channel_id=1, source_target_pairs={{1,17},{3,19},{5,21},{7,23},{9,25},{11,27},{13,29},{15,31},{17,1},... | collective-permute-start | bytes 491528 | tf_op jit(solution)/shard_map/ppermute | solution.py:522
  16.9 1.6 %collective-permute-start.7 = (f32[320,128]{1,0:T(8,128)S(1)}, f32[320,128]{1,0:T(8,128)S(1)}, u32[]{:S(2)}, u32[]{:S(2)}) collective-permute-start(f32[320,128]{1,0:T(8,128)S(1)} %get-tuple-element.61), channel_id=1, source_target_pairs={{1,9},{3,11},{5,13},{7,15},{9,17},{11,19},{13,21},{15,23},{17,25},... | collective-permute-start | bytes 491528 | tf_op jit(solution)/shard_map/ppermute | solution.py:522
  18.5 1.8 %collective-permute-start.8 = (f32[320,128]{1,0:T(8,128)S(1)}, f32[320,128]{1,0:T(8,128)S(1)}, u32[]{:S(2)}, u32[]{:S(2)}) collective-permute-start(f32[320,128]{1,0:T(8,128)S(1)} %get-tuple-element.62), channel_id=1, source_target_pairs={{1,25},{3,27},{5,29},{7,31},{9,1},{11,3},{13,5},{15,7},{17,9},{19,... | collective-permute-start | bytes 491528 | tf_op jit(solution)/shard_map/ppermute | solution.py:522
  20.3 0.7 %collective-permute-start.13 = (f32[656,128]{1,0:T(8,128)S(1)}, f32[656,128]{1,0:T(8,128)S(1)}, u32[]{:S(2)}, u32[]{:S(2)}) collective-permute-start(f32[656,128]{1,0:T(8,128)S(1)} %get-tuple-element.76), channel_id=1, source_target_pairs={{7,2},{15,10},{23,18},{31,26}} | collective-permute-start | bytes 1007624 | tf_op jit(solution)/shard_map/ppermute | solution.py:522
  21.0 0.1 collective-permute-start.9
  21.1 2.8 %shard_map.103.part_ref = f32[10,512,128]{2,1,0:T(8,128)S(1)} custom-call(f32[10,512,128]{2,1,0:T(8,128)S(1)} %get-tuple-element.44.q_ref.rest_6_, f32[10,512,128]{2,1,0:T(8,128)S(1)} %get-tuple-element.57.q1_ref, f32[2,512,128]{2,1,0:T(8,128)S(1)} %get-tuple-element.53.vel_ref.rest_7_, f32[80,240]{1,0:T(8,128)S(1)} %get-tuple-element.54.a_ref.rest_2_, ...), custom_call_target="tpu_custom_call" | custom-call | flops 19660800 | bytes 12000000 | tf_op jit(solution)/shard_map/pallas_call | solution.py:495
  23.9 1.6 %collective-permute-done.8.rest_2_ = f32[320,128]{1,0:T(8,128)S(1)} collective-permute-done((f32[320,128]{1,0:T(8,128)S(1)}, f32[320,128]{1,0:T(8,128)S(1)}, u32[]{:S(2)}, u32[]{:S(2)}) %collective-permute-start.8) | collective-permute-done | bytes 163872 | tf_op jit(solution)/shard_map/ppermute | solution.py:522
  25.6 0.7 %collective-permute-start.14 = (f32[656,128]{1,0:T(8,128)S(1)}, f32[656,128]{1,0:T(8,128)S(1)}, u32[]{:S(2)}, u32[]{:S(2)}) collective-permute-start(f32[656,128]{1,0:T(8,128)S(1)} %get-tuple-element.76), channel_id=1, source_target_pairs={{5,2},{13,10},{21,18},{29,26}} | collective-permute-start | bytes 1007624 | tf_op jit(solution)/shard_map/ppermute | solution.py:522
  26.4 1.3 %collective-permute-start.15 = (f32[656,128]{1,0:T(8,128)S(1)}, f32[656,128]{1,0:T(8,128)S(1)}, u32[]{:S(2)}, u32[]{:S(2)}) collective-permute-start(f32[656,128]{1,0:T(8,128)S(1)} %shard_map.106.near_ref), channel_id=1, source_target_pairs={{2,0},{10,8},{18,16},{26,24}} | collective-permute-start | bytes 1007624 | tf_op jit(solution)/shard_map/ppermute | solution.py:522
  27.7 0.7 %collective-permute-start.10 = (f32[640,128]{1,0:T(8,128)S(1)}, f32[640,128]{1,0:T(8,128)S(1)}, u32[]{:S(2)}, u32[]{:S(2)}) collective-permute-start(f32[640,128]{1,0:T(8,128)S(1)} %shard_map.104.refs_0_), channel_id=1, source_target_pairs={{3,1},{7,5},{11,9},{15,13},{19,17},{23,21},{27,25},{31,29},{2,4},{... | collective-permute-start | bytes 983048 | tf_op jit(solution)/shard_map/ppermute | solution.py:522
  28.4 1.9 %collective-permute-start.11 = (f32[80,128]{1,0:T(8,128)S(1)}, f32[80,128]{1,0:T(8,128)S(1)}, u32[]{:S(2)}, u32[]{:S(2)}) collective-permute-start(f32[80,128]{1,0:T(8,128)S(1)} %get-tuple-element.73), channel_id=1, source_target_pairs={{0,8},{1,9},{2,10},{3,11},{4,12},{5,13},{6,14},{7,15},{8,16},{9,17... | collective-permute-start | bytes 122888 | tf_op jit(solution)/shard_map/ppermute | solution.py:522
  30.2 1.1 %collective-permute-start.12 = (f32[80,128]{1,0:T(8,128)S(1)}, f32[80,128]{1,0:T(8,128)S(1)}, u32[]{:S(2)}, u32[]{:S(2)}) collective-permute-start(f32[80,128]{1,0:T(8,128)S(1)} %get-tuple-element.74), channel_id=1, source_target_pairs={{0,24},{1,25},{2,26},{3,27},{4,28},{5,29},{6,30},{7,31},{8,0},{9,1... | collective-permute-start | bytes 122888 | tf_op jit(solution)/shard_map/ppermute | solution.py:522
  31.4 1.3 %collective-permute-start.17 = (f32[640,128]{1,0:T(8,128)S(1)}, f32[640,128]{1,0:T(8,128)S(1)}, u32[]{:S(2)}, u32[]{:S(2)}) collective-permute-start(f32[640,128]{1,0:T(8,128)S(1)} %shard_map.105.pair_ref), channel_id=1, source_target_pairs={{5,0},{13,8},{21,16},{29,24}} | collective-permute-start | bytes 983048 | tf_op jit(solution)/shard_map/ppermute | solution.py:522
  32.7 1.1 %collective-permute-done.11.hl_ref = f32[80,128]{1,0:T(8,128)S(1)} collective-permute-done((f32[80,128]{1,0:T(8,128)S(1)}, f32[80,128]{1,0:T(8,128)S(1)}, u32[]{:S(2)}, u32[]{:S(2)}) %collective-permute-start.11) | collective-permute-done | bytes 40992 | tf_op jit(solution)/shard_map/ppermute | solution.py:522
  33.8 0.5 collective-permute-done.12.hr_ref
  34.2 6.8 %collective-permute-done.15.far_ref = f32[656,128]{1,0:T(8,128)S(1)} collective-permute-done((f32[656,128]{1,0:T(8,128)S(1)}, f32[656,128]{1,0:T(8,128)S(1)}, u32[]{:S(2)}, u32[]{:S(2)}) %collective-permute-start.15) | collective-permute-done | bytes 335904 | tf_op jit(solution)/shard_map/ppermute | solution.py:522
  41.1 0.1 collective-permute-start.16
  41.2 2.3 %shard_map.108 = (f32[10,512,128]{2,1,0:T(8,128)}, f32[640,128]{1,0:T(8,128)S(1)}) custom-call(f32[10,512,128]{2,1,0:T(8,128)S(1)} %shard_map.103.part_ref, f32[10,512,128]{2,1,0:T(8,128)S(1)} %get-tuple-element.44.q_ref.rest_6_, f32[10,512,128]{2,1,0:T(8,128)S(1)} %get-tuple-element.57.q1_ref, f32[2,512,128]{2,1,0:T(8,128)S(1)} %get-tuple-element.53.vel_ref.rest_7_, ...), custom_call_target="tpu_custom_call" | custom-call | flops 19660800 | bytes 12000000 | tf_op jit(solution)/shard_map/pallas_call | solution.py:495
  43.4 4.8 %collective-permute-done.17.far_ref = f32[640,128]{1,0:T(8,128)S(1)} collective-permute-done((f32[640,128]{1,0:T(8,128)S(1)}, f32[640,128]{1,0:T(8,128)S(1)}, u32[]{:S(2)}, u32[]{:S(2)}) %collective-permute-start.17) | collective-permute-done | bytes 327712 | tf_op jit(solution)/shard_map/ppermute | solution.py:522
  48.2 0.9 %shard_map.109 = f32[10,64,8,128]{3,2,1,0:T(8,128)} custom-call(f32[10,64,8,128]{3,2,1,0:T(8,128)} %bitcast.21, f32[640,128]{1,0:T(8,128)S(1)} %get-tuple-element.81.keep_ref, f32[640,128]{1,0:T(8,128)S(1)} %collective-permute-done.16.core_ref, f32[640,128]{1,0:T(8,128)S(1)} %collective-permute-done.17.far_ref), custom_call_target="tpu_custom_call", output_to_operand_aliasing={{}: (0, {})} | custom-call | tf_op jit(solution)/shard_map/pallas_call | solution.py:495
  (22 shorter events, 0.3 us)
Async XLA Ops:
  2.3 7.7 %collective-permute-start = (f32[640,128]{1,0:T(8,128)S(1)}, f32[640,128]{1,0:T(8,128)S(1)}, u32[]{:S(2)}, u32[]{:S(2)}) collective-permute-start(f32[640,128]{1,0:T(8,128)S(1)} %get-tuple-element.46), channel_id=1, source_target_pairs={{0,1},{1,0},{2,3},{3,2},{4,5},{5,4},{6,7},{7,6},{8,9},{9,8},{10,11... | collective-permute-start | bytes 983048 | tf_op jit(solution)/shard_map/ppermute | solution.py:522
  2.9 12.1 %collective-permute-start.1 = (f32[664,128]{1,0:T(8,128)S(1)}, f32[664,128]{1,0:T(8,128)S(1)}, u32[]{:S(2)}, u32[]{:S(2)}) collective-permute-start(f32[664,128]{1,0:T(8,128)S(1)} %get-tuple-element.48), channel_id=1, source_target_pairs={{1,17},{3,19},{5,21},{7,23},{9,25},{11,27},{13,29},{15,31},{17,1},... | collective-permute-start | bytes 1019912 | tf_op jit(solution)/shard_map/ppermute | solution.py:522
  5.4 9.5 %collective-permute-start.2 = (f32[344,128]{1,0:T(8,128)S(1)}, f32[344,128]{1,0:T(8,128)S(1)}, u32[]{:S(2)}, u32[]{:S(2)}) collective-permute-start(f32[344,128]{1,0:T(8,128)S(1)} %get-tuple-element.49), channel_id=1, source_target_pairs={{1,9},{3,11},{5,13},{7,15},{9,17},{11,19},{13,21},{15,23},{17,25},... | collective-permute-start | bytes 528392 | tf_op jit(solution)/shard_map/ppermute | solution.py:522
  6.9 8.2 %collective-permute-start.3 = (f32[344,128]{1,0:T(8,128)S(1)}, f32[344,128]{1,0:T(8,128)S(1)}, u32[]{:S(2)}, u32[]{:S(2)}) collective-permute-start(f32[344,128]{1,0:T(8,128)S(1)} %get-tuple-element.50), channel_id=1, source_target_pairs={{1,25},{3,27},{5,29},{7,31},{9,1},{11,3},{13,5},{15,7},{17,9},{19,... | collective-permute-start | bytes 528392 | tf_op jit(solution)/shard_map/ppermute | solution.py:522
  9.4 5.5 %collective-permute-start.4 = (f32[88,128]{1,0:T(8,128)S(1)}, f32[88,128]{1,0:T(8,128)S(1)}, u32[]{:S(2)}, u32[]{:S(2)}) collective-permute-start(f32[88,128]{1,0:T(8,128)S(1)} %get-tuple-element.51), channel_id=1, source_target_pairs={{0,8},{1,9},{2,10},{3,11},{4,12},{5,13},{6,14},{7,15},{8,16},{9,17... | collective-permute-start | bytes 135176 | tf_op jit(solution)/shard_map/ppermute | solution.py:522
  9.9 5.6 %collective-permute-start.5 = (f32[88,128]{1,0:T(8,128)S(1)}, f32[88,128]{1,0:T(8,128)S(1)}, u32[]{:S(2)}, u32[]{:S(2)}) collective-permute-start(f32[88,128]{1,0:T(8,128)S(1)} %get-tuple-element.52), channel_id=1, source_target_pairs={{0,24},{1,25},{2,26},{3,27},{4,28},{5,29},{6,30},{7,31},{8,0},{9,1... | collective-permute-start | bytes 135176 | tf_op jit(solution)/shard_map/ppermute | solution.py:522
  12.3 3.2 %copy-start = (f32[10,1,8192]{2,1,0:T(1,128)S(1)}, f32[10,1,8192]{2,1,0:T(1,128)}, u32[]{:S(2)}) copy-start(f32[10,1,8192]{2,1,0:T(1,128)} %param.12) | copy-start | bytes 983044
  12.3 3.2 %copy-start.1 = (s32[8,1]{0,1:T(1,128)S(1)}, s32[8,1]{0,1:T(1,128)}, u32[]{:S(2)}) copy-start(s32[8,1]{0,1:T(1,128)} %param.17) | copy-start | bytes 100
  12.3 3.2 %copy-start.2 = (s32[8]{0:T(128)S(1)}, s32[8]{0:T(128)}, u32[]{:S(2)}) copy-start(s32[8]{0:T(128)} %rest_11_.1) | copy-start | bytes 100
  12.3 3.2 %copy-start.3 = (s32[8]{0:T(128)S(1)}, s32[8]{0:T(128)}, u32[]{:S(2)}) copy-start(s32[8]{0:T(128)} %rest_12_.1) | copy-start | bytes 100
  16.4 7.5 %collective-permute-start.6 = (f32[320,128]{1,0:T(8,128)S(1)}, f32[320,128]{1,0:T(8,128)S(1)}, u32[]{:S(2)}, u32[]{:S(2)}) collective-permute-start(f32[320,128]{1,0:T(8,128)S(1)} %get-tuple-element.60), channel_id=1, source_target_pairs={{1,17},{3,19},{5,21},{7,23},{9,25},{11,27},{13,29},{15,31},{17,1},... | collective-permute-start | bytes 491528 | tf_op jit(solution)/shard_map/ppermute | solution.py:522
  16.9 7.0 %collective-permute-start.7 = (f32[320,128]{1,0:T(8,128)S(1)}, f32[320,128]{1,0:T(8,128)S(1)}, u32[]{:S(2)}, u32[]{:S(2)}) collective-permute-start(f32[320,128]{1,0:T(8,128)S(1)} %get-tuple-element.61), channel_id=1, source_target_pairs={{1,9},{3,11},{5,13},{7,15},{9,17},{11,19},{13,21},{15,23},{17,25},... | collective-permute-start | bytes 491528 | tf_op jit(solution)/shard_map/ppermute | solution.py:522
  18.5 7.1 %collective-permute-start.8 = (f32[320,128]{1,0:T(8,128)S(1)}, f32[320,128]{1,0:T(8,128)S(1)}, u32[]{:S(2)}, u32[]{:S(2)}) collective-permute-start(f32[320,128]{1,0:T(8,128)S(1)} %get-tuple-element.62), channel_id=1, source_target_pairs={{1,25},{3,27},{5,29},{7,31},{9,1},{11,3},{13,5},{15,7},{17,9},{19,... | collective-permute-start | bytes 491528 | tf_op jit(solution)/shard_map/ppermute | solution.py:522
  20.3 6.0 %collective-permute-start.13 = (f32[656,128]{1,0:T(8,128)S(1)}, f32[656,128]{1,0:T(8,128)S(1)}, u32[]{:S(2)}, u32[]{:S(2)}) collective-permute-start(f32[656,128]{1,0:T(8,128)S(1)} %get-tuple-element.76), channel_id=1, source_target_pairs={{7,2},{15,10},{23,18},{31,26}} | collective-permute-start | bytes 1007624 | tf_op jit(solution)/shard_map/ppermute | solution.py:522
  21.0 5.3 %collective-permute-start.9 = (f32[656,128]{1,0:T(8,128)S(1)}, f32[656,128]{1,0:T(8,128)S(1)}, u32[]{:S(2)}, u32[]{:S(2)}) collective-permute-start(f32[656,128]{1,0:T(8,128)S(1)} %get-tuple-element.76), channel_id=1, source_target_pairs={{0,1},{1,0},{2,3},{3,2},{4,5},{5,4},{6,7},{7,6},{8,9},{9,8},{10,11... | collective-permute-start | bytes 1007624 | tf_op jit(solution)/shard_map/ppermute | solution.py:522
  25.6 0.7 %collective-permute-start.14 = (f32[656,128]{1,0:T(8,128)S(1)}, f32[656,128]{1,0:T(8,128)S(1)}, u32[]{:S(2)}, u32[]{:S(2)}) collective-permute-start(f32[656,128]{1,0:T(8,128)S(1)} %get-tuple-element.76), channel_id=1, source_target_pairs={{5,2},{13,10},{21,18},{29,26}} | collective-permute-start | bytes 1007624 | tf_op jit(solution)/shard_map/ppermute | solution.py:522
  26.4 14.6 %collective-permute-start.15 = (f32[656,128]{1,0:T(8,128)S(1)}, f32[656,128]{1,0:T(8,128)S(1)}, u32[]{:S(2)}, u32[]{:S(2)}) collective-permute-start(f32[656,128]{1,0:T(8,128)S(1)} %shard_map.106.near_ref), channel_id=1, source_target_pairs={{2,0},{10,8},{18,16},{26,24}} | collective-permute-start | bytes 1007624 | tf_op jit(solution)/shard_map/ppermute | solution.py:522
  27.7 3.7 %collective-permute-start.10 = (f32[640,128]{1,0:T(8,128)S(1)}, f32[640,128]{1,0:T(8,128)S(1)}, u32[]{:S(2)}, u32[]{:S(2)}) collective-permute-start(f32[640,128]{1,0:T(8,128)S(1)} %shard_map.104.refs_0_), channel_id=1, source_target_pairs={{3,1},{7,5},{11,9},{15,13},{19,17},{23,21},{27,25},{31,29},{2,4},{... | collective-permute-start | bytes 983048 | tf_op jit(solution)/shard_map/ppermute | solution.py:522
  28.4 5.4 %collective-permute-start.11 = (f32[80,128]{1,0:T(8,128)S(1)}, f32[80,128]{1,0:T(8,128)S(1)}, u32[]{:S(2)}, u32[]{:S(2)}) collective-permute-start(f32[80,128]{1,0:T(8,128)S(1)} %get-tuple-element.73), channel_id=1, source_target_pairs={{0,8},{1,9},{2,10},{3,11},{4,12},{5,13},{6,14},{7,15},{8,16},{9,17... | collective-permute-start | bytes 122888 | tf_op jit(solution)/shard_map/ppermute | solution.py:522
  30.2 4.0 %collective-permute-start.12 = (f32[80,128]{1,0:T(8,128)S(1)}, f32[80,128]{1,0:T(8,128)S(1)}, u32[]{:S(2)}, u32[]{:S(2)}) collective-permute-start(f32[80,128]{1,0:T(8,128)S(1)} %get-tuple-element.74), channel_id=1, source_target_pairs={{0,24},{1,25},{2,26},{3,27},{4,28},{5,29},{6,30},{7,31},{8,0},{9,1... | collective-permute-start | bytes 122888 | tf_op jit(solution)/shard_map/ppermute | solution.py:522
  31.4 16.8 %collective-permute-start.17 = (f32[640,128]{1,0:T(8,128)S(1)}, f32[640,128]{1,0:T(8,128)S(1)}, u32[]{:S(2)}, u32[]{:S(2)}) collective-permute-start(f32[640,128]{1,0:T(8,128)S(1)} %shard_map.105.pair_ref), channel_id=1, source_target_pairs={{5,0},{13,8},{21,16},{29,24}} | collective-permute-start | bytes 983048 | tf_op jit(solution)/shard_map/ppermute | solution.py:522
  41.1 7.1 %collective-permute-start.16 = (f32[640,128]{1,0:T(8,128)S(1)}, f32[640,128]{1,0:T(8,128)S(1)}, u32[]{:S(2)}, u32[]{:S(2)}) collective-permute-start(f32[640,128]{1,0:T(8,128)S(1)} %get-tuple-element.82), channel_id=1, source_target_pairs={{0,1},{1,0},{2,3},{3,2},{4,5},{5,4},{6,7},{7,6},{8,9},{9,8},{10,11... | collective-permute-start | bytes 983048 | tf_op jit(solution)/shard_map/ppermute | solution.py:522

commit v10 on v9

--- a/solution.py
+++ b/solution.py
@@ -587,17 +587,16 @@
     inner = [((i, j, 0), (i, mate(1, j), 0)) for i, j in every if 0 < j < n_ax - 1]
     rb = [send(x, compact(k)) for k, x in enumerate(outs)]
     core_in = send(core, swap)
-    down0 = send(core, [((i, 3, 1), (i, 1, 0)) for i in range(n_az)])
+    down0 = send(core, [((i, j, 1), (i, j - 1, 0)) for i, j in every if j % 2 == 1])
 
     part, = call(inside_two_kernel, (qv, q1, velv, matrix, power), "vvvvv", [whole], cost=work)
-    part, own1, late, rb = lax.optimization_barrier((part, own1, core, rb))
-    down1 = send(late, [((i, 2, 1), (i, 1, 0)) for i in range(n_az)])
+    part, own1 = lax.optimization_barrier((part, own1))
     step, = call(functools.partial(tile_kernel, n_out, cap), (own1, z1, *rb, *ra), "v" * (2 + 2 * n_out), [row])
     step_in = send(step, down + inner)
     er, el, core_in, step = lax.optimization_barrier((er, el, core_in, step))
     hl1, hr1 = send(er, ring(1)), send(el, ring(-1))
-    pair0, = call(add_kernel, (core_in, down0, down1), "vvv", [wide])
-    far0 = send(pair0, [((i, 1, 0), (i, 0, 0)) for i in range(n_az)])
+    pair0, = call(add_kernel, (core_in, down0), "vv", [wide])
+    far0 = send(pair0, [((i, 2, 0), (i, 0, 0)) for i in range(n_az)])
     pair1, = call(add_kernel, (step, step_in), "vv", [row])
     far1 = send(pair1, across)
     pair1, hl1, hr1 = lax.optimization_barrier((pair1, hl1, hr1))

time: 49.3 us -> 47.5 us (0.963)
  waiting for transfers between devices: 15.4 us -> 12.8 us
  starting transfers between devices: 21.7 us -> 22.6 us
    ppermute x18 -> x17, waiting for transfers between devices: 15.4 us -> 12.8 us  [send(): return lax.ppermute(x, AXES, [(number(*a), number(*b)) for a, b in route])]
    ppermute x18 -> x17, starting transfers between devices: 21.7 us -> 22.6 us  [send(): return lax.ppermute(x, AXES, [(number(*a), number(*b)) for a, b in route])]
  transfers between devices with their start and end apart: 18 -> 17, of which waited for: 8 -> 9; matrix products, arithmetic and copies ran while one was open for 0% -> 0% of each run, Pallas kernels for 16% -> 16%
where the time goes in v10:
time: 47.5 us; the launch traced here: 47.3 us
  starting transfers between devices  22.6 us (48%)
  waiting for transfers between devices  12.8 us (27%)
  Pallas kernels  11.7 us (25%)
    ppermute x17, starting transfers between devices, send(): return lax.ppermute(x, AXES, [(number(*a), number(*b)) for a, b in route])  22.6 us
    ppermute x17, waiting for transfers between devices, send(): return lax.ppermute(x, AXES, [(number(*a), number(*b)) for a, b in route])  12.8 us
    pallas_call x10, Pallas kernels, call(): pl.pallas_call(kernel, in_specs=[pl.BlockSpec(memory_space=SPACES[k]) for...  11.7 us
  transfers between devices with their start and end apart: 17, of which 9 were waited for; matrix products, arithmetic and copies ran while one was open for 0% of the time, Pallas kernels for 16%

profile of v10, /device:TPU:0, one launch (start us, length us, event | category | flops | bytes accessed | tf_op | source)
XLA Modules:
  0.0 47.3 jit_solution(17988955414252854053)
XLA Ops:
  0.0 2.2 %shard_map.100 = (f32[664,128]{1,0:T(8,128)S(1)}, f32[344,128]{1,0:T(8,128)S(1)}, f32[344,128]{1,0:T(8,128)S(1)}, f32[10,512,128]{2,1,0:T(8,128)S(1)}, f32[2,512...) custom-call(f32[10,512,128]{2,1,0:T(8,128)} %bitcast.20, ...), custom_call_target="tpu_custom_call" | custom-call | tf_op jit(solution)/shard_map/pallas_call | solution.py:495
  2.3 0.7 %collective-permute-start = (f32[640,128]{1,0:T(8,128)S(1)}, f32[640,128]{1,0:T(8,128)S(1)}, u32[]{:S(2)}, u32[]{:S(2)}) collective-permute-start(f32[640,128]{1,0:T(8,128)S(1)} %get-tuple-element.42), channel_id=1, source_target_pairs={{0,1},{1,0},{2,3},{3,2},{4,5},{5,4},{6,7},{7,6},{8,9},{9,8},{10,11... | collective-permute-start | bytes 983048 | tf_op jit(solution)/shard_map/ppermute | solution.py:522
  3.0 2.5 %collective-permute-start.1 = (f32[664,128]{1,0:T(8,128)S(1)}, f32[664,128]{1,0:T(8,128)S(1)}, u32[]{:S(2)}, u32[]{:S(2)}) collective-permute-start(f32[664,128]{1,0:T(8,128)S(1)} %get-tuple-element.44), channel_id=1, source_target_pairs={{1,17},{3,19},{5,21},{7,23},{9,25},{11,27},{13,29},{15,31},{17,1},... | collective-permute-start | bytes 1019912 | tf_op jit(solution)/shard_map/ppermute | solution.py:522
  5.4 1.5 %collective-permute-start.2 = (f32[344,128]{1,0:T(8,128)S(1)}, f32[344,128]{1,0:T(8,128)S(1)}, u32[]{:S(2)}, u32[]{:S(2)}) collective-permute-start(f32[344,128]{1,0:T(8,128)S(1)} %get-tuple-element.45), channel_id=1, source_target_pairs={{1,9},{3,11},{5,13},{7,15},{9,17},{11,19},{13,21},{15,23},{17,25},... | collective-permute-start | bytes 528392 | tf_op jit(solution)/shard_map/ppermute | solution.py:522
  6.9 2.5 %collective-permute-start.3 = (f32[344,128]{1,0:T(8,128)S(1)}, f32[344,128]{1,0:T(8,128)S(1)}, u32[]{:S(2)}, u32[]{:S(2)}) collective-permute-start(f32[344,128]{1,0:T(8,128)S(1)} %get-tuple-element.46), channel_id=1, source_target_pairs={{1,25},{3,27},{5,29},{7,31},{9,1},{11,3},{13,5},{15,7},{17,9},{19,... | collective-permute-start | bytes 528392 | tf_op jit(solution)/shard_map/ppermute | solution.py:522
  9.4 0.5 %collective-permute-start.4 = (f32[88,128]{1,0:T(8,128)S(1)}, f32[88,128]{1,0:T(8,128)S(1)}, u32[]{:S(2)}, u32[]{:S(2)}) collective-permute-start(f32[88,128]{1,0:T(8,128)S(1)} %get-tuple-element.47), channel_id=1, source_target_pairs={{0,8},{1,9},{2,10},{3,11},{4,12},{5,13},{6,14},{7,15},{8,16},{9,17... | collective-permute-start | bytes 135176 | tf_op jit(solution)/shard_map/ppermute | solution.py:522
  9.9 2.4 %collective-permute-start.5 = (f32[88,128]{1,0:T(8,128)S(1)}, f32[88,128]{1,0:T(8,128)S(1)}, u32[]{:S(2)}, u32[]{:S(2)}) collective-permute-start(f32[88,128]{1,0:T(8,128)S(1)} %get-tuple-element.48), channel_id=1, source_target_pairs={{0,24},{1,25},{2,26},{3,27},{4,28},{5,29},{6,30},{7,31},{8,0},{9,1... | collective-permute-start | bytes 135176 | tf_op jit(solution)/shard_map/ppermute | solution.py:522
  12.3 2.4 %shard_map.101.rest_5_ = f32[10,512,128]{2,1,0:T(8,128)S(1)} custom-call(f32[10,512,128]{2,1,0:T(8,128)S(1)} %get-tuple-element.40.q_ref.rest_6_, f32[2,512,128]{2,1,0:T(8,128)S(1)} %get-tuple-element.49.vel_ref.rest_7_, f32[80,240]{1,0:T(8,128)S(1)} %get-tuple-element.50.a_ref.rest_2_, f32[72,128]{1,0:T(8,128)S(1)} %get-tuple-element.51.power_ref.rest_3_), custom_call_target="tpu_custom_call" | custom-call | flops 19660800 | bytes 12000000 | tf_op jit(solution)/shard_map/pallas_call | solution.py:495
  14.8 0.1 collective-permute-done.4.rest_3_.hl0_ref
  14.9 0.2 collective-permute-done.3.rest_2_.rest_5_
  15.1 0.4 collective-permute-done.5.rest_4_.hr0_ref
  15.5 0.9 %shard_map.102 = (f32[320,128]{1,0:T(8,128)S(1)}, f32[320,128]{1,0:T(8,128)S(1)}, f32[320,128]{1,0:T(8,128)S(1)}, f32[10,512,128]{2,1,0:T(8,128)S(1)}, f32[656,1...) custom-call(f32[640,128]{1,0:T(8,128)S(1)} %collective-permute-done., ...), custom_call_target="tpu_custom_call" | custom-call | tf_op jit(solution)/shard_map/pallas_call | solution.py:495
  16.4 0.9 %collective-permute-start.6 = (f32[656,128]{1,0:T(8,128)S(1)}, f32[656,128]{1,0:T(8,128)S(1)}, u32[]{:S(2)}, u32[]{:S(2)}) collective-permute-start(f32[656,128]{1,0:T(8,128)S(1)} %get-tuple-element.58), channel_id=1, source_target_pairs={{0,1},{1,0},{2,3},{3,2},{4,5},{5,4},{6,7},{7,6},{8,9},{9,8},{10,11... | collective-permute-start | bytes 1007624 | tf_op jit(solution)/shard_map/ppermute | solution.py:522
  17.3 1.3 %collective-permute-start.13 = (f32[656,128]{1,0:T(8,128)S(1)}, f32[656,128]{1,0:T(8,128)S(1)}, u32[]{:S(2)}, u32[]{:S(2)}) collective-permute-start(f32[656,128]{1,0:T(8,128)S(1)} %get-tuple-element.58), channel_id=1, source_target_pairs={{3,0},{7,4},{11,8},{15,12},{19,16},{23,20},{27,24},{31,28}} | collective-permute-start | bytes 1007624 | tf_op jit(solution)/shard_map/ppermute | solution.py:522
  18.5 0.1 collective-permute-start.7
  18.6 2.0 %collective-permute-start.8 = (f32[320,128]{1,0:T(8,128)S(1)}, f32[320,128]{1,0:T(8,128)S(1)}, u32[]{:S(2)}, u32[]{:S(2)}) collective-permute-start(f32[320,128]{1,0:T(8,128)S(1)} %get-tuple-element.62), channel_id=1, source_target_pairs={{1,9},{3,11},{5,13},{7,15},{9,17},{11,19},{13,21},{15,23},{17,25},... | collective-permute-start | bytes 491528 | tf_op jit(solution)/shard_map/ppermute | solution.py:522
  20.6 1.1 %collective-permute-start.9 = (f32[320,128]{1,0:T(8,128)S(1)}, f32[320,128]{1,0:T(8,128)S(1)}, u32[]{:S(2)}, u32[]{:S(2)}) collective-permute-start(f32[320,128]{1,0:T(8,128)S(1)} %get-tuple-element.63), channel_id=1, source_target_pairs={{1,25},{3,27},{5,29},{7,31},{9,1},{11,3},{13,5},{15,7},{17,9},{19,... | collective-permute-start | bytes 491528 | tf_op jit(solution)/shard_map/ppermute | solution.py:522
  21.7 2.8 %shard_map.103.part_ref = f32[10,512,128]{2,1,0:T(8,128)S(1)} custom-call(f32[10,512,128]{2,1,0:T(8,128)S(1)} %get-tuple-element.40.q_ref.rest_6_, f32[10,512,128]{2,1,0:T(8,128)S(1)} %get-tuple-element.53.q1_ref, f32[2,512,128]{2,1,0:T(8,128)S(1)} %get-tuple-element.49.vel_ref.rest_7_, f32[80,240]{1,0:T(8,128)S(1)} %get-tuple-element.50.a_ref.rest_2_, ...), custom_call_target="tpu_custom_call" | custom-call | flops 19660800 | bytes 12000000 | tf_op jit(solution)/shard_map/pallas_call | solution.py:495
  24.5 1.2 %collective-permute-done.7.rest_0_ = f32[320,128]{1,0:T(8,128)S(1)} collective-permute-done((f32[320,128]{1,0:T(8,128)S(1)}, f32[320,128]{1,0:T(8,128)S(1)}, u32[]{:S(2)}, u32[]{:S(2)}) %collective-permute-start.7) | collective-permute-done | bytes 163872 | tf_op jit(solution)/shard_map/ppermute | solution.py:522
  25.7 3.5 %collective-permute-done.8.rest_1_ = f32[320,128]{1,0:T(8,128)S(1)} collective-permute-done((f32[320,128]{1,0:T(8,128)S(1)}, f32[320,128]{1,0:T(8,128)S(1)}, u32[]{:S(2)}, u32[]{:S(2)}) %collective-permute-start.8) | collective-permute-done | bytes 163872 | tf_op jit(solution)/shard_map/ppermute | solution.py:522
  29.3 1.3 %collective-permute-start.14 = (f32[656,128]{1,0:T(8,128)S(1)}, f32[656,128]{1,0:T(8,128)S(1)}, u32[]{:S(2)}, u32[]{:S(2)}) collective-permute-start(f32[656,128]{1,0:T(8,128)S(1)} %shard_map.106.near_ref), channel_id=1, source_target_pairs={{4,0},{12,8},{20,16},{28,24}} | collective-permute-start | bytes 1007624 | tf_op jit(solution)/shard_map/ppermute | solution.py:522
  30.6 0.7 %collective-permute-start.10 = (f32[640,128]{1,0:T(8,128)S(1)}, f32[640,128]{1,0:T(8,128)S(1)}, u32[]{:S(2)}, u32[]{:S(2)}) collective-permute-start(f32[640,128]{1,0:T(8,128)S(1)} %shard_map.104.refs_0_), channel_id=1, source_target_pairs={{3,1},{7,5},{11,9},{15,13},{19,17},{23,21},{27,25},{31,29},{2,4},{... | collective-permute-start | bytes 983048 | tf_op jit(solution)/shard_map/ppermute | solution.py:522
  31.3 1.1 %collective-permute-start.11 = (f32[80,128]{1,0:T(8,128)S(1)}, f32[80,128]{1,0:T(8,128)S(1)}, u32[]{:S(2)}, u32[]{:S(2)}) collective-permute-start(f32[80,128]{1,0:T(8,128)S(1)} %get-tuple-element.66), channel_id=1, source_target_pairs={{0,8},{1,9},{2,10},{3,11},{4,12},{5,13},{6,14},{7,15},{8,16},{9,17... | collective-permute-start | bytes 122888 | tf_op jit(solution)/shard_map/ppermute | solution.py:522
  32.4 1.9 %collective-permute-start.12 = (f32[80,128]{1,0:T(8,128)S(1)}, f32[80,128]{1,0:T(8,128)S(1)}, u32[]{:S(2)}, u32[]{:S(2)}) collective-permute-start(f32[80,128]{1,0:T(8,128)S(1)} %get-tuple-element.67), channel_id=1, source_target_pairs={{0,24},{1,25},{2,26},{3,27},{4,28},{5,29},{6,30},{7,31},{8,0},{9,1... | collective-permute-start | bytes 122888 | tf_op jit(solution)/shard_map/ppermute | solution.py:522
  34.3 1.3 %collective-permute-start.16 = (f32[640,128]{1,0:T(8,128)S(1)}, f32[640,128]{1,0:T(8,128)S(1)}, u32[]{:S(2)}, u32[]{:S(2)}) collective-permute-start(f32[640,128]{1,0:T(8,128)S(1)} %shard_map.105.pair_ref), channel_id=1, source_target_pairs={{5,0},{13,8},{21,16},{29,24}} | collective-permute-start | bytes 983048 | tf_op jit(solution)/shard_map/ppermute | solution.py:522
  35.6 0.6 %collective-permute-done.11.hl_ref = f32[80,128]{1,0:T(8,128)S(1)} collective-permute-done((f32[80,128]{1,0:T(8,128)S(1)}, f32[80,128]{1,0:T(8,128)S(1)}, u32[]{:S(2)}, u32[]{:S(2)}) %collective-permute-start.11) | collective-permute-done | bytes 40992 | tf_op jit(solution)/shard_map/ppermute | solution.py:522
  36.2 0.2 collective-permute-done.12.hr_ref
  36.4 3.0 %collective-permute-done.14.far_ref = f32[656,128]{1,0:T(8,128)S(1)} collective-permute-done((f32[656,128]{1,0:T(8,128)S(1)}, f32[656,128]{1,0:T(8,128)S(1)}, u32[]{:S(2)}, u32[]{:S(2)}) %collective-permute-start.14) | collective-permute-done | bytes 335904 | tf_op jit(solution)/shard_map/ppermute | solution.py:522
  39.4 1.0 %collective-permute-start.15 = (f32[640,128]{1,0:T(8,128)S(1)}, f32[640,128]{1,0:T(8,128)S(1)}, u32[]{:S(2)}, u32[]{:S(2)}) collective-permute-start(f32[640,128]{1,0:T(8,128)S(1)} %get-tuple-element.74), channel_id=1, source_target_pairs={{0,1},{1,0},{2,3},{3,2},{4,5},{5,4},{6,7},{7,6},{8,9},{9,8},{10,11... | collective-permute-start | bytes 983048 | tf_op jit(solution)/shard_map/ppermute | solution.py:522
  40.4 2.2 %shard_map.108 = (f32[10,512,128]{2,1,0:T(8,128)}, f32[640,128]{1,0:T(8,128)S(1)}) custom-call(f32[10,512,128]{2,1,0:T(8,128)S(1)} %shard_map.103.part_ref, f32[10,512,128]{2,1,0:T(8,128)S(1)} %get-tuple-element.40.q_ref.rest_6_, f32[10,512,128]{2,1,0:T(8,128)S(1)} %get-tuple-element.53.q1_ref, f32[2,512,128]{2,1,0:T(8,128)S(1)} %get-tuple-element.49.vel_ref.rest_7_, ...), custom_call_target="tpu_custom_call" | custom-call | flops 19660800 | bytes 12000000 | tf_op jit(solution)/shard_map/pallas_call | solution.py:495
  42.7 3.6 %collective-permute-done.16.far_ref = f32[640,128]{1,0:T(8,128)S(1)} collective-permute-done((f32[640,128]{1,0:T(8,128)S(1)}, f32[640,128]{1,0:T(8,128)S(1)}, u32[]{:S(2)}, u32[]{:S(2)}) %collective-permute-start.16) | collective-permute-done | bytes 327712 | tf_op jit(solution)/shard_map/ppermute | solution.py:522
  46.3 0.9 %shard_map.109 = f32[10,64,8,128]{3,2,1,0:T(8,128)} custom-call(f32[10,64,8,128]{3,2,1,0:T(8,128)} %bitcast.21, f32[640,128]{1,0:T(8,128)S(1)} %get-tuple-element.73.keep_ref, f32[640,128]{1,0:T(8,128)S(1)} %collective-permute-done.15.core_ref, f32[640,128]{1,0:T(8,128)S(1)} %collective-permute-done.16.far_ref), custom_call_target="tpu_custom_call", output_to_operand_aliasing={{}: (0, {})} | custom-call | tf_op jit(solution)/shard_map/pallas_call | solution.py:495
  (20 shorter events, 0.2 us)
Async XLA Ops:
  2.3 7.7 %collective-permute-start = (f32[640,128]{1,0:T(8,128)S(1)}, f32[640,128]{1,0:T(8,128)S(1)}, u32[]{:S(2)}, u32[]{:S(2)}) collective-permute-start(f32[640,128]{1,0:T(8,128)S(1)} %get-tuple-element.42), channel_id=1, source_target_pairs={{0,1},{1,0},{2,3},{3,2},{4,5},{5,4},{6,7},{7,6},{8,9},{9,8},{10,11... | collective-permute-start | bytes 983048 | tf_op jit(solution)/shard_map/ppermute | solution.py:522
  3.0 12.1 %collective-permute-start.1 = (f32[664,128]{1,0:T(8,128)S(1)}, f32[664,128]{1,0:T(8,128)S(1)}, u32[]{:S(2)}, u32[]{:S(2)}) collective-permute-start(f32[664,128]{1,0:T(8,128)S(1)} %get-tuple-element.44), channel_id=1, source_target_pairs={{1,17},{3,19},{5,21},{7,23},{9,25},{11,27},{13,29},{15,31},{17,1},... | collective-permute-start | bytes 1019912 | tf_op jit(solution)/shard_map/ppermute | solution.py:522
  5.4 9.5 %collective-permute-start.2 = (f32[344,128]{1,0:T(8,128)S(1)}, f32[344,128]{1,0:T(8,128)S(1)}, u32[]{:S(2)}, u32[]{:S(2)}) collective-permute-start(f32[344,128]{1,0:T(8,128)S(1)} %get-tuple-element.45), channel_id=1, source_target_pairs={{1,9},{3,11},{5,13},{7,15},{9,17},{11,19},{13,21},{15,23},{17,25},... | collective-permute-start | bytes 528392 | tf_op jit(solution)/shard_map/ppermute | solution.py:522
  6.9 8.2 %collective-permute-start.3 = (f32[344,128]{1,0:T(8,128)S(1)}, f32[344,128]{1,0:T(8,128)S(1)}, u32[]{:S(2)}, u32[]{:S(2)}) collective-permute-start(f32[344,128]{1,0:T(8,128)S(1)} %get-tuple-element.46), channel_id=1, source_target_pairs={{1,25},{3,27},{5,29},{7,31},{9,1},{11,3},{13,5},{15,7},{17,9},{19,... | collective-permute-start | bytes 528392 | tf_op jit(solution)/shard_map/ppermute | solution.py:522
  9.4 5.5 %collective-permute-start.4 = (f32[88,128]{1,0:T(8,128)S(1)}, f32[88,128]{1,0:T(8,128)S(1)}, u32[]{:S(2)}, u32[]{:S(2)}) collective-permute-start(f32[88,128]{1,0:T(8,128)S(1)} %get-tuple-element.47), channel_id=1, source_target_pairs={{0,8},{1,9},{2,10},{3,11},{4,12},{5,13},{6,14},{7,15},{8,16},{9,17... | collective-permute-start | bytes 135176 | tf_op jit(solution)/shard_map/ppermute | solution.py:522
  9.9 5.6 %collective-permute-start.5 = (f32[88,128]{1,0:T(8,128)S(1)}, f32[88,128]{1,0:T(8,128)S(1)}, u32[]{:S(2)}, u32[]{:S(2)}) collective-permute-start(f32[88,128]{1,0:T(8,128)S(1)} %get-tuple-element.48), channel_id=1, source_target_pairs={{0,24},{1,25},{2,26},{3,27},{4,28},{5,29},{6,30},{7,31},{8,0},{9,1... | collective-permute-start | bytes 135176 | tf_op jit(solution)/shard_map/ppermute | solution.py:522
  12.3 3.2 %copy-start = (f32[10,1,8192]{2,1,0:T(1,128)S(1)}, f32[10,1,8192]{2,1,0:T(1,128)}, u32[]{:S(2)}) copy-start(f32[10,1,8192]{2,1,0:T(1,128)} %param.12) | copy-start | bytes 983044
  12.3 3.2 %copy-start.1 = (s32[8,1]{0,1:T(1,128)S(1)}, s32[8,1]{0,1:T(1,128)}, u32[]{:S(2)}) copy-start(s32[8,1]{0,1:T(1,128)} %param.17) | copy-start | bytes 100
  12.3 3.2 %copy-start.2 = (s32[8]{0:T(128)S(1)}, s32[8]{0:T(128)}, u32[]{:S(2)}) copy-start(s32[8]{0:T(128)} %rest_11_.1) | copy-start | bytes 100
  12.3 3.2 %copy-start.3 = (s32[8]{0:T(128)S(1)}, s32[8]{0:T(128)}, u32[]{:S(2)}) copy-start(s32[8]{0:T(128)} %rest_12_.1) | copy-start | bytes 100
  16.4 12.8 %collective-permute-start.6 = (f32[656,128]{1,0:T(8,128)S(1)}, f32[656,128]{1,0:T(8,128)S(1)}, u32[]{:S(2)}, u32[]{:S(2)}) collective-permute-start(f32[656,128]{1,0:T(8,128)S(1)} %get-tuple-element.58), channel_id=1, source_target_pairs={{0,1},{1,0},{2,3},{3,2},{4,5},{5,4},{6,7},{7,6},{8,9},{9,8},{10,11... | collective-permute-start | bytes 1007624 | tf_op jit(solution)/shard_map/ppermute | solution.py:522
  17.3 12.0 %collective-permute-start.13 = (f32[656,128]{1,0:T(8,128)S(1)}, f32[656,128]{1,0:T(8,128)S(1)}, u32[]{:S(2)}, u32[]{:S(2)}) collective-permute-start(f32[656,128]{1,0:T(8,128)S(1)} %get-tuple-element.58), channel_id=1, source_target_pairs={{3,0},{7,4},{11,8},{15,12},{19,16},{23,20},{27,24},{31,28}} | collective-permute-start | bytes 1007624 | tf_op jit(solution)/shard_map/ppermute | solution.py:522
  18.5 7.1 %collective-permute-start.7 = (f32[320,128]{1,0:T(8,128)S(1)}, f32[320,128]{1,0:T(8,128)S(1)}, u32[]{:S(2)}, u32[]{:S(2)}) collective-permute-start(f32[320,128]{1,0:T(8,128)S(1)} %get-tuple-element.61), channel_id=1, source_target_pairs={{1,17},{3,19},{5,21},{7,23},{9,25},{11,27},{13,29},{15,31},{17,1},... | collective-permute-start | bytes 491528 | tf_op jit(solution)/shard_map/ppermute | solution.py:522
  18.6 10.6 %collective-permute-start.8 = (f32[320,128]{1,0:T(8,128)S(1)}, f32[320,128]{1,0:T(8,128)S(1)}, u32[]{:S(2)}, u32[]{:S(2)}) collective-permute-start(f32[320,128]{1,0:T(8,128)S(1)} %get-tuple-element.62), channel_id=1, source_target_pairs={{1,9},{3,11},{5,13},{7,15},{9,17},{11,19},{13,21},{15,23},{17,25},... | collective-permute-start | bytes 491528 | tf_op jit(solution)/shard_map/ppermute | solution.py:522
  20.6 8.6 %collective-permute-start.9 = (f32[320,128]{1,0:T(8,128)S(1)}, f32[320,128]{1,0:T(8,128)S(1)}, u32[]{:S(2)}, u32[]{:S(2)}) collective-permute-start(f32[320,128]{1,0:T(8,128)S(1)} %get-tuple-element.63), channel_id=1, source_target_pairs={{1,25},{3,27},{5,29},{7,31},{9,1},{11,3},{13,5},{15,7},{17,9},{19,... | collective-permute-start | bytes 491528 | tf_op jit(solution)/shard_map/ppermute | solution.py:522
  29.3 10.1 %collective-permute-start.14 = (f32[656,128]{1,0:T(8,128)S(1)}, f32[656,128]{1,0:T(8,128)S(1)}, u32[]{:S(2)}, u32[]{:S(2)}) collective-permute-start(f32[656,128]{1,0:T(8,128)S(1)} %shard_map.106.near_ref), channel_id=1, source_target_pairs={{4,0},{12,8},{20,16},{28,24}} | collective-permute-start | bytes 1007624 | tf_op jit(solution)/shard_map/ppermute | solution.py:522
  30.6 3.7 %collective-permute-start.10 = (f32[640,128]{1,0:T(8,128)S(1)}, f32[640,128]{1,0:T(8,128)S(1)}, u32[]{:S(2)}, u32[]{:S(2)}) collective-permute-start(f32[640,128]{1,0:T(8,128)S(1)} %shard_map.104.refs_0_), channel_id=1, source_target_pairs={{3,1},{7,5},{11,9},{15,13},{19,17},{23,21},{27,25},{31,29},{2,4},{... | collective-permute-start | bytes 983048 | tf_op jit(solution)/shard_map/ppermute | solution.py:522
  31.3 5.0 %collective-permute-start.11 = (f32[80,128]{1,0:T(8,128)S(1)}, f32[80,128]{1,0:T(8,128)S(1)}, u32[]{:S(2)}, u32[]{:S(2)}) collective-permute-start(f32[80,128]{1,0:T(8,128)S(1)} %get-tuple-element.66), channel_id=1, source_target_pairs={{0,8},{1,9},{2,10},{3,11},{4,12},{5,13},{6,14},{7,15},{8,16},{9,17... | collective-permute-start | bytes 122888 | tf_op jit(solution)/shard_map/ppermute | solution.py:522
  32.4 4.0 %collective-permute-start.12 = (f32[80,128]{1,0:T(8,128)S(1)}, f32[80,128]{1,0:T(8,128)S(1)}, u32[]{:S(2)}, u32[]{:S(2)}) collective-permute-start(f32[80,128]{1,0:T(8,128)S(1)} %get-tuple-element.67), channel_id=1, source_target_pairs={{0,24},{1,25},{2,26},{3,27},{4,28},{5,29},{6,30},{7,31},{8,0},{9,1... | collective-permute-start | bytes 122888 | tf_op jit(solution)/shard_map/ppermute | solution.py:522
  34.3 12.0 %collective-permute-start.16 = (f32[640,128]{1,0:T(8,128)S(1)}, f32[640,128]{1,0:T(8,128)S(1)}, u32[]{:S(2)}, u32[]{:S(2)}) collective-permute-start(f32[640,128]{1,0:T(8,128)S(1)} %shard_map.105.pair_ref), channel_id=1, source_target_pairs={{5,0},{13,8},{21,16},{29,24}} | collective-permute-start | bytes 983048 | tf_op jit(solution)/shard_map/ppermute | solution.py:522
  39.4 6.9 %collective-permute-start.15 = (f32[640,128]{1,0:T(8,128)S(1)}, f32[640,128]{1,0:T(8,128)S(1)}, u32[]{:S(2)}, u32[]{:S(2)}) collective-permute-start(f32[640,128]{1,0:T(8,128)S(1)} %get-tuple-element.74), channel_id=1, source_target_pairs={{0,1},{1,0},{2,3},{3,2},{4,5},{5,4},{6,7},{7,6},{8,9},{9,8},{10,11... | collective-permute-start | bytes 983048 | tf_op jit(solution)/shard_map/ppermute | solution.py:522

commit v11 on v10

--- a/solution.py
+++ b/solution.py
@@ -338,7 +338,7 @@
         core_ref[pl.ds(rows, EXT), :] = jnp.zeros((EXT, LANES), f32)
         for v in range(NV):
             core_ref[pl.ds(v * n, n), :] = q1_ref[v, pl.ds(0, n, stride=CAX), :]
-        axial_rows(q1_ref, vel_ref, out_refs[:CAX // cap], (z_ref,))
+        axial_rows(q1_ref, vel_ref, (z_ref,), out_refs[:CAX // cap])
 
     @pl.when(plen == 1)
     def _():
@@ -372,13 +372,13 @@
                 used[k] = used[k] + here.astype(jnp.int32)
 
 
-def tile_kernel(n_out, cap, own_ref, z_ref, *rest):
+def tile_kernel(n_out, cap, own_ref, *rest):
     got, tables, (step_ref,) = rest[:n_out], rest[n_out:2 * n_out], rest[2 * n_out:]
     _, _, plen = roles()
 
     @pl.when(plen == 0)
     def _():
-        step_ref[...] = z_ref[...]
+        step_ref[...] = jnp.zeros_like(step_ref)
 
     @pl.when(plen == 1)
     def _():
@@ -405,16 +405,16 @@
         out_ref[...] = pair_ref[...]
 
 
-def border_two_kernel(n_ax, n_z, part_ref, q_ref, q1_ref, vel_ref, core_ref, supply_ref, step_ref, dq_ref, hl_ref, hr_ref,
+def border_two_kernel(n_ax, n_z, part_ref, q_ref, q1_ref, vel_ref, core_ref, supply_ref, ra_ref, dq_ref, hl_ref, hr_ref,
                       hl0_ref, hr0_ref, *rest):
-    ra_refs, rest = rest[:n_z], rest[n_z:]
+    rb_refs, rest = rest[:n_z], rest[n_z:]
     a_ref, power_ref, out_any, keep_ref, out_ref, lo_ref, hi_ref, sems = rest
     n = out_ref.shape[1] // CAX
     rows = NV * n
     _, ax, plen = roles()
     inlet_side = jnp.logical_and(ax == 0, plen == 0)
     ul_ref, ur_ref = hl0_ref.at[pl.ds(NV * CAX, CAX)], hr0_ref.at[pl.ds(NV * CAX, CAX)]
-    fill_ghosts(q1_ref, lo_ref, hi_ref, ra_refs, (step_ref,), core_ref, supply_ref, n_ax)
+    fill_ghosts(q1_ref, lo_ref, hi_ref, (ra_ref,), rb_refs, core_ref, supply_ref, n_ax)
 
     @pl.when(inlet_side)
     def _():
@@ -548,7 +548,13 @@
 
     def compact(k):
         out = [((i, j, 1), ((i + shifts[k]) % n_az, j, 1)) for i, j in every]
-        return out + [((i, j, 0), (i, mate(0, j), 0) if k < pieces else (i ^ 1, j, 0)) for i, j in every]
+        for i, j in every:
+            if k >= pieces or 0 < j < n_ax - 1:
+                to = (i, mate(int(k < pieces), j), 0)
+            else:
+                to = (i ^ (1 if k % 2 == 0 else n_az // 2), j, 0)
+            out.append(((i, j, 0), to))
+        return out
 
     q, vel = view(cells[0]), view(speeds[0])
     sup = supply.reshape(rows, LANES)
@@ -584,27 +590,27 @@
     outs, (q1, core, z1, own1, er, el) = got[:n_out], got[n_out:]
     down = [((i, j, 1), (i, j - 1, 1)) for i, j in every if j % 2 == 1]
     across = [((i, 2, 1), (i, 0, 0)) for i in range(n_az)]
-    inner = [((i, j, 0), (i, mate(1, j), 0)) for i, j in every if 0 < j < n_ax - 1]
     rb = [send(x, compact(k)) for k, x in enumerate(outs)]
     core_in = send(core, swap)
     down0 = send(core, [((i, j, 1), (i, j - 1, 0)) for i, j in every if j % 2 == 1])
 
     part, = call(inside_two_kernel, (qv, q1, velv, matrix, power), "vvvvv", [whole], cost=work)
     part, own1 = lax.optimization_barrier((part, own1))
-    step, = call(functools.partial(tile_kernel, n_out, cap), (own1, z1, *rb, *ra), "v" * (2 + 2 * n_out), [row])
-    step_in = send(step, down + inner)
+    step, = call(functools.partial(tile_kernel, n_out, cap), (own1, *rb, *ra), "v" * (1 + 2 * n_out), [row])
+    step_in = send(step, down)
     er, el, core_in, step = lax.optimization_barrier((er, el, core_in, step))
     hl1, hr1 = send(er, ring(1)), send(el, ring(-1))
     pair0, = call(add_kernel, (core_in, down0), "vv", [wide])
     far0 = send(pair0, [((i, 2, 0), (i, 0, 0)) for i in range(n_az)])
     pair1, = call(add_kernel, (step, step_in), "vv", [row])
     far1 = send(pair1, across)
-    pair1, hl1, hr1 = lax.optimization_barrier((pair1, hl1, hr1))
+    z1, pair1 = lax.optimization_barrier((z1, pair1))
+    z1_in = send(z1, [((i, j, 0), (i, mate(0, j), 0)) for i, j in every])
 
     dq, core2 = call(inlet_kernel, (pair1, far0, pair0), "vvv", [wide, row])
     core2_in = send(core2, swap)
     out, keep = call(functools.partial(border_two_kernel, n_ax, pieces),
-                     (part, qv, q1, velv, core_in, sup, step_in, dq, hl1, hr1, hl0, hr0, *rb[:pieces], matrix, power),
+                     (part, qv, q1, velv, core_in, sup, z1_in, dq, hl1, hr1, hl0, hr0, *rb[:pieces], matrix, power),
                      "v" * (14 + pieces), [whole, row],
                      [pltpu.VMEM(q.shape, f32)] + [pltpu.VMEM((rows, LANES), f32)] * 2 + [pltpu.SemaphoreType.DMA((NV,))],
                      cost=work, to="hv")

time: 47.5 us -> 56.2 us (1.18)
  starting transfers between devices: 22.6 us -> 32.5 us
  waiting for transfers between devices: 12.8 us -> 11.5 us
    ppermute x17 -> x18, starting transfers between devices: 22.6 us -> 32.5 us  [send(): return lax.ppermute(x, AXES, [(number(*a), number(*b)) for a, b in route])]
    ppermute x17 -> x18, waiting for transfers between devices: 12.8 us -> 11.5 us  [send(): return lax.ppermute(x, AXES, [(number(*a), number(*b)) for a, b in route])]
  transfers between devices with their start and end apart: 17 -> 18, of which waited for: 9 -> 9; matrix products, arithmetic and copies ran while one was open for 0% -> 0% of each run, Pallas kernels for 16% -> 14%
where the time goes in v11:
time: 56.2 us; the launch traced here: 55.9 us
  starting transfers between devices  32.5 us (58%)
  Pallas kernels  11.7 us (21%)
  waiting for transfers between devices  11.5 us (20%)
    ppermute x18, starting transfers between devices, send(): return lax.ppermute(x, AXES, [(number(*a), number(*b)) for a, b in route])  32.5 us
    pallas_call x10, Pallas kernels, call(): pl.pallas_call(kernel, in_specs=[pl.BlockSpec(memory_space=SPACES[k]) for...  11.7 us
    ppermute x18, waiting for transfers between devices, send(): return lax.ppermute(x, AXES, [(number(*a), number(*b)) for a, b in route])  11.5 us
  transfers between devices with their start and end apart: 18, of which 9 were waited for; matrix products, arithmetic and copies ran while one was open for 0% of the time, Pallas kernels for 14%

profile of v11, /device:TPU:0, one launch (start us, length us, event | category | flops | bytes accessed | tf_op | source)
XLA Modules:
  0.0 55.9 jit_solution(11109714525367233094)
XLA Ops:
  0.0 2.2 %shard_map.100 = (f32[664,128]{1,0:T(8,128)S(1)}, f32[344,128]{1,0:T(8,128)S(1)}, f32[344,128]{1,0:T(8,128)S(1)}, f32[10,512,128]{2,1,0:T(8,128)S(1)}, f32[2,512...) custom-call(f32[10,512,128]{2,1,0:T(8,128)} %bitcast.20, ...), custom_call_target="tpu_custom_call" | custom-call | tf_op jit(solution)/shard_map/pallas_call | solution.py:495
  2.3 0.7 %collective-permute-start = (f32[640,128]{1,0:T(8,128)S(1)}, f32[640,128]{1,0:T(8,128)S(1)}, u32[]{:S(2)}, u32[]{:S(2)}) collective-permute-start(f32[640,128]{1,0:T(8,128)S(1)} %get-tuple-element.41), channel_id=1, source_target_pairs={{0,1},{1,0},{2,3},{3,2},{4,5},{5,4},{6,7},{7,6},{8,9},{9,8},{10,11... | collective-permute-start | bytes 983048 | tf_op jit(solution)/shard_map/ppermute | solution.py:522
  3.0 2.4 %collective-permute-start.1 = (f32[664,128]{1,0:T(8,128)S(1)}, f32[664,128]{1,0:T(8,128)S(1)}, u32[]{:S(2)}, u32[]{:S(2)}) collective-permute-start(f32[664,128]{1,0:T(8,128)S(1)} %get-tuple-element.43), channel_id=1, source_target_pairs={{1,17},{3,19},{5,21},{7,23},{9,25},{11,27},{13,29},{15,31},{17,1},... | collective-permute-start | bytes 1019912 | tf_op jit(solution)/shard_map/ppermute | solution.py:522
  5.4 1.5 %collective-permute-start.2 = (f32[344,128]{1,0:T(8,128)S(1)}, f32[344,128]{1,0:T(8,128)S(1)}, u32[]{:S(2)}, u32[]{:S(2)}) collective-permute-start(f32[344,128]{1,0:T(8,128)S(1)} %get-tuple-element.44), channel_id=1, source_target_pairs={{1,9},{3,11},{5,13},{7,15},{9,17},{11,19},{13,21},{15,23},{17,25},... | collective-permute-start | bytes 528392 | tf_op jit(solution)/shard_map/ppermute | solution.py:522
  6.9 2.5 %collective-permute-start.3 = (f32[344,128]{1,0:T(8,128)S(1)}, f32[344,128]{1,0:T(8,128)S(1)}, u32[]{:S(2)}, u32[]{:S(2)}) collective-permute-start(f32[344,128]{1,0:T(8,128)S(1)} %get-tuple-element.45), channel_id=1, source_target_pairs={{1,25},{3,27},{5,29},{7,31},{9,1},{11,3},{13,5},{15,7},{17,9},{19,... | collective-permute-start | bytes 528392 | tf_op jit(solution)/shard_map/ppermute | solution.py:522
  9.4 0.5 collective-permute-start.4
  9.9 2.4 %collective-permute-start.5 = (f32[88,128]{1,0:T(8,128)S(1)}, f32[88,128]{1,0:T(8,128)S(1)}, u32[]{:S(2)}, u32[]{:S(2)}) collective-permute-start(f32[88,128]{1,0:T(8,128)S(1)} %get-tuple-element.47), channel_id=1, source_target_pairs={{0,24},{1,25},{2,26},{3,27},{4,28},{5,29},{6,30},{7,31},{8,0},{9,1... | collective-permute-start | bytes 135176 | tf_op jit(solution)/shard_map/ppermute | solution.py:522
  12.3 2.5 %shard_map.101.rest_5_ = f32[10,512,128]{2,1,0:T(8,128)S(1)} custom-call(f32[10,512,128]{2,1,0:T(8,128)S(1)} %get-tuple-element.39.q_ref.rest_6_, f32[2,512,128]{2,1,0:T(8,128)S(1)} %get-tuple-element.48.vel_ref.rest_7_, f32[80,240]{1,0:T(8,128)S(1)} %get-tuple-element.49.a_ref.rest_2_, f32[72,128]{1,0:T(8,128)S(1)} %get-tuple-element.50.power_ref.rest_3_), custom_call_target="tpu_custom_call" | custom-call | flops 19660800 | bytes 12000000 | tf_op jit(solution)/shard_map/pallas_call | solution.py:495
  14.8 0.1 collective-permute-done.4.rest_3_.hl0_ref
  14.9 0.2 collective-permute-done.3.rest_2_.rest_5_
  15.1 0.4 collective-permute-done.5.rest_4_.hr0_ref
  15.5 0.9 %shard_map.102 = (f32[320,128]{1,0:T(8,128)S(1)}, f32[320,128]{1,0:T(8,128)S(1)}, f32[320,128]{1,0:T(8,128)S(1)}, f32[10,512,128]{2,1,0:T(8,128)S(1)}, f32[656,1...) custom-call(f32[640,128]{1,0:T(8,128)S(1)} %collective-permute-done., ...), custom_call_target="tpu_custom_call" | custom-call | tf_op jit(solution)/shard_map/pallas_call | solution.py:495
  16.4 0.9 %collective-permute-start.6 = (f32[656,128]{1,0:T(8,128)S(1)}, f32[656,128]{1,0:T(8,128)S(1)}, u32[]{:S(2)}, u32[]{:S(2)}) collective-permute-start(f32[656,128]{1,0:T(8,128)S(1)} %get-tuple-element.57), channel_id=1, source_target_pairs={{0,1},{1,0},{2,3},{3,2},{4,5},{5,4},{6,7},{7,6},{8,9},{9,8},{10,11... | collective-permute-start | bytes 1007624 | tf_op jit(solution)/shard_map/ppermute | solution.py:522
  17.3 1.3 %collective-permute-start.12 = (f32[656,128]{1,0:T(8,128)S(1)}, f32[656,128]{1,0:T(8,128)S(1)}, u32[]{:S(2)}, u32[]{:S(2)}) collective-permute-start(f32[656,128]{1,0:T(8,128)S(1)} %get-tuple-element.57), channel_id=1, source_target_pairs={{3,0},{7,4},{11,8},{15,12},{19,16},{23,20},{27,24},{31,28}} | collective-permute-start | bytes 1007624 | tf_op jit(solution)/shard_map/ppermute | solution.py:522
  18.6 1.1 %collective-permute-start.7 = (f32[320,128]{1,0:T(8,128)S(1)}, f32[320,128]{1,0:T(8,128)S(1)}, u32[]{:S(2)}, u32[]{:S(2)}) collective-permute-start(f32[320,128]{1,0:T(8,128)S(1)} %get-tuple-element.59), channel_id=1, source_target_pairs={{1,17},{3,19},{5,21},{7,23},{9,25},{11,27},{13,29},{15,31},{17,1},... | collective-permute-start | bytes 491528 | tf_op jit(solution)/shard_map/ppermute | solution.py:522
  19.7 1.5 %collective-permute-start.8 = (f32[320,128]{1,0:T(8,128)S(1)}, f32[320,128]{1,0:T(8,128)S(1)}, u32[]{:S(2)}, u32[]{:S(2)}) collective-permute-start(f32[320,128]{1,0:T(8,128)S(1)} %get-tuple-element.60), channel_id=1, source_target_pairs={{1,9},{3,11},{5,13},{7,15},{9,17},{11,19},{13,21},{15,23},{17,25},... | collective-permute-start | bytes 491528 | tf_op jit(solution)/shard_map/ppermute | solution.py:522
  21.1 2.8 %shard_map.103.part_ref = f32[10,512,128]{2,1,0:T(8,128)S(1)} custom-call(f32[10,512,128]{2,1,0:T(8,128)S(1)} %get-tuple-element.39.q_ref.rest_6_, f32[10,512,128]{2,1,0:T(8,128)S(1)} %get-tuple-element.52.q1_ref, f32[2,512,128]{2,1,0:T(8,128)S(1)} %get-tuple-element.48.vel_ref.rest_7_, f32[80,240]{1,0:T(8,128)S(1)} %get-tuple-element.49.a_ref.rest_2_, ...), custom_call_target="tpu_custom_call" | custom-call | flops 19660800 | bytes 12000000 | tf_op jit(solution)/shard_map/pallas_call | solution.py:495
  23.9 1.7 %collective-permute-done.7.rest_0_ = f32[320,128]{1,0:T(8,128)S(1)} collective-permute-done((f32[320,128]{1,0:T(8,128)S(1)}, f32[320,128]{1,0:T(8,128)S(1)}, u32[]{:S(2)}, u32[]{:S(2)}) %collective-permute-start.7) | collective-permute-done | bytes 163872 | tf_op jit(solution)/shard_map/ppermute | solution.py:522
  25.6 0.5 collective-permute-done.8.rest_1_
  26.1 1.4 %collective-permute-done.9.rest_2_ = f32[320,128]{1,0:T(8,128)S(1)} collective-permute-done((f32[320,128]{1,0:T(8,128)S(1)}, f32[320,128]{1,0:T(8,128)S(1)}, u32[]{:S(2)}, u32[]{:S(2)}) %collective-permute-start.9) | collective-permute-done | bytes 163872 | tf_op jit(solution)/shard_map/ppermute | solution.py:522
  27.6 1.3 %collective-permute-start.13 = (f32[656,128]{1,0:T(8,128)S(1)}, f32[656,128]{1,0:T(8,128)S(1)}, u32[]{:S(2)}, u32[]{:S(2)}) collective-permute-start(f32[656,128]{1,0:T(8,128)S(1)} %shard_map.106.near_ref), channel_id=1, source_target_pairs={{4,0},{12,8},{20,16},{28,24}} | collective-permute-start | bytes 1007624 | tf_op jit(solution)/shard_map/ppermute | solution.py:522
  28.9 0.7 %collective-permute-start.10 = (f32[640,128]{1,0:T(8,128)S(1)}, f32[640,128]{1,0:T(8,128)S(1)}, u32[]{:S(2)}, u32[]{:S(2)}) collective-permute-start(f32[640,128]{1,0:T(8,128)S(1)} %shard_map.104.refs_0_), channel_id=1, source_target_pairs={{3,1},{7,5},{11,9},{15,13},{19,17},{23,21},{27,25},{31,29}} | collective-permute-start | bytes 983048 | tf_op jit(solution)/shard_map/ppermute | solution.py:522
  29.6 1.9 %collective-permute-start.11 = (f32[640,128]{1,0:T(8,128)S(1)}, f32[640,128]{1,0:T(8,128)S(1)}, u32[]{:S(2)}, u32[]{:S(2)}) collective-permute-start(f32[640,128]{1,0:T(8,128)S(1)} %get-tuple-element.65), channel_id=1, source_target_pairs={{0,2},{2,0},{4,6},{6,4},{8,10},{10,8},{12,14},{14,12},{16,18},{18,... | collective-permute-start | bytes 983048 | tf_op jit(solution)/shard_map/ppermute | solution.py:522
  31.6 1.3 %collective-permute-start.17 = (f32[640,128]{1,0:T(8,128)S(1)}, f32[640,128]{1,0:T(8,128)S(1)}, u32[]{:S(2)}, u32[]{:S(2)}) collective-permute-start(f32[640,128]{1,0:T(8,128)S(1)} %shard_map.105.pair_ref), channel_id=1, source_target_pairs={{5,0},{13,8},{21,16},{29,24}} | collective-permute-start | bytes 983048 | tf_op jit(solution)/shard_map/ppermute | solution.py:522
  32.9 4.8 %collective-permute-done.13.far_ref = f32[656,128]{1,0:T(8,128)S(1)} collective-permute-done((f32[656,128]{1,0:T(8,128)S(1)}, f32[656,128]{1,0:T(8,128)S(1)}, u32[]{:S(2)}, u32[]{:S(2)}) %collective-permute-start.13) | collective-permute-done | bytes 335904 | tf_op jit(solution)/shard_map/ppermute | solution.py:522
  37.7 9.6 %collective-permute-start.16 = (f32[640,128]{1,0:T(8,128)S(1)}, f32[640,128]{1,0:T(8,128)S(1)}, u32[]{:S(2)}, u32[]{:S(2)}) collective-permute-start(f32[640,128]{1,0:T(8,128)S(1)} %get-tuple-element.72), channel_id=1, source_target_pairs={{0,1},{1,0},{2,3},{3,2},{4,5},{5,4},{6,7},{7,6},{8,9},{9,8},{10,11... | collective-permute-start | bytes 983048 | tf_op jit(solution)/shard_map/ppermute | solution.py:522
  47.3 1.4 %collective-permute-start.14 = (f32[80,128]{1,0:T(8,128)S(1)}, f32[80,128]{1,0:T(8,128)S(1)}, u32[]{:S(2)}, u32[]{:S(2)}) collective-permute-start(f32[80,128]{1,0:T(8,128)S(1)} %get-tuple-element.68), channel_id=1, source_target_pairs={{0,8},{1,9},{2,10},{3,11},{4,12},{5,13},{6,14},{7,15},{8,16},{9,17... | collective-permute-start | bytes 122888 | tf_op jit(solution)/shard_map/ppermute | solution.py:522
  48.7 1.6 %collective-permute-start.15 = (f32[80,128]{1,0:T(8,128)S(1)}, f32[80,128]{1,0:T(8,128)S(1)}, u32[]{:S(2)}, u32[]{:S(2)}) collective-permute-start(f32[80,128]{1,0:T(8,128)S(1)} %get-tuple-element.69), channel_id=1, source_target_pairs={{0,24},{1,25},{2,26},{3,27},{4,28},{5,29},{6,30},{7,31},{8,0},{9,1... | collective-permute-start | bytes 122888 | tf_op jit(solution)/shard_map/ppermute | solution.py:522
  50.3 2.0 %collective-permute-done.14.hl_ref = f32[80,128]{1,0:T(8,128)S(1)} collective-permute-done((f32[80,128]{1,0:T(8,128)S(1)}, f32[80,128]{1,0:T(8,128)S(1)}, u32[]{:S(2)}, u32[]{:S(2)}) %collective-permute-start.14) | collective-permute-done | bytes 40992 | tf_op jit(solution)/shard_map/ppermute | solution.py:522
  52.2 0.5 collective-permute-done.15.hr_ref
  52.7 2.2 %shard_map.108 = (f32[10,512,128]{2,1,0:T(8,128)}, f32[640,128]{1,0:T(8,128)S(1)}) custom-call(f32[10,512,128]{2,1,0:T(8,128)S(1)} %shard_map.103.part_ref, f32[10,512,128]{2,1,0:T(8,128)S(1)} %get-tuple-element.39.q_ref.rest_6_, f32[10,512,128]{2,1,0:T(8,128)S(1)} %get-tuple-element.52.q1_ref, f32[2,512,128]{2,1,0:T(8,128)S(1)} %get-tuple-element.48.vel_ref.rest_7_, ...), custom_call_target="tpu_custom_call" | custom-call | flops 19660800 | bytes 12000000 | tf_op jit(solution)/shard_map/pallas_call | solution.py:495
  55.0 1.0 %shard_map.109 = f32[10,64,8,128]{3,2,1,0:T(8,128)} custom-call(f32[10,64,8,128]{3,2,1,0:T(8,128)} %bitcast.21, f32[640,128]{1,0:T(8,128)S(1)} %get-tuple-element.71.keep_ref, f32[640,128]{1,0:T(8,128)S(1)} %collective-permute-done.16.core_ref, f32[640,128]{1,0:T(8,128)S(1)} %collective-permute-done.17.far_ref), custom_call_target="tpu_custom_call", output_to_operand_aliasing={{}: (0, {})} | custom-call | tf_op jit(solution)/shard_map/pallas_call | solution.py:495
  (22 shorter events, 0.2 us)
Async XLA Ops:
  2.3 7.7 %collective-permute-start = (f32[640,128]{1,0:T(8,128)S(1)}, f32[640,128]{1,0:T(8,128)S(1)}, u32[]{:S(2)}, u32[]{:S(2)}) collective-permute-start(f32[640,128]{1,0:T(8,128)S(1)} %get-tuple-element.41), channel_id=1, source_target_pairs={{0,1},{1,0},{2,3},{3,2},{4,5},{5,4},{6,7},{7,6},{8,9},{9,8},{10,11... | collective-permute-start | bytes 983048 | tf_op jit(solution)/shard_map/ppermute | solution.py:522
  3.0 12.1 %collective-permute-start.1 = (f32[664,128]{1,0:T(8,128)S(1)}, f32[664,128]{1,0:T(8,128)S(1)}, u32[]{:S(2)}, u32[]{:S(2)}) collective-permute-start(f32[664,128]{1,0:T(8,128)S(1)} %get-tuple-element.43), channel_id=1, source_target_pairs={{1,17},{3,19},{5,21},{7,23},{9,25},{11,27},{13,29},{15,31},{17,1},... | collective-permute-start | bytes 1019912 | tf_op jit(solution)/shard_map/ppermute | solution.py:522
  5.4 9.5 %collective-permute-start.2 = (f32[344,128]{1,0:T(8,128)S(1)}, f32[344,128]{1,0:T(8,128)S(1)}, u32[]{:S(2)}, u32[]{:S(2)}) collective-permute-start(f32[344,128]{1,0:T(8,128)S(1)} %get-tuple-element.44), channel_id=1, source_target_pairs={{1,9},{3,11},{5,13},{7,15},{9,17},{11,19},{13,21},{15,23},{17,25},... | collective-permute-start | bytes 528392 | tf_op jit(solution)/shard_map/ppermute | solution.py:522
  6.9 8.2 %collective-permute-start.3 = (f32[344,128]{1,0:T(8,128)S(1)}, f32[344,128]{1,0:T(8,128)S(1)}, u32[]{:S(2)}, u32[]{:S(2)}) collective-permute-start(f32[344,128]{1,0:T(8,128)S(1)} %get-tuple-element.45), channel_id=1, source_target_pairs={{1,25},{3,27},{5,29},{7,31},{9,1},{11,3},{13,5},{15,7},{17,9},{19,... | collective-permute-start | bytes 528392 | tf_op jit(solution)/shard_map/ppermute | solution.py:522
  9.4 5.5 %collective-permute-start.4 = (f32[88,128]{1,0:T(8,128)S(1)}, f32[88,128]{1,0:T(8,128)S(1)}, u32[]{:S(2)}, u32[]{:S(2)}) collective-permute-start(f32[88,128]{1,0:T(8,128)S(1)} %get-tuple-element.46), channel_id=1, source_target_pairs={{0,8},{1,9},{2,10},{3,11},{4,12},{5,13},{6,14},{7,15},{8,16},{9,17... | collective-permute-start | bytes 135176 | tf_op jit(solution)/shard_map/ppermute | solution.py:522
  9.9 5.6 %collective-permute-start.5 = (f32[88,128]{1,0:T(8,128)S(1)}, f32[88,128]{1,0:T(8,128)S(1)}, u32[]{:S(2)}, u32[]{:S(2)}) collective-permute-start(f32[88,128]{1,0:T(8,128)S(1)} %get-tuple-element.47), channel_id=1, source_target_pairs={{0,24},{1,25},{2,26},{3,27},{4,28},{5,29},{6,30},{7,31},{8,0},{9,1... | collective-permute-start | bytes 135176 | tf_op jit(solution)/shard_map/ppermute | solution.py:522
  12.3 3.2 %copy-start = (f32[10,1,8192]{2,1,0:T(1,128)S(1)}, f32[10,1,8192]{2,1,0:T(1,128)}, u32[]{:S(2)}) copy-start(f32[10,1,8192]{2,1,0:T(1,128)} %param.12) | copy-start | bytes 983044
  12.3 3.2 %copy-start.1 = (s32[8,1]{0,1:T(1,128)S(1)}, s32[8,1]{0,1:T(1,128)}, u32[]{:S(2)}) copy-start(s32[8,1]{0,1:T(1,128)} %param.17) | copy-start | bytes 100
  12.3 3.2 %copy-start.2 = (s32[8]{0:T(128)S(1)}, s32[8]{0:T(128)}, u32[]{:S(2)}) copy-start(s32[8]{0:T(128)} %rest_11_.1) | copy-start | bytes 100
  12.3 3.2 %copy-start.3 = (s32[8]{0:T(128)S(1)}, s32[8]{0:T(128)}, u32[]{:S(2)}) copy-start(s32[8]{0:T(128)} %rest_12_.1) | copy-start | bytes 100
  16.4 11.1 %collective-permute-start.6 = (f32[656,128]{1,0:T(8,128)S(1)}, f32[656,128]{1,0:T(8,128)S(1)}, u32[]{:S(2)}, u32[]{:S(2)}) collective-permute-start(f32[656,128]{1,0:T(8,128)S(1)} %get-tuple-element.57), channel_id=1, source_target_pairs={{0,1},{1,0},{2,3},{3,2},{4,5},{5,4},{6,7},{7,6},{8,9},{9,8},{10,11... | collective-permute-start | bytes 1007624 | tf_op jit(solution)/shard_map/ppermute | solution.py:522
  17.3 10.3 %collective-permute-start.12 = (f32[656,128]{1,0:T(8,128)S(1)}, f32[656,128]{1,0:T(8,128)S(1)}, u32[]{:S(2)}, u32[]{:S(2)}) collective-permute-start(f32[656,128]{1,0:T(8,128)S(1)} %get-tuple-element.57), channel_id=1, source_target_pairs={{3,0},{7,4},{11,8},{15,12},{19,16},{23,20},{27,24},{31,28}} | collective-permute-start | bytes 1007624 | tf_op jit(solution)/shard_map/ppermute | solution.py:522
  18.6 7.0 %collective-permute-start.7 = (f32[320,128]{1,0:T(8,128)S(1)}, f32[320,128]{1,0:T(8,128)S(1)}, u32[]{:S(2)}, u32[]{:S(2)}) collective-permute-start(f32[320,128]{1,0:T(8,128)S(1)} %get-tuple-element.59), channel_id=1, source_target_pairs={{1,17},{3,19},{5,21},{7,23},{9,25},{11,27},{13,29},{15,31},{17,1},... | collective-permute-start | bytes 491528 | tf_op jit(solution)/shard_map/ppermute | solution.py:522
  19.7 6.4 %collective-permute-start.8 = (f32[320,128]{1,0:T(8,128)S(1)}, f32[320,128]{1,0:T(8,128)S(1)}, u32[]{:S(2)}, u32[]{:S(2)}) collective-permute-start(f32[320,128]{1,0:T(8,128)S(1)} %get-tuple-element.60), channel_id=1, source_target_pairs={{1,9},{3,11},{5,13},{7,15},{9,17},{11,19},{13,21},{15,23},{17,25},... | collective-permute-start | bytes 491528 | tf_op jit(solution)/shard_map/ppermute | solution.py:522
  21.1 6.4 %collective-permute-start.9 = (f32[320,128]{1,0:T(8,128)S(1)}, f32[320,128]{1,0:T(8,128)S(1)}, u32[]{:S(2)}, u32[]{:S(2)}) collective-permute-start(f32[320,128]{1,0:T(8,128)S(1)} %get-tuple-element.61), channel_id=1, source_target_pairs={{1,25},{3,27},{5,29},{7,31},{9,1},{11,3},{13,5},{15,7},{17,9},{19,... | collective-permute-start | bytes 491528 | tf_op jit(solution)/shard_map/ppermute | solution.py:522
  27.6 10.1 %collective-permute-start.13 = (f32[656,128]{1,0:T(8,128)S(1)}, f32[656,128]{1,0:T(8,128)S(1)}, u32[]{:S(2)}, u32[]{:S(2)}) collective-permute-start(f32[656,128]{1,0:T(8,128)S(1)} %shard_map.106.near_ref), channel_id=1, source_target_pairs={{4,0},{12,8},{20,16},{28,24}} | collective-permute-start | bytes 1007624 | tf_op jit(solution)/shard_map/ppermute | solution.py:522
  28.9 0.7 %collective-permute-start.10 = (f32[640,128]{1,0:T(8,128)S(1)}, f32[640,128]{1,0:T(8,128)S(1)}, u32[]{:S(2)}, u32[]{:S(2)}) collective-permute-start(f32[640,128]{1,0:T(8,128)S(1)} %shard_map.104.refs_0_), channel_id=1, source_target_pairs={{3,1},{7,5},{11,9},{15,13},{19,17},{23,21},{27,25},{31,29}} | collective-permute-start | bytes 983048 | tf_op jit(solution)/shard_map/ppermute | solution.py:522
  29.6 23.1 %collective-permute-start.11 = (f32[640,128]{1,0:T(8,128)S(1)}, f32[640,128]{1,0:T(8,128)S(1)}, u32[]{:S(2)}, u32[]{:S(2)}) collective-permute-start(f32[640,128]{1,0:T(8,128)S(1)} %get-tuple-element.65), channel_id=1, source_target_pairs={{0,2},{2,0},{4,6},{6,4},{8,10},{10,8},{12,14},{14,12},{16,18},{18,... | collective-permute-start | bytes 983048 | tf_op jit(solution)/shard_map/ppermute | solution.py:522
  31.6 23.4 %collective-permute-start.17 = (f32[640,128]{1,0:T(8,128)S(1)}, f32[640,128]{1,0:T(8,128)S(1)}, u32[]{:S(2)}, u32[]{:S(2)}) collective-permute-start(f32[640,128]{1,0:T(8,128)S(1)} %shard_map.105.pair_ref), channel_id=1, source_target_pairs={{5,0},{13,8},{21,16},{29,24}} | collective-permute-start | bytes 983048 | tf_op jit(solution)/shard_map/ppermute | solution.py:522
  37.7 17.2 %collective-permute-start.16 = (f32[640,128]{1,0:T(8,128)S(1)}, f32[640,128]{1,0:T(8,128)S(1)}, u32[]{:S(2)}, u32[]{:S(2)}) collective-permute-start(f32[640,128]{1,0:T(8,128)S(1)} %get-tuple-element.72), channel_id=1, source_target_pairs={{0,1},{1,0},{2,3},{3,2},{4,5},{5,4},{6,7},{7,6},{8,9},{9,8},{10,11... | collective-permute-start | bytes 983048 | tf_op jit(solution)/shard_map/ppermute | solution.py:522
  47.3 4.9 %collective-permute-start.14 = (f32[80,128]{1,0:T(8,128)S(1)}, f32[80,128]{1,0:T(8,128)S(1)}, u32[]{:S(2)}, u32[]{:S(2)}) collective-permute-start(f32[80,128]{1,0:T(8,128)S(1)} %get-tuple-element.68), channel_id=1, source_target_pairs={{0,8},{1,9},{2,10},{3,11},{4,12},{5,13},{6,14},{7,15},{8,16},{9,17... | collective-permute-start | bytes 122888 | tf_op jit(solution)/shard_map/ppermute | solution.py:522
  48.7 4.0 %collective-permute-start.15 = (f32[80,128]{1,0:T(8,128)S(1)}, f32[80,128]{1,0:T(8,128)S(1)}, u32[]{:S(2)}, u32[]{:S(2)}) collective-permute-start(f32[80,128]{1,0:T(8,128)S(1)} %get-tuple-element.69), channel_id=1, source_target_pairs={{0,24},{1,25},{2,26},{3,27},{4,28},{5,29},{6,30},{7,31},{8,0},{9,1... | collective-permute-start | bytes 122888 | tf_op jit(solution)/shard_map/ppermute | solution.py:522

commit v12 on v9

--- a/solution.py
+++ b/solution.py
@@ -587,11 +587,10 @@
     inner = [((i, j, 0), (i, mate(1, j), 0)) for i, j in every if 0 < j < n_ax - 1]
     rb = [send(x, compact(k)) for k, x in enumerate(outs)]
     core_in = send(core, swap)
-    down0 = send(core, [((i, 3, 1), (i, 1, 0)) for i in range(n_az)])
+    down0, down1 = [send(core, [((i, j, 1), (i, 1, 0)) for i in range(n_az)]) for j in (3, 2)]
 
     part, = call(inside_two_kernel, (qv, q1, velv, matrix, power), "vvvvv", [whole], cost=work)
-    part, own1, late, rb = lax.optimization_barrier((part, own1, core, rb))
-    down1 = send(late, [((i, 2, 1), (i, 1, 0)) for i in range(n_az)])
+    part, own1 = lax.optimization_barrier((part, own1))
     step, = call(functools.partial(tile_kernel, n_out, cap), (own1, z1, *rb, *ra), "v" * (2 + 2 * n_out), [row])
     step_in = send(step, down + inner)
     er, el, core_in, step = lax.optimization_barrier((er, el, core_in, step))

time: 49.3 us -> 51.6 us (1.047)
  waiting for transfers between devices: 15.4 us -> 16.9 us
  starting transfers between devices: 21.7 us -> 22.6 us
    ppermute x18, waiting for transfers between devices: 15.4 us -> 16.9 us  [send(): return lax.ppermute(x, AXES, [(number(*a), number(*b)) for a, b in route])]
    ppermute x18, starting transfers between devices: 21.7 us -> 22.6 us  [send(): return lax.ppermute(x, AXES, [(number(*a), number(*b)) for a, b in route])]
  transfers between devices with their start and end apart: 18 -> 18, of which waited for: 8 -> 7; matrix products, arithmetic and copies ran while one was open for 0% -> 0% of each run, Pallas kernels for 16% -> 15%
where the time goes in v12:
time: 51.6 us; the launch traced here: 51.4 us
  starting transfers between devices  22.6 us (44%)
  waiting for transfers between devices  16.9 us (33%)
  Pallas kernels  11.8 us (23%)
    ppermute x18, starting transfers between devices, send(): return lax.ppermute(x, AXES, [(number(*a), number(*b)) for a, b in route])  22.6 us
    ppermute x18, waiting for transfers between devices, send(): return lax.ppermute(x, AXES, [(number(*a), number(*b)) for a, b in route])  16.9 us
    pallas_call x10, Pallas kernels, call(): pl.pallas_call(kernel, in_specs=[pl.BlockSpec(memory_space=SPACES[k]) for...  11.8 us
  transfers between devices with their start and end apart: 18, of which 7 were waited for; matrix products, arithmetic and copies ran while one was open for 0% of the time, Pallas kernels for 15%

profile of v12, /device:TPU:0, one launch (start us, length us, event | category | flops | bytes accessed | tf_op | source)
XLA Modules:
  0.0 51.4 jit_solution(427328026019398022)
XLA Ops:
  0.0 2.2 %shard_map.100 = (f32[664,128]{1,0:T(8,128)S(1)}, f32[344,128]{1,0:T(8,128)S(1)}, f32[344,128]{1,0:T(8,128)S(1)}, f32[10,512,128]{2,1,0:T(8,128)S(1)}, f32[2,512...) custom-call(f32[10,512,128]{2,1,0:T(8,128)} %bitcast.20, ...), custom_call_target="tpu_custom_call" | custom-call | tf_op jit(solution)/shard_map/pallas_call | solution.py:495
  2.3 0.7 %collective-permute-start = (f32[640,128]{1,0:T(8,128)S(1)}, f32[640,128]{1,0:T(8,128)S(1)}, u32[]{:S(2)}, u32[]{:S(2)}) collective-permute-start(f32[640,128]{1,0:T(8,128)S(1)} %get-tuple-element.42), channel_id=1, source_target_pairs={{0,1},{1,0},{2,3},{3,2},{4,5},{5,4},{6,7},{7,6},{8,9},{9,8},{10,11... | collective-permute-start | bytes 983048 | tf_op jit(solution)/shard_map/ppermute | solution.py:522
  3.0 2.5 %collective-permute-start.1 = (f32[664,128]{1,0:T(8,128)S(1)}, f32[664,128]{1,0:T(8,128)S(1)}, u32[]{:S(2)}, u32[]{:S(2)}) collective-permute-start(f32[664,128]{1,0:T(8,128)S(1)} %get-tuple-element.44), channel_id=1, source_target_pairs={{1,17},{3,19},{5,21},{7,23},{9,25},{11,27},{13,29},{15,31},{17,1},... | collective-permute-start | bytes 1019912 | tf_op jit(solution)/shard_map/ppermute | solution.py:522
  5.4 1.5 %collective-permute-start.2 = (f32[344,128]{1,0:T(8,128)S(1)}, f32[344,128]{1,0:T(8,128)S(1)}, u32[]{:S(2)}, u32[]{:S(2)}) collective-permute-start(f32[344,128]{1,0:T(8,128)S(1)} %get-tuple-element.45), channel_id=1, source_target_pairs={{1,9},{3,11},{5,13},{7,15},{9,17},{11,19},{13,21},{15,23},{17,25},... | collective-permute-start | bytes 528392 | tf_op jit(solution)/shard_map/ppermute | solution.py:522
  6.9 2.5 %collective-permute-start.3 = (f32[344,128]{1,0:T(8,128)S(1)}, f32[344,128]{1,0:T(8,128)S(1)}, u32[]{:S(2)}, u32[]{:S(2)}) collective-permute-start(f32[344,128]{1,0:T(8,128)S(1)} %get-tuple-element.46), channel_id=1, source_target_pairs={{1,25},{3,27},{5,29},{7,31},{9,1},{11,3},{13,5},{15,7},{17,9},{19,... | collective-permute-start | bytes 528392 | tf_op jit(solution)/shard_map/ppermute | solution.py:522
  9.4 0.5 %collective-permute-start.4 = (f32[88,128]{1,0:T(8,128)S(1)}, f32[88,128]{1,0:T(8,128)S(1)}, u32[]{:S(2)}, u32[]{:S(2)}) collective-permute-start(f32[88,128]{1,0:T(8,128)S(1)} %get-tuple-element.47), channel_id=1, source_target_pairs={{0,8},{1,9},{2,10},{3,11},{4,12},{5,13},{6,14},{7,15},{8,16},{9,17... | collective-permute-start | bytes 135176 | tf_op jit(solution)/shard_map/ppermute | solution.py:522
  9.9 2.4 %collective-permute-start.5 = (f32[88,128]{1,0:T(8,128)S(1)}, f32[88,128]{1,0:T(8,128)S(1)}, u32[]{:S(2)}, u32[]{:S(2)}) collective-permute-start(f32[88,128]{1,0:T(8,128)S(1)} %get-tuple-element.48), channel_id=1, source_target_pairs={{0,24},{1,25},{2,26},{3,27},{4,28},{5,29},{6,30},{7,31},{8,0},{9,1... | collective-permute-start | bytes 135176 | tf_op jit(solution)/shard_map/ppermute | solution.py:522
  12.3 2.4 %shard_map.101.rest_5_ = f32[10,512,128]{2,1,0:T(8,128)S(1)} custom-call(f32[10,512,128]{2,1,0:T(8,128)S(1)} %get-tuple-element.40.q_ref.rest_6_, f32[2,512,128]{2,1,0:T(8,128)S(1)} %get-tuple-element.49.vel_ref.rest_7_, f32[80,240]{1,0:T(8,128)S(1)} %get-tuple-element.50.a_ref.rest_2_, f32[72,128]{1,0:T(8,128)S(1)} %get-tuple-element.51.power_ref.rest_3_), custom_call_target="tpu_custom_call" | custom-call | flops 19660800 | bytes 12000000 | tf_op jit(solution)/shard_map/pallas_call | solution.py:495
  14.8 0.1 collective-permute-done.4.rest_3_.hl0_ref
  14.9 0.2 collective-permute-done.3.rest_2_.rest_5_
  15.1 0.4 collective-permute-done.5.rest_4_.hr0_ref
  15.5 0.9 %shard_map.102 = (f32[320,128]{1,0:T(8,128)S(1)}, f32[320,128]{1,0:T(8,128)S(1)}, f32[320,128]{1,0:T(8,128)S(1)}, f32[10,512,128]{2,1,0:T(8,128)S(1)}, f32[656,1...) custom-call(f32[640,128]{1,0:T(8,128)S(1)} %collective-permute-done., ...), custom_call_target="tpu_custom_call" | custom-call | tf_op jit(solution)/shard_map/pallas_call | solution.py:495
  16.4 0.9 %collective-permute-start.6 = (f32[656,128]{1,0:T(8,128)S(1)}, f32[656,128]{1,0:T(8,128)S(1)}, u32[]{:S(2)}, u32[]{:S(2)}) collective-permute-start(f32[656,128]{1,0:T(8,128)S(1)} %get-tuple-element.58), channel_id=1, source_target_pairs={{0,1},{1,0},{2,3},{3,2},{4,5},{5,4},{6,7},{7,6},{8,9},{9,8},{10,11... | collective-permute-start | bytes 1007624 | tf_op jit(solution)/shard_map/ppermute | solution.py:522
  17.3 0.7 %collective-permute-start.14 = (f32[656,128]{1,0:T(8,128)S(1)}, f32[656,128]{1,0:T(8,128)S(1)}, u32[]{:S(2)}, u32[]{:S(2)}) collective-permute-start(f32[656,128]{1,0:T(8,128)S(1)} %get-tuple-element.58), channel_id=1, source_target_pairs={{5,2},{13,10},{21,18},{29,26}} | collective-permute-start | bytes 1007624 | tf_op jit(solution)/shard_map/ppermute | solution.py:522
  17.9 0.7 %collective-permute-start.13 = (f32[656,128]{1,0:T(8,128)S(1)}, f32[656,128]{1,0:T(8,128)S(1)}, u32[]{:S(2)}, u32[]{:S(2)}) collective-permute-start(f32[656,128]{1,0:T(8,128)S(1)} %get-tuple-element.58), channel_id=1, source_target_pairs={{7,2},{15,10},{23,18},{31,26}} | collective-permute-start | bytes 1007624 | tf_op jit(solution)/shard_map/ppermute | solution.py:522
  18.6 1.0 %collective-permute-start.7 = (f32[320,128]{1,0:T(8,128)S(1)}, f32[320,128]{1,0:T(8,128)S(1)}, u32[]{:S(2)}, u32[]{:S(2)}) collective-permute-start(f32[320,128]{1,0:T(8,128)S(1)} %get-tuple-element.61), channel_id=1, source_target_pairs={{1,17},{3,19},{5,21},{7,23},{9,25},{11,27},{13,29},{15,31},{17,1},... | collective-permute-start | bytes 491528 | tf_op jit(solution)/shard_map/ppermute | solution.py:522
  19.6 1.1 %collective-permute-start.8 = (f32[320,128]{1,0:T(8,128)S(1)}, f32[320,128]{1,0:T(8,128)S(1)}, u32[]{:S(2)}, u32[]{:S(2)}) collective-permute-start(f32[320,128]{1,0:T(8,128)S(1)} %get-tuple-element.62), channel_id=1, source_target_pairs={{1,9},{3,11},{5,13},{7,15},{9,17},{11,19},{13,21},{15,23},{17,25},... | collective-permute-start | bytes 491528 | tf_op jit(solution)/shard_map/ppermute | solution.py:522
  20.7 3.3 %collective-permute-done.7.rest_0_ = f32[320,128]{1,0:T(8,128)S(1)} collective-permute-done((f32[320,128]{1,0:T(8,128)S(1)}, f32[320,128]{1,0:T(8,128)S(1)}, u32[]{:S(2)}, u32[]{:S(2)}) %collective-permute-start.7) | collective-permute-done | bytes 163872 | tf_op jit(solution)/shard_map/ppermute | solution.py:522
  24.0 1.0 %collective-permute-start.9 = (f32[320,128]{1,0:T(8,128)S(1)}, f32[320,128]{1,0:T(8,128)S(1)}, u32[]{:S(2)}, u32[]{:S(2)}) collective-permute-start(f32[320,128]{1,0:T(8,128)S(1)} %get-tuple-element.63), channel_id=1, source_target_pairs={{1,25},{3,27},{5,29},{7,31},{9,1},{11,3},{13,5},{15,7},{17,9},{19,... | collective-permute-start | bytes 491528 | tf_op jit(solution)/shard_map/ppermute | solution.py:522
  25.1 2.8 %shard_map.103.part_ref = f32[10,512,128]{2,1,0:T(8,128)S(1)} custom-call(f32[10,512,128]{2,1,0:T(8,128)S(1)} %get-tuple-element.40.q_ref.rest_6_, f32[10,512,128]{2,1,0:T(8,128)S(1)} %get-tuple-element.53.q1_ref, f32[2,512,128]{2,1,0:T(8,128)S(1)} %get-tuple-element.49.vel_ref.rest_7_, f32[80,240]{1,0:T(8,128)S(1)} %get-tuple-element.50.a_ref.rest_2_, ...), custom_call_target="tpu_custom_call" | custom-call | flops 19660800 | bytes 12000000 | tf_op jit(solution)/shard_map/pallas_call | solution.py:495
  27.9 3.2 %collective-permute-done.9.rest_2_ = f32[320,128]{1,0:T(8,128)S(1)} collective-permute-done((f32[320,128]{1,0:T(8,128)S(1)}, f32[320,128]{1,0:T(8,128)S(1)}, u32[]{:S(2)}, u32[]{:S(2)}) %collective-permute-start.9) | collective-permute-done | bytes 163872 | tf_op jit(solution)/shard_map/ppermute | solution.py:522
  31.2 1.3 %collective-permute-start.15 = (f32[656,128]{1,0:T(8,128)S(1)}, f32[656,128]{1,0:T(8,128)S(1)}, u32[]{:S(2)}, u32[]{:S(2)}) collective-permute-start(f32[656,128]{1,0:T(8,128)S(1)} %shard_map.106.near_ref), channel_id=1, source_target_pairs={{2,0},{10,8},{18,16},{26,24}} | collective-permute-start | bytes 1007624 | tf_op jit(solution)/shard_map/ppermute | solution.py:522
  32.5 0.7 %collective-permute-start.10 = (f32[640,128]{1,0:T(8,128)S(1)}, f32[640,128]{1,0:T(8,128)S(1)}, u32[]{:S(2)}, u32[]{:S(2)}) collective-permute-start(f32[640,128]{1,0:T(8,128)S(1)} %shard_map.104.refs_0_), channel_id=1, source_target_pairs={{3,1},{7,5},{11,9},{15,13},{19,17},{23,21},{27,25},{31,29},{2,4},{... | collective-permute-start | bytes 983048 | tf_op jit(solution)/shard_map/ppermute | solution.py:522
  33.2 0.3 collective-permute-start.11
  33.5 2.6 %collective-permute-start.12 = (f32[80,128]{1,0:T(8,128)S(1)}, f32[80,128]{1,0:T(8,128)S(1)}, u32[]{:S(2)}, u32[]{:S(2)}) collective-permute-start(f32[80,128]{1,0:T(8,128)S(1)} %get-tuple-element.67), channel_id=1, source_target_pairs={{0,24},{1,25},{2,26},{3,27},{4,28},{5,29},{6,30},{7,31},{8,0},{9,1... | collective-permute-start | bytes 122888 | tf_op jit(solution)/shard_map/ppermute | solution.py:522
  36.2 1.3 %collective-permute-start.17 = (f32[640,128]{1,0:T(8,128)S(1)}, f32[640,128]{1,0:T(8,128)S(1)}, u32[]{:S(2)}, u32[]{:S(2)}) collective-permute-start(f32[640,128]{1,0:T(8,128)S(1)} %shard_map.105.pair_ref), channel_id=1, source_target_pairs={{5,0},{13,8},{21,16},{29,24}} | collective-permute-start | bytes 983048 | tf_op jit(solution)/shard_map/ppermute | solution.py:522
  37.5 1.0 %collective-permute-done.11.hl_ref = f32[80,128]{1,0:T(8,128)S(1)} collective-permute-done((f32[80,128]{1,0:T(8,128)S(1)}, f32[80,128]{1,0:T(8,128)S(1)}, u32[]{:S(2)}, u32[]{:S(2)}) %collective-permute-start.11) | collective-permute-done | bytes 40992 | tf_op jit(solution)/shard_map/ppermute | solution.py:522
  38.5 8.7 %collective-permute-done.15.far_ref = f32[656,128]{1,0:T(8,128)S(1)} collective-permute-done((f32[656,128]{1,0:T(8,128)S(1)}, f32[656,128]{1,0:T(8,128)S(1)}, u32[]{:S(2)}, u32[]{:S(2)}) %collective-permute-start.15) | collective-permute-done | bytes 335904 | tf_op jit(solution)/shard_map/ppermute | solution.py:522
  47.2 0.1 shard_map.107
  47.3 0.9 %collective-permute-start.16 = (f32[640,128]{1,0:T(8,128)S(1)}, f32[640,128]{1,0:T(8,128)S(1)}, u32[]{:S(2)}, u32[]{:S(2)}) collective-permute-start(f32[640,128]{1,0:T(8,128)S(1)} %get-tuple-element.74), channel_id=1, source_target_pairs={{0,1},{1,0},{2,3},{3,2},{4,5},{5,4},{6,7},{7,6},{8,9},{9,8},{10,11... | collective-permute-start | bytes 983048 | tf_op jit(solution)/shard_map/ppermute | solution.py:522
  48.2 2.2 %shard_map.108 = (f32[10,512,128]{2,1,0:T(8,128)}, f32[640,128]{1,0:T(8,128)S(1)}) custom-call(f32[10,512,128]{2,1,0:T(8,128)S(1)} %shard_map.103.part_ref, f32[10,512,128]{2,1,0:T(8,128)S(1)} %get-tuple-element.40.q_ref.rest_6_, f32[10,512,128]{2,1,0:T(8,128)S(1)} %get-tuple-element.53.q1_ref, f32[2,512,128]{2,1,0:T(8,128)S(1)} %get-tuple-element.49.vel_ref.rest_7_, ...), custom_call_target="tpu_custom_call" | custom-call | flops 19660800 | bytes 12000000 | tf_op jit(solution)/shard_map/pallas_call | solution.py:495
  50.5 1.0 %shard_map.109 = f32[10,64,8,128]{3,2,1,0:T(8,128)} custom-call(f32[10,64,8,128]{3,2,1,0:T(8,128)} %bitcast.21, f32[640,128]{1,0:T(8,128)S(1)} %get-tuple-element.73.keep_ref, f32[640,128]{1,0:T(8,128)S(1)} %collective-permute-done.16.core_ref, f32[640,128]{1,0:T(8,128)S(1)} %collective-permute-done.17.far_ref), custom_call_target="tpu_custom_call", output_to_operand_aliasing={{}: (0, {})} | custom-call | tf_op jit(solution)/shard_map/pallas_call | solution.py:495
  (22 shorter events, 0.2 us)
Async XLA Ops:
  2.3 7.7 %collective-permute-start = (f32[640,128]{1,0:T(8,128)S(1)}, f32[640,128]{1,0:T(8,128)S(1)}, u32[]{:S(2)}, u32[]{:S(2)}) collective-permute-start(f32[640,128]{1,0:T(8,128)S(1)} %get-tuple-element.42), channel_id=1, source_target_pairs={{0,1},{1,0},{2,3},{3,2},{4,5},{5,4},{6,7},{7,6},{8,9},{9,8},{10,11... | collective-permute-start | bytes 983048 | tf_op jit(solution)/shard_map/ppermute | solution.py:522
  3.0 12.1 %collective-permute-start.1 = (f32[664,128]{1,0:T(8,128)S(1)}, f32[664,128]{1,0:T(8,128)S(1)}, u32[]{:S(2)}, u32[]{:S(2)}) collective-permute-start(f32[664,128]{1,0:T(8,128)S(1)} %get-tuple-element.44), channel_id=1, source_target_pairs={{1,17},{3,19},{5,21},{7,23},{9,25},{11,27},{13,29},{15,31},{17,1},... | collective-permute-start | bytes 1019912 | tf_op jit(solution)/shard_map/ppermute | solution.py:522
  5.4 9.5 %collective-permute-start.2 = (f32[344,128]{1,0:T(8,128)S(1)}, f32[344,128]{1,0:T(8,128)S(1)}, u32[]{:S(2)}, u32[]{:S(2)}) collective-permute-start(f32[344,128]{1,0:T(8,128)S(1)} %get-tuple-element.45), channel_id=1, source_target_pairs={{1,9},{3,11},{5,13},{7,15},{9,17},{11,19},{13,21},{15,23},{17,25},... | collective-permute-start | bytes 528392 | tf_op jit(solution)/shard_map/ppermute | solution.py:522
  6.9 8.2 %collective-permute-start.3 = (f32[344,128]{1,0:T(8,128)S(1)}, f32[344,128]{1,0:T(8,128)S(1)}, u32[]{:S(2)}, u32[]{:S(2)}) collective-permute-start(f32[344,128]{1,0:T(8,128)S(1)} %get-tuple-element.46), channel_id=1, source_target_pairs={{1,25},{3,27},{5,29},{7,31},{9,1},{11,3},{13,5},{15,7},{17,9},{19,... | collective-permute-start | bytes 528392 | tf_op jit(solution)/shard_map/ppermute | solution.py:522
  9.4 5.5 %collective-permute-start.4 = (f32[88,128]{1,0:T(8,128)S(1)}, f32[88,128]{1,0:T(8,128)S(1)}, u32[]{:S(2)}, u32[]{:S(2)}) collective-permute-start(f32[88,128]{1,0:T(8,128)S(1)} %get-tuple-element.47), channel_id=1, source_target_pairs={{0,8},{1,9},{2,10},{3,11},{4,12},{5,13},{6,14},{7,15},{8,16},{9,17... | collective-permute-start | bytes 135176 | tf_op jit(solution)/shard_map/ppermute | solution.py:522
  9.9 5.6 %collective-permute-start.5 = (f32[88,128]{1,0:T(8,128)S(1)}, f32[88,128]{1,0:T(8,128)S(1)}, u32[]{:S(2)}, u32[]{:S(2)}) collective-permute-start(f32[88,128]{1,0:T(8,128)S(1)} %get-tuple-element.48), channel_id=1, source_target_pairs={{0,24},{1,25},{2,26},{3,27},{4,28},{5,29},{6,30},{7,31},{8,0},{9,1... | collective-permute-start | bytes 135176 | tf_op jit(solution)/shard_map/ppermute | solution.py:522
  12.3 3.2 %copy-start = (f32[10,1,8192]{2,1,0:T(1,128)S(1)}, f32[10,1,8192]{2,1,0:T(1,128)}, u32[]{:S(2)}) copy-start(f32[10,1,8192]{2,1,0:T(1,128)} %param.12) | copy-start | bytes 983044
  12.3 3.2 %copy-start.1 = (s32[8,1]{0,1:T(1,128)S(1)}, s32[8,1]{0,1:T(1,128)}, u32[]{:S(2)}) copy-start(s32[8,1]{0,1:T(1,128)} %param.17) | copy-start | bytes 100
  12.3 3.2 %copy-start.2 = (s32[8]{0:T(128)S(1)}, s32[8]{0:T(128)}, u32[]{:S(2)}) copy-start(s32[8]{0:T(128)} %rest_11_.1) | copy-start | bytes 100
  12.3 3.2 %copy-start.3 = (s32[8]{0:T(128)S(1)}, s32[8]{0:T(128)}, u32[]{:S(2)}) copy-start(s32[8]{0:T(128)} %rest_12_.1) | copy-start | bytes 100
  16.4 14.7 %collective-permute-start.6 = (f32[656,128]{1,0:T(8,128)S(1)}, f32[656,128]{1,0:T(8,128)S(1)}, u32[]{:S(2)}, u32[]{:S(2)}) collective-permute-start(f32[656,128]{1,0:T(8,128)S(1)} %get-tuple-element.58), channel_id=1, source_target_pairs={{0,1},{1,0},{2,3},{3,2},{4,5},{5,4},{6,7},{7,6},{8,9},{9,8},{10,11... | collective-permute-start | bytes 1007624 | tf_op jit(solution)/shard_map/ppermute | solution.py:522
  17.3 13.8 %collective-permute-start.14 = (f32[656,128]{1,0:T(8,128)S(1)}, f32[656,128]{1,0:T(8,128)S(1)}, u32[]{:S(2)}, u32[]{:S(2)}) collective-permute-start(f32[656,128]{1,0:T(8,128)S(1)} %get-tuple-element.58), channel_id=1, source_target_pairs={{5,2},{13,10},{21,18},{29,26}} | collective-permute-start | bytes 1007624 | tf_op jit(solution)/shard_map/ppermute | solution.py:522
  17.9 13.2 %collective-permute-start.13 = (f32[656,128]{1,0:T(8,128)S(1)}, f32[656,128]{1,0:T(8,128)S(1)}, u32[]{:S(2)}, u32[]{:S(2)}) collective-permute-start(f32[656,128]{1,0:T(8,128)S(1)} %get-tuple-element.58), channel_id=1, source_target_pairs={{7,2},{15,10},{23,18},{31,26}} | collective-permute-start | bytes 1007624 | tf_op jit(solution)/shard_map/ppermute | solution.py:522
  18.6 5.4 %collective-permute-start.7 = (f32[320,128]{1,0:T(8,128)S(1)}, f32[320,128]{1,0:T(8,128)S(1)}, u32[]{:S(2)}, u32[]{:S(2)}) collective-permute-start(f32[320,128]{1,0:T(8,128)S(1)} %get-tuple-element.61), channel_id=1, source_target_pairs={{1,17},{3,19},{5,21},{7,23},{9,25},{11,27},{13,29},{15,31},{17,1},... | collective-permute-start | bytes 491528 | tf_op jit(solution)/shard_map/ppermute | solution.py:522
  19.6 8.3 %collective-permute-start.8 = (f32[320,128]{1,0:T(8,128)S(1)}, f32[320,128]{1,0:T(8,128)S(1)}, u32[]{:S(2)}, u32[]{:S(2)}) collective-permute-start(f32[320,128]{1,0:T(8,128)S(1)} %get-tuple-element.62), channel_id=1, source_target_pairs={{1,9},{3,11},{5,13},{7,15},{9,17},{11,19},{13,21},{15,23},{17,25},... | collective-permute-start | bytes 491528 | tf_op jit(solution)/shard_map/ppermute | solution.py:522
  24.0 7.0 %collective-permute-start.9 = (f32[320,128]{1,0:T(8,128)S(1)}, f32[320,128]{1,0:T(8,128)S(1)}, u32[]{:S(2)}, u32[]{:S(2)}) collective-permute-start(f32[320,128]{1,0:T(8,128)S(1)} %get-tuple-element.63), channel_id=1, source_target_pairs={{1,25},{3,27},{5,29},{7,31},{9,1},{11,3},{13,5},{15,7},{17,9},{19,... | collective-permute-start | bytes 491528 | tf_op jit(solution)/shard_map/ppermute | solution.py:522
  31.2 16.0 %collective-permute-start.15 = (f32[656,128]{1,0:T(8,128)S(1)}, f32[656,128]{1,0:T(8,128)S(1)}, u32[]{:S(2)}, u32[]{:S(2)}) collective-permute-start(f32[656,128]{1,0:T(8,128)S(1)} %shard_map.106.near_ref), channel_id=1, source_target_pairs={{2,0},{10,8},{18,16},{26,24}} | collective-permute-start | bytes 1007624 | tf_op jit(solution)/shard_map/ppermute | solution.py:522
  32.5 3.7 %collective-permute-start.10 = (f32[640,128]{1,0:T(8,128)S(1)}, f32[640,128]{1,0:T(8,128)S(1)}, u32[]{:S(2)}, u32[]{:S(2)}) collective-permute-start(f32[640,128]{1,0:T(8,128)S(1)} %shard_map.104.refs_0_), channel_id=1, source_target_pairs={{3,1},{7,5},{11,9},{15,13},{19,17},{23,21},{27,25},{31,29},{2,4},{... | collective-permute-start | bytes 983048 | tf_op jit(solution)/shard_map/ppermute | solution.py:522
  33.2 5.3 %collective-permute-start.11 = (f32[80,128]{1,0:T(8,128)S(1)}, f32[80,128]{1,0:T(8,128)S(1)}, u32[]{:S(2)}, u32[]{:S(2)}) collective-permute-start(f32[80,128]{1,0:T(8,128)S(1)} %get-tuple-element.66), channel_id=1, source_target_pairs={{0,8},{1,9},{2,10},{3,11},{4,12},{5,13},{6,14},{7,15},{8,16},{9,17... | collective-permute-start | bytes 122888 | tf_op jit(solution)/shard_map/ppermute | solution.py:522
  33.5 5.0 %collective-permute-start.12 = (f32[80,128]{1,0:T(8,128)S(1)}, f32[80,128]{1,0:T(8,128)S(1)}, u32[]{:S(2)}, u32[]{:S(2)}) collective-permute-start(f32[80,128]{1,0:T(8,128)S(1)} %get-tuple-element.67), channel_id=1, source_target_pairs={{0,24},{1,25},{2,26},{3,27},{4,28},{5,29},{6,30},{7,31},{8,0},{9,1... | collective-permute-start | bytes 122888 | tf_op jit(solution)/shard_map/ppermute | solution.py:522
  36.2 14.3 %collective-permute-start.17 = (f32[640,128]{1,0:T(8,128)S(1)}, f32[640,128]{1,0:T(8,128)S(1)}, u32[]{:S(2)}, u32[]{:S(2)}) collective-permute-start(f32[640,128]{1,0:T(8,128)S(1)} %shard_map.105.pair_ref), channel_id=1, source_target_pairs={{5,0},{13,8},{21,16},{29,24}} | collective-permute-start | bytes 983048 | tf_op jit(solution)/shard_map/ppermute | solution.py:522
  47.3 3.2 %collective-permute-start.16 = (f32[640,128]{1,0:T(8,128)S(1)}, f32[640,128]{1,0:T(8,128)S(1)}, u32[]{:S(2)}, u32[]{:S(2)}) collective-permute-start(f32[640,128]{1,0:T(8,128)S(1)} %get-tuple-element.74), channel_id=1, source_target_pairs={{0,1},{1,0},{2,3},{3,2},{4,5},{5,4},{6,7},{7,6},{8,9},{9,8},{10,11... | collective-permute-start | bytes 983048 | tf_op jit(solution)/shard_map/ppermute | solution.py:522

commit v13 on v10

--- a/solution.py
+++ b/solution.py
@@ -590,13 +590,14 @@
     down0 = send(core, [((i, j, 1), (i, j - 1, 0)) for i, j in every if j % 2 == 1])
 
     part, = call(inside_two_kernel, (qv, q1, velv, matrix, power), "vvvvv", [whole], cost=work)
-    part, own1 = lax.optimization_barrier((part, own1))
+    part, down0 = lax.optimization_barrier((part, down0))
+    pair0, = call(add_kernel, (core_in, down0), "vv", [wide])
+    part, own1, pair0 = lax.optimization_barrier((part, own1, pair0))
+    far0 = send(pair0, [((i, 2, 0), (i, 0, 0)) for i in range(n_az)])
     step, = call(functools.partial(tile_kernel, n_out, cap), (own1, z1, *rb, *ra), "v" * (2 + 2 * n_out), [row])
     step_in = send(step, down + inner)
-    er, el, core_in, step = lax.optimization_barrier((er, el, core_in, step))
+    er, el, step = lax.optimization_barrier((er, el, step))
     hl1, hr1 = send(er, ring(1)), send(el, ring(-1))
-    pair0, = call(add_kernel, (core_in, down0), "vv", [wide])
-    far0 = send(pair0, [((i, 2, 0), (i, 0, 0)) for i in range(n_az)])
     pair1, = call(add_kernel, (step, step_in), "vv", [row])
     far1 = send(pair1, across)
     pair1, hl1, hr1 = lax.optimization_barrier((pair1, hl1, hr1))

time: 47.5 us -> 46 us (0.968)
  waiting for transfers between devices: 12.8 us -> 9.29 us
  starting transfers between devices: 22.6 us -> 24.5 us
    ppermute x17, waiting for transfers between devices: 12.8 us -> 9.29 us  [send(): return lax.ppermute(x, AXES, [(number(*a), number(*b)) for a, b in route])]
    ppermute x17, starting transfers between devices: 22.6 us -> 24.5 us  [send(): return lax.ppermute(x, AXES, [(number(*a), number(*b)) for a, b in route])]
  transfers between devices with their start and end apart: 17 -> 17, of which waited for: 9 -> 8; matrix products, arithmetic and copies ran while one was open for 0% -> 0% of each run, Pallas kernels for 16% -> 17%
where the time goes in v13:
time: 46 us; the launch traced here: 45.7 us
  starting transfers between devices  24.5 us (53%)
  Pallas kernels  11.8 us (26%)
  waiting for transfers between devices  9.29 us (20%)
    ppermute x17, starting transfers between devices, send(): return lax.ppermute(x, AXES, [(number(*a), number(*b)) for a, b in route])  24.5 us
    pallas_call x10, Pallas kernels, call(): pl.pallas_call(kernel, in_specs=[pl.BlockSpec(memory_space=SPACES[k]) for...  11.8 us
    ppermute x17, waiting for transfers between devices, send(): return lax.ppermute(x, AXES, [(number(*a), number(*b)) for a, b in route])  9.29 us
  transfers between devices with their start and end apart: 17, of which 8 were waited for; matrix products, arithmetic and copies ran while one was open for 0% of the time, Pallas kernels for 17%

profile of v13, /device:TPU:0, one launch (start us, length us, event | category | flops | bytes accessed | tf_op | source)
XLA Modules:
  0.0 45.7 jit_solution(14906892218401723472)
XLA Ops:
  0.0 2.2 %shard_map.100 = (f32[664,128]{1,0:T(8,128)S(1)}, f32[344,128]{1,0:T(8,128)S(1)}, f32[344,128]{1,0:T(8,128)S(1)}, f32[10,512,128]{2,1,0:T(8,128)S(1)}, f32[2,512...) custom-call(f32[10,512,128]{2,1,0:T(8,128)} %bitcast.20, ...), custom_call_target="tpu_custom_call" | custom-call | tf_op jit(solution)/shard_map/pallas_call | solution.py:495
  2.3 0.8 %collective-permute-start = (f32[640,128]{1,0:T(8,128)S(1)}, f32[640,128]{1,0:T(8,128)S(1)}, u32[]{:S(2)}, u32[]{:S(2)}) collective-permute-start(f32[640,128]{1,0:T(8,128)S(1)} %get-tuple-element.44), channel_id=1, source_target_pairs={{0,1},{1,0},{2,3},{3,2},{4,5},{5,4},{6,7},{7,6},{8,9},{9,8},{10,11... | collective-permute-start | bytes 983048 | tf_op jit(solution)/shard_map/ppermute | solution.py:522
  3.0 2.4 %collective-permute-start.1 = (f32[664,128]{1,0:T(8,128)S(1)}, f32[664,128]{1,0:T(8,128)S(1)}, u32[]{:S(2)}, u32[]{:S(2)}) collective-permute-start(f32[664,128]{1,0:T(8,128)S(1)} %get-tuple-element.46), channel_id=1, source_target_pairs={{1,17},{3,19},{5,21},{7,23},{9,25},{11,27},{13,29},{15,31},{17,1},... | collective-permute-start | bytes 1019912 | tf_op jit(solution)/shard_map/ppermute | solution.py:522
  5.4 1.5 %collective-permute-start.2 = (f32[344,128]{1,0:T(8,128)S(1)}, f32[344,128]{1,0:T(8,128)S(1)}, u32[]{:S(2)}, u32[]{:S(2)}) collective-permute-start(f32[344,128]{1,0:T(8,128)S(1)} %get-tuple-element.47), channel_id=1, source_target_pairs={{1,9},{3,11},{5,13},{7,15},{9,17},{11,19},{13,21},{15,23},{17,25},... | collective-permute-start | bytes 528392 | tf_op jit(solution)/shard_map/ppermute | solution.py:522
  6.9 2.5 %collective-permute-start.3 = (f32[344,128]{1,0:T(8,128)S(1)}, f32[344,128]{1,0:T(8,128)S(1)}, u32[]{:S(2)}, u32[]{:S(2)}) collective-permute-start(f32[344,128]{1,0:T(8,128)S(1)} %get-tuple-element.48), channel_id=1, source_target_pairs={{1,25},{3,27},{5,29},{7,31},{9,1},{11,3},{13,5},{15,7},{17,9},{19,... | collective-permute-start | bytes 528392 | tf_op jit(solution)/shard_map/ppermute | solution.py:522
  9.4 0.5 %collective-permute-start.4 = (f32[88,128]{1,0:T(8,128)S(1)}, f32[88,128]{1,0:T(8,128)S(1)}, u32[]{:S(2)}, u32[]{:S(2)}) collective-permute-start(f32[88,128]{1,0:T(8,128)S(1)} %get-tuple-element.49), channel_id=1, source_target_pairs={{0,8},{1,9},{2,10},{3,11},{4,12},{5,13},{6,14},{7,15},{8,16},{9,17... | collective-permute-start | bytes 135176 | tf_op jit(solution)/shard_map/ppermute | solution.py:522
  9.9 2.4 %collective-permute-start.5 = (f32[88,128]{1,0:T(8,128)S(1)}, f32[88,128]{1,0:T(8,128)S(1)}, u32[]{:S(2)}, u32[]{:S(2)}) collective-permute-start(f32[88,128]{1,0:T(8,128)S(1)} %get-tuple-element.50), channel_id=1, source_target_pairs={{0,24},{1,25},{2,26},{3,27},{4,28},{5,29},{6,30},{7,31},{8,0},{9,1... | collective-permute-start | bytes 135176 | tf_op jit(solution)/shard_map/ppermute | solution.py:522
  12.3 2.5 %shard_map.101.rest_5_ = f32[10,512,128]{2,1,0:T(8,128)S(1)} custom-call(f32[10,512,128]{2,1,0:T(8,128)S(1)} %get-tuple-element.42.q_ref.rest_6_, f32[2,512,128]{2,1,0:T(8,128)S(1)} %get-tuple-element.51.vel_ref.rest_7_, f32[80,240]{1,0:T(8,128)S(1)} %get-tuple-element.52.a_ref.rest_2_, f32[72,128]{1,0:T(8,128)S(1)} %get-tuple-element.53.power_ref.rest_3_), custom_call_target="tpu_custom_call" | custom-call | flops 19660800 | bytes 12000000 | tf_op jit(solution)/shard_map/pallas_call | solution.py:495
  14.8 0.1 collective-permute-done.4.rest_3_.hl0_ref
  14.9 0.2 collective-permute-done.3.rest_2_.rest_5_
  15.1 0.4 collective-permute-done.5.rest_4_.hr0_ref
  15.5 0.9 %shard_map.102 = (f32[320,128]{1,0:T(8,128)S(1)}, f32[320,128]{1,0:T(8,128)S(1)}, f32[320,128]{1,0:T(8,128)S(1)}, f32[10,512,128]{2,1,0:T(8,128)S(1)}, f32[656,1...) custom-call(f32[640,128]{1,0:T(8,128)S(1)} %collective-permute-done., ...), custom_call_target="tpu_custom_call" | custom-call | tf_op jit(solution)/shard_map/pallas_call | solution.py:495
  16.4 1.3 %collective-permute-start.6 = (f32[656,128]{1,0:T(8,128)S(1)}, f32[656,128]{1,0:T(8,128)S(1)}, u32[]{:S(2)}, u32[]{:S(2)}) collective-permute-start(f32[656,128]{1,0:T(8,128)S(1)} %get-tuple-element.56), channel_id=1, source_target_pairs={{3,0},{7,4},{11,8},{15,12},{19,16},{23,20},{27,24},{31,28}} | collective-permute-start | bytes 1007624 | tf_op jit(solution)/shard_map/ppermute | solution.py:522
  17.7 0.3 collective-permute-start.7
  18.0 2.6 %collective-permute-start.8 = (f32[320,128]{1,0:T(8,128)S(1)}, f32[320,128]{1,0:T(8,128)S(1)}, u32[]{:S(2)}, u32[]{:S(2)}) collective-permute-start(f32[320,128]{1,0:T(8,128)S(1)} %get-tuple-element.63), channel_id=1, source_target_pairs={{1,17},{3,19},{5,21},{7,23},{9,25},{11,27},{13,29},{15,31},{17,1},... | collective-permute-start | bytes 491528 | tf_op jit(solution)/shard_map/ppermute | solution.py:522
  20.5 0.0 collective-permute-start.9
  20.6 1.8 %collective-permute-start.10 = (f32[320,128]{1,0:T(8,128)S(1)}, f32[320,128]{1,0:T(8,128)S(1)}, u32[]{:S(2)}, u32[]{:S(2)}) collective-permute-start(f32[320,128]{1,0:T(8,128)S(1)} %get-tuple-element.65), channel_id=1, source_target_pairs={{1,25},{3,27},{5,29},{7,31},{9,1},{11,3},{13,5},{15,7},{17,9},{19,... | collective-permute-start | bytes 491528 | tf_op jit(solution)/shard_map/ppermute | solution.py:522
  22.4 2.8 %shard_map.103.part_ref = f32[10,512,128]{2,1,0:T(8,128)S(1)} custom-call(f32[10,512,128]{2,1,0:T(8,128)S(1)} %get-tuple-element.42.q_ref.rest_6_, f32[10,512,128]{2,1,0:T(8,128)S(1)} %get-tuple-element.55.q1_ref, f32[2,512,128]{2,1,0:T(8,128)S(1)} %get-tuple-element.51.vel_ref.rest_7_, f32[80,240]{1,0:T(8,128)S(1)} %get-tuple-element.52.a_ref.rest_2_, ...), custom_call_target="tpu_custom_call" | custom-call | flops 19660800 | bytes 12000000 | tf_op jit(solution)/shard_map/pallas_call | solution.py:495
  25.2 2.5 %collective-permute-done.6.refs_1_ = f32[656,128]{1,0:T(8,128)S(1)} collective-permute-done((f32[656,128]{1,0:T(8,128)S(1)}, f32[656,128]{1,0:T(8,128)S(1)}, u32[]{:S(2)}, u32[]{:S(2)}) %collective-permute-start.6) | collective-permute-done | bytes 335904 | tf_op jit(solution)/shard_map/ppermute | solution.py:522
  27.8 1.3 %collective-permute-start.14 = (f32[656,128]{1,0:T(8,128)S(1)}, f32[656,128]{1,0:T(8,128)S(1)}, u32[]{:S(2)}, u32[]{:S(2)}) collective-permute-start(f32[656,128]{1,0:T(8,128)S(1)} %shard_map.104.near_ref), channel_id=1, source_target_pairs={{4,0},{12,8},{20,16},{28,24}} | collective-permute-start | bytes 1007624 | tf_op jit(solution)/shard_map/ppermute | solution.py:522
  29.1 0.7 %collective-permute-start.11 = (f32[640,128]{1,0:T(8,128)S(1)}, f32[640,128]{1,0:T(8,128)S(1)}, u32[]{:S(2)}, u32[]{:S(2)}) collective-permute-start(f32[640,128]{1,0:T(8,128)S(1)} %shard_map.105.refs_0_), channel_id=1, source_target_pairs={{3,1},{7,5},{11,9},{15,13},{19,17},{23,21},{27,25},{31,29},{2,4},{... | collective-permute-start | bytes 983048 | tf_op jit(solution)/shard_map/ppermute | solution.py:522
  29.8 1.9 %collective-permute-start.12 = (f32[80,128]{1,0:T(8,128)S(1)}, f32[80,128]{1,0:T(8,128)S(1)}, u32[]{:S(2)}, u32[]{:S(2)}) collective-permute-start(f32[80,128]{1,0:T(8,128)S(1)} %get-tuple-element.69), channel_id=1, source_target_pairs={{0,8},{1,9},{2,10},{3,11},{4,12},{5,13},{6,14},{7,15},{8,16},{9,17... | collective-permute-start | bytes 122888 | tf_op jit(solution)/shard_map/ppermute | solution.py:522
  31.7 1.1 %collective-permute-start.13 = (f32[80,128]{1,0:T(8,128)S(1)}, f32[80,128]{1,0:T(8,128)S(1)}, u32[]{:S(2)}, u32[]{:S(2)}) collective-permute-start(f32[80,128]{1,0:T(8,128)S(1)} %get-tuple-element.70), channel_id=1, source_target_pairs={{0,24},{1,25},{2,26},{3,27},{4,28},{5,29},{6,30},{7,31},{8,0},{9,1... | collective-permute-start | bytes 122888 | tf_op jit(solution)/shard_map/ppermute | solution.py:522
  32.9 1.3 %collective-permute-start.16 = (f32[640,128]{1,0:T(8,128)S(1)}, f32[640,128]{1,0:T(8,128)S(1)}, u32[]{:S(2)}, u32[]{:S(2)}) collective-permute-start(f32[640,128]{1,0:T(8,128)S(1)} %shard_map.106.pair_ref), channel_id=1, source_target_pairs={{5,0},{13,8},{21,16},{29,24}} | collective-permute-start | bytes 983048 | tf_op jit(solution)/shard_map/ppermute | solution.py:522
  34.1 0.6 %collective-permute-done.12.hl_ref = f32[80,128]{1,0:T(8,128)S(1)} collective-permute-done((f32[80,128]{1,0:T(8,128)S(1)}, f32[80,128]{1,0:T(8,128)S(1)}, u32[]{:S(2)}, u32[]{:S(2)}) %collective-permute-start.12) | collective-permute-done | bytes 40992 | tf_op jit(solution)/shard_map/ppermute | solution.py:522
  34.8 0.9 %collective-permute-done.13.hr_ref = f32[80,128]{1,0:T(8,128)S(1)} collective-permute-done((f32[80,128]{1,0:T(8,128)S(1)}, f32[80,128]{1,0:T(8,128)S(1)}, u32[]{:S(2)}, u32[]{:S(2)}) %collective-permute-start.13) | collective-permute-done | bytes 40992 | tf_op jit(solution)/shard_map/ppermute | solution.py:522
  35.7 2.1 %collective-permute-done.14.far_ref = f32[656,128]{1,0:T(8,128)S(1)} collective-permute-done((f32[656,128]{1,0:T(8,128)S(1)}, f32[656,128]{1,0:T(8,128)S(1)}, u32[]{:S(2)}, u32[]{:S(2)}) %collective-permute-start.14) | collective-permute-done | bytes 335904 | tf_op jit(solution)/shard_map/ppermute | solution.py:522
  37.8 0.1 shard_map.107
  37.9 2.2 %collective-permute-start.15 = (f32[640,128]{1,0:T(8,128)S(1)}, f32[640,128]{1,0:T(8,128)S(1)}, u32[]{:S(2)}, u32[]{:S(2)}) collective-permute-start(f32[640,128]{1,0:T(8,128)S(1)} %get-tuple-element.78), channel_id=1, source_target_pairs={{0,1},{1,0},{2,3},{3,2},{4,5},{5,4},{6,7},{7,6},{8,9},{9,8},{10,11... | collective-permute-start | bytes 983048 | tf_op jit(solution)/shard_map/ppermute | solution.py:522
  40.1 2.2 %shard_map.108 = (f32[10,512,128]{2,1,0:T(8,128)}, f32[640,128]{1,0:T(8,128)S(1)}) custom-call(f32[10,512,128]{2,1,0:T(8,128)S(1)} %shard_map.103.part_ref, f32[10,512,128]{2,1,0:T(8,128)S(1)} %get-tuple-element.42.q_ref.rest_6_, f32[10,512,128]{2,1,0:T(8,128)S(1)} %get-tuple-element.55.q1_ref, f32[2,512,128]{2,1,0:T(8,128)S(1)} %get-tuple-element.51.vel_ref.rest_7_, ...), custom_call_target="tpu_custom_call" | custom-call | flops 19660800 | bytes 12000000 | tf_op jit(solution)/shard_map/pallas_call | solution.py:495
  42.4 2.4 %collective-permute-done.16.far_ref = f32[640,128]{1,0:T(8,128)S(1)} collective-permute-done((f32[640,128]{1,0:T(8,128)S(1)}, f32[640,128]{1,0:T(8,128)S(1)}, u32[]{:S(2)}, u32[]{:S(2)}) %collective-permute-start.16) | collective-permute-done | bytes 327712 | tf_op jit(solution)/shard_map/ppermute | solution.py:522
  44.8 1.0 %shard_map.109 = f32[10,64,8,128]{3,2,1,0:T(8,128)} custom-call(f32[10,64,8,128]{3,2,1,0:T(8,128)} %bitcast.21, f32[640,128]{1,0:T(8,128)S(1)} %get-tuple-element.77.keep_ref, f32[640,128]{1,0:T(8,128)S(1)} %collective-permute-done.15.core_ref, f32[640,128]{1,0:T(8,128)S(1)} %collective-permute-done.16.far_ref), custom_call_target="tpu_custom_call", output_to_operand_aliasing={{}: (0, {})} | custom-call | tf_op jit(solution)/shard_map/pallas_call | solution.py:495
  (20 shorter events, 0.2 us)
Async XLA Ops:
  2.3 7.7 %collective-permute-start = (f32[640,128]{1,0:T(8,128)S(1)}, f32[640,128]{1,0:T(8,128)S(1)}, u32[]{:S(2)}, u32[]{:S(2)}) collective-permute-start(f32[640,128]{1,0:T(8,128)S(1)} %get-tuple-element.44), channel_id=1, source_target_pairs={{0,1},{1,0},{2,3},{3,2},{4,5},{5,4},{6,7},{7,6},{8,9},{9,8},{10,11... | collective-permute-start | bytes 983048 | tf_op jit(solution)/shard_map/ppermute | solution.py:522
  3.0 12.1 %collective-permute-start.1 = (f32[664,128]{1,0:T(8,128)S(1)}, f32[664,128]{1,0:T(8,128)S(1)}, u32[]{:S(2)}, u32[]{:S(2)}) collective-permute-start(f32[664,128]{1,0:T(8,128)S(1)} %get-tuple-element.46), channel_id=1, source_target_pairs={{1,17},{3,19},{5,21},{7,23},{9,25},{11,27},{13,29},{15,31},{17,1},... | collective-permute-start | bytes 1019912 | tf_op jit(solution)/shard_map/ppermute | solution.py:522
  5.4 9.5 %collective-permute-start.2 = (f32[344,128]{1,0:T(8,128)S(1)}, f32[344,128]{1,0:T(8,128)S(1)}, u32[]{:S(2)}, u32[]{:S(2)}) collective-permute-start(f32[344,128]{1,0:T(8,128)S(1)} %get-tuple-element.47), channel_id=1, source_target_pairs={{1,9},{3,11},{5,13},{7,15},{9,17},{11,19},{13,21},{15,23},{17,25},... | collective-permute-start | bytes 528392 | tf_op jit(solution)/shard_map/ppermute | solution.py:522
  6.9 8.2 %collective-permute-start.3 = (f32[344,128]{1,0:T(8,128)S(1)}, f32[344,128]{1,0:T(8,128)S(1)}, u32[]{:S(2)}, u32[]{:S(2)}) collective-permute-start(f32[344,128]{1,0:T(8,128)S(1)} %get-tuple-element.48), channel_id=1, source_target_pairs={{1,25},{3,27},{5,29},{7,31},{9,1},{11,3},{13,5},{15,7},{17,9},{19,... | collective-permute-start | bytes 528392 | tf_op jit(solution)/shard_map/ppermute | solution.py:522
  9.4 5.5 %collective-permute-start.4 = (f32[88,128]{1,0:T(8,128)S(1)}, f32[88,128]{1,0:T(8,128)S(1)}, u32[]{:S(2)}, u32[]{:S(2)}) collective-permute-start(f32[88,128]{1,0:T(8,128)S(1)} %get-tuple-element.49), channel_id=1, source_target_pairs={{0,8},{1,9},{2,10},{3,11},{4,12},{5,13},{6,14},{7,15},{8,16},{9,17... | collective-permute-start | bytes 135176 | tf_op jit(solution)/shard_map/ppermute | solution.py:522
  9.9 5.6 %collective-permute-start.5 = (f32[88,128]{1,0:T(8,128)S(1)}, f32[88,128]{1,0:T(8,128)S(1)}, u32[]{:S(2)}, u32[]{:S(2)}) collective-permute-start(f32[88,128]{1,0:T(8,128)S(1)} %get-tuple-element.50), channel_id=1, source_target_pairs={{0,24},{1,25},{2,26},{3,27},{4,28},{5,29},{6,30},{7,31},{8,0},{9,1... | collective-permute-start | bytes 135176 | tf_op jit(solution)/shard_map/ppermute | solution.py:522
  12.3 3.2 %copy-start = (f32[10,1,8192]{2,1,0:T(1,128)S(1)}, f32[10,1,8192]{2,1,0:T(1,128)}, u32[]{:S(2)}) copy-start(f32[10,1,8192]{2,1,0:T(1,128)} %param.12) | copy-start | bytes 983044
  12.3 3.2 %copy-start.1 = (s32[8,1]{0,1:T(1,128)S(1)}, s32[8,1]{0,1:T(1,128)}, u32[]{:S(2)}) copy-start(s32[8,1]{0,1:T(1,128)} %param.17) | copy-start | bytes 100
  12.3 3.2 %copy-start.2 = (s32[8]{0:T(128)S(1)}, s32[8]{0:T(128)}, u32[]{:S(2)}) copy-start(s32[8]{0:T(128)} %rest_11_.1) | copy-start | bytes 100
  12.3 3.2 %copy-start.3 = (s32[8]{0:T(128)S(1)}, s32[8]{0:T(128)}, u32[]{:S(2)}) copy-start(s32[8]{0:T(128)} %rest_12_.1) | copy-start | bytes 100
  16.4 11.3 %collective-permute-start.6 = (f32[656,128]{1,0:T(8,128)S(1)}, f32[656,128]{1,0:T(8,128)S(1)}, u32[]{:S(2)}, u32[]{:S(2)}) collective-permute-start(f32[656,128]{1,0:T(8,128)S(1)} %get-tuple-element.56), channel_id=1, source_target_pairs={{3,0},{7,4},{11,8},{15,12},{19,16},{23,20},{27,24},{31,28}} | collective-permute-start | bytes 1007624 | tf_op jit(solution)/shard_map/ppermute | solution.py:522
  17.7 10.0 %collective-permute-start.7 = (f32[656,128]{1,0:T(8,128)S(1)}, f32[656,128]{1,0:T(8,128)S(1)}, u32[]{:S(2)}, u32[]{:S(2)}) collective-permute-start(f32[656,128]{1,0:T(8,128)S(1)} %get-tuple-element.56), channel_id=1, source_target_pairs={{0,1},{1,0},{2,3},{3,2},{4,5},{5,4},{6,7},{7,6},{8,9},{9,8},{10,11... | collective-permute-start | bytes 1007624 | tf_op jit(solution)/shard_map/ppermute | solution.py:522
  18.0 11.1 %collective-permute-start.8 = (f32[320,128]{1,0:T(8,128)S(1)}, f32[320,128]{1,0:T(8,128)S(1)}, u32[]{:S(2)}, u32[]{:S(2)}) collective-permute-start(f32[320,128]{1,0:T(8,128)S(1)} %get-tuple-element.63), channel_id=1, source_target_pairs={{1,17},{3,19},{5,21},{7,23},{9,25},{11,27},{13,29},{15,31},{17,1},... | collective-permute-start | bytes 491528 | tf_op jit(solution)/shard_map/ppermute | solution.py:522
  20.5 8.5 %collective-permute-start.9 = (f32[320,128]{1,0:T(8,128)S(1)}, f32[320,128]{1,0:T(8,128)S(1)}, u32[]{:S(2)}, u32[]{:S(2)}) collective-permute-start(f32[320,128]{1,0:T(8,128)S(1)} %get-tuple-element.64), channel_id=1, source_target_pairs={{1,9},{3,11},{5,13},{7,15},{9,17},{11,19},{13,21},{15,23},{17,25},... | collective-permute-start | bytes 491528 | tf_op jit(solution)/shard_map/ppermute | solution.py:522
  20.6 8.5 %collective-permute-start.10 = (f32[320,128]{1,0:T(8,128)S(1)}, f32[320,128]{1,0:T(8,128)S(1)}, u32[]{:S(2)}, u32[]{:S(2)}) collective-permute-start(f32[320,128]{1,0:T(8,128)S(1)} %get-tuple-element.65), channel_id=1, source_target_pairs={{1,25},{3,27},{5,29},{7,31},{9,1},{11,3},{13,5},{15,7},{17,9},{19,... | collective-permute-start | bytes 491528 | tf_op jit(solution)/shard_map/ppermute | solution.py:522
  27.8 10.1 %collective-permute-start.14 = (f32[656,128]{1,0:T(8,128)S(1)}, f32[656,128]{1,0:T(8,128)S(1)}, u32[]{:S(2)}, u32[]{:S(2)}) collective-permute-start(f32[656,128]{1,0:T(8,128)S(1)} %shard_map.104.near_ref), channel_id=1, source_target_pairs={{4,0},{12,8},{20,16},{28,24}} | collective-permute-start | bytes 1007624 | tf_op jit(solution)/shard_map/ppermute | solution.py:522
  29.1 3.7 %collective-permute-start.11 = (f32[640,128]{1,0:T(8,128)S(1)}, f32[640,128]{1,0:T(8,128)S(1)}, u32[]{:S(2)}, u32[]{:S(2)}) collective-permute-start(f32[640,128]{1,0:T(8,128)S(1)} %shard_map.105.refs_0_), channel_id=1, source_target_pairs={{3,1},{7,5},{11,9},{15,13},{19,17},{23,21},{27,25},{31,29},{2,4},{... | collective-permute-start | bytes 983048 | tf_op jit(solution)/shard_map/ppermute | solution.py:522
  29.8 5.0 %collective-permute-start.12 = (f32[80,128]{1,0:T(8,128)S(1)}, f32[80,128]{1,0:T(8,128)S(1)}, u32[]{:S(2)}, u32[]{:S(2)}) collective-permute-start(f32[80,128]{1,0:T(8,128)S(1)} %get-tuple-element.69), channel_id=1, source_target_pairs={{0,8},{1,9},{2,10},{3,11},{4,12},{5,13},{6,14},{7,15},{8,16},{9,17... | collective-permute-start | bytes 122888 | tf_op jit(solution)/shard_map/ppermute | solution.py:522
  31.7 4.0 %collective-permute-start.13 = (f32[80,128]{1,0:T(8,128)S(1)}, f32[80,128]{1,0:T(8,128)S(1)}, u32[]{:S(2)}, u32[]{:S(2)}) collective-permute-start(f32[80,128]{1,0:T(8,128)S(1)} %get-tuple-element.70), channel_id=1, source_target_pairs={{0,24},{1,25},{2,26},{3,27},{4,28},{5,29},{6,30},{7,31},{8,0},{9,1... | collective-permute-start | bytes 122888 | tf_op jit(solution)/shard_map/ppermute | solution.py:522
  32.9 11.9 %collective-permute-start.16 = (f32[640,128]{1,0:T(8,128)S(1)}, f32[640,128]{1,0:T(8,128)S(1)}, u32[]{:S(2)}, u32[]{:S(2)}) collective-permute-start(f32[640,128]{1,0:T(8,128)S(1)} %shard_map.106.pair_ref), channel_id=1, source_target_pairs={{5,0},{13,8},{21,16},{29,24}} | collective-permute-start | bytes 983048 | tf_op jit(solution)/shard_map/ppermute | solution.py:522
  37.9 6.9 %collective-permute-start.15 = (f32[640,128]{1,0:T(8,128)S(1)}, f32[640,128]{1,0:T(8,128)S(1)}, u32[]{:S(2)}, u32[]{:S(2)}) collective-permute-start(f32[640,128]{1,0:T(8,128)S(1)} %get-tuple-element.78), channel_id=1, source_target_pairs={{0,1},{1,0},{2,3},{3,2},{4,5},{5,4},{6,7},{7,6},{8,9},{9,8},{10,11... | collective-permute-start | bytes 983048 | tf_op jit(solution)/shard_map/ppermute | solution.py:522

commit v14 on v13

--- a/solution.py
+++ b/solution.py
@@ -338,7 +338,7 @@
         core_ref[pl.ds(rows, EXT), :] = jnp.zeros((EXT, LANES), f32)
         for v in range(NV):
             core_ref[pl.ds(v * n, n), :] = q1_ref[v, pl.ds(0, n, stride=CAX), :]
-        axial_rows(q1_ref, vel_ref, out_refs[:CAX // cap], (z_ref,))
+        axial_rows(q1_ref, vel_ref, out_refs[n_out - CAX // cap:], (z_ref,))
 
     @pl.when(plen == 1)
     def _():
@@ -548,7 +548,8 @@
 
     def compact(k):
         out = [((i, j, 1), ((i + shifts[k]) % n_az, j, 1)) for i, j in every]
-        return out + [((i, j, 0), (i, mate(0, j), 0) if k < pieces else (i ^ 1, j, 0)) for i, j in every]
+        return out + [((i, j, 0), (i, mate(0, j), 0) if k >= n_out - pieces else (i ^ 1, j, 0))
+                      for i, j in every]
 
     q, vel = view(cells[0]), view(speeds[0])
     sup = supply.reshape(rows, LANES)
@@ -605,7 +606,7 @@
     dq, core2 = call(inlet_kernel, (pair1, far0, pair0), "vvv", [wide, row])
     core2_in = send(core2, swap)
     out, keep = call(functools.partial(border_two_kernel, n_ax, pieces),
-                     (part, qv, q1, velv, core_in, sup, step_in, dq, hl1, hr1, hl0, hr0, *rb[:pieces], matrix, power),
+                     (part, qv, q1, velv, core_in, sup, step_in, dq, hl1, hr1, hl0, hr0, *rb[n_out - pieces:], matrix, power),
                      "v" * (14 + pieces), [whole, row],
                      [pltpu.VMEM(q.shape, f32)] + [pltpu.VMEM((rows, LANES), f32)] * 2 + [pltpu.SemaphoreType.DMA((NV,))],
                      cost=work, to="hv")

time: 46 us -> 44.6 us (0.970)
  waiting for transfers between devices: 9.29 us -> 5.93 us
  starting transfers between devices: 24.5 us -> 26.1 us
    ppermute x17, waiting for transfers between devices: 9.29 us -> 5.93 us  [send(): return lax.ppermute(x, AXES, [(number(*a), number(*b)) for a, b in route])]
    ppermute x17, starting transfers between devices: 24.5 us -> 26.1 us  [send(): return lax.ppermute(x, AXES, [(number(*a), number(*b)) for a, b in route])]
  transfers between devices with their start and end apart: 17 -> 17, of which waited for: 8 -> 9; matrix products, arithmetic and copies ran while one was open for 0% -> 0% of each run, Pallas kernels for 17% -> 17%
where the time goes in v14:
time: 44.6 us; the launch traced here: 44 us
  starting transfers between devices  26.1 us (59%)
  Pallas kernels  11.8 us (26%)
  waiting for transfers between devices  5.93 us (13%)
    ppermute x17, starting transfers between devices, send(): return lax.ppermute(x, AXES, [(number(*a), number(*b)) for a, b in route])  26.1 us
    pallas_call x10, Pallas kernels, call(): pl.pallas_call(kernel, in_specs=[pl.BlockSpec(memory_space=SPACES[k]) for...  11.8 us
    ppermute x17, waiting for transfers between devices, send(): return lax.ppermute(x, AXES, [(number(*a), number(*b)) for a, b in route])  5.93 us
  transfers between devices with their start and end apart: 17, of which 9 were waited for; matrix products, arithmetic and copies ran while one was open for 0% of the time, Pallas kernels for 17%

profile of v14, /device:TPU:0, one launch (start us, length us, event | category | flops | bytes accessed | tf_op | source)
XLA Modules:
  0.0 44.0 jit_solution(1534469056514959568)
XLA Ops:
  0.0 2.2 %shard_map.100 = (f32[664,128]{1,0:T(8,128)S(1)}, f32[344,128]{1,0:T(8,128)S(1)}, f32[344,128]{1,0:T(8,128)S(1)}, f32[10,512,128]{2,1,0:T(8,128)S(1)}, f32[2,512...) custom-call(f32[10,512,128]{2,1,0:T(8,128)} %bitcast.20, ...), custom_call_target="tpu_custom_call" | custom-call | tf_op jit(solution)/shard_map/pallas_call | solution.py:495
  2.3 0.7 %collective-permute-start = (f32[640,128]{1,0:T(8,128)S(1)}, f32[640,128]{1,0:T(8,128)S(1)}, u32[]{:S(2)}, u32[]{:S(2)}) collective-permute-start(f32[640,128]{1,0:T(8,128)S(1)} %get-tuple-element.44), channel_id=1, source_target_pairs={{0,1},{1,0},{2,3},{3,2},{4,5},{5,4},{6,7},{7,6},{8,9},{9,8},{10,11... | collective-permute-start | bytes 983048 | tf_op jit(solution)/shard_map/ppermute | solution.py:522
  3.0 2.4 %collective-permute-start.1 = (f32[664,128]{1,0:T(8,128)S(1)}, f32[664,128]{1,0:T(8,128)S(1)}, u32[]{:S(2)}, u32[]{:S(2)}) collective-permute-start(f32[664,128]{1,0:T(8,128)S(1)} %get-tuple-element.46), channel_id=1, source_target_pairs={{1,17},{3,19},{5,21},{7,23},{9,25},{11,27},{13,29},{15,31},{17,1},... | collective-permute-start | bytes 1019912 | tf_op jit(solution)/shard_map/ppermute | solution.py:522
  5.4 1.5 %collective-permute-start.2 = (f32[344,128]{1,0:T(8,128)S(1)}, f32[344,128]{1,0:T(8,128)S(1)}, u32[]{:S(2)}, u32[]{:S(2)}) collective-permute-start(f32[344,128]{1,0:T(8,128)S(1)} %get-tuple-element.47), channel_id=1, source_target_pairs={{1,9},{3,11},{5,13},{7,15},{9,17},{11,19},{13,21},{15,23},{17,25},... | collective-permute-start | bytes 528392 | tf_op jit(solution)/shard_map/ppermute | solution.py:522
  6.9 2.5 %collective-permute-start.3 = (f32[344,128]{1,0:T(8,128)S(1)}, f32[344,128]{1,0:T(8,128)S(1)}, u32[]{:S(2)}, u32[]{:S(2)}) collective-permute-start(f32[344,128]{1,0:T(8,128)S(1)} %get-tuple-element.48), channel_id=1, source_target_pairs={{1,25},{3,27},{5,29},{7,31},{9,1},{11,3},{13,5},{15,7},{17,9},{19,... | collective-permute-start | bytes 528392 | tf_op jit(solution)/shard_map/ppermute | solution.py:522
  9.4 0.5 %collective-permute-start.4 = (f32[88,128]{1,0:T(8,128)S(1)}, f32[88,128]{1,0:T(8,128)S(1)}, u32[]{:S(2)}, u32[]{:S(2)}) collective-permute-start(f32[88,128]{1,0:T(8,128)S(1)} %get-tuple-element.49), channel_id=1, source_target_pairs={{0,8},{1,9},{2,10},{3,11},{4,12},{5,13},{6,14},{7,15},{8,16},{9,17... | collective-permute-start | bytes 135176 | tf_op jit(solution)/shard_map/ppermute | solution.py:522
  9.9 2.4 %collective-permute-start.5 = (f32[88,128]{1,0:T(8,128)S(1)}, f32[88,128]{1,0:T(8,128)S(1)}, u32[]{:S(2)}, u32[]{:S(2)}) collective-permute-start(f32[88,128]{1,0:T(8,128)S(1)} %get-tuple-element.50), channel_id=1, source_target_pairs={{0,24},{1,25},{2,26},{3,27},{4,28},{5,29},{6,30},{7,31},{8,0},{9,1... | collective-permute-start | bytes 135176 | tf_op jit(solution)/shard_map/ppermute | solution.py:522
  12.3 2.5 %shard_map.101.rest_5_ = f32[10,512,128]{2,1,0:T(8,128)S(1)} custom-call(f32[10,512,128]{2,1,0:T(8,128)S(1)} %get-tuple-element.42.q_ref.rest_6_, f32[2,512,128]{2,1,0:T(8,128)S(1)} %get-tuple-element.51.vel_ref.rest_7_, f32[80,240]{1,0:T(8,128)S(1)} %get-tuple-element.52.a_ref.rest_2_, f32[72,128]{1,0:T(8,128)S(1)} %get-tuple-element.53.power_ref.rest_3_), custom_call_target="tpu_custom_call" | custom-call | flops 19660800 | bytes 12000000 | tf_op jit(solution)/shard_map/pallas_call | solution.py:495
  14.8 0.1 collective-permute-done.4.rest_3_.hl0_ref
  14.9 0.2 collective-permute-done.3.rest_2_.rest_5_
  15.1 0.4 collective-permute-done.5.rest_4_.hr0_ref
  15.5 0.9 %shard_map.102 = (f32[320,128]{1,0:T(8,128)S(1)}, f32[320,128]{1,0:T(8,128)S(1)}, f32[320,128]{1,0:T(8,128)S(1)}, f32[10,512,128]{2,1,0:T(8,128)S(1)}, f32[656,1...) custom-call(f32[640,128]{1,0:T(8,128)S(1)} %collective-permute-done., ...), custom_call_target="tpu_custom_call" | custom-call | tf_op jit(solution)/shard_map/pallas_call | solution.py:495
  16.4 1.3 %collective-permute-start.6 = (f32[656,128]{1,0:T(8,128)S(1)}, f32[656,128]{1,0:T(8,128)S(1)}, u32[]{:S(2)}, u32[]{:S(2)}) collective-permute-start(f32[656,128]{1,0:T(8,128)S(1)} %get-tuple-element.56), channel_id=1, source_target_pairs={{3,0},{7,4},{11,8},{15,12},{19,16},{23,20},{27,24},{31,28}} | collective-permute-start | bytes 1007624 | tf_op jit(solution)/shard_map/ppermute | solution.py:522
  17.7 0.3 collective-permute-start.7
  18.0 1.7 %collective-permute-start.8 = (f32[320,128]{1,0:T(8,128)S(1)}, f32[320,128]{1,0:T(8,128)S(1)}, u32[]{:S(2)}, u32[]{:S(2)}) collective-permute-start(f32[320,128]{1,0:T(8,128)S(1)} %get-tuple-element.63), channel_id=1, source_target_pairs={{1,17},{3,19},{5,21},{7,23},{9,25},{11,27},{13,29},{15,31},{17,1},... | collective-permute-start | bytes 491528 | tf_op jit(solution)/shard_map/ppermute | solution.py:522
  19.7 2.7 %collective-permute-start.9 = (f32[320,128]{1,0:T(8,128)S(1)}, f32[320,128]{1,0:T(8,128)S(1)}, u32[]{:S(2)}, u32[]{:S(2)}) collective-permute-start(f32[320,128]{1,0:T(8,128)S(1)} %get-tuple-element.64), channel_id=1, source_target_pairs={{1,9},{3,11},{5,13},{7,15},{9,17},{11,19},{13,21},{15,23},{17,25},... | collective-permute-start | bytes 491528 | tf_op jit(solution)/shard_map/ppermute | solution.py:522
  22.4 2.8 %shard_map.103.part_ref = f32[10,512,128]{2,1,0:T(8,128)S(1)} custom-call(f32[10,512,128]{2,1,0:T(8,128)S(1)} %get-tuple-element.42.q_ref.rest_6_, f32[10,512,128]{2,1,0:T(8,128)S(1)} %get-tuple-element.55.q1_ref, f32[2,512,128]{2,1,0:T(8,128)S(1)} %get-tuple-element.51.vel_ref.rest_7_, f32[80,240]{1,0:T(8,128)S(1)} %get-tuple-element.52.a_ref.rest_2_, ...), custom_call_target="tpu_custom_call" | custom-call | flops 19660800 | bytes 12000000 | tf_op jit(solution)/shard_map/pallas_call | solution.py:495
  25.2 0.6 %collective-permute-done.6.refs_1_ = f32[656,128]{1,0:T(8,128)S(1)} collective-permute-done((f32[656,128]{1,0:T(8,128)S(1)}, f32[656,128]{1,0:T(8,128)S(1)}, u32[]{:S(2)}, u32[]{:S(2)}) %collective-permute-start.6) | collective-permute-done | bytes 335904 | tf_op jit(solution)/shard_map/ppermute | solution.py:522
  25.8 1.3 %collective-permute-start.14 = (f32[656,128]{1,0:T(8,128)S(1)}, f32[656,128]{1,0:T(8,128)S(1)}, u32[]{:S(2)}, u32[]{:S(2)}) collective-permute-start(f32[656,128]{1,0:T(8,128)S(1)} %shard_map.104.near_ref), channel_id=1, source_target_pairs={{4,0},{12,8},{20,16},{28,24}} | collective-permute-start | bytes 1007624 | tf_op jit(solution)/shard_map/ppermute | solution.py:522
  27.2 1.2 %collective-permute-done.10.rest_2_.rest_1_ = f32[320,128]{1,0:T(8,128)S(1)} collective-permute-done((f32[320,128]{1,0:T(8,128)S(1)}, f32[320,128]{1,0:T(8,128)S(1)}, u32[]{:S(2)}, u32[]{:S(2)}) %collective-permute-start.10) | collective-permute-done | bytes 163872 | tf_op jit(solution)/shard_map/ppermute | solution.py:522
  28.4 0.7 %collective-permute-start.11 = (f32[640,128]{1,0:T(8,128)S(1)}, f32[640,128]{1,0:T(8,128)S(1)}, u32[]{:S(2)}, u32[]{:S(2)}) collective-permute-start(f32[640,128]{1,0:T(8,128)S(1)} %shard_map.105.refs_0_), channel_id=1, source_target_pairs={{3,1},{7,5},{11,9},{15,13},{19,17},{23,21},{27,25},{31,29},{2,4},{... | collective-permute-start | bytes 983048 | tf_op jit(solution)/shard_map/ppermute | solution.py:522
  29.1 2.4 %collective-permute-start.12 = (f32[80,128]{1,0:T(8,128)S(1)}, f32[80,128]{1,0:T(8,128)S(1)}, u32[]{:S(2)}, u32[]{:S(2)}) collective-permute-start(f32[80,128]{1,0:T(8,128)S(1)} %get-tuple-element.69), channel_id=1, source_target_pairs={{0,8},{1,9},{2,10},{3,11},{4,12},{5,13},{6,14},{7,15},{8,16},{9,17... | collective-permute-start | bytes 122888 | tf_op jit(solution)/shard_map/ppermute | solution.py:522
  31.5 0.6 %collective-permute-start.13 = (f32[80,128]{1,0:T(8,128)S(1)}, f32[80,128]{1,0:T(8,128)S(1)}, u32[]{:S(2)}, u32[]{:S(2)}) collective-permute-start(f32[80,128]{1,0:T(8,128)S(1)} %get-tuple-element.70), channel_id=1, source_target_pairs={{0,24},{1,25},{2,26},{3,27},{4,28},{5,29},{6,30},{7,31},{8,0},{9,1... | collective-permute-start | bytes 122888 | tf_op jit(solution)/shard_map/ppermute | solution.py:522
  32.1 1.3 %collective-permute-start.16 = (f32[640,128]{1,0:T(8,128)S(1)}, f32[640,128]{1,0:T(8,128)S(1)}, u32[]{:S(2)}, u32[]{:S(2)}) collective-permute-start(f32[640,128]{1,0:T(8,128)S(1)} %shard_map.106.pair_ref), channel_id=1, source_target_pairs={{5,0},{13,8},{21,16},{29,24}} | collective-permute-start | bytes 983048 | tf_op jit(solution)/shard_map/ppermute | solution.py:522
  33.4 0.7 %collective-permute-done.12.hl_ref = f32[80,128]{1,0:T(8,128)S(1)} collective-permute-done((f32[80,128]{1,0:T(8,128)S(1)}, f32[80,128]{1,0:T(8,128)S(1)}, u32[]{:S(2)}, u32[]{:S(2)}) %collective-permute-start.12) | collective-permute-done | bytes 40992 | tf_op jit(solution)/shard_map/ppermute | solution.py:522
  34.1 1.3 %collective-permute-done.13.hr_ref = f32[80,128]{1,0:T(8,128)S(1)} collective-permute-done((f32[80,128]{1,0:T(8,128)S(1)}, f32[80,128]{1,0:T(8,128)S(1)}, u32[]{:S(2)}, u32[]{:S(2)}) %collective-permute-start.13) | collective-permute-done | bytes 40992 | tf_op jit(solution)/shard_map/ppermute | solution.py:522
  35.5 0.4 collective-permute-done.14.far_ref
  35.9 0.1 shard_map.107
  36.0 3.8 %collective-permute-start.15 = (f32[640,128]{1,0:T(8,128)S(1)}, f32[640,128]{1,0:T(8,128)S(1)}, u32[]{:S(2)}, u32[]{:S(2)}) collective-permute-start(f32[640,128]{1,0:T(8,128)S(1)} %get-tuple-element.78), channel_id=1, source_target_pairs={{0,1},{1,0},{2,3},{3,2},{4,5},{5,4},{6,7},{7,6},{8,9},{9,8},{10,11... | collective-permute-start | bytes 983048 | tf_op jit(solution)/shard_map/ppermute | solution.py:522
  39.8 2.2 %shard_map.108 = (f32[10,512,128]{2,1,0:T(8,128)}, f32[640,128]{1,0:T(8,128)S(1)}) custom-call(f32[10,512,128]{2,1,0:T(8,128)S(1)} %shard_map.103.part_ref, f32[10,512,128]{2,1,0:T(8,128)S(1)} %get-tuple-element.42.q_ref.rest_6_, f32[10,512,128]{2,1,0:T(8,128)S(1)} %get-tuple-element.55.q1_ref, f32[2,512,128]{2,1,0:T(8,128)S(1)} %get-tuple-element.51.vel_ref.rest_7_, ...), custom_call_target="tpu_custom_call" | custom-call | flops 19660800 | bytes 12000000 | tf_op jit(solution)/shard_map/pallas_call | solution.py:495
  42.1 1.0 %collective-permute-done.16.far_ref = f32[640,128]{1,0:T(8,128)S(1)} collective-permute-done((f32[640,128]{1,0:T(8,128)S(1)}, f32[640,128]{1,0:T(8,128)S(1)}, u32[]{:S(2)}, u32[]{:S(2)}) %collective-permute-start.16) | collective-permute-done | bytes 327712 | tf_op jit(solution)/shard_map/ppermute | solution.py:522
  43.0 1.0 %shard_map.109 = f32[10,64,8,128]{3,2,1,0:T(8,128)} custom-call(f32[10,64,8,128]{3,2,1,0:T(8,128)} %bitcast.21, f32[640,128]{1,0:T(8,128)S(1)} %get-tuple-element.77.keep_ref, f32[640,128]{1,0:T(8,128)S(1)} %collective-permute-done.15.core_ref, f32[640,128]{1,0:T(8,128)S(1)} %collective-permute-done.16.far_ref), custom_call_target="tpu_custom_call", output_to_operand_aliasing={{}: (0, {})} | custom-call | tf_op jit(solution)/shard_map/pallas_call | solution.py:495
  (20 shorter events, 0.2 us)
Async XLA Ops:
  2.3 7.7 %collective-permute-start = (f32[640,128]{1,0:T(8,128)S(1)}, f32[640,128]{1,0:T(8,128)S(1)}, u32[]{:S(2)}, u32[]{:S(2)}) collective-permute-start(f32[640,128]{1,0:T(8,128)S(1)} %get-tuple-element.44), channel_id=1, source_target_pairs={{0,1},{1,0},{2,3},{3,2},{4,5},{5,4},{6,7},{7,6},{8,9},{9,8},{10,11... | collective-permute-start | bytes 983048 | tf_op jit(solution)/shard_map/ppermute | solution.py:522
  3.0 12.1 %collective-permute-start.1 = (f32[664,128]{1,0:T(8,128)S(1)}, f32[664,128]{1,0:T(8,128)S(1)}, u32[]{:S(2)}, u32[]{:S(2)}) collective-permute-start(f32[664,128]{1,0:T(8,128)S(1)} %get-tuple-element.46), channel_id=1, source_target_pairs={{1,17},{3,19},{5,21},{7,23},{9,25},{11,27},{13,29},{15,31},{17,1},... | collective-permute-start | bytes 1019912 | tf_op jit(solution)/shard_map/ppermute | solution.py:522
  5.4 9.5 %collective-permute-start.2 = (f32[344,128]{1,0:T(8,128)S(1)}, f32[344,128]{1,0:T(8,128)S(1)}, u32[]{:S(2)}, u32[]{:S(2)}) collective-permute-start(f32[344,128]{1,0:T(8,128)S(1)} %get-tuple-element.47), channel_id=1, source_target_pairs={{1,9},{3,11},{5,13},{7,15},{9,17},{11,19},{13,21},{15,23},{17,25},... | collective-permute-start | bytes 528392 | tf_op jit(solution)/shard_map/ppermute | solution.py:522
  6.9 8.2 %collective-permute-start.3 = (f32[344,128]{1,0:T(8,128)S(1)}, f32[344,128]{1,0:T(8,128)S(1)}, u32[]{:S(2)}, u32[]{:S(2)}) collective-permute-start(f32[344,128]{1,0:T(8,128)S(1)} %get-tuple-element.48), channel_id=1, source_target_pairs={{1,25},{3,27},{5,29},{7,31},{9,1},{11,3},{13,5},{15,7},{17,9},{19,... | collective-permute-start | bytes 528392 | tf_op jit(solution)/shard_map/ppermute | solution.py:522
  9.4 5.5 %collective-permute-start.4 = (f32[88,128]{1,0:T(8,128)S(1)}, f32[88,128]{1,0:T(8,128)S(1)}, u32[]{:S(2)}, u32[]{:S(2)}) collective-permute-start(f32[88,128]{1,0:T(8,128)S(1)} %get-tuple-element.49), channel_id=1, source_target_pairs={{0,8},{1,9},{2,10},{3,11},{4,12},{5,13},{6,14},{7,15},{8,16},{9,17... | collective-permute-start | bytes 135176 | tf_op jit(solution)/shard_map/ppermute | solution.py:522
  9.9 5.6 %collective-permute-start.5 = (f32[88,128]{1,0:T(8,128)S(1)}, f32[88,128]{1,0:T(8,128)S(1)}, u32[]{:S(2)}, u32[]{:S(2)}) collective-permute-start(f32[88,128]{1,0:T(8,128)S(1)} %get-tuple-element.50), channel_id=1, source_target_pairs={{0,24},{1,25},{2,26},{3,27},{4,28},{5,29},{6,30},{7,31},{8,0},{9,1... | collective-permute-start | bytes 135176 | tf_op jit(solution)/shard_map/ppermute | solution.py:522
  12.3 3.2 %copy-start = (f32[10,1,8192]{2,1,0:T(1,128)S(1)}, f32[10,1,8192]{2,1,0:T(1,128)}, u32[]{:S(2)}) copy-start(f32[10,1,8192]{2,1,0:T(1,128)} %param.12) | copy-start | bytes 983044
  12.3 3.2 %copy-start.1 = (s32[8,1]{0,1:T(1,128)S(1)}, s32[8,1]{0,1:T(1,128)}, u32[]{:S(2)}) copy-start(s32[8,1]{0,1:T(1,128)} %param.17) | copy-start | bytes 100
  12.3 3.2 %copy-start.2 = (s32[8]{0:T(128)S(1)}, s32[8]{0:T(128)}, u32[]{:S(2)}) copy-start(s32[8]{0:T(128)} %rest_11_.1) | copy-start | bytes 100
  12.3 3.2 %copy-start.3 = (s32[8]{0:T(128)S(1)}, s32[8]{0:T(128)}, u32[]{:S(2)}) copy-start(s32[8]{0:T(128)} %rest_12_.1) | copy-start | bytes 100
  16.4 9.4 %collective-permute-start.6 = (f32[656,128]{1,0:T(8,128)S(1)}, f32[656,128]{1,0:T(8,128)S(1)}, u32[]{:S(2)}, u32[]{:S(2)}) collective-permute-start(f32[656,128]{1,0:T(8,128)S(1)} %get-tuple-element.56), channel_id=1, source_target_pairs={{3,0},{7,4},{11,8},{15,12},{19,16},{23,20},{27,24},{31,28}} | collective-permute-start | bytes 1007624 | tf_op jit(solution)/shard_map/ppermute | solution.py:522
  17.7 8.1 %collective-permute-start.7 = (f32[656,128]{1,0:T(8,128)S(1)}, f32[656,128]{1,0:T(8,128)S(1)}, u32[]{:S(2)}, u32[]{:S(2)}) collective-permute-start(f32[656,128]{1,0:T(8,128)S(1)} %get-tuple-element.56), channel_id=1, source_target_pairs={{0,1},{1,0},{2,3},{3,2},{4,5},{5,4},{6,7},{7,6},{8,9},{9,8},{10,11... | collective-permute-start | bytes 1007624 | tf_op jit(solution)/shard_map/ppermute | solution.py:522
  18.0 9.2 %collective-permute-start.8 = (f32[320,128]{1,0:T(8,128)S(1)}, f32[320,128]{1,0:T(8,128)S(1)}, u32[]{:S(2)}, u32[]{:S(2)}) collective-permute-start(f32[320,128]{1,0:T(8,128)S(1)} %get-tuple-element.63), channel_id=1, source_target_pairs={{1,17},{3,19},{5,21},{7,23},{9,25},{11,27},{13,29},{15,31},{17,1},... | collective-permute-start | bytes 491528 | tf_op jit(solution)/shard_map/ppermute | solution.py:522
  19.7 7.5 %collective-permute-start.9 = (f32[320,128]{1,0:T(8,128)S(1)}, f32[320,128]{1,0:T(8,128)S(1)}, u32[]{:S(2)}, u32[]{:S(2)}) collective-permute-start(f32[320,128]{1,0:T(8,128)S(1)} %get-tuple-element.64), channel_id=1, source_target_pairs={{1,9},{3,11},{5,13},{7,15},{9,17},{11,19},{13,21},{15,23},{17,25},... | collective-permute-start | bytes 491528 | tf_op jit(solution)/shard_map/ppermute | solution.py:522
  22.4 6.0 %collective-permute-start.10 = (f32[320,128]{1,0:T(8,128)S(1)}, f32[320,128]{1,0:T(8,128)S(1)}, u32[]{:S(2)}, u32[]{:S(2)}) collective-permute-start(f32[320,128]{1,0:T(8,128)S(1)} %get-tuple-element.65), channel_id=1, source_target_pairs={{1,25},{3,27},{5,29},{7,31},{9,1},{11,3},{13,5},{15,7},{17,9},{19,... | collective-permute-start | bytes 491528 | tf_op jit(solution)/shard_map/ppermute | solution.py:522
  25.8 10.1 %collective-permute-start.14 = (f32[656,128]{1,0:T(8,128)S(1)}, f32[656,128]{1,0:T(8,128)S(1)}, u32[]{:S(2)}, u32[]{:S(2)}) collective-permute-start(f32[656,128]{1,0:T(8,128)S(1)} %shard_map.104.near_ref), channel_id=1, source_target_pairs={{4,0},{12,8},{20,16},{28,24}} | collective-permute-start | bytes 1007624 | tf_op jit(solution)/shard_map/ppermute | solution.py:522
  28.4 3.7 %collective-permute-start.11 = (f32[640,128]{1,0:T(8,128)S(1)}, f32[640,128]{1,0:T(8,128)S(1)}, u32[]{:S(2)}, u32[]{:S(2)}) collective-permute-start(f32[640,128]{1,0:T(8,128)S(1)} %shard_map.105.refs_0_), channel_id=1, source_target_pairs={{3,1},{7,5},{11,9},{15,13},{19,17},{23,21},{27,25},{31,29},{2,4},{... | collective-permute-start | bytes 983048 | tf_op jit(solution)/shard_map/ppermute | solution.py:522
  29.1 5.0 %collective-permute-start.12 = (f32[80,128]{1,0:T(8,128)S(1)}, f32[80,128]{1,0:T(8,128)S(1)}, u32[]{:S(2)}, u32[]{:S(2)}) collective-permute-start(f32[80,128]{1,0:T(8,128)S(1)} %get-tuple-element.69), channel_id=1, source_target_pairs={{0,8},{1,9},{2,10},{3,11},{4,12},{5,13},{6,14},{7,15},{8,16},{9,17... | collective-permute-start | bytes 122888 | tf_op jit(solution)/shard_map/ppermute | solution.py:522
  31.5 4.0 %collective-permute-start.13 = (f32[80,128]{1,0:T(8,128)S(1)}, f32[80,128]{1,0:T(8,128)S(1)}, u32[]{:S(2)}, u32[]{:S(2)}) collective-permute-start(f32[80,128]{1,0:T(8,128)S(1)} %get-tuple-element.70), channel_id=1, source_target_pairs={{0,24},{1,25},{2,26},{3,27},{4,28},{5,29},{6,30},{7,31},{8,0},{9,1... | collective-permute-start | bytes 122888 | tf_op jit(solution)/shard_map/ppermute | solution.py:522
  32.1 10.9 %collective-permute-start.16 = (f32[640,128]{1,0:T(8,128)S(1)}, f32[640,128]{1,0:T(8,128)S(1)}, u32[]{:S(2)}, u32[]{:S(2)}) collective-permute-start(f32[640,128]{1,0:T(8,128)S(1)} %shard_map.106.pair_ref), channel_id=1, source_target_pairs={{5,0},{13,8},{21,16},{29,24}} | collective-permute-start | bytes 983048 | tf_op jit(solution)/shard_map/ppermute | solution.py:522
  36.0 7.0 %collective-permute-start.15 = (f32[640,128]{1,0:T(8,128)S(1)}, f32[640,128]{1,0:T(8,128)S(1)}, u32[]{:S(2)}, u32[]{:S(2)}) collective-permute-start(f32[640,128]{1,0:T(8,128)S(1)} %get-tuple-element.78), channel_id=1, source_target_pairs={{0,1},{1,0},{2,3},{3,2},{4,5},{5,4},{6,7},{7,6},{8,9},{9,8},{10,11... | collective-permute-start | bytes 983048 | tf_op jit(solution)/shard_map/ppermute | solution.py:522

commit v15 on v14

--- a/solution.py
+++ b/solution.py
@@ -548,7 +548,7 @@
 
     def compact(k):
         out = [((i, j, 1), ((i + shifts[k]) % n_az, j, 1)) for i, j in every]
-        return out + [((i, j, 0), (i, mate(0, j), 0) if k >= n_out - pieces else (i ^ 1, j, 0))
+        return out + [((i, j, 0), (i, mate(0, j), 0) if k >= n_out - pieces else (i ^ (n_az // 2), j, 0))
                       for i, j in every]
 
     q, vel = view(cells[0]), view(speeds[0])

time: 44.6 us -> 44.7 us (level); the launches traced: 44 us -> 44.5 us
  waiting for transfers between devices: 5.93 us -> 9.29 us
  starting transfers between devices: 26.1 us -> 23.3 us
    ppermute x17, waiting for transfers between devices: 5.93 us -> 9.29 us  [send(): return lax.ppermute(x, AXES, [(number(*a), number(*b)) for a, b in route])]
    ppermute x17, starting transfers between devices: 26.1 us -> 23.3 us  [send(): return lax.ppermute(x, AXES, [(number(*a), number(*b)) for a, b in route])]
where the time goes in v15:
time: 44.7 us; the launch traced here: 44.5 us
  starting transfers between devices  23.3 us (52%)
  Pallas kernels  11.8 us (26%)
  waiting for transfers between devices  9.29 us (21%)
    ppermute x17, starting transfers between devices, send(): return lax.ppermute(x, AXES, [(number(*a), number(*b)) for a, b in route])  23.3 us
    pallas_call x10, Pallas kernels, call(): pl.pallas_call(kernel, in_specs=[pl.BlockSpec(memory_space=SPACES[k]) for...  11.8 us
    ppermute x17, waiting for transfers between devices, send(): return lax.ppermute(x, AXES, [(number(*a), number(*b)) for a, b in route])  9.29 us
  transfers between devices with their start and end apart: 17, of which 9 were waited for; matrix products, arithmetic and copies ran while one was open for 0% of the time, Pallas kernels for 17%

profile of v15, /device:TPU:0, one launch (start us, length us, event | category | flops | bytes accessed | tf_op | source)
XLA Modules:
  0.0 44.5 jit_solution(12160183404348029972)
XLA Ops:
  0.0 2.2 %shard_map.100 = (f32[664,128]{1,0:T(8,128)S(1)}, f32[344,128]{1,0:T(8,128)S(1)}, f32[344,128]{1,0:T(8,128)S(1)}, f32[10,512,128]{2,1,0:T(8,128)S(1)}, f32[2,512...) custom-call(f32[10,512,128]{2,1,0:T(8,128)} %bitcast.20, ...), custom_call_target="tpu_custom_call" | custom-call | tf_op jit(solution)/shard_map/pallas_call | solution.py:495
  2.3 0.8 %collective-permute-start = (f32[640,128]{1,0:T(8,128)S(1)}, f32[640,128]{1,0:T(8,128)S(1)}, u32[]{:S(2)}, u32[]{:S(2)}) collective-permute-start(f32[640,128]{1,0:T(8,128)S(1)} %get-tuple-element.44), channel_id=1, source_target_pairs={{0,1},{1,0},{2,3},{3,2},{4,5},{5,4},{6,7},{7,6},{8,9},{9,8},{10,11... | collective-permute-start | bytes 983048 | tf_op jit(solution)/shard_map/ppermute | solution.py:522
  3.0 2.4 %collective-permute-start.1 = (f32[664,128]{1,0:T(8,128)S(1)}, f32[664,128]{1,0:T(8,128)S(1)}, u32[]{:S(2)}, u32[]{:S(2)}) collective-permute-start(f32[664,128]{1,0:T(8,128)S(1)} %get-tuple-element.46), channel_id=1, source_target_pairs={{1,17},{3,19},{5,21},{7,23},{9,25},{11,27},{13,29},{15,31},{17,1},... | collective-permute-start | bytes 1019912 | tf_op jit(solution)/shard_map/ppermute | solution.py:522
  5.4 1.5 %collective-permute-start.2 = (f32[344,128]{1,0:T(8,128)S(1)}, f32[344,128]{1,0:T(8,128)S(1)}, u32[]{:S(2)}, u32[]{:S(2)}) collective-permute-start(f32[344,128]{1,0:T(8,128)S(1)} %get-tuple-element.47), channel_id=1, source_target_pairs={{1,9},{3,11},{5,13},{7,15},{9,17},{11,19},{13,21},{15,23},{17,25},... | collective-permute-start | bytes 528392 | tf_op jit(solution)/shard_map/ppermute | solution.py:522
  6.9 2.5 %collective-permute-start.3 = (f32[344,128]{1,0:T(8,128)S(1)}, f32[344,128]{1,0:T(8,128)S(1)}, u32[]{:S(2)}, u32[]{:S(2)}) collective-permute-start(f32[344,128]{1,0:T(8,128)S(1)} %get-tuple-element.48), channel_id=1, source_target_pairs={{1,25},{3,27},{5,29},{7,31},{9,1},{11,3},{13,5},{15,7},{17,9},{19,... | collective-permute-start | bytes 528392 | tf_op jit(solution)/shard_map/ppermute | solution.py:522
  9.4 0.6 %collective-permute-start.4 = (f32[88,128]{1,0:T(8,128)S(1)}, f32[88,128]{1,0:T(8,128)S(1)}, u32[]{:S(2)}, u32[]{:S(2)}) collective-permute-start(f32[88,128]{1,0:T(8,128)S(1)} %get-tuple-element.49), channel_id=1, source_target_pairs={{0,8},{1,9},{2,10},{3,11},{4,12},{5,13},{6,14},{7,15},{8,16},{9,17... | collective-permute-start | bytes 135176 | tf_op jit(solution)/shard_map/ppermute | solution.py:522
  10.0 2.4 %collective-permute-start.5 = (f32[88,128]{1,0:T(8,128)S(1)}, f32[88,128]{1,0:T(8,128)S(1)}, u32[]{:S(2)}, u32[]{:S(2)}) collective-permute-start(f32[88,128]{1,0:T(8,128)S(1)} %get-tuple-element.50), channel_id=1, source_target_pairs={{0,24},{1,25},{2,26},{3,27},{4,28},{5,29},{6,30},{7,31},{8,0},{9,1... | collective-permute-start | bytes 135176 | tf_op jit(solution)/shard_map/ppermute | solution.py:522
  12.3 2.5 %shard_map.101.rest_5_ = f32[10,512,128]{2,1,0:T(8,128)S(1)} custom-call(f32[10,512,128]{2,1,0:T(8,128)S(1)} %get-tuple-element.42.q_ref.rest_6_, f32[2,512,128]{2,1,0:T(8,128)S(1)} %get-tuple-element.51.vel_ref.rest_7_, f32[80,240]{1,0:T(8,128)S(1)} %get-tuple-element.52.a_ref.rest_2_, f32[72,128]{1,0:T(8,128)S(1)} %get-tuple-element.53.power_ref.rest_3_), custom_call_target="tpu_custom_call" | custom-call | flops 19660800 | bytes 12000000 | tf_op jit(solution)/shard_map/pallas_call | solution.py:495
  14.8 0.1 collective-permute-done.4.rest_3_.hl0_ref
  14.9 0.2 collective-permute-done.3.rest_2_.rest_5_
  15.1 0.4 collective-permute-done.5.rest_4_.hr0_ref
  15.5 0.9 %shard_map.102 = (f32[320,128]{1,0:T(8,128)S(1)}, f32[320,128]{1,0:T(8,128)S(1)}, f32[320,128]{1,0:T(8,128)S(1)}, f32[10,512,128]{2,1,0:T(8,128)S(1)}, f32[656,1...) custom-call(f32[640,128]{1,0:T(8,128)S(1)} %collective-permute-done., ...), custom_call_target="tpu_custom_call" | custom-call | tf_op jit(solution)/shard_map/pallas_call | solution.py:495
  16.4 1.3 %collective-permute-start.6 = (f32[656,128]{1,0:T(8,128)S(1)}, f32[656,128]{1,0:T(8,128)S(1)}, u32[]{:S(2)}, u32[]{:S(2)}) collective-permute-start(f32[656,128]{1,0:T(8,128)S(1)} %get-tuple-element.56), channel_id=1, source_target_pairs={{3,0},{7,4},{11,8},{15,12},{19,16},{23,20},{27,24},{31,28}} | collective-permute-start | bytes 1007624 | tf_op jit(solution)/shard_map/ppermute | solution.py:522
  17.7 0.3 collective-permute-start.7
  18.0 1.0 %collective-permute-start.8 = (f32[320,128]{1,0:T(8,128)S(1)}, f32[320,128]{1,0:T(8,128)S(1)}, u32[]{:S(2)}, u32[]{:S(2)}) collective-permute-start(f32[320,128]{1,0:T(8,128)S(1)} %get-tuple-element.63), channel_id=1, source_target_pairs={{1,17},{3,19},{5,21},{7,23},{9,25},{11,27},{13,29},{15,31},{17,1},... | collective-permute-start | bytes 491528 | tf_op jit(solution)/shard_map/ppermute | solution.py:522
  19.0 2.7 %collective-permute-start.9 = (f32[320,128]{1,0:T(8,128)S(1)}, f32[320,128]{1,0:T(8,128)S(1)}, u32[]{:S(2)}, u32[]{:S(2)}) collective-permute-start(f32[320,128]{1,0:T(8,128)S(1)} %get-tuple-element.64), channel_id=1, source_target_pairs={{1,9},{3,11},{5,13},{7,15},{9,17},{11,19},{13,21},{15,23},{17,25},... | collective-permute-start | bytes 491528 | tf_op jit(solution)/shard_map/ppermute | solution.py:522
  21.7 2.8 %shard_map.103.part_ref = f32[10,512,128]{2,1,0:T(8,128)S(1)} custom-call(f32[10,512,128]{2,1,0:T(8,128)S(1)} %get-tuple-element.42.q_ref.rest_6_, f32[10,512,128]{2,1,0:T(8,128)S(1)} %get-tuple-element.55.q1_ref, f32[2,512,128]{2,1,0:T(8,128)S(1)} %get-tuple-element.51.vel_ref.rest_7_, f32[80,240]{1,0:T(8,128)S(1)} %get-tuple-element.52.a_ref.rest_2_, ...), custom_call_target="tpu_custom_call" | custom-call | flops 19660800 | bytes 12000000 | tf_op jit(solution)/shard_map/pallas_call | solution.py:495
  24.5 2.0 %collective-permute-done.6.refs_1_ = f32[656,128]{1,0:T(8,128)S(1)} collective-permute-done((f32[656,128]{1,0:T(8,128)S(1)}, f32[656,128]{1,0:T(8,128)S(1)}, u32[]{:S(2)}, u32[]{:S(2)}) %collective-permute-start.6) | collective-permute-done | bytes 335904 | tf_op jit(solution)/shard_map/ppermute | solution.py:522
  26.5 1.3 %collective-permute-start.14 = (f32[656,128]{1,0:T(8,128)S(1)}, f32[656,128]{1,0:T(8,128)S(1)}, u32[]{:S(2)}, u32[]{:S(2)}) collective-permute-start(f32[656,128]{1,0:T(8,128)S(1)} %shard_map.104.near_ref), channel_id=1, source_target_pairs={{4,0},{12,8},{20,16},{28,24}} | collective-permute-start | bytes 1007624 | tf_op jit(solution)/shard_map/ppermute | solution.py:522
  27.9 0.5 %collective-permute-done.10.rest_2_.rest_1_ = f32[320,128]{1,0:T(8,128)S(1)} collective-permute-done((f32[320,128]{1,0:T(8,128)S(1)}, f32[320,128]{1,0:T(8,128)S(1)}, u32[]{:S(2)}, u32[]{:S(2)}) %collective-permute-start.10) | collective-permute-done | bytes 163872 | tf_op jit(solution)/shard_map/ppermute | solution.py:522
  28.4 0.7 %collective-permute-start.11 = (f32[640,128]{1,0:T(8,128)S(1)}, f32[640,128]{1,0:T(8,128)S(1)}, u32[]{:S(2)}, u32[]{:S(2)}) collective-permute-start(f32[640,128]{1,0:T(8,128)S(1)} %shard_map.105.refs_0_), channel_id=1, source_target_pairs={{3,1},{7,5},{11,9},{15,13},{19,17},{23,21},{27,25},{31,29},{2,4},{... | collective-permute-start | bytes 983048 | tf_op jit(solution)/shard_map/ppermute | solution.py:522
  29.1 1.9 %collective-permute-start.12 = (f32[80,128]{1,0:T(8,128)S(1)}, f32[80,128]{1,0:T(8,128)S(1)}, u32[]{:S(2)}, u32[]{:S(2)}) collective-permute-start(f32[80,128]{1,0:T(8,128)S(1)} %get-tuple-element.69), channel_id=1, source_target_pairs={{0,8},{1,9},{2,10},{3,11},{4,12},{5,13},{6,14},{7,15},{8,16},{9,17... | collective-permute-start | bytes 122888 | tf_op jit(solution)/shard_map/ppermute | solution.py:522
  31.0 1.1 %collective-permute-start.13 = (f32[80,128]{1,0:T(8,128)S(1)}, f32[80,128]{1,0:T(8,128)S(1)}, u32[]{:S(2)}, u32[]{:S(2)}) collective-permute-start(f32[80,128]{1,0:T(8,128)S(1)} %get-tuple-element.70), channel_id=1, source_target_pairs={{0,24},{1,25},{2,26},{3,27},{4,28},{5,29},{6,30},{7,31},{8,0},{9,1... | collective-permute-start | bytes 122888 | tf_op jit(solution)/shard_map/ppermute | solution.py:522
  32.1 1.3 %collective-permute-start.16 = (f32[640,128]{1,0:T(8,128)S(1)}, f32[640,128]{1,0:T(8,128)S(1)}, u32[]{:S(2)}, u32[]{:S(2)}) collective-permute-start(f32[640,128]{1,0:T(8,128)S(1)} %shard_map.106.pair_ref), channel_id=1, source_target_pairs={{5,0},{13,8},{21,16},{29,24}} | collective-permute-start | bytes 983048 | tf_op jit(solution)/shard_map/ppermute | solution.py:522
  33.4 0.6 %collective-permute-done.12.hl_ref = f32[80,128]{1,0:T(8,128)S(1)} collective-permute-done((f32[80,128]{1,0:T(8,128)S(1)}, f32[80,128]{1,0:T(8,128)S(1)}, u32[]{:S(2)}, u32[]{:S(2)}) %collective-permute-start.12) | collective-permute-done | bytes 40992 | tf_op jit(solution)/shard_map/ppermute | solution.py:522
  34.1 0.9 %collective-permute-done.13.hr_ref = f32[80,128]{1,0:T(8,128)S(1)} collective-permute-done((f32[80,128]{1,0:T(8,128)S(1)}, f32[80,128]{1,0:T(8,128)S(1)}, u32[]{:S(2)}, u32[]{:S(2)}) %collective-permute-start.13) | collective-permute-done | bytes 40992 | tf_op jit(solution)/shard_map/ppermute | solution.py:522
  35.0 1.6 %collective-permute-done.14.far_ref = f32[656,128]{1,0:T(8,128)S(1)} collective-permute-done((f32[656,128]{1,0:T(8,128)S(1)}, f32[656,128]{1,0:T(8,128)S(1)}, u32[]{:S(2)}, u32[]{:S(2)}) %collective-permute-start.14) | collective-permute-done | bytes 335904 | tf_op jit(solution)/shard_map/ppermute | solution.py:522
  36.6 0.1 shard_map.107
  36.7 1.7 %collective-permute-start.15 = (f32[640,128]{1,0:T(8,128)S(1)}, f32[640,128]{1,0:T(8,128)S(1)}, u32[]{:S(2)}, u32[]{:S(2)}) collective-permute-start(f32[640,128]{1,0:T(8,128)S(1)} %get-tuple-element.78), channel_id=1, source_target_pairs={{0,1},{1,0},{2,3},{3,2},{4,5},{5,4},{6,7},{7,6},{8,9},{9,8},{10,11... | collective-permute-start | bytes 983048 | tf_op jit(solution)/shard_map/ppermute | solution.py:522
  38.4 2.2 %shard_map.108 = (f32[10,512,128]{2,1,0:T(8,128)}, f32[640,128]{1,0:T(8,128)S(1)}) custom-call(f32[10,512,128]{2,1,0:T(8,128)S(1)} %shard_map.103.part_ref, f32[10,512,128]{2,1,0:T(8,128)S(1)} %get-tuple-element.42.q_ref.rest_6_, f32[10,512,128]{2,1,0:T(8,128)S(1)} %get-tuple-element.55.q1_ref, f32[2,512,128]{2,1,0:T(8,128)S(1)} %get-tuple-element.51.vel_ref.rest_7_, ...), custom_call_target="tpu_custom_call" | custom-call | flops 19660800 | bytes 12000000 | tf_op jit(solution)/shard_map/pallas_call | solution.py:495
  40.7 2.9 %collective-permute-done.16.far_ref = f32[640,128]{1,0:T(8,128)S(1)} collective-permute-done((f32[640,128]{1,0:T(8,128)S(1)}, f32[640,128]{1,0:T(8,128)S(1)}, u32[]{:S(2)}, u32[]{:S(2)}) %collective-permute-start.16) | collective-permute-done | bytes 327712 | tf_op jit(solution)/shard_map/ppermute | solution.py:522
  43.6 1.0 %shard_map.109 = f32[10,64,8,128]{3,2,1,0:T(8,128)} custom-call(f32[10,64,8,128]{3,2,1,0:T(8,128)} %bitcast.21, f32[640,128]{1,0:T(8,128)S(1)} %get-tuple-element.77.keep_ref, f32[640,128]{1,0:T(8,128)S(1)} %collective-permute-done.15.core_ref, f32[640,128]{1,0:T(8,128)S(1)} %collective-permute-done.16.far_ref), custom_call_target="tpu_custom_call", output_to_operand_aliasing={{}: (0, {})} | custom-call | tf_op jit(solution)/shard_map/pallas_call | solution.py:495
  (20 shorter events, 0.2 us)
Async XLA Ops:
  2.3 7.7 %collective-permute-start = (f32[640,128]{1,0:T(8,128)S(1)}, f32[640,128]{1,0:T(8,128)S(1)}, u32[]{:S(2)}, u32[]{:S(2)}) collective-permute-start(f32[640,128]{1,0:T(8,128)S(1)} %get-tuple-element.44), channel_id=1, source_target_pairs={{0,1},{1,0},{2,3},{3,2},{4,5},{5,4},{6,7},{7,6},{8,9},{9,8},{10,11... | collective-permute-start | bytes 983048 | tf_op jit(solution)/shard_map/ppermute | solution.py:522
  3.0 12.1 %collective-permute-start.1 = (f32[664,128]{1,0:T(8,128)S(1)}, f32[664,128]{1,0:T(8,128)S(1)}, u32[]{:S(2)}, u32[]{:S(2)}) collective-permute-start(f32[664,128]{1,0:T(8,128)S(1)} %get-tuple-element.46), channel_id=1, source_target_pairs={{1,17},{3,19},{5,21},{7,23},{9,25},{11,27},{13,29},{15,31},{17,1},... | collective-permute-start | bytes 1019912 | tf_op jit(solution)/shard_map/ppermute | solution.py:522
  5.4 9.5 %collective-permute-start.2 = (f32[344,128]{1,0:T(8,128)S(1)}, f32[344,128]{1,0:T(8,128)S(1)}, u32[]{:S(2)}, u32[]{:S(2)}) collective-permute-start(f32[344,128]{1,0:T(8,128)S(1)} %get-tuple-element.47), channel_id=1, source_target_pairs={{1,9},{3,11},{5,13},{7,15},{9,17},{11,19},{13,21},{15,23},{17,25},... | collective-permute-start | bytes 528392 | tf_op jit(solution)/shard_map/ppermute | solution.py:522
  6.9 8.2 %collective-permute-start.3 = (f32[344,128]{1,0:T(8,128)S(1)}, f32[344,128]{1,0:T(8,128)S(1)}, u32[]{:S(2)}, u32[]{:S(2)}) collective-permute-start(f32[344,128]{1,0:T(8,128)S(1)} %get-tuple-element.48), channel_id=1, source_target_pairs={{1,25},{3,27},{5,29},{7,31},{9,1},{11,3},{13,5},{15,7},{17,9},{19,... | collective-permute-start | bytes 528392 | tf_op jit(solution)/shard_map/ppermute | solution.py:522
  9.4 5.5 %collective-permute-start.4 = (f32[88,128]{1,0:T(8,128)S(1)}, f32[88,128]{1,0:T(8,128)S(1)}, u32[]{:S(2)}, u32[]{:S(2)}) collective-permute-start(f32[88,128]{1,0:T(8,128)S(1)} %get-tuple-element.49), channel_id=1, source_target_pairs={{0,8},{1,9},{2,10},{3,11},{4,12},{5,13},{6,14},{7,15},{8,16},{9,17... | collective-permute-start | bytes 135176 | tf_op jit(solution)/shard_map/ppermute | solution.py:522
  10.0 5.5 %collective-permute-start.5 = (f32[88,128]{1,0:T(8,128)S(1)}, f32[88,128]{1,0:T(8,128)S(1)}, u32[]{:S(2)}, u32[]{:S(2)}) collective-permute-start(f32[88,128]{1,0:T(8,128)S(1)} %get-tuple-element.50), channel_id=1, source_target_pairs={{0,24},{1,25},{2,26},{3,27},{4,28},{5,29},{6,30},{7,31},{8,0},{9,1... | collective-permute-start | bytes 135176 | tf_op jit(solution)/shard_map/ppermute | solution.py:522
  12.3 3.2 %copy-start = (f32[10,1,8192]{2,1,0:T(1,128)S(1)}, f32[10,1,8192]{2,1,0:T(1,128)}, u32[]{:S(2)}) copy-start(f32[10,1,8192]{2,1,0:T(1,128)} %param.12) | copy-start | bytes 983044
  12.3 3.2 %copy-start.1 = (s32[8,1]{0,1:T(1,128)S(1)}, s32[8,1]{0,1:T(1,128)}, u32[]{:S(2)}) copy-start(s32[8,1]{0,1:T(1,128)} %param.17) | copy-start | bytes 100
  12.3 3.2 %copy-start.2 = (s32[8]{0:T(128)S(1)}, s32[8]{0:T(128)}, u32[]{:S(2)}) copy-start(s32[8]{0:T(128)} %rest_11_.1) | copy-start | bytes 100
  12.3 3.2 %copy-start.3 = (s32[8]{0:T(128)S(1)}, s32[8]{0:T(128)}, u32[]{:S(2)}) copy-start(s32[8]{0:T(128)} %rest_12_.1) | copy-start | bytes 100
  16.4 10.1 %collective-permute-start.6 = (f32[656,128]{1,0:T(8,128)S(1)}, f32[656,128]{1,0:T(8,128)S(1)}, u32[]{:S(2)}, u32[]{:S(2)}) collective-permute-start(f32[656,128]{1,0:T(8,128)S(1)} %get-tuple-element.56), channel_id=1, source_target_pairs={{3,0},{7,4},{11,8},{15,12},{19,16},{23,20},{27,24},{31,28}} | collective-permute-start | bytes 1007624 | tf_op jit(solution)/shard_map/ppermute | solution.py:522
  17.7 8.8 %collective-permute-start.7 = (f32[656,128]{1,0:T(8,128)S(1)}, f32[656,128]{1,0:T(8,128)S(1)}, u32[]{:S(2)}, u32[]{:S(2)}) collective-permute-start(f32[656,128]{1,0:T(8,128)S(1)} %get-tuple-element.56), channel_id=1, source_target_pairs={{0,1},{1,0},{2,3},{3,2},{4,5},{5,4},{6,7},{7,6},{8,9},{9,8},{10,11... | collective-permute-start | bytes 1007624 | tf_op jit(solution)/shard_map/ppermute | solution.py:522
  18.0 9.9 %collective-permute-start.8 = (f32[320,128]{1,0:T(8,128)S(1)}, f32[320,128]{1,0:T(8,128)S(1)}, u32[]{:S(2)}, u32[]{:S(2)}) collective-permute-start(f32[320,128]{1,0:T(8,128)S(1)} %get-tuple-element.63), channel_id=1, source_target_pairs={{1,17},{3,19},{5,21},{7,23},{9,25},{11,27},{13,29},{15,31},{17,1},... | collective-permute-start | bytes 491528 | tf_op jit(solution)/shard_map/ppermute | solution.py:522
  19.0 8.9 %collective-permute-start.9 = (f32[320,128]{1,0:T(8,128)S(1)}, f32[320,128]{1,0:T(8,128)S(1)}, u32[]{:S(2)}, u32[]{:S(2)}) collective-permute-start(f32[320,128]{1,0:T(8,128)S(1)} %get-tuple-element.64), channel_id=1, source_target_pairs={{1,9},{3,11},{5,13},{7,15},{9,17},{11,19},{13,21},{15,23},{17,25},... | collective-permute-start | bytes 491528 | tf_op jit(solution)/shard_map/ppermute | solution.py:522
  21.7 6.7 %collective-permute-start.10 = (f32[320,128]{1,0:T(8,128)S(1)}, f32[320,128]{1,0:T(8,128)S(1)}, u32[]{:S(2)}, u32[]{:S(2)}) collective-permute-start(f32[320,128]{1,0:T(8,128)S(1)} %get-tuple-element.65), channel_id=1, source_target_pairs={{1,25},{3,27},{5,29},{7,31},{9,1},{11,3},{13,5},{15,7},{17,9},{19,... | collective-permute-start | bytes 491528 | tf_op jit(solution)/shard_map/ppermute | solution.py:522
  26.5 10.1 %collective-permute-start.14 = (f32[656,128]{1,0:T(8,128)S(1)}, f32[656,128]{1,0:T(8,128)S(1)}, u32[]{:S(2)}, u32[]{:S(2)}) collective-permute-start(f32[656,128]{1,0:T(8,128)S(1)} %shard_map.104.near_ref), channel_id=1, source_target_pairs={{4,0},{12,8},{20,16},{28,24}} | collective-permute-start | bytes 1007624 | tf_op jit(solution)/shard_map/ppermute | solution.py:522
  28.4 3.7 %collective-permute-start.11 = (f32[640,128]{1,0:T(8,128)S(1)}, f32[640,128]{1,0:T(8,128)S(1)}, u32[]{:S(2)}, u32[]{:S(2)}) collective-permute-start(f32[640,128]{1,0:T(8,128)S(1)} %shard_map.105.refs_0_), channel_id=1, source_target_pairs={{3,1},{7,5},{11,9},{15,13},{19,17},{23,21},{27,25},{31,29},{2,4},{... | collective-permute-start | bytes 983048 | tf_op jit(solution)/shard_map/ppermute | solution.py:522
  29.1 5.0 %collective-permute-start.12 = (f32[80,128]{1,0:T(8,128)S(1)}, f32[80,128]{1,0:T(8,128)S(1)}, u32[]{:S(2)}, u32[]{:S(2)}) collective-permute-start(f32[80,128]{1,0:T(8,128)S(1)} %get-tuple-element.69), channel_id=1, source_target_pairs={{0,8},{1,9},{2,10},{3,11},{4,12},{5,13},{6,14},{7,15},{8,16},{9,17... | collective-permute-start | bytes 122888 | tf_op jit(solution)/shard_map/ppermute | solution.py:522
  31.0 4.0 %collective-permute-start.13 = (f32[80,128]{1,0:T(8,128)S(1)}, f32[80,128]{1,0:T(8,128)S(1)}, u32[]{:S(2)}, u32[]{:S(2)}) collective-permute-start(f32[80,128]{1,0:T(8,128)S(1)} %get-tuple-element.70), channel_id=1, source_target_pairs={{0,24},{1,25},{2,26},{3,27},{4,28},{5,29},{6,30},{7,31},{8,0},{9,1... | collective-permute-start | bytes 122888 | tf_op jit(solution)/shard_map/ppermute | solution.py:522
  32.1 11.4 %collective-permute-start.16 = (f32[640,128]{1,0:T(8,128)S(1)}, f32[640,128]{1,0:T(8,128)S(1)}, u32[]{:S(2)}, u32[]{:S(2)}) collective-permute-start(f32[640,128]{1,0:T(8,128)S(1)} %shard_map.106.pair_ref), channel_id=1, source_target_pairs={{5,0},{13,8},{21,16},{29,24}} | collective-permute-start | bytes 983048 | tf_op jit(solution)/shard_map/ppermute | solution.py:522
  36.7 6.9 %collective-permute-start.15 = (f32[640,128]{1,0:T(8,128)S(1)}, f32[640,128]{1,0:T(8,128)S(1)}, u32[]{:S(2)}, u32[]{:S(2)}) collective-permute-start(f32[640,128]{1,0:T(8,128)S(1)} %get-tuple-element.78), channel_id=1, source_target_pairs={{0,1},{1,0},{2,3},{3,2},{4,5},{5,4},{6,7},{7,6},{8,9},{9,8},{10,11... | collective-permute-start | bytes 983048 | tf_op jit(solution)/shard_map/ppermute | solution.py:522
